TPU v7x, 32 devices: a whole 2x2x4 slice. The times are simulated.
32 devices in a mesh: row: 8 (over z, y), col: 4 (over x, core).
Axes of the slice: x: 2, y: 2, z: 4, core: 2. Of those that a mesh axis runs over, the one named last changes fastest.
Arguments:
- inv_interior: bfloat16 [64, 1024, 1024], P(('row', 'col')), may hold values from -1 to 3
- coupling: bfloat16 [64, 1024, 512], P(('row', 'col')), may hold values from -0.375 to 0.375
- boundary_stiff: bfloat16 [64, 512, 512], P(('row', 'col')), may hold values from -6 to 6
- mass_interior: float32 [64, 1024], P(('row', 'col')), may hold values from 0.5 to 2
- mass_boundary: float32 [64, 512], P(('row', 'col')), may hold values from 0.5 to 2
- block_map: int32 [64, 4], P(('row', 'col')), may hold values from 0 to 127, as said below
- modes: bfloat16 [16384, 1024], P('col', 'row'), may hold values from -0.046875 to 0.046875
Outputs:
- iface_stiff: bfloat16 [16384, 16384], P('row', 'col')
- iface_mass: bfloat16 [16384, 16384], P('row', 'col')
- reduced_stiff: float32 [1024, 1024], P(('row', 'col'))
- reduced_mass: float32 [1024, 1024], P(('row', 'col'))
- mass_diagonal: float32 [16384], P(('row', 'col'))
Inputs may be any that keep to these rules, and one draw needn't show every extreme that they name: Interface block p belongs to tile row p // 16 and tile column p // 32; the pair (block_map[s, a], block_map[s, b]) belongs to the tile of its row's tile row and its column's tile column. Over the 2 substructures of one device (aligned blocks of rows), no two triples (s, a, b) fall into the same tile, and in every draw some tile receives a pair from every device.
All inputs are finite; a program needn't handle non-finite values.
Results may differ from a plain program's by a relative error of at most 0.0058.
Values may be sent and summed in bfloat16 or wider, within the bound.
No kernel may reach another device: no remote copies, remote signals or barrier semaphores. Data moves between devices by JAX's collectives and lax.ppermute only.
A program may use at most 192 MiB of HBM per device.

v0:
```python
from typing import NamedTuple

import jax
import jax.numpy as jnp
from jax import lax
from jax.experimental import pallas as pl
from jax.experimental.pallas import tpu as pltpu
from jax.sharding import PartitionSpec as P


BLK = 128
EXTRA = 16
AXES = ("row", "col")
F32 = jnp.float32
BF16 = jnp.bfloat16
VMEM = pl.BlockSpec(memory_space=pltpu.VMEM)
SMEM = pl.BlockSpec(memory_space=pltpu.SMEM)
ANY = pl.BlockSpec(memory_space=pl.ANY)


class Sizes(NamedTuple):
    devices: int
    cols: int
    ratio: int
    row_blocks: int
    col_blocks: int
    share_blocks: int
    plane: int


def exchange(value):
    return lax.all_to_all(value, AXES, split_axis=0, concat_axis=0, tiled=True)


def quotient(value, size):
    return lax.shift_right_logical(value, jnp.int32(size.bit_length() - 1))


def remainder(value, size):
    return value & jnp.int32(size - 1)


def describe(block_map, sizes):
    local_subs, per_sub = block_map.shape

    def kernel(map_ref, out_ref):
        shape = out_ref.shape
        device = lax.broadcasted_iota(jnp.int32, shape, 0)
        field = lax.broadcasted_iota(jnp.int32, shape, 1)
        row = quotient(device, sizes.cols)
        col = remainder(device, sizes.cols)
        zero = jnp.zeros(shape, jnp.int32)
        wanted, share = zero, zero - 1
        slot = zero + sizes.row_blocks * sizes.col_blocks
        for s in range(local_subs):
            row_slot, col_slot = zero - 1, zero - 1
            for a in range(per_sub):
                block = map_ref[s, a]
                tile_row = quotient(block, sizes.row_blocks)
                wanted = jnp.where(
                    col * sizes.ratio + field == tile_row, remainder(block, sizes.col_blocks), wanted
                )
                share = jnp.where(
                    device == quotient(block, sizes.share_blocks),
                    remainder(block, sizes.share_blocks),
                    share,
                )
                row_slot = jnp.where(row == tile_row, remainder(block, sizes.row_blocks), row_slot)
                col_slot = jnp.where(
                    col == quotient(block, sizes.col_blocks),
                    remainder(block, sizes.col_blocks),
                    col_slot,
                )
            both = jnp.logical_and(row_slot >= 0, col_slot >= 0)
            slot = jnp.where(both, row_slot * sizes.col_blocks + col_slot, slot)
        out_ref[...] = jnp.where(
            field < sizes.ratio, wanted, jnp.where(field == sizes.ratio, slot, share)
        )

    return pl.pallas_call(
        kernel,
        out_shape=jax.ShapeDtypeStruct((sizes.devices, BLK), jnp.int32),
        in_specs=[SMEM],
        out_specs=VMEM,
        name="describe",
    )(block_map)


def pick_modes(table, modes, ratio):
    device_count = table.shape[0]
    width = modes.shape[2]

    def kernel(table_ref, modes_ref, out_ref):
        def one(device, carry):
            for h in range(ratio):
                out_ref[device, h] = modes_ref[table_ref[device, h]]
            return carry

        lax.fori_loop(0, device_count, one, 0, unroll=4)

    return pl.pallas_call(
        kernel,
        out_shape=jax.ShapeDtypeStruct((device_count, ratio, BLK, width), BF16),
        in_specs=[SMEM, VMEM],
        out_specs=VMEM,
        name="pick_modes",
    )(table, modes)


def condense(
    block_map, inv_interior, coupling, boundary_stiff, mass_interior, mass_boundary, sizes
):
    local_subs, interior, boundary = coupling.shape
    per_sub = boundary // BLK

    def kernel(
        map_ref,
        inv_ref,
        cpl_ref,
        stiff_ref,
        mi_ref,
        mb_ref,
        out_ref,
        k_ref,
        m_ref,
        d_ref,
    ):
        sub = pl.program_id(0)
        me = lax.axis_index("row") * sizes.cols + lax.axis_index("col")
        couple = cpl_ref[0]
        static_modes = (-jnp.dot(inv_ref[0], couple, preferred_element_type=F32)).astype(BF16)
        contract = (((0,), (0,)), ((), ()))
        stiff = stiff_ref[0].astype(F32) + lax.dot_general(
            couple, static_modes, contract, preferred_element_type=F32
        )
        weighted = (static_modes.astype(F32) * mi_ref[0]).astype(BF16)
        mass = lax.dot_general(static_modes, weighted, contract, preferred_element_type=F32)
        eye = lax.broadcasted_iota(jnp.int32, (BLK, BLK), 0) == lax.broadcasted_iota(
            jnp.int32, (BLK, BLK), 1
        )
        level = lax.broadcasted_iota(jnp.int32, (EXTRA, BLK), 0)
        for a in range(per_sub):
            block_a = map_ref[sub, a]
            rows = slice(a * BLK, (a + 1) * BLK)
            for b in range(per_sub):
                cols = slice(b * BLK, (b + 1) * BLK)
                owner = quotient(block_a, sizes.row_blocks) * sizes.cols + quotient(
                    map_ref[sub, b], sizes.col_blocks
                )
                owner = owner ^ me
                near, far = remainder(owner, sizes.plane), quotient(owner, sizes.plane)
                stiff_block = stiff[rows, cols].astype(BF16)
                mass_block = mass[rows, cols]
                if a == b:
                    diagonal = (
                        jnp.sum(jnp.where(eye, mass_block, 0.0), axis=0, keepdims=True)
                        + mb_ref[0, :, cols]
                    )
                    d_ref[0, :, cols] = diagonal
                    high = diagonal.astype(BF16).astype(F32)
                    middle = (diagonal - high).astype(BF16).astype(F32)
                    low = diagonal - high - middle
                    parts = jnp.where(level == 0, high, jnp.where(level == 1, middle, low))
                    share = quotient(block_a, sizes.share_blocks) ^ me
                    out_ref[
                        remainder(share, sizes.plane),
                        quotient(share, sizes.plane),
                        2 * BLK : 2 * BLK + EXTRA,
                    ] = parts.astype(BF16)
                    mass_block = jnp.where(eye, 0.0, mass_block)
                mass_block = mass_block.astype(BF16)
                out_ref[near, far, :BLK] = stiff_block
                out_ref[near, far, BLK : 2 * BLK] = mass_block
                k_ref[0, rows, cols] = stiff_block
                m_ref[0, rows, cols] = mass_block

    def piece(*shape):
        return pl.BlockSpec((1,) + shape, lambda s: (s, 0, 0))

    out_blocks = (sizes.plane, sizes.devices // sizes.plane, 2 * BLK + EXTRA, BLK)
    return pl.pallas_call(
        kernel,
        grid=(local_subs,),
        in_specs=[
            SMEM,
            piece(interior, interior),
            piece(interior, boundary),
            piece(boundary, boundary),
            piece(interior, 1),
            piece(1, boundary),
        ],
        out_specs=[
            pl.BlockSpec(out_blocks, lambda s: (0, 0, 0, 0)),
            piece(boundary, boundary),
            piece(boundary, boundary),
            piece(1, boundary),
        ],
        out_shape=[
            jax.ShapeDtypeStruct(out_blocks, BF16),
            jax.ShapeDtypeStruct((local_subs, boundary, boundary), BF16),
            jax.ShapeDtypeStruct((local_subs, boundary, boundary), BF16),
            jax.ShapeDtypeStruct((local_subs, 1, boundary), F32),
        ],
        name="condense",
    )(
        block_map,
        inv_interior,
        coupling,
        boundary_stiff,
        mass_interior[:, :, None],
        mass_boundary[:, None, :],
    )


def project(block_map, fetched, laid_out, matrix, diagonal, dims, row_blocks):
    z_size, y_size, x_size = dims
    local_subs, boundary, _ = matrix.shape
    depth = local_subs * boundary
    per_sub = boundary // BLK
    groups = z_size * y_size * x_size
    gathers = laid_out is None
    if gathers:
        row_count, _, ratio, _, width = fetched.shape
        modes = row_count * width
    else:
        modes = laid_out[0].shape[1]
    share = modes // (2 * groups)
    chunk = modes // 2
    pairs = chunk // (2 * share)

    def kernel(*refs):
        step = pl.program_id(0)
        if gathers:
            map_ref, in_ref, m_ref, send_ref, keep_ref, q_ref, t_ref, y_ref = refs

            @pl.when(step == 0)
            def _():
                for s in range(local_subs):
                    for a in range(per_sub):
                        tile_row = quotient(map_ref[s, a], row_blocks)
                        c = quotient(tile_row, ratio)
                        h = remainder(tile_row, ratio)
                        k = (s * per_sub + a) * BLK
                        for r in range(row_count):
                            block = in_ref[r, c, h]
                            q_ref[k : k + BLK, r * width : (r + 1) * width] = block
                            t_ref[r * width : (r + 1) * width, k : k + BLK] = block.T

            left_rows = pl.ds(pl.multiple_of(step * chunk, chunk), chunk)
        else:
            q_ref, t_ref, m_ref, d_ref, send_ref, keep_ref, y_ref = refs
            left_rows = slice(None)
        row, col = lax.axis_index("row"), lax.axis_index("col")
        my_z, my_y = quotient(row, y_size), remainder(row, y_size)
        my_x, my_core = quotient(col, 2), remainder(col, 2)
        for s in range(local_subs):
            span = slice(s * boundary, (s + 1) * boundary)
            left = t_ref[left_rows, span]
            y = jnp.dot(left, m_ref[s], preferred_element_type=F32)
            if diagonal is not None:
                y = y + left.astype(F32) * d_ref[s]
            y_ref[:, span] = y.astype(BF16)
        out = jnp.dot(y_ref[...], q_ref[...], preferred_element_type=F32)
        for i in range(pairs):
            group = step * pairs + i
            x = remainder(group, x_size)
            y = remainder(quotient(group, x_size), y_size)
            z = quotient(group, x_size * y_size)
            slot = ((y ^ my_y) * x_size + (x ^ my_x)) * z_size + (z ^ my_z)
            even = out[2 * i * share : (2 * i + 1) * share]
            odd = out[(2 * i + 1) * share : (2 * i + 2) * share]
            mine = my_core == 0
            keep_ref[slot] = jnp.where(mine, even, odd)
            send_ref[slot] = jnp.where(mine, odd, even).astype(BF16)

    def whole(*shape):
        return pl.BlockSpec(shape, lambda i: (0,) * len(shape))

    out_specs = [whole(groups, share, modes), whole(groups, share, modes)]
    out_shape = [
        jax.ShapeDtypeStruct((groups, share, modes), BF16),
        jax.ShapeDtypeStruct((groups, share, modes), F32),
    ]
    matrix_spec = whole(local_subs, boundary, boundary)
    if gathers:
        operands = (block_map, fetched, matrix)
        in_specs = [SMEM, whole(*fetched.shape), matrix_spec]
        out_specs += [whole(depth, modes), whole(modes, depth)]
        out_shape += [
            jax.ShapeDtypeStruct((depth, modes), BF16),
            jax.ShapeDtypeStruct((modes, depth), BF16),
        ]
    else:
        operands = (*laid_out, matrix, diagonal)
        in_specs = [
            whole(depth, modes),
            pl.BlockSpec((chunk, depth), lambda i: (i, 0)),
            matrix_spec,
            whole(local_subs, 1, boundary),
        ]
    return pl.pallas_call(
        kernel,
        grid=(modes // chunk,),
        in_specs=in_specs,
        out_specs=out_specs,
        out_shape=out_shape,
        scratch_shapes=[pltpu.VMEM((chunk, depth), BF16)],
        name="project_stiff" if gathers else "project_mass",
    )(*operands)


def swap(value, offset, device_count):
    return lax.ppermute(value, AXES, [(i, i ^ offset) for i in range(device_count)])


def reduce_shares(send, keep, sizes):
    got = swap(send, 1, sizes.devices)
    summed = keep + got.astype(F32)
    depth = sizes.devices // sizes.plane
    summed = summed.reshape((sizes.plane // 2, depth) + summed.shape[1:])
    total = summed[0]
    for d in range(1, sizes.plane // 2):
        got = swap(summed[d].astype(BF16), 2 * d, sizes.devices)
        total = total + got.astype(F32)
    result = total[0]
    for d in range(1, depth):
        got = swap(total[d].astype(BF16), d * sizes.plane, sizes.devices)
        result = result + got.astype(F32)
    return result


def spread_in_plane(blocks, sizes):
    near = [blocks[0]] + [
        swap(blocks[d], d, sizes.devices) for d in range(1, sizes.plane)
    ]
    return [jnp.stack([part[z] for part in near]) for z in range(sizes.devices // sizes.plane)]


def clear_tiles(table, sizes):
    shape = (sizes.row_blocks * BLK, sizes.col_blocks * BLK)

    def kernel(_table, stiff_ref, mass_ref, zero_ref, sem):
        zero_ref[...] = jnp.zeros_like(zero_ref)
        fills = [
            pltpu.make_async_copy(zero_ref, ref.at[pl.ds(i * BLK, BLK), :], sem.at[i, j])
            for i in range(sizes.row_blocks)
            for j, ref in enumerate((stiff_ref, mass_ref))
        ]
        for fill in fills:
            fill.start()
        for fill in fills:
            fill.wait()

    return pl.pallas_call(
        kernel,
        in_specs=[ANY],
        out_specs=[ANY, ANY],
        out_shape=[jax.ShapeDtypeStruct(shape, BF16), jax.ShapeDtypeStruct(shape, BF16)],
        scratch_shapes=[
            pltpu.VMEM((BLK, shape[1]), BF16),
            pltpu.SemaphoreType.DMA((sizes.row_blocks, 2)),
        ],
        name="clear_tiles",
    )(table)


def place(table, order, slots, arrived, stiff_tile, mass_tile, sizes):
    count = sizes.devices
    limit = sizes.row_blocks * sizes.col_blocks
    depth = len(arrived)
    height = 2 * BLK + EXTRA

    def kernel(*refs):
        table_ref, order_ref, slot_ref = refs[:3]
        in_refs = refs[3 : 3 + depth]
        stiff_ref, mass_ref, share_ref, held_ref, sums_ref, in_sem, sem = refs[-7:]
        me = lax.axis_index("row") * sizes.cols + lax.axis_index("col")
        loads = [
            pltpu.make_async_copy(
                ref, held_ref.at[pl.ds(z * sizes.plane, sizes.plane)], in_sem.at[z]
            )
            for z, ref in enumerate(in_refs)
        ]
        for load in loads:
            load.start()
        for load in loads:
            load.wait()

        def copies(j):
            slot = slot_ref[j]
            row = pl.multiple_of(quotient(slot, sizes.col_blocks) * BLK, BLK)
            col = pl.multiple_of(remainder(slot, sizes.col_blocks) * BLK, BLK)
            return [
                pltpu.make_async_copy(
                    sums_ref.at[j, pl.ds(i * BLK, BLK)],
                    ref.at[pl.ds(row, BLK), pl.ds(col, BLK)],
                    sem.at[j, i],
                )
                for i, ref in enumerate((stiff_ref, mass_ref))
            ]

        def last(j):
            ahead = slot_ref[jnp.minimum(j + 1, count - 1)]
            ends = jnp.logical_or(j == count - 1, ahead != slot_ref[j])
            return jnp.logical_and(slot_ref[j] < limit, ends)

        def one(j, total):
            block = held_ref[order_ref[j] ^ me, : 2 * BLK].astype(F32)
            same = jnp.logical_and(j > 0, slot_ref[jnp.maximum(j - 1, 0)] == slot_ref[j])
            total = jnp.where(same, total + block, block)
            sums_ref[j] = total.astype(BF16)

            @pl.when(last(j))
            def _():
                for copy in copies(j):
                    copy.start()

            return total

        lax.fori_loop(0, count, one, jnp.zeros((2 * BLK, BLK), F32))
        share_ref[...] = jnp.zeros_like(share_ref)

        def add(device, carry):
            share = table_ref[device, sizes.ratio + 1]

            @pl.when(share >= 0)
            def _():
                parts = held_ref[device ^ me, 2 * BLK : 2 * BLK + EXTRA].astype(F32)
                share_ref[share] += parts[0:1] + parts[1:2] + parts[2:3]

            return carry

        lax.fori_loop(0, count, add, 0)

        def wait(j, carry):
            @pl.when(last(j))
            def _():
                for copy in copies(j):
                    copy.wait()

            return carry

        lax.fori_loop(0, count, wait, 0)

    return pl.pallas_call(
        kernel,
        in_specs=[SMEM, SMEM, SMEM] + [ANY] * (depth + 2),
        out_specs=[ANY, ANY, VMEM],
        out_shape=[
            jax.ShapeDtypeStruct(stiff_tile.shape, BF16),
            jax.ShapeDtypeStruct(mass_tile.shape, BF16),
            jax.ShapeDtypeStruct((sizes.share_blocks, 1, BLK), F32),
        ],
        input_output_aliases={3 + depth: 0, 4 + depth: 1},
        scratch_shapes=[
            pltpu.VMEM((count, height, BLK), BF16),
            pltpu.VMEM((count, 2 * BLK, BLK), BF16),
            pltpu.SemaphoreType.DMA((depth,)),
            pltpu.SemaphoreType.DMA((count, 2)),
        ],
        name="place",
    )(table, order, slots, *arrived, stiff_tile, mass_tile)


def reduction(inv_interior, coupling, boundary_stiff, mass_interior, mass_boundary, block_map, modes):
    row_count = lax.axis_size("row")
    col_count = lax.axis_size("col")
    tile_cols, width = modes.shape
    tile_rows = tile_cols * col_count // row_count
    sizes = Sizes(
        devices=row_count * col_count,
        cols=col_count,
        ratio=row_count // col_count,
        row_blocks=tile_rows // BLK,
        col_blocks=tile_cols // BLK,
        share_blocks=tile_rows // BLK // col_count,
        plane=col_count // 2 * col_count,
    )
    x_size = col_count // 2
    y_size = x_size
    dims = (row_count // y_size, y_size, x_size)

    table = exchange(describe(block_map, sizes))
    blocks, stiff, mass, diagonal = condense(
        block_map, inv_interior, coupling, boundary_stiff, mass_interior, mass_boundary, sizes
    )
    table, blocks = lax.optimization_barrier((table, blocks))
    spread = spread_in_plane(blocks, sizes)
    beside = swap(spread[1], sizes.plane, sizes.devices)
    wanted = pick_modes(table, modes.reshape(sizes.col_blocks, BLK, width), sizes.ratio)
    fetched = exchange(wanted)
    stiff_tile, mass_tile = clear_tiles(table, sizes)
    late, beside, fetched, stiff_tile, mass_tile = lax.optimization_barrier(
        (spread[2:], beside, fetched, stiff_tile, mass_tile)
    )
    late = [swap(part, (2 + d) * sizes.plane, sizes.devices) for d, part in enumerate(late)]
    arrived = [spread[0], beside, *late]

    fetched = fetched.reshape(row_count, col_count, sizes.ratio, BLK, width)
    send, keep, q, qt = project(block_map, fetched, None, stiff, None, dims, sizes.row_blocks)
    reduced_stiff = reduce_shares(send, keep, sizes)
    send, keep = project(None, None, (q, qt), mass, diagonal, dims, sizes.row_blocks)
    reduced_mass = reduce_shares(send, keep, sizes)

    slot = table[:, sizes.ratio]
    ids = jnp.arange(sizes.devices, dtype=jnp.int32)
    before = jnp.logical_or(
        slot[None, :] < slot[:, None],
        jnp.logical_and(slot[None, :] == slot[:, None], ids[None, :] < ids[:, None]),
    )
    rank = jnp.sum(before.astype(jnp.int32), axis=1)
    chosen = rank[None, :] == ids[:, None]
    order = jnp.sum(jnp.where(chosen, ids[None, :], 0), axis=1)
    slots = jnp.sum(jnp.where(chosen, slot[None, :], 0), axis=1)
    stiff_tile, mass_tile, mass_share = place(
        table, order, slots, arrived, stiff_tile, mass_tile, sizes
    )
    return stiff_tile, mass_tile, reduced_stiff, reduced_mass, mass_share.reshape(-1)


def solution(mesh):
    return jax.shard_map(
        reduction,
        mesh=mesh,
        in_specs=(
            P(AXES, None, None),
            P(AXES, None, None),
            P(AXES, None, None),
            P(AXES, None),
            P(AXES, None),
            P(AXES, None),
            P("col", "row"),
        ),
        out_specs=(P("row", "col"), P("row", "col"), P(AXES, None), P(AXES, None), P(AXES)),
        check_vma=False,
    )
```

profile of v0, /device:TPU:0, one launch (start us, length us, event | category | flops | bytes accessed | tf_op | source)
XLA Modules:
  0.0 210.8 jit_solution(7114963482665216557)
XLA Ops:
  0.6 1.4 describe.1
  2.0 7.3 %all-to-all-start = ((s32[32,1,128]{2,1,0:T(1,128)}), s32[32,1,128]{2,1,0:T(1,128)S(1)}, u32[]{:S(2)}, u32[]{:S(2)}) async-start(s32[32,1,128]{2,1,0:T(1,128)} %bitcast.64), calls=%async_computation | async-start | bytes 32768 | tf_op jit(solution)/shard_map/all_to_all | solution.py:32
  9.3 2.0 copy.18.mi_ref
  11.4 1.3 broadcast_in_dim.26.mb_ref
  12.6 8.8 %condense.1 = (bf16[8,4,272,128]{3,2,1,0:T(8,128)(2,1)}, bf16[2,512,512]{2,1,0:T(8,128)(2,1)}, bf16[2,512,512]{2,1,0:T(8,128)(2,1)}, f32[2,1,512]{2,1,0:T(1,128)}) custom-call(s32[2,4]{1,0:T(2,128)} %refs_0_.1, bf16[2,1024,1024]{2,1,0:T(8,128)(2,1)} %inv_ref.1, bf16[2,1024,512]{2,1,0:T(8,128)(2,1)} %cpl_ref.1, bf16[2,512,512]{2,1,0:T(8,128)(2,1)} %stiff_ref.1, ...), custom_call_target="tpu_custom_call" | custom-call | tf_op jit(solution)/shard_map/condense/pallas_call | solution.py:181
  21.5 0.6 copy-done.6
  22.1 2.7 %pick_modes.1 = bf16[32,2,128,128]{3,2,1,0:T(8,128)(2,1)} custom-call(s32[32,128]{1,0:T(8,128)} %bitcast.60, bf16[32,128,128]{2,1,0:T(8,128)(2,1)} %bitcast.59), custom_call_target="tpu_custom_call" | custom-call | tf_op jit(solution)/shard_map/pick_modes/pallas_call | solution.py:101
  24.8 5.8 %all-to-all-start.1 = ((bf16[32,2,128,128]{3,2,1,0:T(8,128)(2,1)}), bf16[32,2,128,128]{3,2,1,0:T(8,128)(2,1)S(1)}, u32[]{:S(2)}, u32[]{:S(2)}) async-start(bf16[32,2,128,128]{3,2,1,0:T(8,128)(2,1)} %pick_modes.1), calls=%async_computation.1 | async-start | bytes 4194304 | tf_op jit(solution)/shard_map/all_to_all | solution.py:32
  30.6 1.6 slice_bitcast_fusion
  32.2 0.3 collective-permute-start
  32.6 1.6 collective-permute-start.1
  34.2 1.7 bitcast_dynamic-update-slice_fusion
  35.9 1.7 collective-permute-start.3
  37.6 0.1 collective-permute-start.4
  37.7 2.5 %collective-permute-start.5 = (bf16[4,272,128]{2,1,0:T(8,128)(2,1)S(1)}, bf16[4,272,128]{2,1,0:T(8,128)(2,1)S(1)}, u32[]{:S(2)}, u32[]{:S(2)}) collective-permute-start(bf16[4,272,128]{2,1,0:T(8,128)(2,1)S(1)} %get-tuple-element.66), channel_id=1, source_target_pairs={{0,6},{1,7},{2,4},{3,5},{4,2},{5,3},{6,0},{7,1},{8,14},{9,15},{10,... | collective-permute-start | bytes 835592 | tf_op jit(solution)/shard_map/ppermute | solution.py:313
  40.2 0.7 slice_dynamic-update-slice_fusion.6
  40.9 17.3 %collective-permute-done.1 = bf16[4,272,128]{2,1,0:T(8,128)(2,1)S(1)} collective-permute-done((bf16[4,272,128]{2,1,0:T(8,128)(2,1)S(1)}, bf16[4,272,128]{2,1,0:T(8,128)(2,1)S(1)}, u32[]{:S(2)}, u32[]{:S(2)}) %collective-permute-start.1) | collective-permute-done | bytes 278560 | tf_op jit(solution)/shard_map/ppermute | solution.py:313
  58.3 0.1 collective-permute-start.6
  58.4 0.7 slice_dynamic-update-slice_fusion.5
  59.1 5.4 %collective-permute-done.2 = bf16[4,272,128]{2,1,0:T(8,128)(2,1)S(1)} collective-permute-done((bf16[4,272,128]{2,1,0:T(8,128)(2,1)S(1)}, bf16[4,272,128]{2,1,0:T(8,128)(2,1)S(1)}, u32[]{:S(2)}, u32[]{:S(2)}) %collective-permute-start.2) | collective-permute-done | bytes 278560 | tf_op jit(solution)/shard_map/ppermute | solution.py:313
  64.5 0.7 slice_dynamic-update-slice_fusion.4
  65.2 0.7 slice_dynamic-update-slice_fusion.3
  65.9 0.7 slice_dynamic-update-slice_fusion.2
  66.5 8.8 %collective-permute-done.5 = bf16[4,272,128]{2,1,0:T(8,128)(2,1)S(1)} collective-permute-done((bf16[4,272,128]{2,1,0:T(8,128)(2,1)S(1)}, bf16[4,272,128]{2,1,0:T(8,128)(2,1)S(1)}, u32[]{:S(2)}, u32[]{:S(2)}) %collective-permute-start.5) | collective-permute-done | bytes 278560 | tf_op jit(solution)/shard_map/ppermute | solution.py:313
  75.3 0.7 slice_dynamic-update-slice_fusion.1
  76.0 4.9 %collective-permute-done.6 = bf16[4,272,128]{2,1,0:T(8,128)(2,1)S(1)} collective-permute-done((bf16[4,272,128]{2,1,0:T(8,128)(2,1)S(1)}, bf16[4,272,128]{2,1,0:T(8,128)(2,1)S(1)}, u32[]{:S(2)}, u32[]{:S(2)}) %collective-permute-start.6) | collective-permute-done | bytes 278560 | tf_op jit(solution)/shard_map/ppermute | solution.py:313
  80.9 0.7 slice_dynamic-update-slice_fusion
  81.6 0.9 copy-done.8
  82.4 1.9 collective-permute-start.7
  84.3 11.2 %clear_tiles.1 = (bf16[2048,4096]{1,0:T(8,128)(2,1)}, bf16[2048,4096]{1,0:T(8,128)(2,1)}) custom-call(s32[32,128]{1,0:T(8,128)} %bitcast.61), custom_call_target="tpu_custom_call" | custom-call | tf_op jit(solution)/shard_map/clear_tiles/pallas_call | solution.py:354
  95.5 2.0 collective-permute-done.7.refs_4_
  97.5 1.4 copy-done
  98.8 9.2 %project_stiff.1 = (bf16[16,32,1024]{2,1,0:T(8,128)(2,1)}, f32[16,32,1024]{2,1,0:T(8,128)}, bf16[1024,1024]{1,0:T(8,128)(2,1)}, bf16[1024,1024]{1,0:T(8,128)(2,1)}) custom-call(s32[2,4]{1,0:T(2,128)} %refs_0_.1, bf16[8,4,2,128,128]{4,3,2,1,0:T(8,128)(2,1)} %bitcast.58, bf16[2,512,512]{2,1,0:T(8,128)(2,1)} %get-tuple-element.41.refs_2_), custom_call_target="tpu_custom_call" | custom-call | tf_op jit(solution)/shard_map/project_stiff/pallas_call | solution.py:301
  108.1 7.6 %project_mass.1 = (bf16[16,32,1024]{2,1,0:T(8,128)(2,1)}, f32[16,32,1024]{2,1,0:T(8,128)}) custom-call(bf16[1024,1024]{1,0:T(8,128)(2,1)} %get-tuple-element.44.refs_0_, bf16[1024,1024]{1,0:T(8,128)(2,1)} %get-tuple-element.45.refs_1_, bf16[2,512,512]{2,1,0:T(8,128)(2,1)} %get-tuple-element.46.refs_2_, f32[2,1,512]{2,1,0:T(1,128)} %get-tuple-element.47.refs_3_), custom_call_target="tpu_custom_call" | custom-call | tf_op jit(solution)/shard_map/project_mass/pallas_call | solution.py:301
  115.7 2.6 %collective-permute-start.8 = (bf16[8,272,128]{2,1,0:T(8,128)(2,1)}, bf16[8,272,128]{2,1,0:T(8,128)(2,1)S(1)}, u32[]{:S(2)}, u32[]{:S(2)}) collective-permute-start(bf16[8,272,128]{2,1,0:T(8,128)(2,1)} %get-tuple-element.34), channel_id=1, source_target_pairs={{0,16},{1,17},{2,18},{3,19},{4,20},{5,21},{6,22},{7,23},{8,24},{9,... | collective-permute-start | bytes 1671176 | tf_op jit(solution)/shard_map/ppermute | solution.py:313
  118.3 1.5 collective-permute-start.9
  119.8 0.2 slice_reduce_fusion
  120.0 0.2 convert_reduce_fusion
  120.2 0.7 select_reduce_fusion
  120.9 35.3 %collective-permute-done.8.refs_5_ = bf16[8,272,128]{2,1,0:T(8,128)(2,1)S(1)} collective-permute-done((bf16[8,272,128]{2,1,0:T(8,128)(2,1)}, bf16[8,272,128]{2,1,0:T(8,128)(2,1)S(1)}, u32[]{:S(2)}, u32[]{:S(2)}) %collective-permute-start.8) | collective-permute-done | bytes 557088 | tf_op jit(solution)/shard_map/ppermute | solution.py:313
  156.2 0.8 copy-done.4
  157.0 0.2 copy-done.5
  157.2 5.6 %place.1 = (bf16[2048,4096]{1,0:T(8,128)(2,1)}, bf16[2048,4096]{1,0:T(8,128)(2,1)}, f32[4,1,128]{2,1,0:T(1,128)}) custom-call(s32[32,128]{1,0:T(8,128)} %bitcast.62, s32[32]{0:T(128)} %get-tuple-element.52.refs_1_, s32[32]{0:T(128)} %get-tuple-element.51.refs_2_, ...), custom_call_target="tpu_custom_call", output_to_operand_aliasing={{0}: (7, {}), {1}: (8, {})} | custom-call | tf_op jit(solution)/shard_map/place/pallas_call | solution.py:445
  162.8 1.8 fusion.14
  164.7 1.3 collective-permute-start.18
  165.9 1.1 collective-permute-start.19
  167.0 1.2 collective-permute-start.20
  168.2 0.5 fusion.17
  168.8 1.3 collective-permute-start.11
  170.1 1.1 collective-permute-start.12
  171.2 2.7 %collective-permute-done.18 = bf16[4,32,1024]{2,1,0:T(8,128)(2,1)S(1)} collective-permute-done((bf16[4,32,1024]{2,1,0:T(8,128)(2,1)S(1)}, bf16[4,32,1024]{2,1,0:T(8,128)(2,1)S(1)}, u32[]{:S(2)}, u32[]{:S(2)}) %collective-permute-start.18) | collective-permute-done | bytes 262176 | tf_op jit(solution)/shard_map/ppermute | solution.py:313
  173.9 1.7 collective-permute-start.13
  175.6 5.1 %collective-permute-done.19 = bf16[4,32,1024]{2,1,0:T(8,128)(2,1)S(1)} collective-permute-done((bf16[4,32,1024]{2,1,0:T(8,128)(2,1)S(1)}, bf16[4,32,1024]{2,1,0:T(8,128)(2,1)S(1)}, u32[]{:S(2)}, u32[]{:S(2)}) %collective-permute-start.19) | collective-permute-done | bytes 262176 | tf_op jit(solution)/shard_map/ppermute | solution.py:313
  180.7 0.2 fusion.12
  180.9 11.9 %collective-permute-start.21 = (bf16[32,1024]{1,0:T(8,128)(2,1)S(1)}, bf16[32,1024]{1,0:T(8,128)(2,1)S(1)}, u32[]{:S(2)}, u32[]{:S(2)}) collective-permute-start(bf16[32,1024]{1,0:T(8,128)(2,1)S(1)} %get-tuple-element.106), channel_id=1, source_target_pairs={{0,8},{1,9},{2,10},{3,11},{4,12},{5,13},{6,14},{7,15},{8,0},{9,1},... | collective-permute-start | bytes 196616 | tf_op jit(solution)/shard_map/ppermute | solution.py:313
  192.8 0.9 collective-permute-start.22
  193.7 1.6 collective-permute-start.23
  195.3 0.2 fusion.15
  195.5 7.0 %collective-permute-start.14 = (bf16[32,1024]{1,0:T(8,128)(2,1)S(1)}, bf16[32,1024]{1,0:T(8,128)(2,1)S(1)}, u32[]{:S(2)}, u32[]{:S(2)}) collective-permute-start(bf16[32,1024]{1,0:T(8,128)(2,1)S(1)} %get-tuple-element.109), channel_id=1, source_target_pairs={{0,8},{1,9},{2,10},{3,11},{4,12},{5,13},{6,14},{7,15},{8,0},{9,1},... | collective-permute-start | bytes 196616 | tf_op jit(solution)/shard_map/ppermute | solution.py:313
  202.5 1.6 collective-permute-start.15
  204.0 1.4 collective-permute-start.16
  205.4 0.7 fusion.6
  206.1 4.1 %collective-permute-done.15 = bf16[32,1024]{1,0:T(8,128)(2,1)S(1)} collective-permute-done((bf16[32,1024]{1,0:T(8,128)(2,1)S(1)}, bf16[32,1024]{1,0:T(8,128)(2,1)S(1)}, u32[]{:S(2)}, u32[]{:S(2)}) %collective-permute-start.15) | collective-permute-done | bytes 65568 | tf_op jit(solution)/shard_map/ppermute | solution.py:313
  210.2 0.7 fusion.9
  (39 shorter events, 0.2 us)
Async XLA Ops:
  2.0 19.5 %all-to-all-start = ((s32[32,1,128]{2,1,0:T(1,128)}), s32[32,1,128]{2,1,0:T(1,128)S(1)}, u32[]{:S(2)}, u32[]{:S(2)}) async-start(s32[32,1,128]{2,1,0:T(1,128)} %bitcast.64), calls=%async_computation | async-start | bytes 32768 | tf_op jit(solution)/shard_map/all_to_all | solution.py:32
  21.5 0.6 copy-start.6
  24.8 72.7 %all-to-all-start.1 = ((bf16[32,2,128,128]{3,2,1,0:T(8,128)(2,1)}), bf16[32,2,128,128]{3,2,1,0:T(8,128)(2,1)S(1)}, u32[]{:S(2)}, u32[]{:S(2)}) async-start(bf16[32,2,128,128]{3,2,1,0:T(8,128)(2,1)} %pick_modes.1), calls=%async_computation.1 | async-start | bytes 4194304 | tf_op jit(solution)/shard_map/all_to_all | solution.py:32
  32.2 5.5 %collective-permute-start = (bf16[4,272,128]{2,1,0:T(8,128)(2,1)S(1)}, bf16[4,272,128]{2,1,0:T(8,128)(2,1)S(1)}, u32[]{:S(2)}, u32[]{:S(2)}) collective-permute-start(bf16[4,272,128]{2,1,0:T(8,128)(2,1)S(1)} %get-tuple-element.71), channel_id=1, source_target_pairs={{0,1},{1,0},{2,3},{3,2},{4,5},{5,4},{6,7},{7,6},{8,9},{9,8},{10,11... | collective-permute-start | bytes 835592 | tf_op jit(solution)/shard_map/ppermute | solution.py:313
  32.6 25.7 %collective-permute-start.1 = (bf16[4,272,128]{2,1,0:T(8,128)(2,1)S(1)}, bf16[4,272,128]{2,1,0:T(8,128)(2,1)S(1)}, u32[]{:S(2)}, u32[]{:S(2)}) collective-permute-start(bf16[4,272,128]{2,1,0:T(8,128)(2,1)S(1)} %get-tuple-element.70), channel_id=1, source_target_pairs={{0,2},{1,3},{2,0},{3,1},{4,6},{5,7},{6,4},{7,5},{8,10},{9,11},{10,... | collective-permute-start | bytes 835592 | tf_op jit(solution)/shard_map/ppermute | solution.py:313
  35.8 28.6 %collective-permute-start.2 = (bf16[4,272,128]{2,1,0:T(8,128)(2,1)S(1)}, bf16[4,272,128]{2,1,0:T(8,128)(2,1)S(1)}, u32[]{:S(2)}, u32[]{:S(2)}) collective-permute-start(bf16[4,272,128]{2,1,0:T(8,128)(2,1)S(1)} %get-tuple-element.69), channel_id=1, source_target_pairs={{0,3},{1,2},{2,1},{3,0},{4,7},{5,6},{6,5},{7,4},{8,11},{9,10},{10,... | collective-permute-start | bytes 835592 | tf_op jit(solution)/shard_map/ppermute | solution.py:313
  35.9 29.3 %collective-permute-start.3 = (bf16[4,272,128]{2,1,0:T(8,128)(2,1)S(1)}, bf16[4,272,128]{2,1,0:T(8,128)(2,1)S(1)}, u32[]{:S(2)}, u32[]{:S(2)}) collective-permute-start(bf16[4,272,128]{2,1,0:T(8,128)(2,1)S(1)} %get-tuple-element.68), channel_id=1, source_target_pairs={{0,4},{1,5},{2,6},{3,7},{4,0},{5,1},{6,2},{7,3},{8,12},{9,13},{10,... | collective-permute-start | bytes 835592 | tf_op jit(solution)/shard_map/ppermute | solution.py:313
  37.6 28.3 %collective-permute-start.4 = (bf16[4,272,128]{2,1,0:T(8,128)(2,1)S(1)}, bf16[4,272,128]{2,1,0:T(8,128)(2,1)S(1)}, u32[]{:S(2)}, u32[]{:S(2)}) collective-permute-start(bf16[4,272,128]{2,1,0:T(8,128)(2,1)S(1)} %get-tuple-element.67), channel_id=1, source_target_pairs={{0,5},{1,4},{2,7},{3,6},{4,1},{5,0},{6,3},{7,2},{8,13},{9,12},{10,... | collective-permute-start | bytes 835592 | tf_op jit(solution)/shard_map/ppermute | solution.py:313
  37.7 37.6 %collective-permute-start.5 = (bf16[4,272,128]{2,1,0:T(8,128)(2,1)S(1)}, bf16[4,272,128]{2,1,0:T(8,128)(2,1)S(1)}, u32[]{:S(2)}, u32[]{:S(2)}) collective-permute-start(bf16[4,272,128]{2,1,0:T(8,128)(2,1)S(1)} %get-tuple-element.66), channel_id=1, source_target_pairs={{0,6},{1,7},{2,4},{3,5},{4,2},{5,3},{6,0},{7,1},{8,14},{9,15},{10,... | collective-permute-start | bytes 835592 | tf_op jit(solution)/shard_map/ppermute | solution.py:313
  58.3 22.6 %collective-permute-start.6 = (bf16[4,272,128]{2,1,0:T(8,128)(2,1)S(1)}, bf16[4,272,128]{2,1,0:T(8,128)(2,1)S(1)}, u32[]{:S(2)}, u32[]{:S(2)}) collective-permute-start(bf16[4,272,128]{2,1,0:T(8,128)(2,1)S(1)} %get-tuple-element.65), channel_id=1, source_target_pairs={{0,7},{1,6},{2,5},{3,4},{4,3},{5,2},{6,1},{7,0},{8,15},{9,14},{10,... | collective-permute-start | bytes 835592 | tf_op jit(solution)/shard_map/ppermute | solution.py:313
  81.6 0.9 copy-start.8
  82.4 15.0 %collective-permute-start.7 = (bf16[8,272,128]{2,1,0:T(8,128)(2,1)S(1)}, bf16[8,272,128]{2,1,0:T(8,128)(2,1)S(1)}, u32[]{:S(2)}, u32[]{:S(2)}) collective-permute-start(bf16[8,272,128]{2,1,0:T(8,128)(2,1)S(1)} %get-tuple-element.78), channel_id=1, source_target_pairs={{0,8},{1,9},{2,10},{3,11},{4,12},{5,13},{6,14},{7,15},{8,0},{9,1},... | collective-permute-start | bytes 1671176 | tf_op jit(solution)/shard_map/ppermute | solution.py:313
  97.5 22.3 %copy-start.3 = (bf16[8,272,128]{2,1,0:T(8,128)(2,1)}, bf16[8,272,128]{2,1,0:T(8,128)(2,1)S(1)}, u32[]{:S(2)}) copy-start(bf16[8,272,128]{2,1,0:T(8,128)(2,1)S(1)} %collective-permute-done.7.refs_4_) | copy-start | bytes 1671172
  97.5 1.4 copy-start
  108.1 10.2 %copy-start.9 = (bf16[8,272,128]{2,1,0:T(8,128)(2,1)S(1)}, bf16[8,272,128]{2,1,0:T(8,128)(2,1)}, u32[]{:S(2)}) copy-start(bf16[8,272,128]{2,1,0:T(8,128)(2,1)} %copy-done.8) | copy-start | bytes 1671172
  108.1 11.7 %copy-start.7 = (s32[32,1,128]{2,1,0:T(1,128)S(1)}, s32[32,1,128]{2,1,0:T(1,128)}, u32[]{:S(2)}) copy-start(s32[32,1,128]{2,1,0:T(1,128)} %copy-done.6) | copy-start | bytes 49156
  115.7 47.1 %collective-permute-start.17 = (bf16[16,32,1024]{2,1,0:T(8,128)(2,1)}, bf16[16,32,1024]{2,1,0:T(8,128)(2,1)}, u32[]{:S(2)}, u32[]{:S(2)}) collective-permute-start(bf16[16,32,1024]{2,1,0:T(8,128)(2,1)} %get-tuple-element.49), channel_id=1, source_target_pairs={{0,1},{1,0},{2,3},{3,2},{4,5},{5,4},{6,7},{7,6},{8,9},{9,8},{10,11... | collective-permute-start | bytes 3145736 | tf_op jit(solution)/shard_map/ppermute | solution.py:313
  115.7 40.5 %collective-permute-start.8 = (bf16[8,272,128]{2,1,0:T(8,128)(2,1)}, bf16[8,272,128]{2,1,0:T(8,128)(2,1)S(1)}, u32[]{:S(2)}, u32[]{:S(2)}) collective-permute-start(bf16[8,272,128]{2,1,0:T(8,128)(2,1)} %get-tuple-element.34), channel_id=1, source_target_pairs={{0,16},{1,17},{2,18},{3,19},{4,20},{5,21},{6,22},{7,23},{8,24},{9,... | collective-permute-start | bytes 1671176 | tf_op jit(solution)/shard_map/ppermute | solution.py:313
  118.3 37.9 %collective-permute-start.9 = (bf16[8,272,128]{2,1,0:T(8,128)(2,1)S(1)}, bf16[8,272,128]{2,1,0:T(8,128)(2,1)S(1)}, u32[]{:S(2)}, u32[]{:S(2)}) collective-permute-start(bf16[8,272,128]{2,1,0:T(8,128)(2,1)S(1)} %copy-done.9), channel_id=1, source_target_pairs={{0,24},{1,25},{2,26},{3,27},{4,28},{5,29},{6,30},{7,31},{8,16},{9,... | collective-permute-start | bytes 1671176 | tf_op jit(solution)/shard_map/ppermute | solution.py:313
  119.8 48.4 %collective-permute-start.10 = (bf16[16,32,1024]{2,1,0:T(8,128)(2,1)}, bf16[16,32,1024]{2,1,0:T(8,128)(2,1)S(1)}, u32[]{:S(2)}, u32[]{:S(2)}) collective-permute-start(bf16[16,32,1024]{2,1,0:T(8,128)(2,1)} %get-tuple-element.43), channel_id=1, source_target_pairs={{0,1},{1,0},{2,3},{3,2},{4,5},{5,4},{6,7},{7,6},{8,9},{9,8},{10,11... | collective-permute-start | bytes 3145736 | tf_op jit(solution)/shard_map/ppermute | solution.py:313
  156.2 0.8 copy-start.4
  156.2 1.0 copy-start.5
  157.2 5.6 %copy-start.2 = (f32[16,32,1024]{2,1,0:T(8,128)S(1)}, f32[16,32,1024]{2,1,0:T(8,128)}, u32[]{:S(2)}) copy-start(f32[16,32,1024]{2,1,0:T(8,128)} %get-tuple-element.48) | copy-start | bytes 6291460
  162.8 5.4 %copy-start.1 = (f32[16,32,1024]{2,1,0:T(8,128)S(1)}, f32[16,32,1024]{2,1,0:T(8,128)}, u32[]{:S(2)}) copy-start(f32[16,32,1024]{2,1,0:T(8,128)} %get-tuple-element.42) | copy-start | bytes 6291460
  164.7 9.2 %collective-permute-start.18 = (bf16[4,32,1024]{2,1,0:T(8,128)(2,1)S(1)}, bf16[4,32,1024]{2,1,0:T(8,128)(2,1)S(1)}, u32[]{:S(2)}, u32[]{:S(2)}) collective-permute-start(bf16[4,32,1024]{2,1,0:T(8,128)(2,1)S(1)} %get-tuple-element.72), channel_id=1, source_target_pairs={{0,2},{1,3},{2,0},{3,1},{4,6},{5,7},{6,4},{7,5},{8,10},{9,11},{10,... | collective-permute-start | bytes 786440 | tf_op jit(solution)/shard_map/ppermute | solution.py:313
  165.9 14.8 %collective-permute-start.19 = (bf16[4,32,1024]{2,1,0:T(8,128)(2,1)S(1)}, bf16[4,32,1024]{2,1,0:T(8,128)(2,1)S(1)}, u32[]{:S(2)}, u32[]{:S(2)}) collective-permute-start(bf16[4,32,1024]{2,1,0:T(8,128)(2,1)S(1)} %get-tuple-element.74), channel_id=1, source_target_pairs={{0,4},{1,5},{2,6},{3,7},{4,0},{5,1},{6,2},{7,3},{8,12},{9,13},{10,... | collective-permute-start | bytes 786440 | tf_op jit(solution)/shard_map/ppermute | solution.py:313
  167.0 13.7 %collective-permute-start.20 = (bf16[4,32,1024]{2,1,0:T(8,128)(2,1)S(1)}, bf16[4,32,1024]{2,1,0:T(8,128)(2,1)S(1)}, u32[]{:S(2)}, u32[]{:S(2)}) collective-permute-start(bf16[4,32,1024]{2,1,0:T(8,128)(2,1)S(1)} %get-tuple-element.73), channel_id=1, source_target_pairs={{0,6},{1,7},{2,4},{3,5},{4,2},{5,3},{6,0},{7,1},{8,14},{9,15},{10,... | collective-permute-start | bytes 786440 | tf_op jit(solution)/shard_map/ppermute | solution.py:313
  168.8 24.9 %collective-permute-start.11 = (bf16[4,32,1024]{2,1,0:T(8,128)(2,1)S(1)}, bf16[4,32,1024]{2,1,0:T(8,128)(2,1)S(1)}, u32[]{:S(2)}, u32[]{:S(2)}) collective-permute-start(bf16[4,32,1024]{2,1,0:T(8,128)(2,1)S(1)} %get-tuple-element.75), channel_id=1, source_target_pairs={{0,2},{1,3},{2,0},{3,1},{4,6},{5,7},{6,4},{7,5},{8,10},{9,11},{10,... | collective-permute-start | bytes 786440 | tf_op jit(solution)/shard_map/ppermute | solution.py:313
  170.1 25.2 %collective-permute-start.12 = (bf16[4,32,1024]{2,1,0:T(8,128)(2,1)S(1)}, bf16[4,32,1024]{2,1,0:T(8,128)(2,1)S(1)}, u32[]{:S(2)}, u32[]{:S(2)}) collective-permute-start(bf16[4,32,1024]{2,1,0:T(8,128)(2,1)S(1)} %get-tuple-element.77), channel_id=1, source_target_pairs={{0,4},{1,5},{2,6},{3,7},{4,0},{5,1},{6,2},{7,3},{8,12},{9,13},{10,... | collective-permute-start | bytes 786440 | tf_op jit(solution)/shard_map/ppermute | solution.py:313
  173.9 21.4 %collective-permute-start.13 = (bf16[4,32,1024]{2,1,0:T(8,128)(2,1)S(1)}, bf16[4,32,1024]{2,1,0:T(8,128)(2,1)S(1)}, u32[]{:S(2)}, u32[]{:S(2)}) collective-permute-start(bf16[4,32,1024]{2,1,0:T(8,128)(2,1)S(1)} %get-tuple-element.76), channel_id=1, source_target_pairs={{0,6},{1,7},{2,4},{3,5},{4,2},{5,3},{6,0},{7,1},{8,14},{9,15},{10,... | collective-permute-start | bytes 786440 | tf_op jit(solution)/shard_map/ppermute | solution.py:313
  180.9 23.1 %collective-permute-start.21 = (bf16[32,1024]{1,0:T(8,128)(2,1)S(1)}, bf16[32,1024]{1,0:T(8,128)(2,1)S(1)}, u32[]{:S(2)}, u32[]{:S(2)}) collective-permute-start(bf16[32,1024]{1,0:T(8,128)(2,1)S(1)} %get-tuple-element.106), channel_id=1, source_target_pairs={{0,8},{1,9},{2,10},{3,11},{4,12},{5,13},{6,14},{7,15},{8,0},{9,1},... | collective-permute-start | bytes 196616 | tf_op jit(solution)/shard_map/ppermute | solution.py:313
  192.8 12.6 %collective-permute-start.22 = (bf16[32,1024]{1,0:T(8,128)(2,1)S(1)}, bf16[32,1024]{1,0:T(8,128)(2,1)S(1)}, u32[]{:S(2)}, u32[]{:S(2)}) collective-permute-start(bf16[32,1024]{1,0:T(8,128)(2,1)S(1)} %get-tuple-element.108), channel_id=1, source_target_pairs={{0,16},{1,17},{2,18},{3,19},{4,20},{5,21},{6,22},{7,23},{8,24},{9,... | collective-permute-start | bytes 196616 | tf_op jit(solution)/shard_map/ppermute | solution.py:313
  193.7 11.7 %collective-permute-start.23 = (bf16[32,1024]{1,0:T(8,128)(2,1)S(1)}, bf16[32,1024]{1,0:T(8,128)(2,1)S(1)}, u32[]{:S(2)}, u32[]{:S(2)}) collective-permute-start(bf16[32,1024]{1,0:T(8,128)(2,1)S(1)} %get-tuple-element.107), channel_id=1, source_target_pairs={{0,24},{1,25},{2,26},{3,27},{4,28},{5,29},{6,30},{7,31},{8,16},{9,... | collective-permute-start | bytes 196616 | tf_op jit(solution)/shard_map/ppermute | solution.py:313
  195.5 10.6 %collective-permute-start.14 = (bf16[32,1024]{1,0:T(8,128)(2,1)S(1)}, bf16[32,1024]{1,0:T(8,128)(2,1)S(1)}, u32[]{:S(2)}, u32[]{:S(2)}) collective-permute-start(bf16[32,1024]{1,0:T(8,128)(2,1)S(1)} %get-tuple-element.109), channel_id=1, source_target_pairs={{0,8},{1,9},{2,10},{3,11},{4,12},{5,13},{6,14},{7,15},{8,0},{9,1},... | collective-permute-start | bytes 196616 | tf_op jit(solution)/shard_map/ppermute | solution.py:313
  202.5 7.7 %collective-permute-start.15 = (bf16[32,1024]{1,0:T(8,128)(2,1)S(1)}, bf16[32,1024]{1,0:T(8,128)(2,1)S(1)}, u32[]{:S(2)}, u32[]{:S(2)}) collective-permute-start(bf16[32,1024]{1,0:T(8,128)(2,1)S(1)} %get-tuple-element.111), channel_id=1, source_target_pairs={{0,16},{1,17},{2,18},{3,19},{4,20},{5,21},{6,22},{7,23},{8,24},{9,... | collective-permute-start | bytes 196616 | tf_op jit(solution)/shard_map/ppermute | solution.py:313
  204.0 6.1 %collective-permute-start.16 = (bf16[32,1024]{1,0:T(8,128)(2,1)S(1)}, bf16[32,1024]{1,0:T(8,128)(2,1)S(1)}, u32[]{:S(2)}, u32[]{:S(2)}) collective-permute-start(bf16[32,1024]{1,0:T(8,128)(2,1)S(1)} %get-tuple-element.110), channel_id=1, source_target_pairs={{0,24},{1,25},{2,26},{3,27},{4,28},{5,29},{6,30},{7,31},{8,16},{9,... | collective-permute-start | bytes 196616 | tf_op jit(solution)/shard_map/ppermute | solution.py:313
where the time goes:
time: 211 us
  waiting for transfers between devices  85.6 us (41%)
  starting transfers between devices  57.5 us (27%)
  Pallas kernels  46.5 us (22%)
  local copies, waits for them, and re-layouts  15.5 us (7%)
  other arithmetic  4.93 us (2%)
    ppermute x24, waiting for transfers between devices, swap(): lax.ppermute(value, AXES, [(i, i ^ offset) for i in range(device_count)])  85.6 us
    ppermute x24, starting transfers between devices, swap(): lax.ppermute(value, AXES, [(i, i ^ offset) for i in range(device_count)])  44.3 us
    pallas_call x2, Pallas kernels, project(): pl.pallas_call(kernel, grid=(modes // chunk,), in_specs=in_specs, out_spe...  16.9 us
    all_to_all x2, starting transfers between devices, exchange(): return lax.all_to_all(value, AXES, split_axis=0, concat_axis=0, tiled=True)  13.2 us
    pallas_call x1, Pallas kernels, clear_tiles(): pl.pallas_call(kernel, in_specs=[ANY], out_specs=[ANY, ANY], out_shape=[j...  11.2 us
    unnamed x27, local copies, waits for them, and re-layouts  9.55 us
    pallas_call x1, Pallas kernels, condense(): pl.pallas_call(kernel, grid=(local_subs,), in_specs=[SMEM, piece(interior...  8.8 us
    pallas_call x1, Pallas kernels, place(): pl.pallas_call(kernel, in_specs=[SMEM, SMEM, SMEM] + [ANY] * (depth + 2),...  5.57 us
  transfers between devices with their start and end apart: 26, of which 9 were waited for; matrix products, arithmetic and copies ran while one was open for 8% of the time, Pallas kernels for 12%

commit v1 on v0

--- a/solution.py
+++ b/solution.py
@@ -88,7 +88,7 @@
 
 def pick_modes(table, modes, ratio):
     device_count = table.shape[0]
-    width = modes.shape[2]
+    width = modes.shape[1]
 
     def kernel(table_ref, modes_ref, out_ref):
         def one(device, carry):
@@ -100,7 +100,7 @@
 
     return pl.pallas_call(
         kernel,
-        out_shape=jax.ShapeDtypeStruct((device_count, ratio, BLK, width), BF16),
+        out_shape=jax.ShapeDtypeStruct((device_count, ratio, width, BLK), BF16),
         in_specs=[SMEM, VMEM],
         out_specs=VMEM,
         name="pick_modes",
@@ -212,101 +212,130 @@
     )
 
 
-def project(block_map, fetched, laid_out, matrix, diagonal, dims, row_blocks):
-    z_size, y_size, x_size = dims
+def cut_shares(out, step, send_ref, keep_ref, dims):
+    _, y_size, x_size = dims
+    z_size = dims[0]
+    share = send_ref.shape[1]
+    pairs = out.shape[0] // (2 * share)
+    row, col = lax.axis_index("row"), lax.axis_index("col")
+    my_z, my_y = quotient(row, y_size), remainder(row, y_size)
+    my_x, mine = quotient(col, 2), remainder(col, 2) == 0
+    for i in range(pairs):
+        group = step * pairs + i
+        x = remainder(group, x_size)
+        y = remainder(quotient(group, x_size), y_size)
+        z = quotient(group, x_size * y_size)
+        slot = ((y ^ my_y) * x_size + (x ^ my_x)) * z_size + (z ^ my_z)
+        even = out[2 * i * share : (2 * i + 1) * share]
+        odd = out[(2 * i + 1) * share : (2 * i + 2) * share]
+        keep_ref[slot] = jnp.where(mine, even, odd)
+        send_ref[slot] = jnp.where(mine, odd, even).astype(BF16)
+
+
+def whole(*shape):
+    return pl.BlockSpec(shape, lambda i: (0,) * len(shape))
+
+
+def project_stiff(block_map, fetched, matrix, dims, row_blocks):
     local_subs, boundary, _ = matrix.shape
     depth = local_subs * boundary
     per_sub = boundary // BLK
-    groups = z_size * y_size * x_size
-    gathers = laid_out is None
-    if gathers:
-        row_count, _, ratio, _, width = fetched.shape
-        modes = row_count * width
-    else:
-        modes = laid_out[0].shape[1]
+    groups = dims[0] * dims[1] * dims[2]
+    row_count, _, ratio, width, _ = fetched.shape
+    modes = row_count * width
     share = modes // (2 * groups)
     chunk = modes // 2
-    pairs = chunk // (2 * share)
-
-    def kernel(*refs):
+
+    def kernel(map_ref, in_ref, m_ref, send_ref, keep_ref, t_ref, y_ref):
         step = pl.program_id(0)
-        if gathers:
-            map_ref, in_ref, m_ref, send_ref, keep_ref, q_ref, t_ref, y_ref = refs
-
-            @pl.when(step == 0)
-            def _():
-                for s in range(local_subs):
-                    for a in range(per_sub):
-                        tile_row = quotient(map_ref[s, a], row_blocks)
-                        c = quotient(tile_row, ratio)
-                        h = remainder(tile_row, ratio)
-                        k = (s * per_sub + a) * BLK
-                        for r in range(row_count):
-                            block = in_ref[r, c, h]
-                            q_ref[k : k + BLK, r * width : (r + 1) * width] = block
-                            t_ref[r * width : (r + 1) * width, k : k + BLK] = block.T
-
-            left_rows = pl.ds(pl.multiple_of(step * chunk, chunk), chunk)
-        else:
-            q_ref, t_ref, m_ref, d_ref, send_ref, keep_ref, y_ref = refs
-            left_rows = slice(None)
-        row, col = lax.axis_index("row"), lax.axis_index("col")
-        my_z, my_y = quotient(row, y_size), remainder(row, y_size)
-        my_x, my_core = quotient(col, 2), remainder(col, 2)
+
+        @pl.when(step == 0)
+        def _():
+            for s in range(local_subs):
+                for a in range(per_sub):
+                    tile_row = quotient(map_ref[s, a], row_blocks)
+                    c = quotient(tile_row, ratio)
+                    h = remainder(tile_row, ratio)
+                    k = (s * per_sub + a) * BLK
+                    for r in range(row_count):
+                        t_ref[r * width : (r + 1) * width, k : k + BLK] = in_ref[r, c, h]
+
+        rows = pl.ds(pl.multiple_of(step * chunk, chunk), chunk)
         for s in range(local_subs):
             span = slice(s * boundary, (s + 1) * boundary)
-            left = t_ref[left_rows, span]
+            y_ref[:, span] = jnp.dot(
+                t_ref[rows, span], m_ref[s], preferred_element_type=F32
+            ).astype(BF16)
+        out = lax.dot_general(
+            y_ref[...], t_ref[...], (((1,), (1,)), ((), ())), preferred_element_type=F32
+        )
+        cut_shares(out, step, send_ref, keep_ref, dims)
+
+    return pl.pallas_call(
+        kernel,
+        grid=(modes // chunk,),
+        in_specs=[SMEM, whole(*fetched.shape), whole(local_subs, boundary, boundary)],
+        out_specs=[
+            whole(groups, share, modes),
+            whole(groups, share, modes),
+            whole(modes, depth),
+        ],
+        out_shape=[
+            jax.ShapeDtypeStruct((groups, share, modes), BF16),
+            jax.ShapeDtypeStruct((groups, share, modes), F32),
+            jax.ShapeDtypeStruct((modes, depth), BF16),
+        ],
+        scratch_shapes=[pltpu.VMEM((chunk, depth), BF16)],
+        name="project_stiff",
+    )(block_map, fetched, matrix)
+
+
+def mix_mass(qt, matrix, diagonal):
+    modes, depth = qt.shape
+    local_subs, boundary, _ = matrix.shape
+    chunk = modes // 4
+
+    def kernel(t_ref, m_ref, d_ref, y_ref):
+        for s in range(local_subs):
+            span = slice(s * boundary, (s + 1) * boundary)
+            left = t_ref[:, span]
             y = jnp.dot(left, m_ref[s], preferred_element_type=F32)
-            if diagonal is not None:
-                y = y + left.astype(F32) * d_ref[s]
-            y_ref[:, span] = y.astype(BF16)
-        out = jnp.dot(y_ref[...], q_ref[...], preferred_element_type=F32)
-        for i in range(pairs):
-            group = step * pairs + i
-            x = remainder(group, x_size)
-            y = remainder(quotient(group, x_size), y_size)
-            z = quotient(group, x_size * y_size)
-            slot = ((y ^ my_y) * x_size + (x ^ my_x)) * z_size + (z ^ my_z)
-            even = out[2 * i * share : (2 * i + 1) * share]
-            odd = out[(2 * i + 1) * share : (2 * i + 2) * share]
-            mine = my_core == 0
-            keep_ref[slot] = jnp.where(mine, even, odd)
-            send_ref[slot] = jnp.where(mine, odd, even).astype(BF16)
-
-    def whole(*shape):
-        return pl.BlockSpec(shape, lambda i: (0,) * len(shape))
-
-    out_specs = [whole(groups, share, modes), whole(groups, share, modes)]
-    out_shape = [
-        jax.ShapeDtypeStruct((groups, share, modes), BF16),
-        jax.ShapeDtypeStruct((groups, share, modes), F32),
-    ]
-    matrix_spec = whole(local_subs, boundary, boundary)
-    if gathers:
-        operands = (block_map, fetched, matrix)
-        in_specs = [SMEM, whole(*fetched.shape), matrix_spec]
-        out_specs += [whole(depth, modes), whole(modes, depth)]
-        out_shape += [
-            jax.ShapeDtypeStruct((depth, modes), BF16),
-            jax.ShapeDtypeStruct((modes, depth), BF16),
-        ]
-    else:
-        operands = (*laid_out, matrix, diagonal)
-        in_specs = [
-            whole(depth, modes),
-            pl.BlockSpec((chunk, depth), lambda i: (i, 0)),
-            matrix_spec,
-            whole(local_subs, 1, boundary),
-        ]
+            y_ref[:, span] = (y + left.astype(F32) * d_ref[s]).astype(BF16)
+
+    rows = pl.BlockSpec((chunk, depth), lambda i: (i, 0))
     return pl.pallas_call(
         kernel,
         grid=(modes // chunk,),
-        in_specs=in_specs,
-        out_specs=out_specs,
-        out_shape=out_shape,
-        scratch_shapes=[pltpu.VMEM((chunk, depth), BF16)],
-        name="project_stiff" if gathers else "project_mass",
-    )(*operands)
+        in_specs=[rows, whole(local_subs, boundary, boundary), whole(local_subs, 1, boundary)],
+        out_specs=rows,
+        out_shape=jax.ShapeDtypeStruct((modes, depth), BF16),
+        name="mix_mass",
+    )(qt, matrix, diagonal)
+
+
+def project_mass(mixed, qt, dims):
+    modes, depth = qt.shape
+    groups = dims[0] * dims[1] * dims[2]
+    share = modes // (2 * groups)
+    chunk = modes // 2
+
+    def kernel(y_ref, t_ref, send_ref, keep_ref):
+        out = lax.dot_general(
+            y_ref[...], t_ref[...], (((1,), (1,)), ((), ())), preferred_element_type=F32
+        )
+        cut_shares(out, pl.program_id(0), send_ref, keep_ref, dims)
+
+    return pl.pallas_call(
+        kernel,
+        grid=(modes // chunk,),
+        in_specs=[pl.BlockSpec((chunk, depth), lambda i: (i, 0)), whole(modes, depth)],
+        out_specs=[whole(groups, share, modes), whole(groups, share, modes)],
+        out_shape=[
+            jax.ShapeDtypeStruct((groups, share, modes), BF16),
+            jax.ShapeDtypeStruct((groups, share, modes), F32),
+        ],
+        name="project_mass",
+    )(mixed, qt)
 
 
 def swap(value, offset, device_count):
@@ -330,9 +359,9 @@
 
 
 def spread_in_plane(blocks, sizes):
-    near = [blocks[0]] + [
-        swap(blocks[d], d, sizes.devices) for d in range(1, sizes.plane)
-    ]
+    near = [blocks[0]]
+    for d in range(1, sizes.plane):
+        near.append(swap(blocks[d], d, sizes.devices))
     return [jnp.stack([part[z] for part in near]) for z in range(sizes.devices // sizes.plane)]
 
 
@@ -481,25 +510,26 @@
     dims = (row_count // y_size, y_size, x_size)
 
     table = exchange(describe(block_map, sizes))
+    turned = jnp.swapaxes(modes.reshape(sizes.col_blocks, BLK, width), 1, 2)
+    wanted = pick_modes(table, turned, sizes.ratio)
+    fetched = exchange(wanted)
     blocks, stiff, mass, diagonal = condense(
         block_map, inv_interior, coupling, boundary_stiff, mass_interior, mass_boundary, sizes
     )
-    table, blocks = lax.optimization_barrier((table, blocks))
     spread = spread_in_plane(blocks, sizes)
     beside = swap(spread[1], sizes.plane, sizes.devices)
-    wanted = pick_modes(table, modes.reshape(sizes.col_blocks, BLK, width), sizes.ratio)
-    fetched = exchange(wanted)
     stiff_tile, mass_tile = clear_tiles(table, sizes)
-    late, beside, fetched, stiff_tile, mass_tile = lax.optimization_barrier(
-        (spread[2:], beside, fetched, stiff_tile, mass_tile)
+    late, fetched, stiff_tile, mass_tile = lax.optimization_barrier(
+        (spread[2:], fetched, stiff_tile, mass_tile)
     )
     late = [swap(part, (2 + d) * sizes.plane, sizes.devices) for d, part in enumerate(late)]
     arrived = [spread[0], beside, *late]
 
-    fetched = fetched.reshape(row_count, col_count, sizes.ratio, BLK, width)
-    send, keep, q, qt = project(block_map, fetched, None, stiff, None, dims, sizes.row_blocks)
+    fetched = fetched.reshape(row_count, col_count, sizes.ratio, width, BLK)
+    send, keep, qt = project_stiff(block_map, fetched, stiff, dims, sizes.row_blocks)
     reduced_stiff = reduce_shares(send, keep, sizes)
-    send, keep = project(None, None, (q, qt), mass, diagonal, dims, sizes.row_blocks)
+    mixed = mix_mass(qt, mass, diagonal)
+    send, keep = project_mass(mixed, qt, dims)
     reduced_mass = reduce_shares(send, keep, sizes)
 
     slot = table[:, sizes.ratio]

time: 211 us -> 194 us (0.919)
  waiting for transfers between devices: 85.6 us -> 67.3 us
  starting transfers between devices: 57.5 us -> 52.4 us
  local copies, waits for them, and re-layouts: 15.5 us -> 18.6 us
  Pallas kernels: 46.5 us -> 49.5 us
    ppermute x24, waiting for transfers between devices: 85.6 us -> 62.4 us  [swap(): lax.ppermute(value, AXES, [(i, i ^ offset) for i in range(device_count)])]
    all_to_all x2, waiting for transfers between devices: 0.01 us -> 4.84 us  [exchange(): return lax.all_to_all(value, AXES, split_axis=0, concat_axis=0, tiled=True)]
    all_to_all x2, starting transfers between devices: 13.2 us -> 10.2 us  [exchange(): return lax.all_to_all(value, AXES, split_axis=0, concat_axis=0, tiled=True)]
    pallas_call x2 -> x3, Pallas kernels: 16.9 us -> 19.8 us  [the longest x1 8.46 us: project_stiff(): pl.pallas_call(kernel, grid=(modes // chunk,), in_specs=[SMEM, whole(*fet...]
    reshape x0 -> x1, local copies, waits for them, and re-layouts: none -> 2.27 us  [reduction(): turned = jnp.swapaxes(modes.reshape(sizes.col_blocks, BLK, width), 1, 2)]
    ppermute x24, starting transfers between devices: 44.3 us -> 42.2 us  [swap(): lax.ppermute(value, AXES, [(i, i ^ offset) for i in range(device_count)])]
    unnamed x27 -> x33, local copies, waits for them, and re-layouts: 9.55 us -> 10.6 us
  transfers between devices with their start and end apart: 26 -> 26, of which waited for: 9 -> 10; matrix products, arithmetic and copies ran while one was open for 8% -> 10% of each run, Pallas kernels for 12% -> 13%
where the time goes in v1:
time: 194 us; the launch traced here: 193 us
  waiting for transfers between devices  67.3 us (35%)
  starting transfers between devices  52.4 us (27%)
  Pallas kernels  49.5 us (26%)
  local copies, waits for them, and re-layouts  18.6 us (10%)
  other arithmetic  4.84 us (2%)
    ppermute x24, waiting for transfers between devices, swap(): lax.ppermute(value, AXES, [(i, i ^ offset) for i in range(device_count)])  62.4 us
    ppermute x24, starting transfers between devices, swap(): lax.ppermute(value, AXES, [(i, i ^ offset) for i in range(device_count)])  42.2 us
    pallas_call x1, Pallas kernels, clear_tiles(): pl.pallas_call(kernel, in_specs=[ANY], out_specs=[ANY, ANY], out_shape=[j...  11.2 us
    unnamed x33, local copies, waits for them, and re-layouts  10.6 us
    all_to_all x2, starting transfers between devices, exchange(): return lax.all_to_all(value, AXES, split_axis=0, concat_axis=0, tiled=True)  10.2 us
    pallas_call x1, Pallas kernels, condense(): pl.pallas_call(kernel, grid=(local_subs,), in_specs=[SMEM, piece(interior...  8.8 us
    pallas_call x1, Pallas kernels, project_stiff(): pl.pallas_call(kernel, grid=(modes // chunk,), in_specs=[SMEM, whole(*fet...  8.46 us
    pallas_call x1, Pallas kernels, project_mass(): pl.pallas_call(kernel, grid=(modes // chunk,), in_specs=[pl.BlockSpec((ch...  6.29 us
  transfers between devices with their start and end apart: 26, of which 10 were waited for; matrix products, arithmetic and copies ran while one was open for 10% of the time, Pallas kernels for 13%

profile of v1, /device:TPU:0, one launch (start us, length us, event | category | flops | bytes accessed | tf_op | source)
XLA Modules:
  0.0 193.4 jit_solution(4176620553294403490)
XLA Ops:
  0.6 1.4 describe.1
  2.0 7.3 %all-to-all-start = ((s32[32,1,128]{2,1,0:T(1,128)}), s32[32,1,128]{2,1,0:T(1,128)S(1)}, u32[]{:S(2)}, u32[]{:S(2)}) async-start(s32[32,1,128]{2,1,0:T(1,128)} %bitcast.66), calls=%async_computation | async-start | bytes 32768 | tf_op jit(solution)/shard_map/all_to_all | solution.py:32
  9.3 2.3 %copy.21 = bf16[32,128,128]{1,2,0:T(8,128)(2,1)} copy(bf16[32,128,128]{2,1,0:T(8,128)(2,1)} %bitcast.61) | data formatting | bytes 2097152 | tf_op jit(solution)/shard_map/reshape | solution.py:513
  11.6 4.8 %all-to-all-done = s32[32,1,128]{2,1,0:T(1,128)S(1)} async-done(((s32[32,1,128]{2,1,0:T(1,128)}), s32[32,1,128]{2,1,0:T(1,128)S(1)}, u32[]{:S(2)}, u32[]{:S(2)}) %all-to-all-start) | async-done | bytes 16416 | tf_op jit(solution)/shard_map/all_to_all | solution.py:32
  16.4 0.6 copy-done.7
  17.0 2.7 %pick_modes.1 = bf16[32,2,128,128]{3,2,1,0:T(8,128)(2,1)} custom-call(s32[32,128]{1,0:T(8,128)} %bitcast.62, bf16[32,128,128]{2,1,0:T(8,128)(2,1)} %bitcast.60), custom_call_target="tpu_custom_call" | custom-call | tf_op jit(solution)/shard_map/pick_modes/pallas_call | solution.py:101
  19.8 2.9 %all-to-all-start.1 = ((bf16[32,2,128,128]{3,2,1,0:T(8,128)(2,1)}), bf16[32,2,128,128]{3,2,1,0:T(8,128)(2,1)S(1)}, u32[]{:S(2)}, u32[]{:S(2)}) async-start(bf16[32,2,128,128]{3,2,1,0:T(8,128)(2,1)} %pick_modes.1), calls=%async_computation.1 | async-start | bytes 4194304 | tf_op jit(solution)/shard_map/all_to_all | solution.py:32
  22.7 1.3 copy.20.mi_ref
  24.0 0.6 broadcast_in_dim.27.mb_ref
  24.6 8.8 %condense.1 = (bf16[8,4,272,128]{3,2,1,0:T(8,128)(2,1)}, bf16[2,512,512]{2,1,0:T(8,128)(2,1)}, bf16[2,512,512]{2,1,0:T(8,128)(2,1)}, f32[2,1,512]{2,1,0:T(1,128)}) custom-call(s32[2,4]{1,0:T(2,128)} %map_ref.5, bf16[2,1024,1024]{2,1,0:T(8,128)(2,1)} %inv_ref.1, bf16[2,1024,512]{2,1,0:T(8,128)(2,1)} %cpl_ref.1, bf16[2,512,512]{2,1,0:T(8,128)(2,1)} %stiff_ref.1, ...), custom_call_target="tpu_custom_call" | custom-call | tf_op jit(solution)/shard_map/condense/pallas_call | solution.py:181
  33.4 2.8 %slice_bitcast_fusion = (bf16[4,272,128]{2,1,0:T(8,128)(2,1)}, bf16[4,272,128]{2,1,0:T(8,128)(2,1)}, bf16[4,272,128]{2,1,0:T(8,128)(2,1)}, bf16[4,272,128]{2,1,0...) fusion(bf16[8,4,272,128]{3,2,1,0:T(8,128)(2,1)} %get-tuple-element.24), kind=kLoop, calls=%fused_computation.8 | loop fusion | bytes 3899392 | tf_op jit(solution)/shard_map/squeeze | solution.py:364
  36.2 0.1 collective-permute-start
  36.3 1.6 collective-permute-start.1
  38.0 0.1 collective-permute-start.2
  38.1 1.7 collective-permute-start.3
  39.7 0.1 collective-permute-start.4
  39.8 1.7 bitcast_dynamic-update-slice_fusion
  41.5 11.2 %clear_tiles.1 = (bf16[2048,4096]{1,0:T(8,128)(2,1)}, bf16[2048,4096]{1,0:T(8,128)(2,1)}) custom-call(s32[32,128]{1,0:T(8,128)} %bitcast.63), custom_call_target="tpu_custom_call" | custom-call | tf_op jit(solution)/shard_map/clear_tiles/pallas_call | solution.py:383
  52.7 2.6 %collective-permute-start.5 = (bf16[4,272,128]{2,1,0:T(8,128)(2,1)}, bf16[4,272,128]{2,1,0:T(8,128)(2,1)S(1)}, u32[]{:S(2)}, u32[]{:S(2)}) collective-permute-start(bf16[4,272,128]{2,1,0:T(8,128)(2,1)} %get-tuple-element.58), channel_id=1, source_target_pairs={{0,6},{1,7},{2,4},{3,5},{4,2},{5,3},{6,0},{7,1},{8,14},{9,15},{10,... | collective-permute-start | bytes 835592 | tf_op jit(solution)/shard_map/ppermute | solution.py:342
  55.4 1.7 slice_dynamic-update-slice_fusion.6
  57.1 1.7 slice_dynamic-update-slice_fusion.5
  58.8 0.7 slice_dynamic-update-slice_fusion.4
  59.5 0.7 slice_dynamic-update-slice_fusion.3
  60.2 6.7 %collective-permute-done.4 = bf16[4,272,128]{2,1,0:T(8,128)(2,1)S(1)} collective-permute-done((bf16[4,272,128]{2,1,0:T(8,128)(2,1)}, bf16[4,272,128]{2,1,0:T(8,128)(2,1)S(1)}, u32[]{:S(2)}, u32[]{:S(2)}) %collective-permute-start.4) | collective-permute-done | bytes 278560 | tf_op jit(solution)/shard_map/ppermute | solution.py:342
  66.9 0.7 slice_dynamic-update-slice_fusion.2
  67.6 2.1 %collective-permute-done.5 = bf16[4,272,128]{2,1,0:T(8,128)(2,1)S(1)} collective-permute-done((bf16[4,272,128]{2,1,0:T(8,128)(2,1)}, bf16[4,272,128]{2,1,0:T(8,128)(2,1)S(1)}, u32[]{:S(2)}, u32[]{:S(2)}) %collective-permute-start.5) | collective-permute-done | bytes 278560 | tf_op jit(solution)/shard_map/ppermute | solution.py:342
  69.6 0.7 slice_dynamic-update-slice_fusion.1
  70.3 4.2 %collective-permute-done.6 = bf16[4,272,128]{2,1,0:T(8,128)(2,1)S(1)} collective-permute-done((bf16[4,272,128]{2,1,0:T(8,128)(2,1)}, bf16[4,272,128]{2,1,0:T(8,128)(2,1)S(1)}, u32[]{:S(2)}, u32[]{:S(2)}) %collective-permute-start.6) | collective-permute-done | bytes 278560 | tf_op jit(solution)/shard_map/ppermute | solution.py:342
  74.5 0.7 slice_dynamic-update-slice_fusion
  75.2 1.4 copy-done
  76.6 8.5 %project_stiff.1 = (bf16[16,32,1024]{2,1,0:T(8,128)(2,1)}, f32[16,32,1024]{2,1,0:T(8,128)}, bf16[1024,1024]{1,0:T(8,128)(2,1)}) custom-call(s32[2,4]{1,0:T(2,128)} %map_ref.5, bf16[8,4,2,128,128]{4,3,2,1,0:T(8,128)(2,1)} %bitcast.59, bf16[2,512,512]{2,1,0:T(8,128)(2,1)} %get-tuple-element.34.m_ref), custom_call_target="tpu_custom_call" | custom-call | tf_op jit(solution)/shard_map/project_stiff/pallas_call | solution.py:274
  85.1 5.0 %mix_mass.1.y_ref = bf16[1024,1024]{1,0:T(8,128)(2,1)} custom-call(bf16[1024,1024]{1,0:T(8,128)(2,1)} %get-tuple-element.37.t_ref, bf16[2,512,512]{2,1,0:T(8,128)(2,1)} %get-tuple-element.38.m_ref, f32[2,1,512]{2,1,0:T(1,128)} %get-tuple-element.39.d_ref), custom_call_target="tpu_custom_call" | custom-call | tf_op jit(solution)/shard_map/mix_mass/pallas_call | solution.py:306
  90.1 6.3 %project_mass.1 = (bf16[16,32,1024]{2,1,0:T(8,128)(2,1)}, f32[16,32,1024]{2,1,0:T(8,128)}) custom-call(bf16[1024,1024]{1,0:T(8,128)(2,1)} %mix_mass.1.y_ref, bf16[1024,1024]{1,0:T(8,128)(2,1)} %get-tuple-element.37.t_ref), custom_call_target="tpu_custom_call" | custom-call | tf_op jit(solution)/shard_map/project_mass/pallas_call | solution.py:328
  96.4 1.9 collective-permute-start.17
  98.3 0.9 collective-permute-start.7
  99.2 3.1 %collective-permute-start.8 = (bf16[8,272,128]{2,1,0:T(8,128)(2,1)S(1)}, bf16[8,272,128]{2,1,0:T(8,128)(2,1)S(1)}, u32[]{:S(2)}, u32[]{:S(2)}) collective-permute-start(bf16[8,272,128]{2,1,0:T(8,128)(2,1)S(1)} %copy-done.10), channel_id=1, source_target_pairs={{0,16},{1,17},{2,18},{3,19},{4,20},{5,21},{6,22},{7,23},{8,24},{9,... | collective-permute-start | bytes 1671176 | tf_op jit(solution)/shard_map/ppermute | solution.py:342
  102.3 0.8 collective-permute-start.9
  103.1 0.2 slice_reduce_fusion
  103.3 0.2 convert_reduce_fusion
  103.5 0.6 select_reduce_fusion
  104.1 20.9 %collective-permute-done.7.refs_4_ = bf16[8,272,128]{2,1,0:T(8,128)(2,1)S(1)} collective-permute-done((bf16[8,272,128]{2,1,0:T(8,128)(2,1)}, bf16[8,272,128]{2,1,0:T(8,128)(2,1)S(1)}, u32[]{:S(2)}, u32[]{:S(2)}) %collective-permute-start.7) | collective-permute-done | bytes 557088 | tf_op jit(solution)/shard_map/ppermute | solution.py:342
  125.0 15.0 %collective-permute-done.9.refs_6_ = bf16[8,272,128]{2,1,0:T(8,128)(2,1)S(1)} collective-permute-done((bf16[8,272,128]{2,1,0:T(8,128)(2,1)S(1)}, bf16[8,272,128]{2,1,0:T(8,128)(2,1)S(1)}, u32[]{:S(2)}, u32[]{:S(2)}) %collective-permute-start.9) | collective-permute-done | bytes 557088 | tf_op jit(solution)/shard_map/ppermute | solution.py:342
  140.0 0.8 copy-done.6
  140.8 5.6 %place.1 = (bf16[2048,4096]{1,0:T(8,128)(2,1)}, bf16[2048,4096]{1,0:T(8,128)(2,1)}, f32[4,1,128]{2,1,0:T(1,128)}) custom-call(s32[32,128]{1,0:T(8,128)} %bitcast.64, s32[32]{0:T(128)} %get-tuple-element.44.refs_1_, s32[32]{0:T(128)} %get-tuple-element.43.refs_2_, bf16[8,272,128]{2,1,0:T(8,128)(2,1)} %copy-done.3, ...), custom_call_target="tpu_custom_call", output_to_operand_aliasing={{0}: (7, {}), {1}: (8, {})} | custom-call | tf_op jit(solution)/shard_map/place/pallas_call | solution.py:474
  146.4 1.8 fusion.14
  148.3 1.7 collective-permute-start.18
  150.0 1.9 collective-permute-start.20
  151.8 0.5 fusion.17
  152.4 1.7 collective-permute-start.11
  154.1 3.4 %collective-permute-done.18 = bf16[4,32,1024]{2,1,0:T(8,128)(2,1)S(1)} collective-permute-done((bf16[4,32,1024]{2,1,0:T(8,128)(2,1)S(1)}, bf16[4,32,1024]{2,1,0:T(8,128)(2,1)S(1)}, u32[]{:S(2)}, u32[]{:S(2)}) %collective-permute-start.18) | collective-permute-done | bytes 262176 | tf_op jit(solution)/shard_map/ppermute | solution.py:342
  157.5 0.9 collective-permute-start.13
  158.4 6.1 %collective-permute-done.19 = bf16[4,32,1024]{2,1,0:T(8,128)(2,1)S(1)} collective-permute-done((bf16[4,32,1024]{2,1,0:T(8,128)(2,1)S(1)}, bf16[4,32,1024]{2,1,0:T(8,128)(2,1)S(1)}, u32[]{:S(2)}, u32[]{:S(2)}) %collective-permute-start.19) | collective-permute-done | bytes 262176 | tf_op jit(solution)/shard_map/ppermute | solution.py:342
  164.6 0.2 fusion.12
  164.8 11.6 %collective-permute-start.21 = (bf16[32,1024]{1,0:T(8,128)(2,1)S(1)}, bf16[32,1024]{1,0:T(8,128)(2,1)S(1)}, u32[]{:S(2)}, u32[]{:S(2)}) collective-permute-start(bf16[32,1024]{1,0:T(8,128)(2,1)S(1)} %get-tuple-element.98), channel_id=1, source_target_pairs={{0,8},{1,9},{2,10},{3,11},{4,12},{5,13},{6,14},{7,15},{8,0},{9,1},... | collective-permute-start | bytes 196616 | tf_op jit(solution)/shard_map/ppermute | solution.py:342
  176.3 1.0 collective-permute-start.22
  177.3 1.4 collective-permute-start.23
  178.8 0.2 fusion.15
  179.0 6.4 %collective-permute-start.14 = (bf16[32,1024]{1,0:T(8,128)(2,1)S(1)}, bf16[32,1024]{1,0:T(8,128)(2,1)S(1)}, u32[]{:S(2)}, u32[]{:S(2)}) collective-permute-start(bf16[32,1024]{1,0:T(8,128)(2,1)S(1)} %get-tuple-element.101), channel_id=1, source_target_pairs={{0,8},{1,9},{2,10},{3,11},{4,12},{5,13},{6,14},{7,15},{8,0},{9,1},... | collective-permute-start | bytes 196616 | tf_op jit(solution)/shard_map/ppermute | solution.py:342
  185.4 1.1 collective-permute-start.15
  186.5 1.4 collective-permute-start.16
  187.9 0.7 fusion.6
  188.6 2.6 %collective-permute-done.15 = bf16[32,1024]{1,0:T(8,128)(2,1)S(1)} collective-permute-done((bf16[32,1024]{1,0:T(8,128)(2,1)S(1)}, bf16[32,1024]{1,0:T(8,128)(2,1)S(1)}, u32[]{:S(2)}, u32[]{:S(2)}) %collective-permute-start.15) | collective-permute-done | bytes 65568 | tf_op jit(solution)/shard_map/ppermute | solution.py:342
  191.3 1.4 collective-permute-done.16
  192.7 0.7 fusion.9
  (47 shorter events, 0.3 us)
Async XLA Ops:
  2.0 14.4 %all-to-all-start = ((s32[32,1,128]{2,1,0:T(1,128)}), s32[32,1,128]{2,1,0:T(1,128)S(1)}, u32[]{:S(2)}, u32[]{:S(2)}) async-start(s32[32,1,128]{2,1,0:T(1,128)} %bitcast.66), calls=%async_computation | async-start | bytes 32768 | tf_op jit(solution)/shard_map/all_to_all | solution.py:32
  16.4 0.6 copy-start.7
  19.8 2.9 %copy-start.11 = (f32[2,1024]{1,0:T(2,128)S(1)}, f32[2,1024]{1,0:T(2,128)}, u32[]{:S(2)}) copy-start(f32[2,1024]{1,0:T(2,128)} %param.10) | copy-start | bytes 24580
  19.8 4.2 %copy-start.12 = (f32[2,512]{1,0:T(2,128)S(1)}, f32[2,512]{1,0:T(2,128)}, u32[]{:S(2)}) copy-start(f32[2,512]{1,0:T(2,128)} %param.11) | copy-start | bytes 12292
  19.8 55.4 %all-to-all-start.1 = ((bf16[32,2,128,128]{3,2,1,0:T(8,128)(2,1)}), bf16[32,2,128,128]{3,2,1,0:T(8,128)(2,1)S(1)}, u32[]{:S(2)}, u32[]{:S(2)}) async-start(bf16[32,2,128,128]{3,2,1,0:T(8,128)(2,1)} %pick_modes.1), calls=%async_computation.1 | async-start | bytes 4194304 | tf_op jit(solution)/shard_map/all_to_all | solution.py:32
  36.2 16.5 %collective-permute-start = (bf16[4,272,128]{2,1,0:T(8,128)(2,1)}, bf16[4,272,128]{2,1,0:T(8,128)(2,1)}, u32[]{:S(2)}, u32[]{:S(2)}) collective-permute-start(bf16[4,272,128]{2,1,0:T(8,128)(2,1)} %get-tuple-element.63), channel_id=1, source_target_pairs={{0,1},{1,0},{2,3},{3,2},{4,5},{5,4},{6,7},{7,6},{8,9},{9,8},{10,11... | collective-permute-start | bytes 835592 | tf_op jit(solution)/shard_map/ppermute | solution.py:342
  36.3 20.7 %collective-permute-start.1 = (bf16[4,272,128]{2,1,0:T(8,128)(2,1)}, bf16[4,272,128]{2,1,0:T(8,128)(2,1)}, u32[]{:S(2)}, u32[]{:S(2)}) collective-permute-start(bf16[4,272,128]{2,1,0:T(8,128)(2,1)} %get-tuple-element.62), channel_id=1, source_target_pairs={{0,2},{1,3},{2,0},{3,1},{4,6},{5,7},{6,4},{7,5},{8,10},{9,11},{10,... | collective-permute-start | bytes 835592 | tf_op jit(solution)/shard_map/ppermute | solution.py:342
  38.0 20.8 %collective-permute-start.2 = (bf16[4,272,128]{2,1,0:T(8,128)(2,1)}, bf16[4,272,128]{2,1,0:T(8,128)(2,1)S(1)}, u32[]{:S(2)}, u32[]{:S(2)}) collective-permute-start(bf16[4,272,128]{2,1,0:T(8,128)(2,1)} %get-tuple-element.61), channel_id=1, source_target_pairs={{0,3},{1,2},{2,1},{3,0},{4,7},{5,6},{6,5},{7,4},{8,11},{9,10},{10,... | collective-permute-start | bytes 835592 | tf_op jit(solution)/shard_map/ppermute | solution.py:342
  38.1 21.4 %collective-permute-start.3 = (bf16[4,272,128]{2,1,0:T(8,128)(2,1)}, bf16[4,272,128]{2,1,0:T(8,128)(2,1)S(1)}, u32[]{:S(2)}, u32[]{:S(2)}) collective-permute-start(bf16[4,272,128]{2,1,0:T(8,128)(2,1)} %get-tuple-element.60), channel_id=1, source_target_pairs={{0,4},{1,5},{2,6},{3,7},{4,0},{5,1},{6,2},{7,3},{8,12},{9,13},{10,... | collective-permute-start | bytes 835592 | tf_op jit(solution)/shard_map/ppermute | solution.py:342
  39.7 27.1 %collective-permute-start.4 = (bf16[4,272,128]{2,1,0:T(8,128)(2,1)}, bf16[4,272,128]{2,1,0:T(8,128)(2,1)S(1)}, u32[]{:S(2)}, u32[]{:S(2)}) collective-permute-start(bf16[4,272,128]{2,1,0:T(8,128)(2,1)} %get-tuple-element.59), channel_id=1, source_target_pairs={{0,5},{1,4},{2,7},{3,6},{4,1},{5,0},{6,3},{7,2},{8,13},{9,12},{10,... | collective-permute-start | bytes 835592 | tf_op jit(solution)/shard_map/ppermute | solution.py:342
  52.7 16.9 %collective-permute-start.5 = (bf16[4,272,128]{2,1,0:T(8,128)(2,1)}, bf16[4,272,128]{2,1,0:T(8,128)(2,1)S(1)}, u32[]{:S(2)}, u32[]{:S(2)}) collective-permute-start(bf16[4,272,128]{2,1,0:T(8,128)(2,1)} %get-tuple-element.58), channel_id=1, source_target_pairs={{0,6},{1,7},{2,4},{3,5},{4,2},{5,3},{6,0},{7,1},{8,14},{9,15},{10,... | collective-permute-start | bytes 835592 | tf_op jit(solution)/shard_map/ppermute | solution.py:342
  57.1 17.5 %collective-permute-start.6 = (bf16[4,272,128]{2,1,0:T(8,128)(2,1)}, bf16[4,272,128]{2,1,0:T(8,128)(2,1)S(1)}, u32[]{:S(2)}, u32[]{:S(2)}) collective-permute-start(bf16[4,272,128]{2,1,0:T(8,128)(2,1)} %get-tuple-element.57), channel_id=1, source_target_pairs={{0,7},{1,6},{2,5},{3,4},{4,3},{5,2},{6,1},{7,0},{8,15},{9,14},{10,... | collective-permute-start | bytes 835592 | tf_op jit(solution)/shard_map/ppermute | solution.py:342
  75.2 21.2 %copy-start.3 = (bf16[8,272,128]{2,1,0:T(8,128)(2,1)}, bf16[8,272,128]{2,1,0:T(8,128)(2,1)S(1)}, u32[]{:S(2)}) copy-start(bf16[8,272,128]{2,1,0:T(8,128)(2,1)S(1)} %get-tuple-element.73.refs_3_) | copy-start | bytes 1671172
  75.2 1.4 copy-start
  90.1 9.1 %copy-start.10 = (bf16[8,272,128]{2,1,0:T(8,128)(2,1)S(1)}, bf16[8,272,128]{2,1,0:T(8,128)(2,1)}, u32[]{:S(2)}) copy-start(bf16[8,272,128]{2,1,0:T(8,128)(2,1)} %get-tuple-element.27) | copy-start | bytes 1671172
  90.1 12.2 %copy-start.9 = (bf16[8,272,128]{2,1,0:T(8,128)(2,1)S(1)}, bf16[8,272,128]{2,1,0:T(8,128)(2,1)}, u32[]{:S(2)}) copy-start(bf16[8,272,128]{2,1,0:T(8,128)(2,1)} %get-tuple-element.28) | copy-start | bytes 1671172
  90.1 13.0 %copy-start.8 = (s32[32,1,128]{2,1,0:T(1,128)S(1)}, s32[32,1,128]{2,1,0:T(1,128)}, u32[]{:S(2)}) copy-start(s32[32,1,128]{2,1,0:T(1,128)} %copy-done.7) | copy-start | bytes 49156
  96.4 50.0 %collective-permute-start.17 = (bf16[16,32,1024]{2,1,0:T(8,128)(2,1)}, bf16[16,32,1024]{2,1,0:T(8,128)(2,1)}, u32[]{:S(2)}, u32[]{:S(2)}) collective-permute-start(bf16[16,32,1024]{2,1,0:T(8,128)(2,1)} %get-tuple-element.41), channel_id=1, source_target_pairs={{0,1},{1,0},{2,3},{3,2},{4,5},{5,4},{6,7},{7,6},{8,9},{9,8},{10,11... | collective-permute-start | bytes 3145736 | tf_op jit(solution)/shard_map/ppermute | solution.py:342
  98.3 26.7 %collective-permute-start.7 = (bf16[8,272,128]{2,1,0:T(8,128)(2,1)}, bf16[8,272,128]{2,1,0:T(8,128)(2,1)S(1)}, u32[]{:S(2)}, u32[]{:S(2)}) collective-permute-start(bf16[8,272,128]{2,1,0:T(8,128)(2,1)} %get-tuple-element.72), channel_id=1, source_target_pairs={{0,8},{1,9},{2,10},{3,11},{4,12},{5,13},{6,14},{7,15},{8,0},{9,1},... | collective-permute-start | bytes 1671176 | tf_op jit(solution)/shard_map/ppermute | solution.py:342
  99.2 25.9 %collective-permute-start.8 = (bf16[8,272,128]{2,1,0:T(8,128)(2,1)S(1)}, bf16[8,272,128]{2,1,0:T(8,128)(2,1)S(1)}, u32[]{:S(2)}, u32[]{:S(2)}) collective-permute-start(bf16[8,272,128]{2,1,0:T(8,128)(2,1)S(1)} %copy-done.10), channel_id=1, source_target_pairs={{0,16},{1,17},{2,18},{3,19},{4,20},{5,21},{6,22},{7,23},{8,24},{9,... | collective-permute-start | bytes 1671176 | tf_op jit(solution)/shard_map/ppermute | solution.py:342
  102.3 37.7 %collective-permute-start.9 = (bf16[8,272,128]{2,1,0:T(8,128)(2,1)S(1)}, bf16[8,272,128]{2,1,0:T(8,128)(2,1)S(1)}, u32[]{:S(2)}, u32[]{:S(2)}) collective-permute-start(bf16[8,272,128]{2,1,0:T(8,128)(2,1)S(1)} %copy-done.9), channel_id=1, source_target_pairs={{0,24},{1,25},{2,26},{3,27},{4,28},{5,29},{6,30},{7,31},{8,16},{9,... | collective-permute-start | bytes 1671176 | tf_op jit(solution)/shard_map/ppermute | solution.py:342
  103.1 48.7 %collective-permute-start.10 = (bf16[16,32,1024]{2,1,0:T(8,128)(2,1)}, bf16[16,32,1024]{2,1,0:T(8,128)(2,1)S(1)}, u32[]{:S(2)}, u32[]{:S(2)}) collective-permute-start(bf16[16,32,1024]{2,1,0:T(8,128)(2,1)} %get-tuple-element.36), channel_id=1, source_target_pairs={{0,1},{1,0},{2,3},{3,2},{4,5},{5,4},{6,7},{7,6},{8,9},{9,8},{10,11... | collective-permute-start | bytes 3145736 | tf_op jit(solution)/shard_map/ppermute | solution.py:342
  125.0 15.0 %copy-start.4 = (bf16[8,272,128]{2,1,0:T(8,128)(2,1)}, bf16[8,272,128]{2,1,0:T(8,128)(2,1)S(1)}, u32[]{:S(2)}) copy-start(bf16[8,272,128]{2,1,0:T(8,128)(2,1)S(1)} %collective-permute-done.7.refs_4_) | copy-start | bytes 1671172
  125.0 15.0 %copy-start.5 = (bf16[8,272,128]{2,1,0:T(8,128)(2,1)}, bf16[8,272,128]{2,1,0:T(8,128)(2,1)S(1)}, u32[]{:S(2)}) copy-start(bf16[8,272,128]{2,1,0:T(8,128)(2,1)S(1)} %collective-permute-done.8.refs_5_) | copy-start | bytes 1671172
  140.0 0.8 copy-start.6
  140.8 5.6 %copy-start.2 = (f32[16,32,1024]{2,1,0:T(8,128)S(1)}, f32[16,32,1024]{2,1,0:T(8,128)}, u32[]{:S(2)}) copy-start(f32[16,32,1024]{2,1,0:T(8,128)} %get-tuple-element.40) | copy-start | bytes 6291460
  146.4 5.4 %copy-start.1 = (f32[16,32,1024]{2,1,0:T(8,128)S(1)}, f32[16,32,1024]{2,1,0:T(8,128)}, u32[]{:S(2)}) copy-start(f32[16,32,1024]{2,1,0:T(8,128)} %get-tuple-element.35) | copy-start | bytes 6291460
  148.3 9.2 %collective-permute-start.18 = (bf16[4,32,1024]{2,1,0:T(8,128)(2,1)S(1)}, bf16[4,32,1024]{2,1,0:T(8,128)(2,1)S(1)}, u32[]{:S(2)}, u32[]{:S(2)}) collective-permute-start(bf16[4,32,1024]{2,1,0:T(8,128)(2,1)S(1)} %get-tuple-element.64), channel_id=1, source_target_pairs={{0,2},{1,3},{2,0},{3,1},{4,6},{5,7},{6,4},{7,5},{8,10},{9,11},{10,... | collective-permute-start | bytes 786440 | tf_op jit(solution)/shard_map/ppermute | solution.py:342
  150.0 14.6 %collective-permute-start.19 = (bf16[4,32,1024]{2,1,0:T(8,128)(2,1)S(1)}, bf16[4,32,1024]{2,1,0:T(8,128)(2,1)S(1)}, u32[]{:S(2)}, u32[]{:S(2)}) collective-permute-start(bf16[4,32,1024]{2,1,0:T(8,128)(2,1)S(1)} %get-tuple-element.66), channel_id=1, source_target_pairs={{0,4},{1,5},{2,6},{3,7},{4,0},{5,1},{6,2},{7,3},{8,12},{9,13},{10,... | collective-permute-start | bytes 786440 | tf_op jit(solution)/shard_map/ppermute | solution.py:342
  150.0 14.6 %collective-permute-start.20 = (bf16[4,32,1024]{2,1,0:T(8,128)(2,1)S(1)}, bf16[4,32,1024]{2,1,0:T(8,128)(2,1)S(1)}, u32[]{:S(2)}, u32[]{:S(2)}) collective-permute-start(bf16[4,32,1024]{2,1,0:T(8,128)(2,1)S(1)} %get-tuple-element.65), channel_id=1, source_target_pairs={{0,6},{1,7},{2,4},{3,5},{4,2},{5,3},{6,0},{7,1},{8,14},{9,15},{10,... | collective-permute-start | bytes 786440 | tf_op jit(solution)/shard_map/ppermute | solution.py:342
  152.4 24.9 %collective-permute-start.11 = (bf16[4,32,1024]{2,1,0:T(8,128)(2,1)S(1)}, bf16[4,32,1024]{2,1,0:T(8,128)(2,1)S(1)}, u32[]{:S(2)}, u32[]{:S(2)}) collective-permute-start(bf16[4,32,1024]{2,1,0:T(8,128)(2,1)S(1)} %get-tuple-element.67), channel_id=1, source_target_pairs={{0,2},{1,3},{2,0},{3,1},{4,6},{5,7},{6,4},{7,5},{8,10},{9,11},{10,... | collective-permute-start | bytes 786440 | tf_op jit(solution)/shard_map/ppermute | solution.py:342
  154.1 24.6 %collective-permute-start.12 = (bf16[4,32,1024]{2,1,0:T(8,128)(2,1)S(1)}, bf16[4,32,1024]{2,1,0:T(8,128)(2,1)S(1)}, u32[]{:S(2)}, u32[]{:S(2)}) collective-permute-start(bf16[4,32,1024]{2,1,0:T(8,128)(2,1)S(1)} %get-tuple-element.69), channel_id=1, source_target_pairs={{0,4},{1,5},{2,6},{3,7},{4,0},{5,1},{6,2},{7,3},{8,12},{9,13},{10,... | collective-permute-start | bytes 786440 | tf_op jit(solution)/shard_map/ppermute | solution.py:342
  157.5 21.3 %collective-permute-start.13 = (bf16[4,32,1024]{2,1,0:T(8,128)(2,1)S(1)}, bf16[4,32,1024]{2,1,0:T(8,128)(2,1)S(1)}, u32[]{:S(2)}, u32[]{:S(2)}) collective-permute-start(bf16[4,32,1024]{2,1,0:T(8,128)(2,1)S(1)} %get-tuple-element.68), channel_id=1, source_target_pairs={{0,6},{1,7},{2,4},{3,5},{4,2},{5,3},{6,0},{7,1},{8,14},{9,15},{10,... | collective-permute-start | bytes 786440 | tf_op jit(solution)/shard_map/ppermute | solution.py:342
  164.8 21.8 %collective-permute-start.21 = (bf16[32,1024]{1,0:T(8,128)(2,1)S(1)}, bf16[32,1024]{1,0:T(8,128)(2,1)S(1)}, u32[]{:S(2)}, u32[]{:S(2)}) collective-permute-start(bf16[32,1024]{1,0:T(8,128)(2,1)S(1)} %get-tuple-element.98), channel_id=1, source_target_pairs={{0,8},{1,9},{2,10},{3,11},{4,12},{5,13},{6,14},{7,15},{8,0},{9,1},... | collective-permute-start | bytes 196616 | tf_op jit(solution)/shard_map/ppermute | solution.py:342
  176.3 11.6 %collective-permute-start.22 = (bf16[32,1024]{1,0:T(8,128)(2,1)S(1)}, bf16[32,1024]{1,0:T(8,128)(2,1)S(1)}, u32[]{:S(2)}, u32[]{:S(2)}) collective-permute-start(bf16[32,1024]{1,0:T(8,128)(2,1)S(1)} %get-tuple-element.100), channel_id=1, source_target_pairs={{0,16},{1,17},{2,18},{3,19},{4,20},{5,21},{6,22},{7,23},{8,24},{9,... | collective-permute-start | bytes 196616 | tf_op jit(solution)/shard_map/ppermute | solution.py:342
  177.3 10.6 %collective-permute-start.23 = (bf16[32,1024]{1,0:T(8,128)(2,1)S(1)}, bf16[32,1024]{1,0:T(8,128)(2,1)S(1)}, u32[]{:S(2)}, u32[]{:S(2)}) collective-permute-start(bf16[32,1024]{1,0:T(8,128)(2,1)S(1)} %get-tuple-element.99), channel_id=1, source_target_pairs={{0,24},{1,25},{2,26},{3,27},{4,28},{5,29},{6,30},{7,31},{8,16},{9,... | collective-permute-start | bytes 196616 | tf_op jit(solution)/shard_map/ppermute | solution.py:342
  179.0 9.7 %collective-permute-start.14 = (bf16[32,1024]{1,0:T(8,128)(2,1)S(1)}, bf16[32,1024]{1,0:T(8,128)(2,1)S(1)}, u32[]{:S(2)}, u32[]{:S(2)}) collective-permute-start(bf16[32,1024]{1,0:T(8,128)(2,1)S(1)} %get-tuple-element.101), channel_id=1, source_target_pairs={{0,8},{1,9},{2,10},{3,11},{4,12},{5,13},{6,14},{7,15},{8,0},{9,1},... | collective-permute-start | bytes 196616 | tf_op jit(solution)/shard_map/ppermute | solution.py:342
  185.4 5.9 %collective-permute-start.15 = (bf16[32,1024]{1,0:T(8,128)(2,1)S(1)}, bf16[32,1024]{1,0:T(8,128)(2,1)S(1)}, u32[]{:S(2)}, u32[]{:S(2)}) collective-permute-start(bf16[32,1024]{1,0:T(8,128)(2,1)S(1)} %get-tuple-element.103), channel_id=1, source_target_pairs={{0,16},{1,17},{2,18},{3,19},{4,20},{5,21},{6,22},{7,23},{8,24},{9,... | collective-permute-start | bytes 196616 | tf_op jit(solution)/shard_map/ppermute | solution.py:342
  186.5 6.2 %collective-permute-start.16 = (bf16[32,1024]{1,0:T(8,128)(2,1)S(1)}, bf16[32,1024]{1,0:T(8,128)(2,1)S(1)}, u32[]{:S(2)}, u32[]{:S(2)}) collective-permute-start(bf16[32,1024]{1,0:T(8,128)(2,1)S(1)} %get-tuple-element.102), channel_id=1, source_target_pairs={{0,24},{1,25},{2,26},{3,27},{4,28},{5,29},{6,30},{7,31},{8,16},{9,... | collective-permute-start | bytes 196616 | tf_op jit(solution)/shard_map/ppermute | solution.py:342

commit v2 on v1

--- a/solution.py
+++ b/solution.py
@@ -9,7 +9,7 @@
 
 
 BLK = 128
-EXTRA = 16
+EXTRA = 8
 AXES = ("row", "col")
 F32 = jnp.float32
 BF16 = jnp.bfloat16
@@ -126,7 +126,6 @@
         d_ref,
     ):
         sub = pl.program_id(0)
-        me = lax.axis_index("row") * sizes.cols + lax.axis_index("col")
         couple = cpl_ref[0]
         static_modes = (-jnp.dot(inv_ref[0], couple, preferred_element_type=F32)).astype(BF16)
         contract = (((0,), (0,)), ((), ()))
@@ -147,8 +146,6 @@
                 owner = quotient(block_a, sizes.row_blocks) * sizes.cols + quotient(
                     map_ref[sub, b], sizes.col_blocks
                 )
-                owner = owner ^ me
-                near, far = remainder(owner, sizes.plane), quotient(owner, sizes.plane)
                 stiff_block = stiff[rows, cols].astype(BF16)
                 mass_block = mass[rows, cols]
                 if a == b:
@@ -161,23 +158,19 @@
                     middle = (diagonal - high).astype(BF16).astype(F32)
                     low = diagonal - high - middle
                     parts = jnp.where(level == 0, high, jnp.where(level == 1, middle, low))
-                    share = quotient(block_a, sizes.share_blocks) ^ me
-                    out_ref[
-                        remainder(share, sizes.plane),
-                        quotient(share, sizes.plane),
-                        2 * BLK : 2 * BLK + EXTRA,
-                    ] = parts.astype(BF16)
+                    share = quotient(block_a, sizes.share_blocks)
+                    out_ref[share, 2 * BLK : 2 * BLK + EXTRA] = parts.astype(BF16)
                     mass_block = jnp.where(eye, 0.0, mass_block)
                 mass_block = mass_block.astype(BF16)
-                out_ref[near, far, :BLK] = stiff_block
-                out_ref[near, far, BLK : 2 * BLK] = mass_block
+                out_ref[owner, :BLK] = stiff_block
+                out_ref[owner, BLK : 2 * BLK] = mass_block
                 k_ref[0, rows, cols] = stiff_block
                 m_ref[0, rows, cols] = mass_block
 
     def piece(*shape):
         return pl.BlockSpec((1,) + shape, lambda s: (s, 0, 0))
 
-    out_blocks = (sizes.plane, sizes.devices // sizes.plane, 2 * BLK + EXTRA, BLK)
+    out_blocks = (sizes.devices, 2 * BLK + EXTRA, BLK)
     return pl.pallas_call(
         kernel,
         grid=(local_subs,),
@@ -190,7 +183,7 @@
             piece(1, boundary),
         ],
         out_specs=[
-            pl.BlockSpec(out_blocks, lambda s: (0, 0, 0, 0)),
+            pl.BlockSpec(out_blocks, lambda s: (0, 0, 0)),
             piece(boundary, boundary),
             piece(boundary, boundary),
             piece(1, boundary),
@@ -358,13 +351,6 @@
     return result
 
 
-def spread_in_plane(blocks, sizes):
-    near = [blocks[0]]
-    for d in range(1, sizes.plane):
-        near.append(swap(blocks[d], d, sizes.devices))
-    return [jnp.stack([part[z] for part in near]) for z in range(sizes.devices // sizes.plane)]
-
-
 def clear_tiles(table, sizes):
     shape = (sizes.row_blocks * BLK, sizes.col_blocks * BLK)
 
@@ -396,25 +382,20 @@
 def place(table, order, slots, arrived, stiff_tile, mass_tile, sizes):
     count = sizes.devices
     limit = sizes.row_blocks * sizes.col_blocks
-    depth = len(arrived)
-    height = 2 * BLK + EXTRA
-
-    def kernel(*refs):
-        table_ref, order_ref, slot_ref = refs[:3]
-        in_refs = refs[3 : 3 + depth]
-        stiff_ref, mass_ref, share_ref, held_ref, sums_ref, in_sem, sem = refs[-7:]
-        me = lax.axis_index("row") * sizes.cols + lax.axis_index("col")
-        loads = [
-            pltpu.make_async_copy(
-                ref, held_ref.at[pl.ds(z * sizes.plane, sizes.plane)], in_sem.at[z]
-            )
-            for z, ref in enumerate(in_refs)
-        ]
-        for load in loads:
-            load.start()
-        for load in loads:
-            load.wait()
-
+
+    def kernel(
+        table_ref,
+        order_ref,
+        slot_ref,
+        held_ref,
+        _stiff,
+        _mass,
+        stiff_ref,
+        mass_ref,
+        share_ref,
+        sums_ref,
+        sem,
+    ):
         def copies(j):
             slot = slot_ref[j]
             row = pl.multiple_of(quotient(slot, sizes.col_blocks) * BLK, BLK)
@@ -434,7 +415,7 @@
             return jnp.logical_and(slot_ref[j] < limit, ends)
 
         def one(j, total):
-            block = held_ref[order_ref[j] ^ me, : 2 * BLK].astype(F32)
+            block = held_ref[order_ref[j], : 2 * BLK].astype(F32)
             same = jnp.logical_and(j > 0, slot_ref[jnp.maximum(j - 1, 0)] == slot_ref[j])
             total = jnp.where(same, total + block, block)
             sums_ref[j] = total.astype(BF16)
@@ -454,7 +435,7 @@
 
             @pl.when(share >= 0)
             def _():
-                parts = held_ref[device ^ me, 2 * BLK : 2 * BLK + EXTRA].astype(F32)
+                parts = held_ref[device, 2 * BLK : 2 * BLK + EXTRA].astype(F32)
                 share_ref[share] += parts[0:1] + parts[1:2] + parts[2:3]
 
             return carry
@@ -473,22 +454,20 @@
 
     return pl.pallas_call(
         kernel,
-        in_specs=[SMEM, SMEM, SMEM] + [ANY] * (depth + 2),
+        in_specs=[SMEM, SMEM, SMEM, VMEM, ANY, ANY],
         out_specs=[ANY, ANY, VMEM],
         out_shape=[
             jax.ShapeDtypeStruct(stiff_tile.shape, BF16),
             jax.ShapeDtypeStruct(mass_tile.shape, BF16),
             jax.ShapeDtypeStruct((sizes.share_blocks, 1, BLK), F32),
         ],
-        input_output_aliases={3 + depth: 0, 4 + depth: 1},
+        input_output_aliases={4: 0, 5: 1},
         scratch_shapes=[
-            pltpu.VMEM((count, height, BLK), BF16),
             pltpu.VMEM((count, 2 * BLK, BLK), BF16),
-            pltpu.SemaphoreType.DMA((depth,)),
             pltpu.SemaphoreType.DMA((count, 2)),
         ],
         name="place",
-    )(table, order, slots, *arrived, stiff_tile, mass_tile)
+    )(table, order, slots, arrived, stiff_tile, mass_tile)
 
 
 def reduction(inv_interior, coupling, boundary_stiff, mass_interior, mass_boundary, block_map, modes):
@@ -516,14 +495,9 @@
     blocks, stiff, mass, diagonal = condense(
         block_map, inv_interior, coupling, boundary_stiff, mass_interior, mass_boundary, sizes
     )
-    spread = spread_in_plane(blocks, sizes)
-    beside = swap(spread[1], sizes.plane, sizes.devices)
     stiff_tile, mass_tile = clear_tiles(table, sizes)
-    late, fetched, stiff_tile, mass_tile = lax.optimization_barrier(
-        (spread[2:], fetched, stiff_tile, mass_tile)
-    )
-    late = [swap(part, (2 + d) * sizes.plane, sizes.devices) for d, part in enumerate(late)]
-    arrived = [spread[0], beside, *late]
+    blocks, fetched = lax.optimization_barrier((blocks, fetched))
+    arrived = exchange(blocks)
 
     fetched = fetched.reshape(row_count, col_count, sizes.ratio, width, BLK)
     send, keep, qt = project_stiff(block_map, fetched, stiff, dims, sizes.row_blocks)

time: 194 us -> 159 us (0.82)
  starting transfers between devices: 52.4 us -> 33.1 us
  local copies, waits for them, and re-layouts: 18.6 us -> 7.83 us
  waiting for transfers between devices: 67.3 us -> 63 us
    ppermute x24 -> x14, waiting for transfers between devices: 62.4 us -> 20 us  [swap(): lax.ppermute(value, AXES, [(i, i ^ offset) for i in range(device_count)])]
    all_to_all x2 -> x3, waiting for transfers between devices: 4.84 us -> 43 us  [exchange(): return lax.all_to_all(value, AXES, split_axis=0, concat_axis=0, tiled=True)]
    ppermute x24 -> x14, starting transfers between devices: 42.2 us -> 19 us  [swap(): lax.ppermute(value, AXES, [(i, i ^ offset) for i in range(device_count)])]
    unnamed x33 -> x14, local copies, waits for them, and re-layouts: 10.6 us -> 3.3 us
    all_to_all x2 -> x3, starting transfers between devices: 10.2 us -> 14.2 us  [exchange(): return lax.all_to_all(value, AXES, split_axis=0, concat_axis=0, tiled=True)]
    squeeze x1 -> x0, local copies, waits for them, and re-layouts: 2.81 us -> none  [spread_in_plane(): near.append(swap(blocks[d], d, sizes.devices))]
  transfers between devices with their start and end apart: 26 -> 17, of which waited for: 10 -> 8; matrix products, arithmetic and copies ran while one was open for 10% -> 6% of each run, Pallas kernels for 13% -> 25%
where the time goes in v2:
time: 159 us; the launch traced here: 158 us
  waiting for transfers between devices  63 us (40%)
  Pallas kernels  48.2 us (30%)
  starting transfers between devices  33.1 us (21%)
  local copies, waits for them, and re-layouts  7.83 us (5%)
  other arithmetic  5.54 us (3%)
    all_to_all x3, waiting for transfers between devices, exchange(): return lax.all_to_all(value, AXES, split_axis=0, concat_axis=0, tiled=True)  43 us
    ppermute x14, waiting for transfers between devices, swap(): lax.ppermute(value, AXES, [(i, i ^ offset) for i in range(device_count)])  20 us
    ppermute x14, starting transfers between devices, swap(): lax.ppermute(value, AXES, [(i, i ^ offset) for i in range(device_count)])  19 us
    all_to_all x3, starting transfers between devices, exchange(): return lax.all_to_all(value, AXES, split_axis=0, concat_axis=0, tiled=True)  14.2 us
    pallas_call x1, Pallas kernels, clear_tiles(): pl.pallas_call(kernel, in_specs=[ANY], out_specs=[ANY, ANY], out_shape=[j...  11.2 us
    pallas_call x1, Pallas kernels, condense(): pl.pallas_call(kernel, grid=(local_subs,), in_specs=[SMEM, piece(interior...  8.71 us
    pallas_call x1, Pallas kernels, project_stiff(): pl.pallas_call(kernel, grid=(modes // chunk,), in_specs=[SMEM, whole(*fet...  8.45 us
    pallas_call x1, Pallas kernels, project_mass(): pl.pallas_call(kernel, grid=(modes // chunk,), in_specs=[pl.BlockSpec((ch...  6.28 us
  transfers between devices with their start and end apart: 17, of which 8 were waited for; matrix products, arithmetic and copies ran while one was open for 6% of the time, Pallas kernels for 25%

profile of v2, /device:TPU:0, one launch (start us, length us, event | category | flops | bytes accessed | tf_op | source)
XLA Modules:
  0.0 158.5 jit_solution(12432187258219464215)
XLA Ops:
  0.6 1.4 describe.1
  2.0 7.3 %all-to-all-start = ((s32[32,1,128]{2,1,0:T(1,128)}), s32[32,1,128]{2,1,0:T(1,128)S(1)}, u32[]{:S(2)}, u32[]{:S(2)}) async-start(s32[32,1,128]{2,1,0:T(1,128)} %bitcast.44), calls=%async_computation | async-start | bytes 32768 | tf_op jit(solution)/shard_map/all_to_all | solution.py:32
  9.3 2.3 %copy.21 = bf16[32,128,128]{1,2,0:T(8,128)(2,1)} copy(bf16[32,128,128]{2,1,0:T(8,128)(2,1)} %bitcast.39) | data formatting | bytes 2097152 | tf_op jit(solution)/shard_map/reshape | solution.py:492
  11.6 4.8 %all-to-all-done = s32[32,1,128]{2,1,0:T(1,128)S(1)} async-done(((s32[32,1,128]{2,1,0:T(1,128)}), s32[32,1,128]{2,1,0:T(1,128)S(1)}, u32[]{:S(2)}, u32[]{:S(2)}) %all-to-all-start) | async-done | bytes 16416 | tf_op jit(solution)/shard_map/all_to_all | solution.py:32
  16.4 0.0 copy-start.3
  16.4 0.6 copy-done.3
  17.0 2.7 %pick_modes.1 = bf16[32,2,128,128]{3,2,1,0:T(8,128)(2,1)} custom-call(s32[32,128]{1,0:T(8,128)} %bitcast.40, bf16[32,128,128]{2,1,0:T(8,128)(2,1)} %bitcast.38), custom_call_target="tpu_custom_call" | custom-call | tf_op jit(solution)/shard_map/pick_modes/pallas_call | solution.py:101
  19.8 2.9 %all-to-all-start.1 = ((bf16[32,2,128,128]{3,2,1,0:T(8,128)(2,1)}), bf16[32,2,128,128]{3,2,1,0:T(8,128)(2,1)S(1)}, u32[]{:S(2)}, u32[]{:S(2)}) async-start(bf16[32,2,128,128]{3,2,1,0:T(8,128)(2,1)} %pick_modes.1), calls=%async_computation.1 | async-start | bytes 4194304 | tf_op jit(solution)/shard_map/all_to_all | solution.py:32
  22.6 0.0 copy-done.6
  22.6 0.6 broadcast_in_dim.27.mb_ref
  23.2 0.0 copy-done.5
  23.2 1.3 copy.20.mi_ref
  24.6 8.7 %condense.1 = (bf16[32,264,128]{2,1,0:T(8,128)(2,1)}, bf16[2,512,512]{2,1,0:T(8,128)(2,1)}, bf16[2,512,512]{2,1,0:T(8,128)(2,1)}, f32[2,1,512]{2,1,0:T(1,128)}) custom-call(s32[2,4]{1,0:T(2,128)} %map_ref.5, bf16[2,1024,1024]{2,1,0:T(8,128)(2,1)} %inv_ref.1, bf16[2,1024,512]{2,1,0:T(8,128)(2,1)} %cpl_ref.1, bf16[2,512,512]{2,1,0:T(8,128)(2,1)} %stiff_ref.1, ...), custom_call_target="tpu_custom_call" | custom-call | tf_op jit(solution)/shard_map/condense/pallas_call | solution.py:174
  33.3 38.1 %all-to-all-done.1 = bf16[32,2,128,128]{3,2,1,0:T(8,128)(2,1)S(1)} async-done(((bf16[32,2,128,128]{3,2,1,0:T(8,128)(2,1)}), bf16[32,2,128,128]{3,2,1,0:T(8,128)(2,1)S(1)}, u32[]{:S(2)}, u32[]{:S(2)}) %all-to-all-start.1) | async-done | bytes 2097184 | tf_op jit(solution)/shard_map/all_to_all | solution.py:32
  71.4 1.3 copy-done.1
  72.8 4.0 %all-to-all-start.2 = ((bf16[32,264,128]{2,1,0:T(8,128)(2,1)}), bf16[32,264,128]{2,1,0:T(8,128)(2,1)S(1)}, u32[]{:S(2)}, u32[]{:S(2)}) async-start(bf16[32,264,128]{2,1,0:T(8,128)(2,1)} %get-tuple-element.22), calls=%async_computation.2 | async-start | bytes 4325376 | tf_op jit(solution)/shard_map/all_to_all | solution.py:32
  76.7 8.4 %project_stiff.1 = (bf16[16,32,1024]{2,1,0:T(8,128)(2,1)}, f32[16,32,1024]{2,1,0:T(8,128)}, bf16[1024,1024]{1,0:T(8,128)(2,1)}) custom-call(s32[2,4]{1,0:T(2,128)} %map_ref.5, bf16[8,4,2,128,128]{4,3,2,1,0:T(8,128)(2,1)} %bitcast.37, bf16[2,512,512]{2,1,0:T(8,128)(2,1)} %get-tuple-element.28.m_ref), custom_call_target="tpu_custom_call" | custom-call | tf_op jit(solution)/shard_map/project_stiff/pallas_call | solution.py:267
  85.2 4.9 %mix_mass.1.y_ref = bf16[1024,1024]{1,0:T(8,128)(2,1)} custom-call(bf16[1024,1024]{1,0:T(8,128)(2,1)} %get-tuple-element.31.t_ref, bf16[2,512,512]{2,1,0:T(8,128)(2,1)} %get-tuple-element.32.m_ref, f32[2,1,512]{2,1,0:T(1,128)} %get-tuple-element.33.d_ref), custom_call_target="tpu_custom_call" | custom-call | tf_op jit(solution)/shard_map/mix_mass/pallas_call | solution.py:299
  90.1 6.3 %project_mass.1 = (bf16[16,32,1024]{2,1,0:T(8,128)(2,1)}, f32[16,32,1024]{2,1,0:T(8,128)}) custom-call(bf16[1024,1024]{1,0:T(8,128)(2,1)} %mix_mass.1.y_ref, bf16[1024,1024]{1,0:T(8,128)(2,1)} %get-tuple-element.31.t_ref), custom_call_target="tpu_custom_call" | custom-call | tf_op jit(solution)/shard_map/project_mass/pallas_call | solution.py:321
  96.4 0.3 collective-permute-start.7
  96.7 0.3 collective-permute-start
  96.9 11.2 %clear_tiles.1 = (bf16[2048,4096]{1,0:T(8,128)(2,1)}, bf16[2048,4096]{1,0:T(8,128)(2,1)}) custom-call(s32[32,128]{1,0:T(8,128)} %bitcast.41), custom_call_target="tpu_custom_call" | custom-call | tf_op jit(solution)/shard_map/clear_tiles/pallas_call | solution.py:369
  108.1 0.0 copy-done.4
  108.1 0.2 slice_reduce_fusion
  108.3 0.2 convert_reduce_fusion
  108.5 0.7 select_reduce_fusion
  109.2 0.0 collective-permute-done.7
  109.2 2.4 %fusion.14 = (bf16[16,32,1024]{2,1,0:T(8,128)(2,1)S(1)}, f32[16,32,1024]{2,1,0:T(8,128)S(1)}) fusion(f32[16,32,1024]{2,1,0:T(8,128)} %get-tuple-element.34, bf16[16,32,1024]{2,1,0:T(8,128)(2,1)} %collective-permute-done.7), kind=kLoop, calls=%fused_computation.31 | loop fusion | flops 1572864 | bytes 6291456 | tf_op jit(solution)/shard_map/convert.5
  111.7 0.1 fusion.18
  111.7 1.8 %collective-permute-start.8 = (bf16[4,32,1024]{2,1,0:T(8,128)(2,1)S(1)}, bf16[4,32,1024]{2,1,0:T(8,128)(2,1)S(1)}, u32[]{:S(2)}, u32[]{:S(2)}) collective-permute-start(bf16[4,32,1024]{2,1,0:T(8,128)(2,1)S(1)} %get-tuple-element.47), channel_id=1, source_target_pairs={{0,2},{1,3},{2,0},{3,1},{4,6},{5,7},{6,4},{7,5},{8,10},{9,11},{10,... | collective-permute-start | bytes 786440 | tf_op jit(solution)/shard_map/ppermute | solution.py:335
  113.5 1.5 collective-permute-start.10
  115.0 0.3 collective-permute-start.9
  115.3 0.0 collective-permute-done
  115.3 0.0 copy-done.2
  115.3 0.5 fusion.17
  115.8 0.1 fusion.19
  115.9 1.8 %collective-permute-start.1 = (bf16[4,32,1024]{2,1,0:T(8,128)(2,1)S(1)}, bf16[4,32,1024]{2,1,0:T(8,128)(2,1)S(1)}, u32[]{:S(2)}, u32[]{:S(2)}) collective-permute-start(bf16[4,32,1024]{2,1,0:T(8,128)(2,1)S(1)} %get-tuple-element.50), channel_id=1, source_target_pairs={{0,2},{1,3},{2,0},{3,1},{4,6},{5,7},{6,4},{7,5},{8,10},{9,11},{10,... | collective-permute-start | bytes 786440 | tf_op jit(solution)/shard_map/ppermute | solution.py:335
  117.7 1.5 collective-permute-start.3
  119.2 4.4 %collective-permute-done.8 = bf16[4,32,1024]{2,1,0:T(8,128)(2,1)S(1)} collective-permute-done((bf16[4,32,1024]{2,1,0:T(8,128)(2,1)S(1)}, bf16[4,32,1024]{2,1,0:T(8,128)(2,1)S(1)}, u32[]{:S(2)}, u32[]{:S(2)}) %collective-permute-start.8) | collective-permute-done | bytes 262176 | tf_op jit(solution)/shard_map/ppermute | solution.py:335
  123.5 2.4 %collective-permute-start.2 = (bf16[4,32,1024]{2,1,0:T(8,128)(2,1)S(1)}, bf16[4,32,1024]{2,1,0:T(8,128)(2,1)S(1)}, u32[]{:S(2)}, u32[]{:S(2)}) collective-permute-start(bf16[4,32,1024]{2,1,0:T(8,128)(2,1)S(1)} %get-tuple-element.52), channel_id=1, source_target_pairs={{0,4},{1,5},{2,6},{3,7},{4,0},{5,1},{6,2},{7,3},{8,12},{9,13},{10,... | collective-permute-start | bytes 786440 | tf_op jit(solution)/shard_map/ppermute | solution.py:335
  126.0 5.1 %collective-permute-done.10 = bf16[4,32,1024]{2,1,0:T(8,128)(2,1)S(1)} collective-permute-done((bf16[4,32,1024]{2,1,0:T(8,128)(2,1)S(1)}, bf16[4,32,1024]{2,1,0:T(8,128)(2,1)S(1)}, u32[]{:S(2)}, u32[]{:S(2)}) %collective-permute-start.10) | collective-permute-done | bytes 262176 | tf_op jit(solution)/shard_map/ppermute | solution.py:335
  131.0 0.0 collective-permute-done.9
  131.0 0.2 fusion.12
  131.2 2.5 %collective-permute-start.11 = (bf16[32,1024]{1,0:T(8,128)(2,1)S(1)}, bf16[32,1024]{1,0:T(8,128)(2,1)S(1)}, u32[]{:S(2)}, u32[]{:S(2)}) collective-permute-start(bf16[32,1024]{1,0:T(8,128)(2,1)S(1)} %get-tuple-element.53), channel_id=1, source_target_pairs={{0,8},{1,9},{2,10},{3,11},{4,12},{5,13},{6,14},{7,15},{8,0},{9,1},... | collective-permute-start | bytes 196616 | tf_op jit(solution)/shard_map/ppermute | solution.py:335
  133.7 1.4 collective-permute-start.13
  135.1 0.7 collective-permute-done.1
  135.8 1.3 collective-permute-start.12
  137.1 4.8 %collective-permute-done.3 = bf16[4,32,1024]{2,1,0:T(8,128)(2,1)S(1)} collective-permute-done((bf16[4,32,1024]{2,1,0:T(8,128)(2,1)S(1)}, bf16[4,32,1024]{2,1,0:T(8,128)(2,1)S(1)}, u32[]{:S(2)}, u32[]{:S(2)}) %collective-permute-start.3) | collective-permute-done | bytes 262176 | tf_op jit(solution)/shard_map/ppermute | solution.py:335
  141.8 0.0 collective-permute-done.2
  141.8 0.2 fusion.15
  142.0 1.5 collective-permute-start.4
  143.6 2.4 %collective-permute-start.6 = (bf16[32,1024]{1,0:T(8,128)(2,1)S(1)}, bf16[32,1024]{1,0:T(8,128)(2,1)S(1)}, u32[]{:S(2)}, u32[]{:S(2)}) collective-permute-start(bf16[32,1024]{1,0:T(8,128)(2,1)S(1)} %get-tuple-element.57), channel_id=1, source_target_pairs={{0,24},{1,25},{2,26},{3,27},{4,28},{5,29},{6,30},{7,31},{8,16},{9,... | collective-permute-start | bytes 196616 | tf_op jit(solution)/shard_map/ppermute | solution.py:335
  146.0 0.0 collective-permute-done.11
  146.0 0.0 collective-permute-start.5
  146.0 0.0 collective-permute-done.13
  146.0 0.0 collective-permute-done.12
  146.0 0.7 fusion.6
  146.7 0.0 collective-permute-done.4
  146.7 3.1 %collective-permute-done.6 = bf16[32,1024]{1,0:T(8,128)(2,1)S(1)} collective-permute-done((bf16[32,1024]{1,0:T(8,128)(2,1)S(1)}, bf16[32,1024]{1,0:T(8,128)(2,1)S(1)}, u32[]{:S(2)}, u32[]{:S(2)}) %collective-permute-start.6) | collective-permute-done | bytes 65568 | tf_op jit(solution)/shard_map/ppermute | solution.py:335
  149.8 2.1 %collective-permute-done.5 = bf16[32,1024]{1,0:T(8,128)(2,1)S(1)} collective-permute-done((bf16[32,1024]{1,0:T(8,128)(2,1)S(1)}, bf16[32,1024]{1,0:T(8,128)(2,1)S(1)}, u32[]{:S(2)}, u32[]{:S(2)}) %collective-permute-start.5) | collective-permute-done | bytes 65568 | tf_op jit(solution)/shard_map/ppermute | solution.py:335
  151.9 0.7 fusion.9
  152.6 0.0 all-to-all-done.2.held_ref
  152.6 1.4 copy-done
  154.0 4.5 %place.1 = (bf16[2048,4096]{1,0:T(8,128)(2,1)}, bf16[2048,4096]{1,0:T(8,128)(2,1)}, f32[4,1,128]{2,1,0:T(1,128)}) custom-call(s32[32,128]{1,0:T(8,128)} %bitcast.42, s32[32]{0:T(128)} %get-tuple-element.38.order_ref, s32[32]{0:T(128)} %get-tuple-element.37.slot_ref, bf16[32,264,128]{2,1,0:T(8,128)(2,1)} %copy-done, ...), custom_call_target="tpu_custom_call", output_to_operand_aliasing={{0}: (4, {}), {1}: (5, {})} | custom-call | tf_op jit(solution)/shard_map/place/pallas_call | solution.py:455
  (8 shorter events, 0.0 us)
Async XLA Ops:
  2.0 14.4 %all-to-all-start = ((s32[32,1,128]{2,1,0:T(1,128)}), s32[32,1,128]{2,1,0:T(1,128)S(1)}, u32[]{:S(2)}, u32[]{:S(2)}) async-start(s32[32,1,128]{2,1,0:T(1,128)} %bitcast.44), calls=%async_computation | async-start | bytes 32768 | tf_op jit(solution)/shard_map/all_to_all | solution.py:32
  16.4 0.6 copy-start.3
  19.7 2.9 %copy-start.6 = (f32[2,512]{1,0:T(2,128)S(1)}, f32[2,512]{1,0:T(2,128)}, u32[]{:S(2)}) copy-start(f32[2,512]{1,0:T(2,128)} %param.11) | copy-start | bytes 12292
  19.7 3.5 %copy-start.5 = (f32[2,1024]{1,0:T(2,128)S(1)}, f32[2,1024]{1,0:T(2,128)}, u32[]{:S(2)}) copy-start(f32[2,1024]{1,0:T(2,128)} %param.10) | copy-start | bytes 24580
  19.8 51.7 %all-to-all-start.1 = ((bf16[32,2,128,128]{3,2,1,0:T(8,128)(2,1)}), bf16[32,2,128,128]{3,2,1,0:T(8,128)(2,1)S(1)}, u32[]{:S(2)}, u32[]{:S(2)}) async-start(bf16[32,2,128,128]{3,2,1,0:T(8,128)(2,1)} %pick_modes.1), calls=%async_computation.1 | async-start | bytes 4194304 | tf_op jit(solution)/shard_map/all_to_all | solution.py:32
  71.4 1.3 copy-start.1
  72.8 79.8 %all-to-all-start.2 = ((bf16[32,264,128]{2,1,0:T(8,128)(2,1)}), bf16[32,264,128]{2,1,0:T(8,128)(2,1)S(1)}, u32[]{:S(2)}, u32[]{:S(2)}) async-start(bf16[32,264,128]{2,1,0:T(8,128)(2,1)} %get-tuple-element.22), calls=%async_computation.2 | async-start | bytes 4325376 | tf_op jit(solution)/shard_map/all_to_all | solution.py:32
  90.1 18.0 %copy-start.4 = (s32[32,1,128]{2,1,0:T(1,128)S(1)}, s32[32,1,128]{2,1,0:T(1,128)}, u32[]{:S(2)}) copy-start(s32[32,1,128]{2,1,0:T(1,128)} %copy-done.3) | copy-start | bytes 49156
  96.4 12.8 %collective-permute-start.7 = (bf16[16,32,1024]{2,1,0:T(8,128)(2,1)}, bf16[16,32,1024]{2,1,0:T(8,128)(2,1)}, u32[]{:S(2)}, u32[]{:S(2)}) collective-permute-start(bf16[16,32,1024]{2,1,0:T(8,128)(2,1)} %get-tuple-element.35), channel_id=1, source_target_pairs={{0,1},{1,0},{2,3},{3,2},{4,5},{5,4},{6,7},{7,6},{8,9},{9,8},{10,11... | collective-permute-start | bytes 3145736 | tf_op jit(solution)/shard_map/ppermute | solution.py:335
  96.7 18.6 %collective-permute-start = (bf16[16,32,1024]{2,1,0:T(8,128)(2,1)}, bf16[16,32,1024]{2,1,0:T(8,128)(2,1)S(1)}, u32[]{:S(2)}, u32[]{:S(2)}) collective-permute-start(bf16[16,32,1024]{2,1,0:T(8,128)(2,1)} %get-tuple-element.30), channel_id=1, source_target_pairs={{0,1},{1,0},{2,3},{3,2},{4,5},{5,4},{6,7},{7,6},{8,9},{9,8},{10,11... | collective-permute-start | bytes 3145736 | tf_op jit(solution)/shard_map/ppermute | solution.py:335
  109.2 6.1 %copy-start.2 = (f32[16,32,1024]{2,1,0:T(8,128)S(1)}, f32[16,32,1024]{2,1,0:T(8,128)}, u32[]{:S(2)}) copy-start(f32[16,32,1024]{2,1,0:T(8,128)} %get-tuple-element.29) | copy-start | bytes 6291460
  111.7 11.8 %collective-permute-start.8 = (bf16[4,32,1024]{2,1,0:T(8,128)(2,1)S(1)}, bf16[4,32,1024]{2,1,0:T(8,128)(2,1)S(1)}, u32[]{:S(2)}, u32[]{:S(2)}) collective-permute-start(bf16[4,32,1024]{2,1,0:T(8,128)(2,1)S(1)} %get-tuple-element.47), channel_id=1, source_target_pairs={{0,2},{1,3},{2,0},{3,1},{4,6},{5,7},{6,4},{7,5},{8,10},{9,11},{10,... | collective-permute-start | bytes 786440 | tf_op jit(solution)/shard_map/ppermute | solution.py:335
  113.5 17.5 %collective-permute-start.10 = (bf16[4,32,1024]{2,1,0:T(8,128)(2,1)S(1)}, bf16[4,32,1024]{2,1,0:T(8,128)(2,1)S(1)}, u32[]{:S(2)}, u32[]{:S(2)}) collective-permute-start(bf16[4,32,1024]{2,1,0:T(8,128)(2,1)S(1)} %get-tuple-element.48), channel_id=1, source_target_pairs={{0,6},{1,7},{2,4},{3,5},{4,2},{5,3},{6,0},{7,1},{8,14},{9,15},{10,... | collective-permute-start | bytes 786440 | tf_op jit(solution)/shard_map/ppermute | solution.py:335
  115.0 16.0 %collective-permute-start.9 = (bf16[4,32,1024]{2,1,0:T(8,128)(2,1)S(1)}, bf16[4,32,1024]{2,1,0:T(8,128)(2,1)S(1)}, u32[]{:S(2)}, u32[]{:S(2)}) collective-permute-start(bf16[4,32,1024]{2,1,0:T(8,128)(2,1)S(1)} %get-tuple-element.49), channel_id=1, source_target_pairs={{0,4},{1,5},{2,6},{3,7},{4,0},{5,1},{6,2},{7,3},{8,12},{9,13},{10,... | collective-permute-start | bytes 786440 | tf_op jit(solution)/shard_map/ppermute | solution.py:335
  115.9 19.9 %collective-permute-start.1 = (bf16[4,32,1024]{2,1,0:T(8,128)(2,1)S(1)}, bf16[4,32,1024]{2,1,0:T(8,128)(2,1)S(1)}, u32[]{:S(2)}, u32[]{:S(2)}) collective-permute-start(bf16[4,32,1024]{2,1,0:T(8,128)(2,1)S(1)} %get-tuple-element.50), channel_id=1, source_target_pairs={{0,2},{1,3},{2,0},{3,1},{4,6},{5,7},{6,4},{7,5},{8,10},{9,11},{10,... | collective-permute-start | bytes 786440 | tf_op jit(solution)/shard_map/ppermute | solution.py:335
  117.7 24.1 %collective-permute-start.3 = (bf16[4,32,1024]{2,1,0:T(8,128)(2,1)S(1)}, bf16[4,32,1024]{2,1,0:T(8,128)(2,1)S(1)}, u32[]{:S(2)}, u32[]{:S(2)}) collective-permute-start(bf16[4,32,1024]{2,1,0:T(8,128)(2,1)S(1)} %get-tuple-element.51), channel_id=1, source_target_pairs={{0,6},{1,7},{2,4},{3,5},{4,2},{5,3},{6,0},{7,1},{8,14},{9,15},{10,... | collective-permute-start | bytes 786440 | tf_op jit(solution)/shard_map/ppermute | solution.py:335
  123.5 18.3 %collective-permute-start.2 = (bf16[4,32,1024]{2,1,0:T(8,128)(2,1)S(1)}, bf16[4,32,1024]{2,1,0:T(8,128)(2,1)S(1)}, u32[]{:S(2)}, u32[]{:S(2)}) collective-permute-start(bf16[4,32,1024]{2,1,0:T(8,128)(2,1)S(1)} %get-tuple-element.52), channel_id=1, source_target_pairs={{0,4},{1,5},{2,6},{3,7},{4,0},{5,1},{6,2},{7,3},{8,12},{9,13},{10,... | collective-permute-start | bytes 786440 | tf_op jit(solution)/shard_map/ppermute | solution.py:335
  131.2 14.8 %collective-permute-start.11 = (bf16[32,1024]{1,0:T(8,128)(2,1)S(1)}, bf16[32,1024]{1,0:T(8,128)(2,1)S(1)}, u32[]{:S(2)}, u32[]{:S(2)}) collective-permute-start(bf16[32,1024]{1,0:T(8,128)(2,1)S(1)} %get-tuple-element.53), channel_id=1, source_target_pairs={{0,8},{1,9},{2,10},{3,11},{4,12},{5,13},{6,14},{7,15},{8,0},{9,1},... | collective-permute-start | bytes 196616 | tf_op jit(solution)/shard_map/ppermute | solution.py:335
  133.7 12.3 %collective-permute-start.13 = (bf16[32,1024]{1,0:T(8,128)(2,1)S(1)}, bf16[32,1024]{1,0:T(8,128)(2,1)S(1)}, u32[]{:S(2)}, u32[]{:S(2)}) collective-permute-start(bf16[32,1024]{1,0:T(8,128)(2,1)S(1)} %get-tuple-element.54), channel_id=1, source_target_pairs={{0,24},{1,25},{2,26},{3,27},{4,28},{5,29},{6,30},{7,31},{8,16},{9,... | collective-permute-start | bytes 196616 | tf_op jit(solution)/shard_map/ppermute | solution.py:335
  135.8 10.3 %collective-permute-start.12 = (bf16[32,1024]{1,0:T(8,128)(2,1)S(1)}, bf16[32,1024]{1,0:T(8,128)(2,1)S(1)}, u32[]{:S(2)}, u32[]{:S(2)}) collective-permute-start(bf16[32,1024]{1,0:T(8,128)(2,1)S(1)} %get-tuple-element.55), channel_id=1, source_target_pairs={{0,16},{1,17},{2,18},{3,19},{4,20},{5,21},{6,22},{7,23},{8,24},{9,... | collective-permute-start | bytes 196616 | tf_op jit(solution)/shard_map/ppermute | solution.py:335
  142.0 4.7 %collective-permute-start.4 = (bf16[32,1024]{1,0:T(8,128)(2,1)S(1)}, bf16[32,1024]{1,0:T(8,128)(2,1)S(1)}, u32[]{:S(2)}, u32[]{:S(2)}) collective-permute-start(bf16[32,1024]{1,0:T(8,128)(2,1)S(1)} %get-tuple-element.56), channel_id=1, source_target_pairs={{0,8},{1,9},{2,10},{3,11},{4,12},{5,13},{6,14},{7,15},{8,0},{9,1},... | collective-permute-start | bytes 196616 | tf_op jit(solution)/shard_map/ppermute | solution.py:335
  143.6 6.2 %collective-permute-start.6 = (bf16[32,1024]{1,0:T(8,128)(2,1)S(1)}, bf16[32,1024]{1,0:T(8,128)(2,1)S(1)}, u32[]{:S(2)}, u32[]{:S(2)}) collective-permute-start(bf16[32,1024]{1,0:T(8,128)(2,1)S(1)} %get-tuple-element.57), channel_id=1, source_target_pairs={{0,24},{1,25},{2,26},{3,27},{4,28},{5,29},{6,30},{7,31},{8,16},{9,... | collective-permute-start | bytes 196616 | tf_op jit(solution)/shard_map/ppermute | solution.py:335
  146.0 5.9 %collective-permute-start.5 = (bf16[32,1024]{1,0:T(8,128)(2,1)S(1)}, bf16[32,1024]{1,0:T(8,128)(2,1)S(1)}, u32[]{:S(2)}, u32[]{:S(2)}) collective-permute-start(bf16[32,1024]{1,0:T(8,128)(2,1)S(1)} %get-tuple-element.58), channel_id=1, source_target_pairs={{0,16},{1,17},{2,18},{3,19},{4,20},{5,21},{6,22},{7,23},{8,24},{9,... | collective-permute-start | bytes 196616 | tf_op jit(solution)/shard_map/ppermute | solution.py:335
  152.6 1.4 copy-start

commit v3 on v2

--- a/solution.py
+++ b/solution.py
@@ -337,9 +337,10 @@
 
 def reduce_shares(send, keep, sizes):
     got = swap(send, 1, sizes.devices)
-    summed = keep + got.astype(F32)
     depth = sizes.devices // sizes.plane
-    summed = summed.reshape((sizes.plane // 2, depth) + summed.shape[1:])
+    shape = (sizes.plane // 2, depth) + keep.shape[1:]
+    keep, got = keep.reshape(shape), got.reshape(shape)
+    summed = [keep[d] + got[d].astype(F32) for d in range(sizes.plane // 2)]
     total = summed[0]
     for d in range(1, sizes.plane // 2):
         got = swap(summed[d].astype(BF16), 2 * d, sizes.devices)
@@ -393,41 +394,55 @@
         stiff_ref,
         mass_ref,
         share_ref,
+        total_ref,
         sums_ref,
         sem,
     ):
-        def copies(j):
+        def copies(j, blocks):
             slot = slot_ref[j]
             row = pl.multiple_of(quotient(slot, sizes.col_blocks) * BLK, BLK)
             col = pl.multiple_of(remainder(slot, sizes.col_blocks) * BLK, BLK)
             return [
                 pltpu.make_async_copy(
-                    sums_ref.at[j, pl.ds(i * BLK, BLK)],
+                    blocks.at[pl.ds(i * BLK, BLK)],
                     ref.at[pl.ds(row, BLK), pl.ds(col, BLK)],
                     sem.at[j, i],
                 )
                 for i, ref in enumerate((stiff_ref, mass_ref))
             ]
 
-        def last(j):
-            ahead = slot_ref[jnp.minimum(j + 1, count - 1)]
-            ends = jnp.logical_or(j == count - 1, ahead != slot_ref[j])
-            return jnp.logical_and(slot_ref[j] < limit, ends)
-
-        def one(j, total):
-            block = held_ref[order_ref[j], : 2 * BLK].astype(F32)
-            same = jnp.logical_and(j > 0, slot_ref[jnp.maximum(j - 1, 0)] == slot_ref[j])
-            total = jnp.where(same, total + block, block)
-            sums_ref[j] = total.astype(BF16)
-
-            @pl.when(last(j))
+        def ends(j):
+            slot = slot_ref[j]
+            first = jnp.logical_or(j == 0, slot_ref[jnp.maximum(j - 1, 0)] != slot)
+            last = jnp.logical_or(j == count - 1, slot_ref[jnp.minimum(j + 1, count - 1)] != slot)
+            return slot < limit, first, last
+
+        def one(j, carry):
+            valid, first, last = ends(j)
+            single = jnp.logical_and(first, last)
+            source = order_ref[j]
+
+            @pl.when(jnp.logical_and(valid, single))
             def _():
-                for copy in copies(j):
+                for copy in copies(j, held_ref.at[source]):
                     copy.start()
 
-            return total
-
-        lax.fori_loop(0, count, one, jnp.zeros((2 * BLK, BLK), F32))
+            @pl.when(jnp.logical_and(valid, jnp.logical_not(single)))
+            def _():
+                block = held_ref[source, : 2 * BLK].astype(F32)
+                total = block + jnp.where(first, 0.0, total_ref[...])
+                total_ref[...] = total
+
+                @pl.when(last)
+                def _():
+                    sums_ref[j] = total.astype(BF16)
+                    for copy in copies(j, sums_ref.at[j]):
+                        copy.start()
+
+            return carry
+
+        total_ref[...] = jnp.zeros_like(total_ref)
+        lax.fori_loop(0, count, one, 0)
         share_ref[...] = jnp.zeros_like(share_ref)
 
         def add(device, carry):
@@ -443,9 +458,11 @@
         lax.fori_loop(0, count, add, 0)
 
         def wait(j, carry):
-            @pl.when(last(j))
+            valid, _, last = ends(j)
+
+            @pl.when(jnp.logical_and(valid, last))
             def _():
-                for copy in copies(j):
+                for copy in copies(j, sums_ref.at[j]):
                     copy.wait()
 
             return carry
@@ -463,6 +480,7 @@
         ],
         input_output_aliases={4: 0, 5: 1},
         scratch_shapes=[
+            pltpu.VMEM((2 * BLK, BLK), F32),
             pltpu.VMEM((count, 2 * BLK, BLK), BF16),
             pltpu.SemaphoreType.DMA((count, 2)),
         ],

time: 159 us -> 159 us (level)
    convert_element_type x0 -> x2, other arithmetic: none -> 2.11 us  [reduce_shares(): got = swap(summed[d].astype(BF16), 2 * d, sizes.devices)]
    another operation x4 -> x2, other arithmetic: 3.29 us -> 1.54 us
  transfers between devices with their start and end apart: 17 -> 17, of which waited for: 8 -> 9; matrix products, arithmetic and copies ran while one was open for 6% -> 7% of each run, Pallas kernels for 25% -> 25%
where the time goes in v3:
time: 159 us
  waiting for transfers between devices  62.5 us (39%)
  Pallas kernels  48.6 us (31%)
  starting transfers between devices  33.2 us (21%)
  local copies, waits for them, and re-layouts  7.72 us (5%)
  other arithmetic  5.93 us (4%)
    all_to_all x3, waiting for transfers between devices, exchange(): return lax.all_to_all(value, AXES, split_axis=0, concat_axis=0, tiled=True)  43 us
    ppermute x14, waiting for transfers between devices, swap(): lax.ppermute(value, AXES, [(i, i ^ offset) for i in range(device_count)])  19.5 us
    ppermute x14, starting transfers between devices, swap(): lax.ppermute(value, AXES, [(i, i ^ offset) for i in range(device_count)])  19.1 us
    all_to_all x3, starting transfers between devices, exchange(): return lax.all_to_all(value, AXES, split_axis=0, concat_axis=0, tiled=True)  14.2 us
    pallas_call x1, Pallas kernels, clear_tiles(): pl.pallas_call(kernel, in_specs=[ANY], out_specs=[ANY, ANY], out_shape=[j...  11.2 us
    pallas_call x1, Pallas kernels, condense(): pl.pallas_call(kernel, grid=(local_subs,), in_specs=[SMEM, piece(interior...  8.7 us
    pallas_call x1, Pallas kernels, project_stiff(): pl.pallas_call(kernel, grid=(modes // chunk,), in_specs=[SMEM, whole(*fet...  8.46 us
    pallas_call x1, Pallas kernels, project_mass(): pl.pallas_call(kernel, grid=(modes // chunk,), in_specs=[pl.BlockSpec((ch...  6.23 us
  transfers between devices with their start and end apart: 17, of which 9 were waited for; matrix products, arithmetic and copies ran while one was open for 7% of the time, Pallas kernels for 25%

profile of v3, /device:TPU:0, one launch (start us, length us, event | category | flops | bytes accessed | tf_op | source)
XLA Modules:
  0.0 158.8 jit_solution(8960863849058608297)
XLA Ops:
  0.6 1.4 describe.1
  2.0 7.3 %all-to-all-start = ((s32[32,1,128]{2,1,0:T(1,128)}), s32[32,1,128]{2,1,0:T(1,128)S(1)}, u32[]{:S(2)}, u32[]{:S(2)}) async-start(s32[32,1,128]{2,1,0:T(1,128)} %bitcast.44), calls=%async_computation | async-start | bytes 32768 | tf_op jit(solution)/shard_map/all_to_all | solution.py:32
  9.3 2.3 %copy.21 = bf16[32,128,128]{1,2,0:T(8,128)(2,1)} copy(bf16[32,128,128]{2,1,0:T(8,128)(2,1)} %bitcast.39) | data formatting | bytes 2097152 | tf_op jit(solution)/shard_map/reshape | solution.py:510
  11.6 4.8 %all-to-all-done = s32[32,1,128]{2,1,0:T(1,128)S(1)} async-done(((s32[32,1,128]{2,1,0:T(1,128)}), s32[32,1,128]{2,1,0:T(1,128)S(1)}, u32[]{:S(2)}, u32[]{:S(2)}) %all-to-all-start) | async-done | bytes 16416 | tf_op jit(solution)/shard_map/all_to_all | solution.py:32
  16.4 0.0 copy-start.3
  16.4 0.6 copy-done.3
  17.0 2.7 %pick_modes.1 = bf16[32,2,128,128]{3,2,1,0:T(8,128)(2,1)} custom-call(s32[32,128]{1,0:T(8,128)} %bitcast.40, bf16[32,128,128]{2,1,0:T(8,128)(2,1)} %bitcast.38), custom_call_target="tpu_custom_call" | custom-call | tf_op jit(solution)/shard_map/pick_modes/pallas_call | solution.py:101
  19.8 0.0 copy-start.6
  19.8 2.9 %all-to-all-start.1 = ((bf16[32,2,128,128]{3,2,1,0:T(8,128)(2,1)}), bf16[32,2,128,128]{3,2,1,0:T(8,128)(2,1)S(1)}, u32[]{:S(2)}, u32[]{:S(2)}) async-start(bf16[32,2,128,128]{3,2,1,0:T(8,128)(2,1)} %pick_modes.1), calls=%async_computation.1 | async-start | bytes 4194304 | tf_op jit(solution)/shard_map/all_to_all | solution.py:32
  22.6 0.0 copy-done.6
  22.6 0.6 broadcast_in_dim.27.mb_ref
  23.2 0.0 copy-done.5
  23.2 1.3 copy.20.mi_ref
  24.6 8.7 %condense.1 = (bf16[32,264,128]{2,1,0:T(8,128)(2,1)}, bf16[2,512,512]{2,1,0:T(8,128)(2,1)}, bf16[2,512,512]{2,1,0:T(8,128)(2,1)}, f32[2,1,512]{2,1,0:T(1,128)}) custom-call(s32[2,4]{1,0:T(2,128)} %map_ref.5, bf16[2,1024,1024]{2,1,0:T(8,128)(2,1)} %inv_ref.1, bf16[2,1024,512]{2,1,0:T(8,128)(2,1)} %cpl_ref.1, bf16[2,512,512]{2,1,0:T(8,128)(2,1)} %stiff_ref.1, ...), custom_call_target="tpu_custom_call" | custom-call | tf_op jit(solution)/shard_map/condense/pallas_call | solution.py:174
  33.3 38.2 %all-to-all-done.1 = bf16[32,2,128,128]{3,2,1,0:T(8,128)(2,1)S(1)} async-done(((bf16[32,2,128,128]{3,2,1,0:T(8,128)(2,1)}), bf16[32,2,128,128]{3,2,1,0:T(8,128)(2,1)S(1)}, u32[]{:S(2)}, u32[]{:S(2)}) %all-to-all-start.1) | async-done | bytes 2097184 | tf_op jit(solution)/shard_map/all_to_all | solution.py:32
  71.4 1.3 copy-done.1
  72.8 4.0 %all-to-all-start.2 = ((bf16[32,264,128]{2,1,0:T(8,128)(2,1)}), bf16[32,264,128]{2,1,0:T(8,128)(2,1)S(1)}, u32[]{:S(2)}, u32[]{:S(2)}) async-start(bf16[32,264,128]{2,1,0:T(8,128)(2,1)} %get-tuple-element.22), calls=%async_computation.2 | async-start | bytes 4325376 | tf_op jit(solution)/shard_map/all_to_all | solution.py:32
  76.7 8.5 %project_stiff.1 = (bf16[16,32,1024]{2,1,0:T(8,128)(2,1)}, f32[16,32,1024]{2,1,0:T(8,128)}, bf16[1024,1024]{1,0:T(8,128)(2,1)}) custom-call(s32[2,4]{1,0:T(2,128)} %map_ref.5, bf16[8,4,2,128,128]{4,3,2,1,0:T(8,128)(2,1)} %bitcast.37, bf16[2,512,512]{2,1,0:T(8,128)(2,1)} %get-tuple-element.28.m_ref), custom_call_target="tpu_custom_call" | custom-call | tf_op jit(solution)/shard_map/project_stiff/pallas_call | solution.py:267
  85.2 4.9 %mix_mass.1.y_ref = bf16[1024,1024]{1,0:T(8,128)(2,1)} custom-call(bf16[1024,1024]{1,0:T(8,128)(2,1)} %get-tuple-element.31.t_ref, bf16[2,512,512]{2,1,0:T(8,128)(2,1)} %get-tuple-element.32.m_ref, f32[2,1,512]{2,1,0:T(1,128)} %get-tuple-element.33.d_ref), custom_call_target="tpu_custom_call" | custom-call | tf_op jit(solution)/shard_map/mix_mass/pallas_call | solution.py:299
  90.1 6.2 %project_mass.1 = (bf16[16,32,1024]{2,1,0:T(8,128)(2,1)}, f32[16,32,1024]{2,1,0:T(8,128)}) custom-call(bf16[1024,1024]{1,0:T(8,128)(2,1)} %mix_mass.1.y_ref, bf16[1024,1024]{1,0:T(8,128)(2,1)} %get-tuple-element.31.t_ref), custom_call_target="tpu_custom_call" | custom-call | tf_op jit(solution)/shard_map/project_mass/pallas_call | solution.py:321
  96.4 0.3 collective-permute-start.7
  96.6 0.3 collective-permute-start
  96.9 11.2 %clear_tiles.1 = (bf16[2048,4096]{1,0:T(8,128)(2,1)}, bf16[2048,4096]{1,0:T(8,128)(2,1)}) custom-call(s32[32,128]{1,0:T(8,128)} %bitcast.41), custom_call_target="tpu_custom_call" | custom-call | tf_op jit(solution)/shard_map/clear_tiles/pallas_call | solution.py:370
  108.1 0.0 copy-done.4
  108.1 0.0 copy-start.2
  108.1 0.2 slice_reduce_fusion
  108.3 0.2 convert_reduce_fusion
  108.5 0.7 select_reduce_fusion
  109.2 0.0 collective-permute-done.7
  109.2 1.8 %add_convert_fusion.2 = (bf16[4,32,1024]{2,1,0:T(8,128)(2,1)S(1)}, bf16[4,32,1024]{2,1,0:T(8,128)(2,1)S(1)}, bf16[4,32,1024]{2,1,0:T(8,128)(2,1)S(1)}) fusion(f32[16,32,1024]{2,1,0:T(8,128)} %get-tuple-element.34, bf16[16,32,1024]{2,1,0:T(8,128)(2,1)} %collective-permute-done.7), kind=kLoop, calls=%fused_computation.3 | loop fusion | flops 1179648 | bytes 3145728 | tf_op jit(solution)/shard_map/convert_element_type | solution.py:346
  111.0 1.8 %collective-permute-start.8 = (bf16[4,32,1024]{2,1,0:T(8,128)(2,1)S(1)}, bf16[4,32,1024]{2,1,0:T(8,128)(2,1)S(1)}, u32[]{:S(2)}, u32[]{:S(2)}) collective-permute-start(bf16[4,32,1024]{2,1,0:T(8,128)(2,1)S(1)} %get-tuple-element.43), channel_id=1, source_target_pairs={{0,2},{1,3},{2,0},{3,1},{4,6},{5,7},{6,4},{7,5},{8,10},{9,11},{10,... | collective-permute-start | bytes 786440 | tf_op jit(solution)/shard_map/ppermute | solution.py:335
  112.9 1.5 collective-permute-start.10
  114.3 0.3 collective-permute-start.9
  114.6 0.0 collective-permute-done
  114.6 0.0 copy-done.2
  114.6 0.3 add_convert_fusion.5
  114.9 1.8 %collective-permute-start.1 = (bf16[4,32,1024]{2,1,0:T(8,128)(2,1)S(1)}, bf16[4,32,1024]{2,1,0:T(8,128)(2,1)S(1)}, u32[]{:S(2)}, u32[]{:S(2)}) collective-permute-start(bf16[4,32,1024]{2,1,0:T(8,128)(2,1)S(1)} %get-tuple-element.46), channel_id=1, source_target_pairs={{0,2},{1,3},{2,0},{3,1},{4,6},{5,7},{6,4},{7,5},{8,10},{9,11},{10,... | collective-permute-start | bytes 786440 | tf_op jit(solution)/shard_map/ppermute | solution.py:335
  116.7 1.5 collective-permute-start.3
  118.2 3.7 %collective-permute-done.8 = bf16[4,32,1024]{2,1,0:T(8,128)(2,1)S(1)} collective-permute-done((bf16[4,32,1024]{2,1,0:T(8,128)(2,1)S(1)}, bf16[4,32,1024]{2,1,0:T(8,128)(2,1)S(1)}, u32[]{:S(2)}, u32[]{:S(2)}) %collective-permute-start.8) | collective-permute-done | bytes 262176 | tf_op jit(solution)/shard_map/ppermute | solution.py:335
  121.9 3.5 %collective-permute-start.2 = (bf16[4,32,1024]{2,1,0:T(8,128)(2,1)S(1)}, bf16[4,32,1024]{2,1,0:T(8,128)(2,1)S(1)}, u32[]{:S(2)}, u32[]{:S(2)}) collective-permute-start(bf16[4,32,1024]{2,1,0:T(8,128)(2,1)S(1)} %get-tuple-element.48), channel_id=1, source_target_pairs={{0,4},{1,5},{2,6},{3,7},{4,0},{5,1},{6,2},{7,3},{8,12},{9,13},{10,... | collective-permute-start | bytes 786440 | tf_op jit(solution)/shard_map/ppermute | solution.py:335
  125.4 5.3 %collective-permute-done.10 = bf16[4,32,1024]{2,1,0:T(8,128)(2,1)S(1)} collective-permute-done((bf16[4,32,1024]{2,1,0:T(8,128)(2,1)S(1)}, bf16[4,32,1024]{2,1,0:T(8,128)(2,1)S(1)}, u32[]{:S(2)}, u32[]{:S(2)}) %collective-permute-start.10) | collective-permute-done | bytes 262176 | tf_op jit(solution)/shard_map/ppermute | solution.py:335
  130.7 0.6 collective-permute-done.9
  131.3 1.3 fusion.8
  132.7 1.5 collective-permute-start.11
  134.2 2.4 %collective-permute-start.13 = (bf16[32,1024]{1,0:T(8,128)(2,1)S(1)}, bf16[32,1024]{1,0:T(8,128)(2,1)S(1)}, u32[]{:S(2)}, u32[]{:S(2)}) collective-permute-start(bf16[32,1024]{1,0:T(8,128)(2,1)S(1)} %get-tuple-element.50), channel_id=1, source_target_pairs={{0,24},{1,25},{2,26},{3,27},{4,28},{5,29},{6,30},{7,31},{8,16},{9,... | collective-permute-start | bytes 196616 | tf_op jit(solution)/shard_map/ppermute | solution.py:335
  136.6 0.0 collective-permute-done.1
  136.6 0.0 collective-permute-start.12
  136.6 4.6 %collective-permute-done.3 = bf16[4,32,1024]{2,1,0:T(8,128)(2,1)S(1)} collective-permute-done((bf16[4,32,1024]{2,1,0:T(8,128)(2,1)S(1)}, bf16[4,32,1024]{2,1,0:T(8,128)(2,1)S(1)}, u32[]{:S(2)}, u32[]{:S(2)}) %collective-permute-start.3) | collective-permute-done | bytes 262176 | tf_op jit(solution)/shard_map/ppermute | solution.py:335
  141.2 0.3 collective-permute-done.2
  141.5 0.2 fusion.9
  141.8 1.5 collective-permute-start.4
  143.2 2.8 %collective-permute-start.6 = (bf16[32,1024]{1,0:T(8,128)(2,1)S(1)}, bf16[32,1024]{1,0:T(8,128)(2,1)S(1)}, u32[]{:S(2)}, u32[]{:S(2)}) collective-permute-start(bf16[32,1024]{1,0:T(8,128)(2,1)S(1)} %get-tuple-element.53), channel_id=1, source_target_pairs={{0,24},{1,25},{2,26},{3,27},{4,28},{5,29},{6,30},{7,31},{8,16},{9,... | collective-permute-start | bytes 196616 | tf_op jit(solution)/shard_map/ppermute | solution.py:335
  146.1 0.0 collective-permute-done.11
  146.1 0.0 collective-permute-start.5
  146.1 0.0 collective-permute-done.13
  146.1 0.0 collective-permute-done.12
  146.1 0.7 fusion.2
  146.8 0.0 collective-permute-done.4
  146.8 2.8 %collective-permute-done.6 = bf16[32,1024]{1,0:T(8,128)(2,1)S(1)} collective-permute-done((bf16[32,1024]{1,0:T(8,128)(2,1)S(1)}, bf16[32,1024]{1,0:T(8,128)(2,1)S(1)}, u32[]{:S(2)}, u32[]{:S(2)}) %collective-permute-start.6) | collective-permute-done | bytes 65568 | tf_op jit(solution)/shard_map/ppermute | solution.py:335
  149.6 2.1 %collective-permute-done.5 = bf16[32,1024]{1,0:T(8,128)(2,1)S(1)} collective-permute-done((bf16[32,1024]{1,0:T(8,128)(2,1)S(1)}, bf16[32,1024]{1,0:T(8,128)(2,1)S(1)}, u32[]{:S(2)}, u32[]{:S(2)}) %collective-permute-start.5) | collective-permute-done | bytes 65568 | tf_op jit(solution)/shard_map/ppermute | solution.py:335
  151.7 0.7 fusion.5
  152.4 0.0 all-to-all-done.2.held_ref
  152.4 1.4 copy-done
  153.8 5.0 %place.1 = (bf16[2048,4096]{1,0:T(8,128)(2,1)}, bf16[2048,4096]{1,0:T(8,128)(2,1)}, f32[4,1,128]{2,1,0:T(1,128)}) custom-call(s32[32,128]{1,0:T(8,128)} %bitcast.42, s32[32]{0:T(128)} %get-tuple-element.38.order_ref, s32[32]{0:T(128)} %get-tuple-element.37.slot_ref, bf16[32,264,128]{2,1,0:T(8,128)(2,1)} %copy-done, ...), custom_call_target="tpu_custom_call", output_to_operand_aliasing={{0}: (4, {}), {1}: (5, {})} | custom-call | tf_op jit(solution)/shard_map/place/pallas_call | solution.py:472
  (6 shorter events, 0.0 us)
Async XLA Ops:
  2.0 14.4 %all-to-all-start = ((s32[32,1,128]{2,1,0:T(1,128)}), s32[32,1,128]{2,1,0:T(1,128)S(1)}, u32[]{:S(2)}, u32[]{:S(2)}) async-start(s32[32,1,128]{2,1,0:T(1,128)} %bitcast.44), calls=%async_computation | async-start | bytes 32768 | tf_op jit(solution)/shard_map/all_to_all | solution.py:32
  16.4 0.6 copy-start.3
  19.8 2.9 %copy-start.6 = (f32[2,512]{1,0:T(2,128)S(1)}, f32[2,512]{1,0:T(2,128)}, u32[]{:S(2)}) copy-start(f32[2,512]{1,0:T(2,128)} %param.11) | copy-start | bytes 12292
  19.8 3.5 %copy-start.5 = (f32[2,1024]{1,0:T(2,128)S(1)}, f32[2,1024]{1,0:T(2,128)}, u32[]{:S(2)}) copy-start(f32[2,1024]{1,0:T(2,128)} %param.10) | copy-start | bytes 24580
  19.8 51.7 %all-to-all-start.1 = ((bf16[32,2,128,128]{3,2,1,0:T(8,128)(2,1)}), bf16[32,2,128,128]{3,2,1,0:T(8,128)(2,1)S(1)}, u32[]{:S(2)}, u32[]{:S(2)}) async-start(bf16[32,2,128,128]{3,2,1,0:T(8,128)(2,1)} %pick_modes.1), calls=%async_computation.1 | async-start | bytes 4194304 | tf_op jit(solution)/shard_map/all_to_all | solution.py:32
  71.4 1.3 copy-start.1
  72.8 79.7 %all-to-all-start.2 = ((bf16[32,264,128]{2,1,0:T(8,128)(2,1)}), bf16[32,264,128]{2,1,0:T(8,128)(2,1)S(1)}, u32[]{:S(2)}, u32[]{:S(2)}) async-start(bf16[32,264,128]{2,1,0:T(8,128)(2,1)} %get-tuple-element.22), calls=%async_computation.2 | async-start | bytes 4325376 | tf_op jit(solution)/shard_map/all_to_all | solution.py:32
  90.1 18.0 %copy-start.4 = (s32[32,1,128]{2,1,0:T(1,128)S(1)}, s32[32,1,128]{2,1,0:T(1,128)}, u32[]{:S(2)}) copy-start(s32[32,1,128]{2,1,0:T(1,128)} %copy-done.3) | copy-start | bytes 49156
  96.4 12.8 %collective-permute-start.7 = (bf16[16,32,1024]{2,1,0:T(8,128)(2,1)}, bf16[16,32,1024]{2,1,0:T(8,128)(2,1)}, u32[]{:S(2)}, u32[]{:S(2)}) collective-permute-start(bf16[16,32,1024]{2,1,0:T(8,128)(2,1)} %get-tuple-element.35), channel_id=1, source_target_pairs={{0,1},{1,0},{2,3},{3,2},{4,5},{5,4},{6,7},{7,6},{8,9},{9,8},{10,11... | collective-permute-start | bytes 3145736 | tf_op jit(solution)/shard_map/ppermute | solution.py:335
  96.6 18.0 %collective-permute-start = (bf16[16,32,1024]{2,1,0:T(8,128)(2,1)}, bf16[16,32,1024]{2,1,0:T(8,128)(2,1)S(1)}, u32[]{:S(2)}, u32[]{:S(2)}) collective-permute-start(bf16[16,32,1024]{2,1,0:T(8,128)(2,1)} %get-tuple-element.30), channel_id=1, source_target_pairs={{0,1},{1,0},{2,3},{3,2},{4,5},{5,4},{6,7},{7,6},{8,9},{9,8},{10,11... | collective-permute-start | bytes 3145736 | tf_op jit(solution)/shard_map/ppermute | solution.py:335
  108.1 6.5 %copy-start.2 = (f32[16,32,1024]{2,1,0:T(8,128)S(1)}, f32[16,32,1024]{2,1,0:T(8,128)}, u32[]{:S(2)}) copy-start(f32[16,32,1024]{2,1,0:T(8,128)} %get-tuple-element.29) | copy-start | bytes 6291460
  111.0 10.9 %collective-permute-start.8 = (bf16[4,32,1024]{2,1,0:T(8,128)(2,1)S(1)}, bf16[4,32,1024]{2,1,0:T(8,128)(2,1)S(1)}, u32[]{:S(2)}, u32[]{:S(2)}) collective-permute-start(bf16[4,32,1024]{2,1,0:T(8,128)(2,1)S(1)} %get-tuple-element.43), channel_id=1, source_target_pairs={{0,2},{1,3},{2,0},{3,1},{4,6},{5,7},{6,4},{7,5},{8,10},{9,11},{10,... | collective-permute-start | bytes 786440 | tf_op jit(solution)/shard_map/ppermute | solution.py:335
  112.9 17.8 %collective-permute-start.10 = (bf16[4,32,1024]{2,1,0:T(8,128)(2,1)S(1)}, bf16[4,32,1024]{2,1,0:T(8,128)(2,1)S(1)}, u32[]{:S(2)}, u32[]{:S(2)}) collective-permute-start(bf16[4,32,1024]{2,1,0:T(8,128)(2,1)S(1)} %get-tuple-element.44), channel_id=1, source_target_pairs={{0,6},{1,7},{2,4},{3,5},{4,2},{5,3},{6,0},{7,1},{8,14},{9,15},{10,... | collective-permute-start | bytes 786440 | tf_op jit(solution)/shard_map/ppermute | solution.py:335
  114.3 17.0 %collective-permute-start.9 = (bf16[4,32,1024]{2,1,0:T(8,128)(2,1)S(1)}, bf16[4,32,1024]{2,1,0:T(8,128)(2,1)S(1)}, u32[]{:S(2)}, u32[]{:S(2)}) collective-permute-start(bf16[4,32,1024]{2,1,0:T(8,128)(2,1)S(1)} %get-tuple-element.45), channel_id=1, source_target_pairs={{0,4},{1,5},{2,6},{3,7},{4,0},{5,1},{6,2},{7,3},{8,12},{9,13},{10,... | collective-permute-start | bytes 786440 | tf_op jit(solution)/shard_map/ppermute | solution.py:335
  114.9 21.7 %collective-permute-start.1 = (bf16[4,32,1024]{2,1,0:T(8,128)(2,1)S(1)}, bf16[4,32,1024]{2,1,0:T(8,128)(2,1)S(1)}, u32[]{:S(2)}, u32[]{:S(2)}) collective-permute-start(bf16[4,32,1024]{2,1,0:T(8,128)(2,1)S(1)} %get-tuple-element.46), channel_id=1, source_target_pairs={{0,2},{1,3},{2,0},{3,1},{4,6},{5,7},{6,4},{7,5},{8,10},{9,11},{10,... | collective-permute-start | bytes 786440 | tf_op jit(solution)/shard_map/ppermute | solution.py:335
  116.7 24.5 %collective-permute-start.3 = (bf16[4,32,1024]{2,1,0:T(8,128)(2,1)S(1)}, bf16[4,32,1024]{2,1,0:T(8,128)(2,1)S(1)}, u32[]{:S(2)}, u32[]{:S(2)}) collective-permute-start(bf16[4,32,1024]{2,1,0:T(8,128)(2,1)S(1)} %get-tuple-element.47), channel_id=1, source_target_pairs={{0,6},{1,7},{2,4},{3,5},{4,2},{5,3},{6,0},{7,1},{8,14},{9,15},{10,... | collective-permute-start | bytes 786440 | tf_op jit(solution)/shard_map/ppermute | solution.py:335
  121.9 19.6 %collective-permute-start.2 = (bf16[4,32,1024]{2,1,0:T(8,128)(2,1)S(1)}, bf16[4,32,1024]{2,1,0:T(8,128)(2,1)S(1)}, u32[]{:S(2)}, u32[]{:S(2)}) collective-permute-start(bf16[4,32,1024]{2,1,0:T(8,128)(2,1)S(1)} %get-tuple-element.48), channel_id=1, source_target_pairs={{0,4},{1,5},{2,6},{3,7},{4,0},{5,1},{6,2},{7,3},{8,12},{9,13},{10,... | collective-permute-start | bytes 786440 | tf_op jit(solution)/shard_map/ppermute | solution.py:335
  132.7 13.4 %collective-permute-start.11 = (bf16[32,1024]{1,0:T(8,128)(2,1)S(1)}, bf16[32,1024]{1,0:T(8,128)(2,1)S(1)}, u32[]{:S(2)}, u32[]{:S(2)}) collective-permute-start(bf16[32,1024]{1,0:T(8,128)(2,1)S(1)} %get-tuple-element.49), channel_id=1, source_target_pairs={{0,8},{1,9},{2,10},{3,11},{4,12},{5,13},{6,14},{7,15},{8,0},{9,1},... | collective-permute-start | bytes 196616 | tf_op jit(solution)/shard_map/ppermute | solution.py:335
  134.2 11.9 %collective-permute-start.13 = (bf16[32,1024]{1,0:T(8,128)(2,1)S(1)}, bf16[32,1024]{1,0:T(8,128)(2,1)S(1)}, u32[]{:S(2)}, u32[]{:S(2)}) collective-permute-start(bf16[32,1024]{1,0:T(8,128)(2,1)S(1)} %get-tuple-element.50), channel_id=1, source_target_pairs={{0,24},{1,25},{2,26},{3,27},{4,28},{5,29},{6,30},{7,31},{8,16},{9,... | collective-permute-start | bytes 196616 | tf_op jit(solution)/shard_map/ppermute | solution.py:335
  136.6 9.5 %collective-permute-start.12 = (bf16[32,1024]{1,0:T(8,128)(2,1)S(1)}, bf16[32,1024]{1,0:T(8,128)(2,1)S(1)}, u32[]{:S(2)}, u32[]{:S(2)}) collective-permute-start(bf16[32,1024]{1,0:T(8,128)(2,1)S(1)} %get-tuple-element.51), channel_id=1, source_target_pairs={{0,16},{1,17},{2,18},{3,19},{4,20},{5,21},{6,22},{7,23},{8,24},{9,... | collective-permute-start | bytes 196616 | tf_op jit(solution)/shard_map/ppermute | solution.py:335
  141.8 5.0 %collective-permute-start.4 = (bf16[32,1024]{1,0:T(8,128)(2,1)S(1)}, bf16[32,1024]{1,0:T(8,128)(2,1)S(1)}, u32[]{:S(2)}, u32[]{:S(2)}) collective-permute-start(bf16[32,1024]{1,0:T(8,128)(2,1)S(1)} %get-tuple-element.52), channel_id=1, source_target_pairs={{0,8},{1,9},{2,10},{3,11},{4,12},{5,13},{6,14},{7,15},{8,0},{9,1},... | collective-permute-start | bytes 196616 | tf_op jit(solution)/shard_map/ppermute | solution.py:335
  143.2 6.4 %collective-permute-start.6 = (bf16[32,1024]{1,0:T(8,128)(2,1)S(1)}, bf16[32,1024]{1,0:T(8,128)(2,1)S(1)}, u32[]{:S(2)}, u32[]{:S(2)}) collective-permute-start(bf16[32,1024]{1,0:T(8,128)(2,1)S(1)} %get-tuple-element.53), channel_id=1, source_target_pairs={{0,24},{1,25},{2,26},{3,27},{4,28},{5,29},{6,30},{7,31},{8,16},{9,... | collective-permute-start | bytes 196616 | tf_op jit(solution)/shard_map/ppermute | solution.py:335
  146.1 5.7 %collective-permute-start.5 = (bf16[32,1024]{1,0:T(8,128)(2,1)S(1)}, bf16[32,1024]{1,0:T(8,128)(2,1)S(1)}, u32[]{:S(2)}, u32[]{:S(2)}) collective-permute-start(bf16[32,1024]{1,0:T(8,128)(2,1)S(1)} %get-tuple-element.54), channel_id=1, source_target_pairs={{0,16},{1,17},{2,18},{3,19},{4,20},{5,21},{6,22},{7,23},{8,24},{9,... | collective-permute-start | bytes 196616 | tf_op jit(solution)/shard_map/ppermute | solution.py:335
  152.4 1.4 copy-start

commit v4 on v1

--- a/solution.py
+++ b/solution.py
@@ -9,7 +9,7 @@
 
 
 BLK = 128
-EXTRA = 16
+EXTRA = 8
 AXES = ("row", "col")
 F32 = jnp.float32
 BF16 = jnp.bfloat16
@@ -120,11 +120,12 @@
         stiff_ref,
         mi_ref,
         mb_ref,
-        out_ref,
         k_ref,
         m_ref,
         d_ref,
+        *refs,
     ):
+        near_refs, out_ref, sem = refs[: sizes.plane], refs[-2], refs[-1]
         sub = pl.program_id(0)
         me = lax.axis_index("row") * sizes.cols + lax.axis_index("col")
         couple = cpl_ref[0]
@@ -174,10 +175,21 @@
                 k_ref[0, rows, cols] = stiff_block
                 m_ref[0, rows, cols] = mass_block
 
+        @pl.when(sub == local_subs - 1)
+        def _():
+            copies = [
+                pltpu.make_async_copy(out_ref.at[d], ref, sem.at[d])
+                for d, ref in enumerate(near_refs)
+            ]
+            for copy in copies:
+                copy.start()
+            for copy in copies:
+                copy.wait()
+
     def piece(*shape):
         return pl.BlockSpec((1,) + shape, lambda s: (s, 0, 0))
 
-    out_blocks = (sizes.plane, sizes.devices // sizes.plane, 2 * BLK + EXTRA, BLK)
+    out_blocks = (sizes.devices // sizes.plane, 2 * BLK + EXTRA, BLK)
     return pl.pallas_call(
         kernel,
         grid=(local_subs,),
@@ -190,16 +202,20 @@
             piece(1, boundary),
         ],
         out_specs=[
-            pl.BlockSpec(out_blocks, lambda s: (0, 0, 0, 0)),
             piece(boundary, boundary),
             piece(boundary, boundary),
             piece(1, boundary),
-        ],
+        ]
+        + [ANY] * sizes.plane,
         out_shape=[
-            jax.ShapeDtypeStruct(out_blocks, BF16),
             jax.ShapeDtypeStruct((local_subs, boundary, boundary), BF16),
             jax.ShapeDtypeStruct((local_subs, boundary, boundary), BF16),
             jax.ShapeDtypeStruct((local_subs, 1, boundary), F32),
+        ]
+        + [jax.ShapeDtypeStruct(out_blocks, BF16)] * sizes.plane,
+        scratch_shapes=[
+            pltpu.VMEM((sizes.plane,) + out_blocks, BF16),
+            pltpu.SemaphoreType.DMA((sizes.plane,)),
         ],
         name="condense",
     )(
@@ -344,9 +360,10 @@
 
 def reduce_shares(send, keep, sizes):
     got = swap(send, 1, sizes.devices)
-    summed = keep + got.astype(F32)
     depth = sizes.devices // sizes.plane
-    summed = summed.reshape((sizes.plane // 2, depth) + summed.shape[1:])
+    shape = (sizes.plane // 2, depth) + keep.shape[1:]
+    keep, got = keep.reshape(shape), got.reshape(shape)
+    summed = [keep[d] + got[d].astype(F32) for d in range(sizes.plane // 2)]
     total = summed[0]
     for d in range(1, sizes.plane // 2):
         got = swap(summed[d].astype(BF16), 2 * d, sizes.devices)
@@ -513,7 +530,7 @@
     turned = jnp.swapaxes(modes.reshape(sizes.col_blocks, BLK, width), 1, 2)
     wanted = pick_modes(table, turned, sizes.ratio)
     fetched = exchange(wanted)
-    blocks, stiff, mass, diagonal = condense(
+    stiff, mass, diagonal, *blocks = condense(
         block_map, inv_interior, coupling, boundary_stiff, mass_interior, mass_boundary, sizes
     )
     spread = spread_in_plane(blocks, sizes)

time: 194 us -> 191 us (0.985)
  local copies, waits for them, and re-layouts: 18.6 us -> 15.8 us
    squeeze x1 -> x0, local copies, waits for them, and re-layouts: 2.81 us -> none  [spread_in_plane(): near.append(swap(blocks[d], d, sizes.devices))]
  transfers between devices with their start and end apart: 26 -> 26, of which waited for: 10 -> 10; matrix products, arithmetic and copies ran while one was open for 10% -> 9% of each run, Pallas kernels for 13% -> 14%
where the time goes in v4:
time: 191 us; the launch traced here: 190 us
  waiting for transfers between devices  66.1 us (35%)
  starting transfers between devices  52.3 us (27%)
  Pallas kernels  50.2 us (26%)
  local copies, waits for them, and re-layouts  15.8 us (8%)
  other arithmetic  5.35 us (3%)
    ppermute x24, waiting for transfers between devices, swap(): lax.ppermute(value, AXES, [(i, i ^ offset) for i in range(device_count)])  61.2 us
    ppermute x24, starting transfers between devices, swap(): lax.ppermute(value, AXES, [(i, i ^ offset) for i in range(device_count)])  42.2 us
    pallas_call x1, Pallas kernels, clear_tiles(): pl.pallas_call(kernel, in_specs=[ANY], out_specs=[ANY, ANY], out_shape=[j...  11.2 us
    unnamed x33, local copies, waits for them, and re-layouts  10.7 us
    all_to_all x2, starting transfers between devices, exchange(): return lax.all_to_all(value, AXES, split_axis=0, concat_axis=0, tiled=True)  10.2 us
    pallas_call x1, Pallas kernels, condense(): pl.pallas_call(kernel, grid=(local_subs,), in_specs=[SMEM, piece(interior...  9.56 us
    pallas_call x1, Pallas kernels, project_stiff(): pl.pallas_call(kernel, grid=(modes // chunk,), in_specs=[SMEM, whole(*fet...  8.44 us
    pallas_call x1, Pallas kernels, project_mass(): pl.pallas_call(kernel, grid=(modes // chunk,), in_specs=[pl.BlockSpec((ch...  6.31 us
  transfers between devices with their start and end apart: 26, of which 10 were waited for; matrix products, arithmetic and copies ran while one was open for 9% of the time, Pallas kernels for 14%

profile of v4, /device:TPU:0, one launch (start us, length us, event | category | flops | bytes accessed | tf_op | source)
XLA Modules:
  0.0 190.5 jit_solution(13104271469324680907)
XLA Ops:
  0.6 1.4 describe.1
  2.0 7.3 %all-to-all-start = ((s32[32,1,128]{2,1,0:T(1,128)}), s32[32,1,128]{2,1,0:T(1,128)S(1)}, u32[]{:S(2)}, u32[]{:S(2)}) async-start(s32[32,1,128]{2,1,0:T(1,128)} %bitcast.44), calls=%async_computation | async-start | bytes 32768 | tf_op jit(solution)/shard_map/all_to_all | solution.py:32
  9.3 2.3 %copy.21 = bf16[32,128,128]{1,2,0:T(8,128)(2,1)} copy(bf16[32,128,128]{2,1,0:T(8,128)(2,1)} %bitcast.39) | data formatting | bytes 2097152 | tf_op jit(solution)/shard_map/reshape | solution.py:530
  11.6 4.8 %all-to-all-done = s32[32,1,128]{2,1,0:T(1,128)S(1)} async-done(((s32[32,1,128]{2,1,0:T(1,128)}), s32[32,1,128]{2,1,0:T(1,128)S(1)}, u32[]{:S(2)}, u32[]{:S(2)}) %all-to-all-start) | async-done | bytes 16416 | tf_op jit(solution)/shard_map/all_to_all | solution.py:32
  16.4 0.6 copy-done.7
  17.0 2.7 %pick_modes.1 = bf16[32,2,128,128]{3,2,1,0:T(8,128)(2,1)} custom-call(s32[32,128]{1,0:T(8,128)} %bitcast.40, bf16[32,128,128]{2,1,0:T(8,128)(2,1)} %bitcast.38), custom_call_target="tpu_custom_call" | custom-call | tf_op jit(solution)/shard_map/pick_modes/pallas_call | solution.py:101
  19.8 2.9 %all-to-all-start.1 = ((bf16[32,2,128,128]{3,2,1,0:T(8,128)(2,1)}), bf16[32,2,128,128]{3,2,1,0:T(8,128)(2,1)S(1)}, u32[]{:S(2)}, u32[]{:S(2)}) async-start(bf16[32,2,128,128]{3,2,1,0:T(8,128)(2,1)} %pick_modes.1), calls=%async_computation.1 | async-start | bytes 4194304 | tf_op jit(solution)/shard_map/all_to_all | solution.py:32
  22.7 1.3 copy.20.mi_ref
  24.0 0.6 broadcast_in_dim.27.mb_ref
  24.6 9.6 %condense.1 = (bf16[2,512,512]{2,1,0:T(8,128)(2,1)}, bf16[2,512,512]{2,1,0:T(8,128)(2,1)}, f32[2,1,512]{2,1,0:T(1,128)}, bf16[4,264,128]{2,1,0:T(8,128)(2,1)}, b...) custom-call(s32[2,4]{1,0:T(2,128)} %map_ref.5, ...), custom_call_target="tpu_custom_call" | custom-call | tf_op jit(solution)/shard_map/condense/pallas_call | solution.py:193
  34.2 0.2 collective-permute-start
  34.3 1.6 collective-permute-start.1
  36.0 0.1 collective-permute-start.2
  36.1 1.7 collective-permute-start.3
  37.8 1.7 constant_dynamic-update-slice_fusion.3
  39.5 11.2 %clear_tiles.1 = (bf16[2048,4096]{1,0:T(8,128)(2,1)}, bf16[2048,4096]{1,0:T(8,128)(2,1)}) custom-call(s32[32,128]{1,0:T(8,128)} %bitcast.41), custom_call_target="tpu_custom_call" | custom-call | tf_op jit(solution)/shard_map/clear_tiles/pallas_call | solution.py:400
  50.7 2.6 %collective-permute-start.5 = (bf16[4,264,128]{2,1,0:T(8,128)(2,1)}, bf16[4,264,128]{2,1,0:T(8,128)(2,1)S(1)}, u32[]{:S(2)}, u32[]{:S(2)}) collective-permute-start(bf16[4,264,128]{2,1,0:T(8,128)(2,1)} %get-tuple-element.37), channel_id=1, source_target_pairs={{0,6},{1,7},{2,4},{3,5},{4,2},{5,3},{6,0},{7,1},{8,14},{9,15},{10,... | collective-permute-start | bytes 811016 | tf_op jit(solution)/shard_map/ppermute | solution.py:358
  53.4 1.7 slice_dynamic-update-slice_fusion.6
  55.1 1.7 slice_dynamic-update-slice_fusion.5
  56.9 0.1 collective-permute-done.2
  57.0 0.7 slice_dynamic-update-slice_fusion.4
  57.7 0.7 slice_dynamic-update-slice_fusion.3
  58.4 11.6 %collective-permute-done.4 = bf16[4,264,128]{2,1,0:T(8,128)(2,1)S(1)} collective-permute-done((bf16[4,264,128]{2,1,0:T(8,128)(2,1)}, bf16[4,264,128]{2,1,0:T(8,128)(2,1)S(1)}, u32[]{:S(2)}, u32[]{:S(2)}) %collective-permute-start.4) | collective-permute-done | bytes 270368 | tf_op jit(solution)/shard_map/ppermute | solution.py:358
  69.9 0.7 slice_dynamic-update-slice_fusion.2
  70.6 0.7 slice_dynamic-update-slice_fusion.1
  71.3 2.0 %collective-permute-done.6 = bf16[4,264,128]{2,1,0:T(8,128)(2,1)S(1)} collective-permute-done((bf16[4,264,128]{2,1,0:T(8,128)(2,1)}, bf16[4,264,128]{2,1,0:T(8,128)(2,1)S(1)}, u32[]{:S(2)}, u32[]{:S(2)}) %collective-permute-start.6) | collective-permute-done | bytes 270368 | tf_op jit(solution)/shard_map/ppermute | solution.py:358
  73.4 0.7 slice_dynamic-update-slice_fusion
  74.1 1.4 copy-done
  75.4 8.4 %project_stiff.1 = (bf16[16,32,1024]{2,1,0:T(8,128)(2,1)}, f32[16,32,1024]{2,1,0:T(8,128)}, bf16[1024,1024]{1,0:T(8,128)(2,1)}) custom-call(s32[2,4]{1,0:T(2,128)} %map_ref.5, bf16[8,4,2,128,128]{4,3,2,1,0:T(8,128)(2,1)} %bitcast.37, bf16[2,512,512]{2,1,0:T(8,128)(2,1)} %get-tuple-element.48.m_ref), custom_call_target="tpu_custom_call" | custom-call | tf_op jit(solution)/shard_map/project_stiff/pallas_call | solution.py:290
  83.9 5.0 %mix_mass.1.y_ref = bf16[1024,1024]{1,0:T(8,128)(2,1)} custom-call(bf16[1024,1024]{1,0:T(8,128)(2,1)} %get-tuple-element.51.t_ref, bf16[2,512,512]{2,1,0:T(8,128)(2,1)} %get-tuple-element.52.m_ref, f32[2,1,512]{2,1,0:T(1,128)} %get-tuple-element.53.d_ref), custom_call_target="tpu_custom_call" | custom-call | tf_op jit(solution)/shard_map/mix_mass/pallas_call | solution.py:322
  88.9 6.3 %project_mass.1 = (bf16[16,32,1024]{2,1,0:T(8,128)(2,1)}, f32[16,32,1024]{2,1,0:T(8,128)}) custom-call(bf16[1024,1024]{1,0:T(8,128)(2,1)} %mix_mass.1.y_ref, bf16[1024,1024]{1,0:T(8,128)(2,1)} %get-tuple-element.51.t_ref), custom_call_target="tpu_custom_call" | custom-call | tf_op jit(solution)/shard_map/project_mass/pallas_call | solution.py:344
  95.2 1.8 collective-permute-start.17
  97.0 1.5 collective-permute-start.7
  98.5 2.1 %collective-permute-start.8 = (bf16[8,264,128]{2,1,0:T(8,128)(2,1)S(1)}, bf16[8,264,128]{2,1,0:T(8,128)(2,1)S(1)}, u32[]{:S(2)}, u32[]{:S(2)}) collective-permute-start(bf16[8,264,128]{2,1,0:T(8,128)(2,1)S(1)} %copy-done.10), channel_id=1, source_target_pairs={{0,16},{1,17},{2,18},{3,19},{4,20},{5,21},{6,22},{7,23},{8,24},{9,... | collective-permute-start | bytes 1622024 | tf_op jit(solution)/shard_map/ppermute | solution.py:358
  100.6 1.5 collective-permute-start.9
  102.2 0.2 slice_reduce_fusion
  102.3 0.2 convert_reduce_fusion
  102.5 0.6 select_reduce_fusion
  103.2 20.3 %collective-permute-done.7.refs_4_ = bf16[8,264,128]{2,1,0:T(8,128)(2,1)S(1)} collective-permute-done((bf16[8,264,128]{2,1,0:T(8,128)(2,1)}, bf16[8,264,128]{2,1,0:T(8,128)(2,1)S(1)}, u32[]{:S(2)}, u32[]{:S(2)}) %collective-permute-start.7) | collective-permute-done | bytes 540704 | tf_op jit(solution)/shard_map/ppermute | solution.py:358
  123.4 14.4 %collective-permute-done.9.refs_6_ = bf16[8,264,128]{2,1,0:T(8,128)(2,1)S(1)} collective-permute-done((bf16[8,264,128]{2,1,0:T(8,128)(2,1)S(1)}, bf16[8,264,128]{2,1,0:T(8,128)(2,1)S(1)}, u32[]{:S(2)}, u32[]{:S(2)}) %collective-permute-start.9) | collective-permute-done | bytes 540704 | tf_op jit(solution)/shard_map/ppermute | solution.py:358
  137.9 0.8 copy-done.6
  138.7 5.5 %place.1 = (bf16[2048,4096]{1,0:T(8,128)(2,1)}, bf16[2048,4096]{1,0:T(8,128)(2,1)}, f32[4,1,128]{2,1,0:T(1,128)}) custom-call(s32[32,128]{1,0:T(8,128)} %bitcast.42, s32[32]{0:T(128)} %get-tuple-element.58.refs_1_, s32[32]{0:T(128)} %get-tuple-element.57.refs_2_, bf16[8,264,128]{2,1,0:T(8,128)(2,1)} %copy-done.3, ...), custom_call_target="tpu_custom_call", output_to_operand_aliasing={{0}: (7, {}), {1}: (8, {})} | custom-call | tf_op jit(solution)/shard_map/place/pallas_call | solution.py:491
  144.3 1.5 add_convert_fusion.2
  145.8 1.4 collective-permute-start.18
  147.2 0.7 collective-permute-start.19
  147.9 1.4 collective-permute-start.20
  149.3 0.3 add_convert_fusion.5
  149.6 1.4 collective-permute-start.11
  151.0 0.7 collective-permute-start.12
  151.7 3.3 %collective-permute-done.18 = bf16[4,32,1024]{2,1,0:T(8,128)(2,1)S(1)} collective-permute-done((bf16[4,32,1024]{2,1,0:T(8,128)(2,1)S(1)}, bf16[4,32,1024]{2,1,0:T(8,128)(2,1)S(1)}, u32[]{:S(2)}, u32[]{:S(2)}) %collective-permute-start.18) | collective-permute-done | bytes 262176 | tf_op jit(solution)/shard_map/ppermute | solution.py:358
  155.0 1.5 collective-permute-start.13
  156.5 5.4 %collective-permute-done.19 = bf16[4,32,1024]{2,1,0:T(8,128)(2,1)S(1)} collective-permute-done((bf16[4,32,1024]{2,1,0:T(8,128)(2,1)S(1)}, bf16[4,32,1024]{2,1,0:T(8,128)(2,1)S(1)}, u32[]{:S(2)}, u32[]{:S(2)}) %collective-permute-start.19) | collective-permute-done | bytes 262176 | tf_op jit(solution)/shard_map/ppermute | solution.py:358
  161.9 1.2 fusion.8
  163.1 10.9 %collective-permute-start.21 = (bf16[32,1024]{1,0:T(8,128)(2,1)S(1)}, bf16[32,1024]{1,0:T(8,128)(2,1)S(1)}, u32[]{:S(2)}, u32[]{:S(2)}) collective-permute-start(bf16[32,1024]{1,0:T(8,128)(2,1)S(1)} %get-tuple-element.101), channel_id=1, source_target_pairs={{0,8},{1,9},{2,10},{3,11},{4,12},{5,13},{6,14},{7,15},{8,0},{9,1},... | collective-permute-start | bytes 196616 | tf_op jit(solution)/shard_map/ppermute | solution.py:358
  174.1 1.1 collective-permute-start.22
  175.1 1.4 collective-permute-start.23
  176.5 0.2 fusion.9
  176.8 5.3 %collective-permute-start.14 = (bf16[32,1024]{1,0:T(8,128)(2,1)S(1)}, bf16[32,1024]{1,0:T(8,128)(2,1)S(1)}, u32[]{:S(2)}, u32[]{:S(2)}) collective-permute-start(bf16[32,1024]{1,0:T(8,128)(2,1)S(1)} %get-tuple-element.104), channel_id=1, source_target_pairs={{0,8},{1,9},{2,10},{3,11},{4,12},{5,13},{6,14},{7,15},{8,0},{9,1},... | collective-permute-start | bytes 196616 | tf_op jit(solution)/shard_map/ppermute | solution.py:358
  182.1 1.6 collective-permute-start.15
  183.6 1.4 collective-permute-start.16
  185.0 0.7 fusion.2
  185.7 1.8 collective-permute-done.15
  187.5 2.3 %collective-permute-done.16 = bf16[32,1024]{1,0:T(8,128)(2,1)S(1)} collective-permute-done((bf16[32,1024]{1,0:T(8,128)(2,1)S(1)}, bf16[32,1024]{1,0:T(8,128)(2,1)S(1)}, u32[]{:S(2)}, u32[]{:S(2)}) %collective-permute-start.16) | collective-permute-done | bytes 65568 | tf_op jit(solution)/shard_map/ppermute | solution.py:358
  189.8 0.7 fusion.5
  (44 shorter events, 0.3 us)
Async XLA Ops:
  2.0 14.4 %all-to-all-start = ((s32[32,1,128]{2,1,0:T(1,128)}), s32[32,1,128]{2,1,0:T(1,128)S(1)}, u32[]{:S(2)}, u32[]{:S(2)}) async-start(s32[32,1,128]{2,1,0:T(1,128)} %bitcast.44), calls=%async_computation | async-start | bytes 32768 | tf_op jit(solution)/shard_map/all_to_all | solution.py:32
  16.4 0.6 copy-start.7
  19.8 2.9 %copy-start.11 = (f32[2,1024]{1,0:T(2,128)S(1)}, f32[2,1024]{1,0:T(2,128)}, u32[]{:S(2)}) copy-start(f32[2,1024]{1,0:T(2,128)} %param.10) | copy-start | bytes 24580
  19.8 4.2 %copy-start.12 = (f32[2,512]{1,0:T(2,128)S(1)}, f32[2,512]{1,0:T(2,128)}, u32[]{:S(2)}) copy-start(f32[2,512]{1,0:T(2,128)} %param.11) | copy-start | bytes 12292
  19.8 54.3 %all-to-all-start.1 = ((bf16[32,2,128,128]{3,2,1,0:T(8,128)(2,1)}), bf16[32,2,128,128]{3,2,1,0:T(8,128)(2,1)S(1)}, u32[]{:S(2)}, u32[]{:S(2)}) async-start(bf16[32,2,128,128]{3,2,1,0:T(8,128)(2,1)} %pick_modes.1), calls=%async_computation.1 | async-start | bytes 4194304 | tf_op jit(solution)/shard_map/all_to_all | solution.py:32
  34.2 16.6 %collective-permute-start = (bf16[4,264,128]{2,1,0:T(8,128)(2,1)}, bf16[4,264,128]{2,1,0:T(8,128)(2,1)}, u32[]{:S(2)}, u32[]{:S(2)}) collective-permute-start(bf16[4,264,128]{2,1,0:T(8,128)(2,1)} %get-tuple-element.32), channel_id=1, source_target_pairs={{0,1},{1,0},{2,3},{3,2},{4,5},{5,4},{6,7},{7,6},{8,9},{9,8},{10,11... | collective-permute-start | bytes 811016 | tf_op jit(solution)/shard_map/ppermute | solution.py:358
  34.3 20.7 %collective-permute-start.1 = (bf16[4,264,128]{2,1,0:T(8,128)(2,1)}, bf16[4,264,128]{2,1,0:T(8,128)(2,1)}, u32[]{:S(2)}, u32[]{:S(2)}) collective-permute-start(bf16[4,264,128]{2,1,0:T(8,128)(2,1)} %get-tuple-element.33), channel_id=1, source_target_pairs={{0,2},{1,3},{2,0},{3,1},{4,6},{5,7},{6,4},{7,5},{8,10},{9,11},{10,... | collective-permute-start | bytes 811016 | tf_op jit(solution)/shard_map/ppermute | solution.py:358
  36.0 21.0 %collective-permute-start.2 = (bf16[4,264,128]{2,1,0:T(8,128)(2,1)}, bf16[4,264,128]{2,1,0:T(8,128)(2,1)S(1)}, u32[]{:S(2)}, u32[]{:S(2)}) collective-permute-start(bf16[4,264,128]{2,1,0:T(8,128)(2,1)} %get-tuple-element.34), channel_id=1, source_target_pairs={{0,3},{1,2},{2,1},{3,0},{4,7},{5,6},{6,5},{7,4},{8,11},{9,10},{10,... | collective-permute-start | bytes 811016 | tf_op jit(solution)/shard_map/ppermute | solution.py:358
  36.1 21.6 %collective-permute-start.3 = (bf16[4,264,128]{2,1,0:T(8,128)(2,1)}, bf16[4,264,128]{2,1,0:T(8,128)(2,1)S(1)}, u32[]{:S(2)}, u32[]{:S(2)}) collective-permute-start(bf16[4,264,128]{2,1,0:T(8,128)(2,1)} %get-tuple-element.35), channel_id=1, source_target_pairs={{0,4},{1,5},{2,6},{3,7},{4,0},{5,1},{6,2},{7,3},{8,12},{9,13},{10,... | collective-permute-start | bytes 811016 | tf_op jit(solution)/shard_map/ppermute | solution.py:358
  37.7 32.2 %collective-permute-start.4 = (bf16[4,264,128]{2,1,0:T(8,128)(2,1)}, bf16[4,264,128]{2,1,0:T(8,128)(2,1)S(1)}, u32[]{:S(2)}, u32[]{:S(2)}) collective-permute-start(bf16[4,264,128]{2,1,0:T(8,128)(2,1)} %get-tuple-element.36), channel_id=1, source_target_pairs={{0,5},{1,4},{2,7},{3,6},{4,1},{5,0},{6,3},{7,2},{8,13},{9,12},{10,... | collective-permute-start | bytes 811016 | tf_op jit(solution)/shard_map/ppermute | solution.py:358
  50.7 19.9 %collective-permute-start.5 = (bf16[4,264,128]{2,1,0:T(8,128)(2,1)}, bf16[4,264,128]{2,1,0:T(8,128)(2,1)S(1)}, u32[]{:S(2)}, u32[]{:S(2)}) collective-permute-start(bf16[4,264,128]{2,1,0:T(8,128)(2,1)} %get-tuple-element.37), channel_id=1, source_target_pairs={{0,6},{1,7},{2,4},{3,5},{4,2},{5,3},{6,0},{7,1},{8,14},{9,15},{10,... | collective-permute-start | bytes 811016 | tf_op jit(solution)/shard_map/ppermute | solution.py:358
  55.1 18.3 %collective-permute-start.6 = (bf16[4,264,128]{2,1,0:T(8,128)(2,1)}, bf16[4,264,128]{2,1,0:T(8,128)(2,1)S(1)}, u32[]{:S(2)}, u32[]{:S(2)}) collective-permute-start(bf16[4,264,128]{2,1,0:T(8,128)(2,1)} %get-tuple-element.38), channel_id=1, source_target_pairs={{0,7},{1,6},{2,5},{3,4},{4,3},{5,2},{6,1},{7,0},{8,15},{9,14},{10,... | collective-permute-start | bytes 811016 | tf_op jit(solution)/shard_map/ppermute | solution.py:358
  74.1 21.1 %copy-start.3 = (bf16[8,264,128]{2,1,0:T(8,128)(2,1)}, bf16[8,264,128]{2,1,0:T(8,128)(2,1)S(1)}, u32[]{:S(2)}) copy-start(bf16[8,264,128]{2,1,0:T(8,128)(2,1)S(1)} %get-tuple-element.72.refs_3_) | copy-start | bytes 1622020
  74.1 1.4 copy-start
  88.8 9.6 %copy-start.10 = (bf16[8,264,128]{2,1,0:T(8,128)(2,1)S(1)}, bf16[8,264,128]{2,1,0:T(8,128)(2,1)}, u32[]{:S(2)}) copy-start(bf16[8,264,128]{2,1,0:T(8,128)(2,1)} %get-tuple-element.41) | copy-start | bytes 1622020
  88.8 11.8 %copy-start.9 = (bf16[8,264,128]{2,1,0:T(8,128)(2,1)S(1)}, bf16[8,264,128]{2,1,0:T(8,128)(2,1)}, u32[]{:S(2)}) copy-start(bf16[8,264,128]{2,1,0:T(8,128)(2,1)} %get-tuple-element.42) | copy-start | bytes 1622020
  88.8 13.3 %copy-start.8 = (s32[32,1,128]{2,1,0:T(1,128)S(1)}, s32[32,1,128]{2,1,0:T(1,128)}, u32[]{:S(2)}) copy-start(s32[32,1,128]{2,1,0:T(1,128)} %copy-done.7) | copy-start | bytes 49156
  95.2 49.1 %collective-permute-start.17 = (bf16[16,32,1024]{2,1,0:T(8,128)(2,1)}, bf16[16,32,1024]{2,1,0:T(8,128)(2,1)}, u32[]{:S(2)}, u32[]{:S(2)}) collective-permute-start(bf16[16,32,1024]{2,1,0:T(8,128)(2,1)} %get-tuple-element.55), channel_id=1, source_target_pairs={{0,1},{1,0},{2,3},{3,2},{4,5},{5,4},{6,7},{7,6},{8,9},{9,8},{10,11... | collective-permute-start | bytes 3145736 | tf_op jit(solution)/shard_map/ppermute | solution.py:358
  96.9 52.4 %collective-permute-start.10 = (bf16[16,32,1024]{2,1,0:T(8,128)(2,1)}, bf16[16,32,1024]{2,1,0:T(8,128)(2,1)S(1)}, u32[]{:S(2)}, u32[]{:S(2)}) collective-permute-start(bf16[16,32,1024]{2,1,0:T(8,128)(2,1)} %get-tuple-element.50), channel_id=1, source_target_pairs={{0,1},{1,0},{2,3},{3,2},{4,5},{5,4},{6,7},{7,6},{8,9},{9,8},{10,11... | collective-permute-start | bytes 3145736 | tf_op jit(solution)/shard_map/ppermute | solution.py:358
  97.0 26.4 %collective-permute-start.7 = (bf16[8,264,128]{2,1,0:T(8,128)(2,1)}, bf16[8,264,128]{2,1,0:T(8,128)(2,1)S(1)}, u32[]{:S(2)}, u32[]{:S(2)}) collective-permute-start(bf16[8,264,128]{2,1,0:T(8,128)(2,1)} %get-tuple-element.71), channel_id=1, source_target_pairs={{0,8},{1,9},{2,10},{3,11},{4,12},{5,13},{6,14},{7,15},{8,0},{9,1},... | collective-permute-start | bytes 1622024 | tf_op jit(solution)/shard_map/ppermute | solution.py:358
  98.5 24.9 %collective-permute-start.8 = (bf16[8,264,128]{2,1,0:T(8,128)(2,1)S(1)}, bf16[8,264,128]{2,1,0:T(8,128)(2,1)S(1)}, u32[]{:S(2)}, u32[]{:S(2)}) collective-permute-start(bf16[8,264,128]{2,1,0:T(8,128)(2,1)S(1)} %copy-done.10), channel_id=1, source_target_pairs={{0,16},{1,17},{2,18},{3,19},{4,20},{5,21},{6,22},{7,23},{8,24},{9,... | collective-permute-start | bytes 1622024 | tf_op jit(solution)/shard_map/ppermute | solution.py:358
  100.6 37.2 %collective-permute-start.9 = (bf16[8,264,128]{2,1,0:T(8,128)(2,1)S(1)}, bf16[8,264,128]{2,1,0:T(8,128)(2,1)S(1)}, u32[]{:S(2)}, u32[]{:S(2)}) collective-permute-start(bf16[8,264,128]{2,1,0:T(8,128)(2,1)S(1)} %copy-done.9), channel_id=1, source_target_pairs={{0,24},{1,25},{2,26},{3,27},{4,28},{5,29},{6,30},{7,31},{8,16},{9,... | collective-permute-start | bytes 1622024 | tf_op jit(solution)/shard_map/ppermute | solution.py:358
  123.4 14.4 %copy-start.4 = (bf16[8,264,128]{2,1,0:T(8,128)(2,1)}, bf16[8,264,128]{2,1,0:T(8,128)(2,1)S(1)}, u32[]{:S(2)}) copy-start(bf16[8,264,128]{2,1,0:T(8,128)(2,1)S(1)} %collective-permute-done.7.refs_4_) | copy-start | bytes 1622020
  123.4 14.4 %copy-start.5 = (bf16[8,264,128]{2,1,0:T(8,128)(2,1)}, bf16[8,264,128]{2,1,0:T(8,128)(2,1)S(1)}, u32[]{:S(2)}) copy-start(bf16[8,264,128]{2,1,0:T(8,128)(2,1)S(1)} %collective-permute-done.8.refs_5_) | copy-start | bytes 1622020
  137.9 0.8 copy-start.6
  138.7 5.6 %copy-start.2 = (f32[16,32,1024]{2,1,0:T(8,128)S(1)}, f32[16,32,1024]{2,1,0:T(8,128)}, u32[]{:S(2)}) copy-start(f32[16,32,1024]{2,1,0:T(8,128)} %get-tuple-element.54) | copy-start | bytes 6291460
  144.2 5.1 %copy-start.1 = (f32[16,32,1024]{2,1,0:T(8,128)S(1)}, f32[16,32,1024]{2,1,0:T(8,128)}, u32[]{:S(2)}) copy-start(f32[16,32,1024]{2,1,0:T(8,128)} %get-tuple-element.49) | copy-start | bytes 6291460
  145.8 9.2 %collective-permute-start.18 = (bf16[4,32,1024]{2,1,0:T(8,128)(2,1)S(1)}, bf16[4,32,1024]{2,1,0:T(8,128)(2,1)S(1)}, u32[]{:S(2)}, u32[]{:S(2)}) collective-permute-start(bf16[4,32,1024]{2,1,0:T(8,128)(2,1)S(1)} %get-tuple-element.63), channel_id=1, source_target_pairs={{0,2},{1,3},{2,0},{3,1},{4,6},{5,7},{6,4},{7,5},{8,10},{9,11},{10,... | collective-permute-start | bytes 786440 | tf_op jit(solution)/shard_map/ppermute | solution.py:358
  147.2 14.8 %collective-permute-start.19 = (bf16[4,32,1024]{2,1,0:T(8,128)(2,1)S(1)}, bf16[4,32,1024]{2,1,0:T(8,128)(2,1)S(1)}, u32[]{:S(2)}, u32[]{:S(2)}) collective-permute-start(bf16[4,32,1024]{2,1,0:T(8,128)(2,1)S(1)} %get-tuple-element.65), channel_id=1, source_target_pairs={{0,4},{1,5},{2,6},{3,7},{4,0},{5,1},{6,2},{7,3},{8,12},{9,13},{10,... | collective-permute-start | bytes 786440 | tf_op jit(solution)/shard_map/ppermute | solution.py:358
  147.9 14.0 %collective-permute-start.20 = (bf16[4,32,1024]{2,1,0:T(8,128)(2,1)S(1)}, bf16[4,32,1024]{2,1,0:T(8,128)(2,1)S(1)}, u32[]{:S(2)}, u32[]{:S(2)}) collective-permute-start(bf16[4,32,1024]{2,1,0:T(8,128)(2,1)S(1)} %get-tuple-element.64), channel_id=1, source_target_pairs={{0,6},{1,7},{2,4},{3,5},{4,2},{5,3},{6,0},{7,1},{8,14},{9,15},{10,... | collective-permute-start | bytes 786440 | tf_op jit(solution)/shard_map/ppermute | solution.py:358
  149.6 25.5 %collective-permute-start.11 = (bf16[4,32,1024]{2,1,0:T(8,128)(2,1)S(1)}, bf16[4,32,1024]{2,1,0:T(8,128)(2,1)S(1)}, u32[]{:S(2)}, u32[]{:S(2)}) collective-permute-start(bf16[4,32,1024]{2,1,0:T(8,128)(2,1)S(1)} %get-tuple-element.66), channel_id=1, source_target_pairs={{0,2},{1,3},{2,0},{3,1},{4,6},{5,7},{6,4},{7,5},{8,10},{9,11},{10,... | collective-permute-start | bytes 786440 | tf_op jit(solution)/shard_map/ppermute | solution.py:358
  151.0 25.5 %collective-permute-start.12 = (bf16[4,32,1024]{2,1,0:T(8,128)(2,1)S(1)}, bf16[4,32,1024]{2,1,0:T(8,128)(2,1)S(1)}, u32[]{:S(2)}, u32[]{:S(2)}) collective-permute-start(bf16[4,32,1024]{2,1,0:T(8,128)(2,1)S(1)} %get-tuple-element.68), channel_id=1, source_target_pairs={{0,4},{1,5},{2,6},{3,7},{4,0},{5,1},{6,2},{7,3},{8,12},{9,13},{10,... | collective-permute-start | bytes 786440 | tf_op jit(solution)/shard_map/ppermute | solution.py:358
  155.0 21.5 %collective-permute-start.13 = (bf16[4,32,1024]{2,1,0:T(8,128)(2,1)S(1)}, bf16[4,32,1024]{2,1,0:T(8,128)(2,1)S(1)}, u32[]{:S(2)}, u32[]{:S(2)}) collective-permute-start(bf16[4,32,1024]{2,1,0:T(8,128)(2,1)S(1)} %get-tuple-element.67), channel_id=1, source_target_pairs={{0,6},{1,7},{2,4},{3,5},{4,2},{5,3},{6,0},{7,1},{8,14},{9,15},{10,... | collective-permute-start | bytes 786440 | tf_op jit(solution)/shard_map/ppermute | solution.py:358
  163.1 20.5 %collective-permute-start.21 = (bf16[32,1024]{1,0:T(8,128)(2,1)S(1)}, bf16[32,1024]{1,0:T(8,128)(2,1)S(1)}, u32[]{:S(2)}, u32[]{:S(2)}) collective-permute-start(bf16[32,1024]{1,0:T(8,128)(2,1)S(1)} %get-tuple-element.101), channel_id=1, source_target_pairs={{0,8},{1,9},{2,10},{3,11},{4,12},{5,13},{6,14},{7,15},{8,0},{9,1},... | collective-permute-start | bytes 196616 | tf_op jit(solution)/shard_map/ppermute | solution.py:358
  174.1 11.0 %collective-permute-start.22 = (bf16[32,1024]{1,0:T(8,128)(2,1)S(1)}, bf16[32,1024]{1,0:T(8,128)(2,1)S(1)}, u32[]{:S(2)}, u32[]{:S(2)}) collective-permute-start(bf16[32,1024]{1,0:T(8,128)(2,1)S(1)} %get-tuple-element.103), channel_id=1, source_target_pairs={{0,16},{1,17},{2,18},{3,19},{4,20},{5,21},{6,22},{7,23},{8,24},{9,... | collective-permute-start | bytes 196616 | tf_op jit(solution)/shard_map/ppermute | solution.py:358
  175.1 9.9 %collective-permute-start.23 = (bf16[32,1024]{1,0:T(8,128)(2,1)S(1)}, bf16[32,1024]{1,0:T(8,128)(2,1)S(1)}, u32[]{:S(2)}, u32[]{:S(2)}) collective-permute-start(bf16[32,1024]{1,0:T(8,128)(2,1)S(1)} %get-tuple-element.102), channel_id=1, source_target_pairs={{0,24},{1,25},{2,26},{3,27},{4,28},{5,29},{6,30},{7,31},{8,16},{9,... | collective-permute-start | bytes 196616 | tf_op jit(solution)/shard_map/ppermute | solution.py:358
  176.8 8.9 %collective-permute-start.14 = (bf16[32,1024]{1,0:T(8,128)(2,1)S(1)}, bf16[32,1024]{1,0:T(8,128)(2,1)S(1)}, u32[]{:S(2)}, u32[]{:S(2)}) collective-permute-start(bf16[32,1024]{1,0:T(8,128)(2,1)S(1)} %get-tuple-element.104), channel_id=1, source_target_pairs={{0,8},{1,9},{2,10},{3,11},{4,12},{5,13},{6,14},{7,15},{8,0},{9,1},... | collective-permute-start | bytes 196616 | tf_op jit(solution)/shard_map/ppermute | solution.py:358
  182.1 5.4 %collective-permute-start.15 = (bf16[32,1024]{1,0:T(8,128)(2,1)S(1)}, bf16[32,1024]{1,0:T(8,128)(2,1)S(1)}, u32[]{:S(2)}, u32[]{:S(2)}) collective-permute-start(bf16[32,1024]{1,0:T(8,128)(2,1)S(1)} %get-tuple-element.106), channel_id=1, source_target_pairs={{0,16},{1,17},{2,18},{3,19},{4,20},{5,21},{6,22},{7,23},{8,24},{9,... | collective-permute-start | bytes 196616 | tf_op jit(solution)/shard_map/ppermute | solution.py:358
  183.6 6.2 %collective-permute-start.16 = (bf16[32,1024]{1,0:T(8,128)(2,1)S(1)}, bf16[32,1024]{1,0:T(8,128)(2,1)S(1)}, u32[]{:S(2)}, u32[]{:S(2)}) collective-permute-start(bf16[32,1024]{1,0:T(8,128)(2,1)S(1)} %get-tuple-element.105), channel_id=1, source_target_pairs={{0,24},{1,25},{2,26},{3,27},{4,28},{5,29},{6,30},{7,31},{8,16},{9,... | collective-permute-start | bytes 196616 | tf_op jit(solution)/shard_map/ppermute | solution.py:358

commit v5 on v4

--- a/solution.py
+++ b/solution.py
@@ -134,11 +134,24 @@
         stiff = stiff_ref[0].astype(F32) + lax.dot_general(
             couple, static_modes, contract, preferred_element_type=F32
         )
-        weighted = (static_modes.astype(F32) * mi_ref[0]).astype(BF16)
-        mass = lax.dot_general(static_modes, weighted, contract, preferred_element_type=F32)
         eye = lax.broadcasted_iota(jnp.int32, (BLK, BLK), 0) == lax.broadcasted_iota(
             jnp.int32, (BLK, BLK), 1
         )
+
+        def own_row(ref):
+            mine = lax.broadcasted_iota(jnp.int32, ref.shape, 0) == sub
+            return jnp.sum(jnp.where(mine, ref[...], 0.0), axis=0, keepdims=True)
+
+        masses, boundary_masses = own_row(mi_ref), own_row(mb_ref)
+        column = jnp.concatenate(
+            [
+                jnp.sum(jnp.where(eye, masses[:, i : i + BLK], 0.0), axis=1, keepdims=True)
+                for i in range(0, interior, BLK)
+            ],
+            axis=0,
+        )
+        weighted = (static_modes.astype(F32) * column).astype(BF16)
+        mass = lax.dot_general(static_modes, weighted, contract, preferred_element_type=F32)
         level = lax.broadcasted_iota(jnp.int32, (EXTRA, BLK), 0)
         for a in range(per_sub):
             block_a = map_ref[sub, a]
@@ -155,7 +168,7 @@
                 if a == b:
                     diagonal = (
                         jnp.sum(jnp.where(eye, mass_block, 0.0), axis=0, keepdims=True)
-                        + mb_ref[0, :, cols]
+                        + boundary_masses[:, cols]
                     )
                     d_ref[0, :, cols] = diagonal
                     high = diagonal.astype(BF16).astype(F32)
@@ -198,8 +211,8 @@
             piece(interior, interior),
             piece(interior, boundary),
             piece(boundary, boundary),
-            piece(interior, 1),
-            piece(1, boundary),
+            pl.BlockSpec((local_subs, interior), lambda s: (0, 0)),
+            pl.BlockSpec((local_subs, boundary), lambda s: (0, 0)),
         ],
         out_specs=[
             piece(boundary, boundary),
@@ -223,8 +236,8 @@
         inv_interior,
         coupling,
         boundary_stiff,
-        mass_interior[:, :, None],
-        mass_boundary[:, None, :],
+        mass_interior,
+        mass_boundary,
     )
 
 
@@ -358,7 +371,7 @@
     return lax.ppermute(value, AXES, [(i, i ^ offset) for i in range(device_count)])
 
 
-def reduce_shares(send, keep, sizes):
+def reduce_shares(send, keep, halving, sizes):
     got = swap(send, 1, sizes.devices)
     depth = sizes.devices // sizes.plane
     shape = (sizes.plane // 2, depth) + keep.shape[1:]
@@ -368,6 +381,14 @@
     for d in range(1, sizes.plane // 2):
         got = swap(summed[d].astype(BF16), 2 * d, sizes.devices)
         total = total + got.astype(F32)
+    if halving:
+        while depth > 1:
+            first = sizes.devices // sizes.plane // depth
+            pairs = total.reshape((depth // 2, 2) + total.shape[1:])
+            got = swap(pairs[:, 1].astype(BF16), first * sizes.plane, sizes.devices)
+            total = pairs[:, 0] + got.astype(F32)
+            depth //= 2
+        return total[0]
     result = total[0]
     for d in range(1, depth):
         got = swap(total[d].astype(BF16), d * sizes.plane, sizes.devices)
@@ -544,10 +565,10 @@
 
     fetched = fetched.reshape(row_count, col_count, sizes.ratio, width, BLK)
     send, keep, qt = project_stiff(block_map, fetched, stiff, dims, sizes.row_blocks)
-    reduced_stiff = reduce_shares(send, keep, sizes)
+    reduced_stiff = reduce_shares(send, keep, True, sizes)
     mixed = mix_mass(qt, mass, diagonal)
     send, keep = project_mass(mixed, qt, dims)
-    reduced_mass = reduce_shares(send, keep, sizes)
+    reduced_mass = reduce_shares(send, keep, False, sizes)
 
     slot = table[:, sizes.ratio]
     ids = jnp.arange(sizes.devices, dtype=jnp.int32)

time: 191 us -> 192 us (level)
  local copies, waits for them, and re-layouts: 15.8 us -> 13.8 us
    broadcast_in_dim x2 -> x0, local copies, waits for them, and re-layouts: 1.94 us -> none  [the longest x1 1.35 us: condense(): mass_interior[:, :, None]]
    ppermute x24 -> x23, starting transfers between devices: 42.2 us -> 43.7 us  [swap(): lax.ppermute(value, AXES, [(i, i ^ offset) for i in range(device_count)])]
    ppermute x24 -> x23, waiting for transfers between devices: 61.2 us -> 62.4 us  [swap(): lax.ppermute(value, AXES, [(i, i ^ offset) for i in range(device_count)])]
    unnamed x33 -> x29, local copies, waits for them, and re-layouts: 10.7 us -> 10.6 us
  transfers between devices with their start and end apart: 26 -> 25, of which waited for: 10 -> 10; matrix products, arithmetic and copies ran while one was open for 9% -> 8% of each run, Pallas kernels for 14% -> 20%
where the time goes in v5:
time: 192 us; the launch traced here: 191 us
  waiting for transfers between devices  67.2 us (35%)
  starting transfers between devices  53.7 us (28%)
  Pallas kernels  50.2 us (26%)
  local copies, waits for them, and re-layouts  13.8 us (7%)
  other arithmetic  5.36 us (3%)
    ppermute x23, waiting for transfers between devices, swap(): lax.ppermute(value, AXES, [(i, i ^ offset) for i in range(device_count)])  62.4 us
    ppermute x23, starting transfers between devices, swap(): lax.ppermute(value, AXES, [(i, i ^ offset) for i in range(device_count)])  43.7 us
    pallas_call x1, Pallas kernels, clear_tiles(): pl.pallas_call(kernel, in_specs=[ANY], out_specs=[ANY, ANY], out_shape=[j...  11.2 us
    unnamed x29, local copies, waits for them, and re-layouts  10.6 us
    all_to_all x2, starting transfers between devices, exchange(): return lax.all_to_all(value, AXES, split_axis=0, concat_axis=0, tiled=True)  10.1 us
    pallas_call x1, Pallas kernels, condense(): pl.pallas_call(kernel, grid=(local_subs,), in_specs=[SMEM, piece(interior...  9.53 us
    pallas_call x1, Pallas kernels, project_stiff(): pl.pallas_call(kernel, grid=(modes // chunk,), in_specs=[SMEM, whole(*fet...  8.5 us
    pallas_call x1, Pallas kernels, project_mass(): pl.pallas_call(kernel, grid=(modes // chunk,), in_specs=[pl.BlockSpec((ch...  6.29 us
  transfers between devices with their start and end apart: 25, of which 10 were waited for; matrix products, arithmetic and copies ran while one was open for 8% of the time, Pallas kernels for 20%

profile of v5, /device:TPU:0, one launch (start us, length us, event | category | flops | bytes accessed | tf_op | source)
XLA Modules:
  0.0 191.1 jit_solution(11107164195880985252)
XLA Ops:
  0.6 1.4 describe.1
  2.0 7.3 %all-to-all-start = ((s32[32,1,128]{2,1,0:T(1,128)}), s32[32,1,128]{2,1,0:T(1,128)S(1)}, u32[]{:S(2)}, u32[]{:S(2)}) async-start(s32[32,1,128]{2,1,0:T(1,128)} %bitcast.52), calls=%async_computation | async-start | bytes 32768 | tf_op jit(solution)/shard_map/all_to_all | solution.py:32
  9.3 2.3 %copy.24 = bf16[32,128,128]{1,2,0:T(8,128)(2,1)} copy(bf16[32,128,128]{2,1,0:T(8,128)(2,1)} %bitcast.47) | data formatting | bytes 2097152 | tf_op jit(solution)/shard_map/reshape | solution.py:551
  11.6 4.8 %all-to-all-done = s32[32,1,128]{2,1,0:T(1,128)S(1)} async-done(((s32[32,1,128]{2,1,0:T(1,128)}), s32[32,1,128]{2,1,0:T(1,128)S(1)}, u32[]{:S(2)}, u32[]{:S(2)}) %all-to-all-start) | async-done | bytes 16416 | tf_op jit(solution)/shard_map/all_to_all | solution.py:32
  16.4 0.6 copy-done.7
  17.0 2.8 %pick_modes.1 = bf16[32,2,128,128]{3,2,1,0:T(8,128)(2,1)} custom-call(s32[32,128]{1,0:T(8,128)} %bitcast.48, bf16[32,128,128]{2,1,0:T(8,128)(2,1)} %bitcast.44), custom_call_target="tpu_custom_call" | custom-call | tf_op jit(solution)/shard_map/pick_modes/pallas_call | solution.py:101
  19.8 2.7 %all-to-all-start.1 = ((bf16[32,2,128,128]{3,2,1,0:T(8,128)(2,1)}), bf16[32,2,128,128]{3,2,1,0:T(8,128)(2,1)S(1)}, u32[]{:S(2)}, u32[]{:S(2)}) async-start(bf16[32,2,128,128]{3,2,1,0:T(8,128)(2,1)} %pick_modes.1), calls=%async_computation.1 | async-start | bytes 4194304 | tf_op jit(solution)/shard_map/all_to_all | solution.py:32
  22.5 9.5 %condense.1 = (bf16[2,512,512]{2,1,0:T(8,128)(2,1)}, bf16[2,512,512]{2,1,0:T(8,128)(2,1)}, f32[2,1,512]{2,1,0:T(1,128)}, bf16[4,264,128]{2,1,0:T(8,128)(2,1)}, b...) custom-call(s32[2,4]{1,0:T(2,128)} %map_ref.5, ...), custom_call_target="tpu_custom_call" | custom-call | tf_op jit(solution)/shard_map/condense/pallas_call | solution.py:206
  32.1 0.2 collective-permute-start
  32.2 1.6 collective-permute-start.1
  33.9 0.1 collective-permute-start.2
  34.0 1.7 collective-permute-start.3
  35.6 0.1 collective-permute-start.4
  35.7 1.7 constant_dynamic-update-slice_fusion.3
  37.4 11.2 %clear_tiles.1 = (bf16[2048,4096]{1,0:T(8,128)(2,1)}, bf16[2048,4096]{1,0:T(8,128)(2,1)}) custom-call(s32[32,128]{1,0:T(8,128)} %bitcast.49), custom_call_target="tpu_custom_call" | custom-call | tf_op jit(solution)/shard_map/clear_tiles/pallas_call | solution.py:421
  48.6 2.6 %collective-permute-start.5 = (bf16[4,264,128]{2,1,0:T(8,128)(2,1)}, bf16[4,264,128]{2,1,0:T(8,128)(2,1)S(1)}, u32[]{:S(2)}, u32[]{:S(2)}) collective-permute-start(bf16[4,264,128]{2,1,0:T(8,128)(2,1)} %get-tuple-element.37), channel_id=1, source_target_pairs={{0,6},{1,7},{2,4},{3,5},{4,2},{5,3},{6,0},{7,1},{8,14},{9,15},{10,... | collective-permute-start | bytes 811016 | tf_op jit(solution)/shard_map/ppermute | solution.py:371
  51.3 1.7 slice_dynamic-update-slice_fusion.6
  53.0 0.1 collective-permute-start.6
  53.0 1.7 slice_dynamic-update-slice_fusion.5
  54.7 2.2 %collective-permute-done.2 = bf16[4,264,128]{2,1,0:T(8,128)(2,1)S(1)} collective-permute-done((bf16[4,264,128]{2,1,0:T(8,128)(2,1)}, bf16[4,264,128]{2,1,0:T(8,128)(2,1)S(1)}, u32[]{:S(2)}, u32[]{:S(2)}) %collective-permute-start.2) | collective-permute-done | bytes 270368 | tf_op jit(solution)/shard_map/ppermute | solution.py:371
  56.9 0.7 slice_dynamic-update-slice_fusion.4
  57.6 0.7 slice_dynamic-update-slice_fusion.3
  58.3 14.4 %collective-permute-done.4 = bf16[4,264,128]{2,1,0:T(8,128)(2,1)S(1)} collective-permute-done((bf16[4,264,128]{2,1,0:T(8,128)(2,1)}, bf16[4,264,128]{2,1,0:T(8,128)(2,1)S(1)}, u32[]{:S(2)}, u32[]{:S(2)}) %collective-permute-start.4) | collective-permute-done | bytes 270368 | tf_op jit(solution)/shard_map/ppermute | solution.py:371
  72.7 0.7 slice_dynamic-update-slice_fusion.2
  73.4 0.7 slice_dynamic-update-slice_fusion.1
  74.1 0.7 slice_dynamic-update-slice_fusion
  74.8 1.3 copy-done
  76.1 8.5 %project_stiff.1 = (bf16[16,32,1024]{2,1,0:T(8,128)(2,1)}, f32[16,32,1024]{2,1,0:T(8,128)}, bf16[1024,1024]{1,0:T(8,128)(2,1)}) custom-call(s32[2,4]{1,0:T(2,128)} %map_ref.5, bf16[8,4,2,128,128]{4,3,2,1,0:T(8,128)(2,1)} %bitcast.43, bf16[2,512,512]{2,1,0:T(8,128)(2,1)} %get-tuple-element.48.m_ref), custom_call_target="tpu_custom_call" | custom-call | tf_op jit(solution)/shard_map/project_stiff/pallas_call | solution.py:303
  84.6 0.1 collective-permute-start.10
  84.8 5.0 %mix_mass.1.y_ref = bf16[1024,1024]{1,0:T(8,128)(2,1)} custom-call(bf16[1024,1024]{1,0:T(8,128)(2,1)} %get-tuple-element.51.t_ref, bf16[2,512,512]{2,1,0:T(8,128)(2,1)} %get-tuple-element.52.m_ref, f32[2,1,512]{2,1,0:T(1,128)} %get-tuple-element.53.d_ref), custom_call_target="tpu_custom_call" | custom-call | tf_op jit(solution)/shard_map/mix_mass/pallas_call | solution.py:335
  89.7 6.3 %project_mass.1 = (bf16[16,32,1024]{2,1,0:T(8,128)(2,1)}, f32[16,32,1024]{2,1,0:T(8,128)}) custom-call(bf16[1024,1024]{1,0:T(8,128)(2,1)} %mix_mass.1.y_ref, bf16[1024,1024]{1,0:T(8,128)(2,1)} %get-tuple-element.51.t_ref), custom_call_target="tpu_custom_call" | custom-call | tf_op jit(solution)/shard_map/project_mass/pallas_call | solution.py:357
  96.0 0.4 collective-permute-start.16
  96.4 0.4 collective-permute-start.7
  96.8 3.2 %collective-permute-start.8 = (bf16[8,264,128]{2,1,0:T(8,128)(2,1)S(1)}, bf16[8,264,128]{2,1,0:T(8,128)(2,1)S(1)}, u32[]{:S(2)}, u32[]{:S(2)}) collective-permute-start(bf16[8,264,128]{2,1,0:T(8,128)(2,1)S(1)} %copy-done.10), channel_id=1, source_target_pairs={{0,16},{1,17},{2,18},{3,19},{4,20},{5,21},{6,22},{7,23},{8,24},{9,... | collective-permute-start | bytes 1622024 | tf_op jit(solution)/shard_map/ppermute | solution.py:371
  100.0 1.3 collective-permute-start.9
  101.3 0.2 slice_reduce_fusion
  101.5 0.2 convert_reduce_fusion
  101.7 0.7 select_reduce_fusion
  102.3 20.2 %collective-permute-done.7.refs_4_ = bf16[8,264,128]{2,1,0:T(8,128)(2,1)S(1)} collective-permute-done((bf16[8,264,128]{2,1,0:T(8,128)(2,1)}, bf16[8,264,128]{2,1,0:T(8,128)(2,1)S(1)}, u32[]{:S(2)}, u32[]{:S(2)}) %collective-permute-start.7) | collective-permute-done | bytes 540704 | tf_op jit(solution)/shard_map/ppermute | solution.py:371
  122.5 14.5 %collective-permute-done.9.refs_6_ = bf16[8,264,128]{2,1,0:T(8,128)(2,1)S(1)} collective-permute-done((bf16[8,264,128]{2,1,0:T(8,128)(2,1)S(1)}, bf16[8,264,128]{2,1,0:T(8,128)(2,1)S(1)}, u32[]{:S(2)}, u32[]{:S(2)}) %collective-permute-start.9) | collective-permute-done | bytes 540704 | tf_op jit(solution)/shard_map/ppermute | solution.py:371
  137.0 0.8 copy-done.6
  137.8 5.5 %place.1 = (bf16[2048,4096]{1,0:T(8,128)(2,1)}, bf16[2048,4096]{1,0:T(8,128)(2,1)}, f32[4,1,128]{2,1,0:T(1,128)}) custom-call(s32[32,128]{1,0:T(8,128)} %bitcast.50, s32[32]{0:T(128)} %get-tuple-element.58.refs_1_, s32[32]{0:T(128)} %get-tuple-element.57.refs_2_, bf16[8,264,128]{2,1,0:T(8,128)(2,1)} %copy-done.3, ...), custom_call_target="tpu_custom_call", output_to_operand_aliasing={{0}: (7, {}), {1}: (8, {})} | custom-call | tf_op jit(solution)/shard_map/place/pallas_call | solution.py:512
  143.4 1.5 add_convert_fusion.5
  144.9 0.5 collective-permute-start.11
  145.4 1.7 collective-permute-start.12
  147.1 1.3 collective-permute-start.13
  148.5 0.3 add_convert_fusion.2
  148.8 0.5 collective-permute-start.17
  149.3 1.7 collective-permute-start.18
  151.0 3.2 %collective-permute-done.11 = bf16[4,32,1024]{2,1,0:T(8,128)(2,1)S(1)} collective-permute-done((bf16[4,32,1024]{2,1,0:T(8,128)(2,1)S(1)}, bf16[4,32,1024]{2,1,0:T(8,128)(2,1)S(1)}, u32[]{:S(2)}, u32[]{:S(2)}) %collective-permute-start.11) | collective-permute-done | bytes 262176 | tf_op jit(solution)/shard_map/ppermute | solution.py:371
  154.2 1.6 collective-permute-start.19
  155.8 4.4 %collective-permute-done.12 = bf16[4,32,1024]{2,1,0:T(8,128)(2,1)S(1)} collective-permute-done((bf16[4,32,1024]{2,1,0:T(8,128)(2,1)S(1)}, bf16[4,32,1024]{2,1,0:T(8,128)(2,1)S(1)}, u32[]{:S(2)}, u32[]{:S(2)}) %collective-permute-start.12) | collective-permute-done | bytes 262176 | tf_op jit(solution)/shard_map/ppermute | solution.py:371
  160.2 1.1 convert_add_fusion.1
  161.4 11.2 %collective-permute-start.14 = (bf16[2,32,1024]{2,1,0:T(8,128)(2,1)S(1)}, bf16[2,32,1024]{2,1,0:T(8,128)(2,1)S(1)}, u32[]{:S(2)}, u32[]{:S(2)}) collective-permute-start(bf16[2,32,1024]{2,1,0:T(8,128)(2,1)S(1)} %fusion.2), channel_id=1, source_target_pairs={{0,8},{1,9},{2,10},{3,11},{4,12},{5,13},{6,14},{7,15},{8,0},{9,1},... | collective-permute-start | bytes 393224 | tf_op jit(solution)/shard_map/ppermute | solution.py:371
  172.5 0.2 fusion.11
  172.8 8.1 %collective-permute-start.20 = (bf16[32,1024]{1,0:T(8,128)(2,1)S(1)}, bf16[32,1024]{1,0:T(8,128)(2,1)S(1)}, u32[]{:S(2)}, u32[]{:S(2)}) collective-permute-start(bf16[32,1024]{1,0:T(8,128)(2,1)S(1)} %get-tuple-element.99), channel_id=1, source_target_pairs={{0,8},{1,9},{2,10},{3,11},{4,12},{5,13},{6,14},{7,15},{8,0},{9,1},... | collective-permute-start | bytes 196616 | tf_op jit(solution)/shard_map/ppermute | solution.py:371
  180.8 1.8 collective-permute-start.21
  182.6 1.4 collective-permute-start.22
  184.1 2.1 %collective-permute-start.15 = (bf16[1,32,1024]{2,1,0:T(8,128)(2,1)S(1)}, bf16[1,32,1024]{2,1,0:T(8,128)(2,1)S(1)}, u32[]{:S(2)}, u32[]{:S(2)}) collective-permute-start(bf16[1,32,1024]{2,1,0:T(8,128)(2,1)S(1)} %fusion.8), channel_id=1, source_target_pairs={{0,16},{1,17},{2,18},{3,19},{4,20},{5,21},{6,22},{7,23},{8,24},{9,... | collective-permute-start | bytes 196616 | tf_op jit(solution)/shard_map/ppermute | solution.py:371
  186.2 1.4 collective-permute-done.21
  187.6 1.2 collective-permute-done.22
  188.8 0.7 fusion.5
  189.5 0.9 collective-permute-done.15
  190.4 0.7 fusion.7
  (38 shorter events, 0.1 us)
Async XLA Ops:
  2.0 14.4 %all-to-all-start = ((s32[32,1,128]{2,1,0:T(1,128)}), s32[32,1,128]{2,1,0:T(1,128)S(1)}, u32[]{:S(2)}, u32[]{:S(2)}) async-start(s32[32,1,128]{2,1,0:T(1,128)} %bitcast.52), calls=%async_computation | async-start | bytes 32768 | tf_op jit(solution)/shard_map/all_to_all | solution.py:32
  16.4 0.6 copy-start.7
  19.8 55.0 %all-to-all-start.1 = ((bf16[32,2,128,128]{3,2,1,0:T(8,128)(2,1)}), bf16[32,2,128,128]{3,2,1,0:T(8,128)(2,1)S(1)}, u32[]{:S(2)}, u32[]{:S(2)}) async-start(bf16[32,2,128,128]{3,2,1,0:T(8,128)(2,1)} %pick_modes.1), calls=%async_computation.1 | async-start | bytes 4194304 | tf_op jit(solution)/shard_map/all_to_all | solution.py:32
  32.1 16.6 %collective-permute-start = (bf16[4,264,128]{2,1,0:T(8,128)(2,1)}, bf16[4,264,128]{2,1,0:T(8,128)(2,1)}, u32[]{:S(2)}, u32[]{:S(2)}) collective-permute-start(bf16[4,264,128]{2,1,0:T(8,128)(2,1)} %get-tuple-element.32), channel_id=1, source_target_pairs={{0,1},{1,0},{2,3},{3,2},{4,5},{5,4},{6,7},{7,6},{8,9},{9,8},{10,11... | collective-permute-start | bytes 811016 | tf_op jit(solution)/shard_map/ppermute | solution.py:371
  32.2 20.7 %collective-permute-start.1 = (bf16[4,264,128]{2,1,0:T(8,128)(2,1)}, bf16[4,264,128]{2,1,0:T(8,128)(2,1)}, u32[]{:S(2)}, u32[]{:S(2)}) collective-permute-start(bf16[4,264,128]{2,1,0:T(8,128)(2,1)} %get-tuple-element.33), channel_id=1, source_target_pairs={{0,2},{1,3},{2,0},{3,1},{4,6},{5,7},{6,4},{7,5},{8,10},{9,11},{10,... | collective-permute-start | bytes 811016 | tf_op jit(solution)/shard_map/ppermute | solution.py:371
  33.9 23.0 %collective-permute-start.2 = (bf16[4,264,128]{2,1,0:T(8,128)(2,1)}, bf16[4,264,128]{2,1,0:T(8,128)(2,1)S(1)}, u32[]{:S(2)}, u32[]{:S(2)}) collective-permute-start(bf16[4,264,128]{2,1,0:T(8,128)(2,1)} %get-tuple-element.34), channel_id=1, source_target_pairs={{0,3},{1,2},{2,1},{3,0},{4,7},{5,6},{6,5},{7,4},{8,11},{9,10},{10,... | collective-permute-start | bytes 811016 | tf_op jit(solution)/shard_map/ppermute | solution.py:371
  34.0 23.6 %collective-permute-start.3 = (bf16[4,264,128]{2,1,0:T(8,128)(2,1)}, bf16[4,264,128]{2,1,0:T(8,128)(2,1)S(1)}, u32[]{:S(2)}, u32[]{:S(2)}) collective-permute-start(bf16[4,264,128]{2,1,0:T(8,128)(2,1)} %get-tuple-element.35), channel_id=1, source_target_pairs={{0,4},{1,5},{2,6},{3,7},{4,0},{5,1},{6,2},{7,3},{8,12},{9,13},{10,... | collective-permute-start | bytes 811016 | tf_op jit(solution)/shard_map/ppermute | solution.py:371
  35.6 37.0 %collective-permute-start.4 = (bf16[4,264,128]{2,1,0:T(8,128)(2,1)}, bf16[4,264,128]{2,1,0:T(8,128)(2,1)S(1)}, u32[]{:S(2)}, u32[]{:S(2)}) collective-permute-start(bf16[4,264,128]{2,1,0:T(8,128)(2,1)} %get-tuple-element.36), channel_id=1, source_target_pairs={{0,5},{1,4},{2,7},{3,6},{4,1},{5,0},{6,3},{7,2},{8,13},{9,12},{10,... | collective-permute-start | bytes 811016 | tf_op jit(solution)/shard_map/ppermute | solution.py:371
  48.6 24.7 %collective-permute-start.5 = (bf16[4,264,128]{2,1,0:T(8,128)(2,1)}, bf16[4,264,128]{2,1,0:T(8,128)(2,1)S(1)}, u32[]{:S(2)}, u32[]{:S(2)}) collective-permute-start(bf16[4,264,128]{2,1,0:T(8,128)(2,1)} %get-tuple-element.37), channel_id=1, source_target_pairs={{0,6},{1,7},{2,4},{3,5},{4,2},{5,3},{6,0},{7,1},{8,14},{9,15},{10,... | collective-permute-start | bytes 811016 | tf_op jit(solution)/shard_map/ppermute | solution.py:371
  53.0 21.1 %collective-permute-start.6 = (bf16[4,264,128]{2,1,0:T(8,128)(2,1)}, bf16[4,264,128]{2,1,0:T(8,128)(2,1)S(1)}, u32[]{:S(2)}, u32[]{:S(2)}) collective-permute-start(bf16[4,264,128]{2,1,0:T(8,128)(2,1)} %get-tuple-element.38), channel_id=1, source_target_pairs={{0,7},{1,6},{2,5},{3,4},{4,3},{5,2},{6,1},{7,0},{8,15},{9,14},{10,... | collective-permute-start | bytes 811016 | tf_op jit(solution)/shard_map/ppermute | solution.py:371
  74.8 21.3 %copy-start.3 = (bf16[8,264,128]{2,1,0:T(8,128)(2,1)}, bf16[8,264,128]{2,1,0:T(8,128)(2,1)S(1)}, u32[]{:S(2)}) copy-start(bf16[8,264,128]{2,1,0:T(8,128)(2,1)S(1)} %get-tuple-element.70.refs_3_) | copy-start | bytes 1622020
  74.8 1.3 copy-start
  84.6 58.8 %collective-permute-start.10 = (bf16[16,32,1024]{2,1,0:T(8,128)(2,1)}, bf16[16,32,1024]{2,1,0:T(8,128)(2,1)}, u32[]{:S(2)}, u32[]{:S(2)}) collective-permute-start(bf16[16,32,1024]{2,1,0:T(8,128)(2,1)} %get-tuple-element.50), channel_id=1, source_target_pairs={{0,1},{1,0},{2,3},{3,2},{4,5},{5,4},{6,7},{7,6},{8,9},{9,8},{10,11... | collective-permute-start | bytes 3145736 | tf_op jit(solution)/shard_map/ppermute | solution.py:371
  89.7 7.1 %copy-start.10 = (bf16[8,264,128]{2,1,0:T(8,128)(2,1)S(1)}, bf16[8,264,128]{2,1,0:T(8,128)(2,1)}, u32[]{:S(2)}) copy-start(bf16[8,264,128]{2,1,0:T(8,128)(2,1)} %get-tuple-element.41) | copy-start | bytes 1622020
  89.7 10.2 %copy-start.9 = (bf16[8,264,128]{2,1,0:T(8,128)(2,1)S(1)}, bf16[8,264,128]{2,1,0:T(8,128)(2,1)}, u32[]{:S(2)}) copy-start(bf16[8,264,128]{2,1,0:T(8,128)(2,1)} %get-tuple-element.42) | copy-start | bytes 1622020
  89.7 11.6 %copy-start.8 = (s32[32,1,128]{2,1,0:T(1,128)S(1)}, s32[32,1,128]{2,1,0:T(1,128)}, u32[]{:S(2)}) copy-start(s32[32,1,128]{2,1,0:T(1,128)} %copy-done.7) | copy-start | bytes 49156
  96.0 52.4 %collective-permute-start.16 = (bf16[16,32,1024]{2,1,0:T(8,128)(2,1)}, bf16[16,32,1024]{2,1,0:T(8,128)(2,1)S(1)}, u32[]{:S(2)}, u32[]{:S(2)}) collective-permute-start(bf16[16,32,1024]{2,1,0:T(8,128)(2,1)} %get-tuple-element.55), channel_id=1, source_target_pairs={{0,1},{1,0},{2,3},{3,2},{4,5},{5,4},{6,7},{7,6},{8,9},{9,8},{10,11... | collective-permute-start | bytes 3145736 | tf_op jit(solution)/shard_map/ppermute | solution.py:371
  96.4 26.1 %collective-permute-start.7 = (bf16[8,264,128]{2,1,0:T(8,128)(2,1)}, bf16[8,264,128]{2,1,0:T(8,128)(2,1)S(1)}, u32[]{:S(2)}, u32[]{:S(2)}) collective-permute-start(bf16[8,264,128]{2,1,0:T(8,128)(2,1)} %get-tuple-element.69), channel_id=1, source_target_pairs={{0,8},{1,9},{2,10},{3,11},{4,12},{5,13},{6,14},{7,15},{8,0},{9,1},... | collective-permute-start | bytes 1622024 | tf_op jit(solution)/shard_map/ppermute | solution.py:371
  96.8 25.7 %collective-permute-start.8 = (bf16[8,264,128]{2,1,0:T(8,128)(2,1)S(1)}, bf16[8,264,128]{2,1,0:T(8,128)(2,1)S(1)}, u32[]{:S(2)}, u32[]{:S(2)}) collective-permute-start(bf16[8,264,128]{2,1,0:T(8,128)(2,1)S(1)} %copy-done.10), channel_id=1, source_target_pairs={{0,16},{1,17},{2,18},{3,19},{4,20},{5,21},{6,22},{7,23},{8,24},{9,... | collective-permute-start | bytes 1622024 | tf_op jit(solution)/shard_map/ppermute | solution.py:371
  100.0 37.0 %collective-permute-start.9 = (bf16[8,264,128]{2,1,0:T(8,128)(2,1)S(1)}, bf16[8,264,128]{2,1,0:T(8,128)(2,1)S(1)}, u32[]{:S(2)}, u32[]{:S(2)}) collective-permute-start(bf16[8,264,128]{2,1,0:T(8,128)(2,1)S(1)} %copy-done.9), channel_id=1, source_target_pairs={{0,24},{1,25},{2,26},{3,27},{4,28},{5,29},{6,30},{7,31},{8,16},{9,... | collective-permute-start | bytes 1622024 | tf_op jit(solution)/shard_map/ppermute | solution.py:371
  122.5 14.5 %copy-start.4 = (bf16[8,264,128]{2,1,0:T(8,128)(2,1)}, bf16[8,264,128]{2,1,0:T(8,128)(2,1)S(1)}, u32[]{:S(2)}) copy-start(bf16[8,264,128]{2,1,0:T(8,128)(2,1)S(1)} %collective-permute-done.7.refs_4_) | copy-start | bytes 1622020
  122.5 14.5 %copy-start.5 = (bf16[8,264,128]{2,1,0:T(8,128)(2,1)}, bf16[8,264,128]{2,1,0:T(8,128)(2,1)S(1)}, u32[]{:S(2)}) copy-start(bf16[8,264,128]{2,1,0:T(8,128)(2,1)S(1)} %collective-permute-done.8.refs_5_) | copy-start | bytes 1622020
  137.0 0.8 copy-start.6
  137.8 5.6 %copy-start.2 = (f32[16,32,1024]{2,1,0:T(8,128)S(1)}, f32[16,32,1024]{2,1,0:T(8,128)}, u32[]{:S(2)}) copy-start(f32[16,32,1024]{2,1,0:T(8,128)} %get-tuple-element.49) | copy-start | bytes 6291460
  143.4 5.1 %copy-start.1 = (f32[16,32,1024]{2,1,0:T(8,128)S(1)}, f32[16,32,1024]{2,1,0:T(8,128)}, u32[]{:S(2)}) copy-start(f32[16,32,1024]{2,1,0:T(8,128)} %get-tuple-element.54) | copy-start | bytes 6291460
  144.9 9.2 %collective-permute-start.11 = (bf16[4,32,1024]{2,1,0:T(8,128)(2,1)S(1)}, bf16[4,32,1024]{2,1,0:T(8,128)(2,1)S(1)}, u32[]{:S(2)}, u32[]{:S(2)}) collective-permute-start(bf16[4,32,1024]{2,1,0:T(8,128)(2,1)S(1)} %get-tuple-element.64), channel_id=1, source_target_pairs={{0,2},{1,3},{2,0},{3,1},{4,6},{5,7},{6,4},{7,5},{8,10},{9,11},{10,... | collective-permute-start | bytes 786440 | tf_op jit(solution)/shard_map/ppermute | solution.py:371
  145.4 14.8 %collective-permute-start.12 = (bf16[4,32,1024]{2,1,0:T(8,128)(2,1)S(1)}, bf16[4,32,1024]{2,1,0:T(8,128)(2,1)S(1)}, u32[]{:S(2)}, u32[]{:S(2)}) collective-permute-start(bf16[4,32,1024]{2,1,0:T(8,128)(2,1)S(1)} %get-tuple-element.66), channel_id=1, source_target_pairs={{0,4},{1,5},{2,6},{3,7},{4,0},{5,1},{6,2},{7,3},{8,12},{9,13},{10,... | collective-permute-start | bytes 786440 | tf_op jit(solution)/shard_map/ppermute | solution.py:371
  147.1 13.1 %collective-permute-start.13 = (bf16[4,32,1024]{2,1,0:T(8,128)(2,1)S(1)}, bf16[4,32,1024]{2,1,0:T(8,128)(2,1)S(1)}, u32[]{:S(2)}, u32[]{:S(2)}) collective-permute-start(bf16[4,32,1024]{2,1,0:T(8,128)(2,1)S(1)} %get-tuple-element.65), channel_id=1, source_target_pairs={{0,6},{1,7},{2,4},{3,5},{4,2},{5,3},{6,0},{7,1},{8,14},{9,15},{10,... | collective-permute-start | bytes 786440 | tf_op jit(solution)/shard_map/ppermute | solution.py:371
  148.8 23.8 %collective-permute-start.17 = (bf16[4,32,1024]{2,1,0:T(8,128)(2,1)S(1)}, bf16[4,32,1024]{2,1,0:T(8,128)(2,1)S(1)}, u32[]{:S(2)}, u32[]{:S(2)}) collective-permute-start(bf16[4,32,1024]{2,1,0:T(8,128)(2,1)S(1)} %get-tuple-element.61), channel_id=1, source_target_pairs={{0,2},{1,3},{2,0},{3,1},{4,6},{5,7},{6,4},{7,5},{8,10},{9,11},{10,... | collective-permute-start | bytes 786440 | tf_op jit(solution)/shard_map/ppermute | solution.py:371
  149.3 23.3 %collective-permute-start.18 = (bf16[4,32,1024]{2,1,0:T(8,128)(2,1)S(1)}, bf16[4,32,1024]{2,1,0:T(8,128)(2,1)S(1)}, u32[]{:S(2)}, u32[]{:S(2)}) collective-permute-start(bf16[4,32,1024]{2,1,0:T(8,128)(2,1)S(1)} %get-tuple-element.63), channel_id=1, source_target_pairs={{0,4},{1,5},{2,6},{3,7},{4,0},{5,1},{6,2},{7,3},{8,12},{9,13},{10,... | collective-permute-start | bytes 786440 | tf_op jit(solution)/shard_map/ppermute | solution.py:371
  154.2 18.4 %collective-permute-start.19 = (bf16[4,32,1024]{2,1,0:T(8,128)(2,1)S(1)}, bf16[4,32,1024]{2,1,0:T(8,128)(2,1)S(1)}, u32[]{:S(2)}, u32[]{:S(2)}) collective-permute-start(bf16[4,32,1024]{2,1,0:T(8,128)(2,1)S(1)} %get-tuple-element.62), channel_id=1, source_target_pairs={{0,6},{1,7},{2,4},{3,5},{4,2},{5,3},{6,0},{7,1},{8,14},{9,15},{10,... | collective-permute-start | bytes 786440 | tf_op jit(solution)/shard_map/ppermute | solution.py:371
  161.4 22.6 %collective-permute-start.14 = (bf16[2,32,1024]{2,1,0:T(8,128)(2,1)S(1)}, bf16[2,32,1024]{2,1,0:T(8,128)(2,1)S(1)}, u32[]{:S(2)}, u32[]{:S(2)}) collective-permute-start(bf16[2,32,1024]{2,1,0:T(8,128)(2,1)S(1)} %fusion.2), channel_id=1, source_target_pairs={{0,8},{1,9},{2,10},{3,11},{4,12},{5,13},{6,14},{7,15},{8,0},{9,1},... | collective-permute-start | bytes 393224 | tf_op jit(solution)/shard_map/ppermute | solution.py:371
  172.8 13.4 %collective-permute-start.20 = (bf16[32,1024]{1,0:T(8,128)(2,1)S(1)}, bf16[32,1024]{1,0:T(8,128)(2,1)S(1)}, u32[]{:S(2)}, u32[]{:S(2)}) collective-permute-start(bf16[32,1024]{1,0:T(8,128)(2,1)S(1)} %get-tuple-element.99), channel_id=1, source_target_pairs={{0,8},{1,9},{2,10},{3,11},{4,12},{5,13},{6,14},{7,15},{8,0},{9,1},... | collective-permute-start | bytes 196616 | tf_op jit(solution)/shard_map/ppermute | solution.py:371
  180.8 6.8 %collective-permute-start.21 = (bf16[32,1024]{1,0:T(8,128)(2,1)S(1)}, bf16[32,1024]{1,0:T(8,128)(2,1)S(1)}, u32[]{:S(2)}, u32[]{:S(2)}) collective-permute-start(bf16[32,1024]{1,0:T(8,128)(2,1)S(1)} %get-tuple-element.101), channel_id=1, source_target_pairs={{0,16},{1,17},{2,18},{3,19},{4,20},{5,21},{6,22},{7,23},{8,24},{9,... | collective-permute-start | bytes 196616 | tf_op jit(solution)/shard_map/ppermute | solution.py:371
  182.6 6.2 %collective-permute-start.22 = (bf16[32,1024]{1,0:T(8,128)(2,1)S(1)}, bf16[32,1024]{1,0:T(8,128)(2,1)S(1)}, u32[]{:S(2)}, u32[]{:S(2)}) collective-permute-start(bf16[32,1024]{1,0:T(8,128)(2,1)S(1)} %get-tuple-element.100), channel_id=1, source_target_pairs={{0,24},{1,25},{2,26},{3,27},{4,28},{5,29},{6,30},{7,31},{8,16},{9,... | collective-permute-start | bytes 196616 | tf_op jit(solution)/shard_map/ppermute | solution.py:371
  184.1 6.3 %collective-permute-start.15 = (bf16[1,32,1024]{2,1,0:T(8,128)(2,1)S(1)}, bf16[1,32,1024]{2,1,0:T(8,128)(2,1)S(1)}, u32[]{:S(2)}, u32[]{:S(2)}) collective-permute-start(bf16[1,32,1024]{2,1,0:T(8,128)(2,1)S(1)} %fusion.8), channel_id=1, source_target_pairs={{0,16},{1,17},{2,18},{3,19},{4,20},{5,21},{6,22},{7,23},{8,24},{9,... | collective-permute-start | bytes 196616 | tf_op jit(solution)/shard_map/ppermute | solution.py:371

commit v6 on v5

--- a/solution.py
+++ b/solution.py
@@ -241,14 +241,20 @@
     )
 
 
-def cut_shares(out, step, send_ref, keep_ref, dims):
-    _, y_size, x_size = dims
-    z_size = dims[0]
-    share = send_ref.shape[1]
+def cut_shares(out, step, steps, held, results, sem, dims):
+    z_size, y_size, x_size = dims
+    groups, share, _ = results[0].shape
     pairs = out.shape[0] // (2 * share)
     row, col = lax.axis_index("row"), lax.axis_index("col")
     my_z, my_y = quotient(row, y_size), remainder(row, y_size)
     my_x, mine = quotient(col, 2), remainder(col, 2) == 0
+
+    def copies(slot):
+        return [
+            pltpu.make_async_copy(ref.at[slot], result.at[slot], sem.at[i, slot])
+            for i, (ref, result) in enumerate(zip(held, results))
+        ]
+
     for i in range(pairs):
         group = step * pairs + i
         x = remainder(group, x_size)
@@ -257,8 +263,16 @@
         slot = ((y ^ my_y) * x_size + (x ^ my_x)) * z_size + (z ^ my_z)
         even = out[2 * i * share : (2 * i + 1) * share]
         odd = out[(2 * i + 1) * share : (2 * i + 2) * share]
-        keep_ref[slot] = jnp.where(mine, even, odd)
-        send_ref[slot] = jnp.where(mine, odd, even).astype(BF16)
+        held[0][slot] = jnp.where(mine, odd, even).astype(BF16)
+        held[1][slot] = jnp.where(mine, even, odd)
+        for copy in copies(slot):
+            copy.start()
+
+    @pl.when(step == steps - 1)
+    def _():
+        for slot in range(groups):
+            for copy in copies(slot):
+                copy.wait()
 
 
 def whole(*shape):
@@ -275,8 +289,11 @@
     share = modes // (2 * groups)
     chunk = modes // 2
 
-    def kernel(map_ref, in_ref, m_ref, send_ref, keep_ref, t_ref, y_ref):
+    def kernel(
+        map_ref, in_ref, m_ref, send_ref, keep_ref, qt_ref, t_ref, y_ref, s_ref, k_ref, t_sem, sem
+    ):
         step = pl.program_id(0)
+        copy_out = pltpu.make_async_copy(t_ref, qt_ref, t_sem.at[0])
 
         @pl.when(step == 0)
         def _():
@@ -288,6 +305,7 @@
                     k = (s * per_sub + a) * BLK
                     for r in range(row_count):
                         t_ref[r * width : (r + 1) * width, k : k + BLK] = in_ref[r, c, h]
+            copy_out.start()
 
         rows = pl.ds(pl.multiple_of(step * chunk, chunk), chunk)
         for s in range(local_subs):
@@ -298,23 +316,30 @@
         out = lax.dot_general(
             y_ref[...], t_ref[...], (((1,), (1,)), ((), ())), preferred_element_type=F32
         )
-        cut_shares(out, step, send_ref, keep_ref, dims)
-
-    return pl.pallas_call(
-        kernel,
-        grid=(modes // chunk,),
+        cut_shares(out, step, 2, (s_ref, k_ref), (send_ref, keep_ref), sem, dims)
+
+        @pl.when(step == 1)
+        def _():
+            copy_out.wait()
+
+    return pl.pallas_call(
+        kernel,
+        grid=(2,),
         in_specs=[SMEM, whole(*fetched.shape), whole(local_subs, boundary, boundary)],
-        out_specs=[
-            whole(groups, share, modes),
-            whole(groups, share, modes),
-            whole(modes, depth),
-        ],
+        out_specs=[ANY, ANY, ANY],
         out_shape=[
             jax.ShapeDtypeStruct((groups, share, modes), BF16),
             jax.ShapeDtypeStruct((groups, share, modes), F32),
             jax.ShapeDtypeStruct((modes, depth), BF16),
         ],
-        scratch_shapes=[pltpu.VMEM((chunk, depth), BF16)],
+        scratch_shapes=[
+            pltpu.VMEM((modes, depth), BF16),
+            pltpu.VMEM((chunk, depth), BF16),
+            pltpu.VMEM((groups, share, modes), BF16),
+            pltpu.VMEM((groups, share, modes), F32),
+            pltpu.SemaphoreType.DMA((1,)),
+            pltpu.SemaphoreType.DMA((2, groups)),
+        ],
         name="project_stiff",
     )(block_map, fetched, matrix)
 
@@ -348,21 +373,26 @@
     share = modes // (2 * groups)
     chunk = modes // 2
 
-    def kernel(y_ref, t_ref, send_ref, keep_ref):
+    def kernel(y_ref, t_ref, send_ref, keep_ref, s_ref, k_ref, sem):
         out = lax.dot_general(
             y_ref[...], t_ref[...], (((1,), (1,)), ((), ())), preferred_element_type=F32
         )
-        cut_shares(out, pl.program_id(0), send_ref, keep_ref, dims)
-
-    return pl.pallas_call(
-        kernel,
-        grid=(modes // chunk,),
+        cut_shares(out, pl.program_id(0), 2, (s_ref, k_ref), (send_ref, keep_ref), sem, dims)
+
+    return pl.pallas_call(
+        kernel,
+        grid=(2,),
         in_specs=[pl.BlockSpec((chunk, depth), lambda i: (i, 0)), whole(modes, depth)],
-        out_specs=[whole(groups, share, modes), whole(groups, share, modes)],
+        out_specs=[ANY, ANY],
         out_shape=[
             jax.ShapeDtypeStruct((groups, share, modes), BF16),
             jax.ShapeDtypeStruct((groups, share, modes), F32),
         ],
+        scratch_shapes=[
+            pltpu.VMEM((groups, share, modes), BF16),
+            pltpu.VMEM((groups, share, modes), F32),
+            pltpu.SemaphoreType.DMA((2, groups)),
+        ],
         name="project_mass",
     )(mixed, qt)
 
@@ -371,7 +401,7 @@
     return lax.ppermute(value, AXES, [(i, i ^ offset) for i in range(device_count)])
 
 
-def reduce_shares(send, keep, halving, sizes):
+def reduce_shares(send, keep, sizes):
     got = swap(send, 1, sizes.devices)
     depth = sizes.devices // sizes.plane
     shape = (sizes.plane // 2, depth) + keep.shape[1:]
@@ -381,14 +411,6 @@
     for d in range(1, sizes.plane // 2):
         got = swap(summed[d].astype(BF16), 2 * d, sizes.devices)
         total = total + got.astype(F32)
-    if halving:
-        while depth > 1:
-            first = sizes.devices // sizes.plane // depth
-            pairs = total.reshape((depth // 2, 2) + total.shape[1:])
-            got = swap(pairs[:, 1].astype(BF16), first * sizes.plane, sizes.devices)
-            total = pairs[:, 0] + got.astype(F32)
-            depth //= 2
-        return total[0]
     result = total[0]
     for d in range(1, depth):
         got = swap(total[d].astype(BF16), d * sizes.plane, sizes.devices)
@@ -565,10 +587,10 @@
 
     fetched = fetched.reshape(row_count, col_count, sizes.ratio, width, BLK)
     send, keep, qt = project_stiff(block_map, fetched, stiff, dims, sizes.row_blocks)
-    reduced_stiff = reduce_shares(send, keep, True, sizes)
+    reduced_stiff = reduce_shares(send, keep, sizes)
     mixed = mix_mass(qt, mass, diagonal)
     send, keep = project_mass(mixed, qt, dims)
-    reduced_mass = reduce_shares(send, keep, False, sizes)
+    reduced_mass = reduce_shares(send, keep, sizes)
 
     slot = table[:, sizes.ratio]
     ids = jnp.arange(sizes.devices, dtype=jnp.int32)

time: 192 us -> 189 us (0.984)
  starting transfers between devices: 53.7 us -> 51.7 us
    ppermute x23 -> x24, starting transfers between devices: 43.7 us -> 41.7 us  [swap(): lax.ppermute(value, AXES, [(i, i ^ offset) for i in range(device_count)])]
    ppermute x23 -> x24, waiting for transfers between devices: 62.4 us -> 62.8 us  [swap(): lax.ppermute(value, AXES, [(i, i ^ offset) for i in range(device_count)])]
  transfers between devices with their start and end apart: 25 -> 26, of which waited for: 10 -> 9; matrix products, arithmetic and copies ran while one was open for 8% -> 8% of each run, Pallas kernels for 20% -> 14%
where the time goes in v6:
time: 189 us; the launch traced here: 188 us
  waiting for transfers between devices  67.6 us (36%)
  starting transfers between devices  51.7 us (27%)
  Pallas kernels  48.8 us (26%)
  local copies, waits for them, and re-layouts  13.8 us (7%)
  other arithmetic  5.37 us (3%)
    ppermute x24, waiting for transfers between devices, swap(): lax.ppermute(value, AXES, [(i, i ^ offset) for i in range(device_count)])  62.8 us
    ppermute x24, starting transfers between devices, swap(): lax.ppermute(value, AXES, [(i, i ^ offset) for i in range(device_count)])  41.7 us
    pallas_call x1, Pallas kernels, clear_tiles(): pl.pallas_call(kernel, in_specs=[ANY], out_specs=[ANY, ANY], out_shape=[j...  11.2 us
    unnamed x29, local copies, waits for them, and re-layouts  10.7 us
    all_to_all x2, starting transfers between devices, exchange(): return lax.all_to_all(value, AXES, split_axis=0, concat_axis=0, tiled=True)  10.1 us
    pallas_call x1, Pallas kernels, condense(): pl.pallas_call(kernel, grid=(local_subs,), in_specs=[SMEM, piece(interior...  9.5 us
    pallas_call x1, Pallas kernels, project_stiff(): pl.pallas_call(kernel, grid=(2,), in_specs=[SMEM, whole(*fetched.shape),...  7.44 us
    pallas_call x1, Pallas kernels, project_mass(): pl.pallas_call(kernel, grid=(2,), in_specs=[pl.BlockSpec((chunk, depth),...  6.01 us
  transfers between devices with their start and end apart: 26, of which 9 were waited for; matrix products, arithmetic and copies ran while one was open for 8% of the time, Pallas kernels for 14%

profile of v6, /device:TPU:0, one launch (start us, length us, event | category | flops | bytes accessed | tf_op | source)
XLA Modules:
  0.0 188.2 jit_solution(851091744355747124)
XLA Ops:
  0.6 1.4 describe.1
  2.0 7.3 %all-to-all-start = ((s32[32,1,128]{2,1,0:T(1,128)}), s32[32,1,128]{2,1,0:T(1,128)S(1)}, u32[]{:S(2)}, u32[]{:S(2)}) async-start(s32[32,1,128]{2,1,0:T(1,128)} %bitcast.43), calls=%async_computation | async-start | bytes 32768 | tf_op jit(solution)/shard_map/all_to_all | solution.py:32
  9.3 2.3 %copy.18 = bf16[32,128,128]{1,2,0:T(8,128)(2,1)} copy(bf16[32,128,128]{2,1,0:T(8,128)(2,1)} %bitcast.38) | data formatting | bytes 2097152 | tf_op jit(solution)/shard_map/reshape | solution.py:573
  11.6 4.8 %all-to-all-done = s32[32,1,128]{2,1,0:T(1,128)S(1)} async-done(((s32[32,1,128]{2,1,0:T(1,128)}), s32[32,1,128]{2,1,0:T(1,128)S(1)}, u32[]{:S(2)}, u32[]{:S(2)}) %all-to-all-start) | async-done | bytes 16416 | tf_op jit(solution)/shard_map/all_to_all | solution.py:32
  16.4 0.6 copy-done.7
  17.0 2.8 %pick_modes.1 = bf16[32,2,128,128]{3,2,1,0:T(8,128)(2,1)} custom-call(s32[32,128]{1,0:T(8,128)} %bitcast.39, bf16[32,128,128]{2,1,0:T(8,128)(2,1)} %bitcast.37), custom_call_target="tpu_custom_call" | custom-call | tf_op jit(solution)/shard_map/pick_modes/pallas_call | solution.py:101
  19.8 2.7 %all-to-all-start.1 = ((bf16[32,2,128,128]{3,2,1,0:T(8,128)(2,1)}), bf16[32,2,128,128]{3,2,1,0:T(8,128)(2,1)S(1)}, u32[]{:S(2)}, u32[]{:S(2)}) async-start(bf16[32,2,128,128]{3,2,1,0:T(8,128)(2,1)} %pick_modes.1), calls=%async_computation.1 | async-start | bytes 4194304 | tf_op jit(solution)/shard_map/all_to_all | solution.py:32
  22.5 9.5 %condense.1 = (bf16[2,512,512]{2,1,0:T(8,128)(2,1)}, bf16[2,512,512]{2,1,0:T(8,128)(2,1)}, f32[2,1,512]{2,1,0:T(1,128)}, bf16[4,264,128]{2,1,0:T(8,128)(2,1)}, b...) custom-call(s32[2,4]{1,0:T(2,128)} %map_ref.5, ...), custom_call_target="tpu_custom_call" | custom-call | tf_op jit(solution)/shard_map/condense/pallas_call | solution.py:206
  32.0 0.2 collective-permute-start
  32.2 1.6 collective-permute-start.1
  33.8 0.1 collective-permute-start.2
  34.0 1.7 collective-permute-start.3
  35.6 0.1 collective-permute-start.4
  35.7 1.7 constant_dynamic-update-slice_fusion.3
  37.4 11.2 %clear_tiles.1 = (bf16[2048,4096]{1,0:T(8,128)(2,1)}, bf16[2048,4096]{1,0:T(8,128)(2,1)}) custom-call(s32[32,128]{1,0:T(8,128)} %bitcast.40), custom_call_target="tpu_custom_call" | custom-call | tf_op jit(solution)/shard_map/clear_tiles/pallas_call | solution.py:443
  48.6 2.7 %collective-permute-start.5 = (bf16[4,264,128]{2,1,0:T(8,128)(2,1)}, bf16[4,264,128]{2,1,0:T(8,128)(2,1)S(1)}, u32[]{:S(2)}, u32[]{:S(2)}) collective-permute-start(bf16[4,264,128]{2,1,0:T(8,128)(2,1)} %get-tuple-element.37), channel_id=1, source_target_pairs={{0,6},{1,7},{2,4},{3,5},{4,2},{5,3},{6,0},{7,1},{8,14},{9,15},{10,... | collective-permute-start | bytes 811016 | tf_op jit(solution)/shard_map/ppermute | solution.py:401
  51.2 1.7 slice_dynamic-update-slice_fusion.6
  52.9 0.1 collective-permute-start.6
  53.0 1.7 slice_dynamic-update-slice_fusion.5
  54.7 2.2 %collective-permute-done.2 = bf16[4,264,128]{2,1,0:T(8,128)(2,1)S(1)} collective-permute-done((bf16[4,264,128]{2,1,0:T(8,128)(2,1)}, bf16[4,264,128]{2,1,0:T(8,128)(2,1)S(1)}, u32[]{:S(2)}, u32[]{:S(2)}) %collective-permute-start.2) | collective-permute-done | bytes 270368 | tf_op jit(solution)/shard_map/ppermute | solution.py:401
  56.9 0.7 slice_dynamic-update-slice_fusion.4
  57.6 0.7 slice_dynamic-update-slice_fusion.3
  58.3 14.3 %collective-permute-done.4 = bf16[4,264,128]{2,1,0:T(8,128)(2,1)S(1)} collective-permute-done((bf16[4,264,128]{2,1,0:T(8,128)(2,1)}, bf16[4,264,128]{2,1,0:T(8,128)(2,1)S(1)}, u32[]{:S(2)}, u32[]{:S(2)}) %collective-permute-start.4) | collective-permute-done | bytes 270368 | tf_op jit(solution)/shard_map/ppermute | solution.py:401
  72.6 0.7 slice_dynamic-update-slice_fusion.2
  73.4 0.7 slice_dynamic-update-slice_fusion.1
  74.1 0.7 slice_dynamic-update-slice_fusion
  74.7 1.4 copy-done
  76.1 7.4 %project_stiff.1 = (bf16[16,32,1024]{2,1,0:T(8,128)(2,1)}, f32[16,32,1024]{2,1,0:T(8,128)}, bf16[1024,1024]{1,0:T(8,128)(2,1)}) custom-call(s32[2,4]{1,0:T(2,128)} %map_ref.5, bf16[8,4,2,128,128]{4,3,2,1,0:T(8,128)(2,1)} %bitcast.36, bf16[2,512,512]{2,1,0:T(8,128)(2,1)} %get-tuple-element.48.m_ref), custom_call_target="tpu_custom_call" | custom-call | tf_op jit(solution)/shard_map/project_stiff/pallas_call | solution.py:325
  83.6 5.0 %mix_mass.1.y_ref = bf16[1024,1024]{1,0:T(8,128)(2,1)} custom-call(bf16[1024,1024]{1,0:T(8,128)(2,1)} %get-tuple-element.51.t_ref, bf16[2,512,512]{2,1,0:T(8,128)(2,1)} %get-tuple-element.52.m_ref, f32[2,1,512]{2,1,0:T(1,128)} %get-tuple-element.53.d_ref), custom_call_target="tpu_custom_call" | custom-call | tf_op jit(solution)/shard_map/mix_mass/pallas_call | solution.py:360
  88.6 6.0 %project_mass.1 = (bf16[16,32,1024]{2,1,0:T(8,128)(2,1)}, f32[16,32,1024]{2,1,0:T(8,128)}) custom-call(bf16[1024,1024]{1,0:T(8,128)(2,1)} %mix_mass.1.y_ref, bf16[1024,1024]{1,0:T(8,128)(2,1)} %get-tuple-element.51.t_ref), custom_call_target="tpu_custom_call" | custom-call | tf_op jit(solution)/shard_map/project_mass/pallas_call | solution.py:382
  94.6 0.2 collective-permute-start.17
  94.8 0.4 collective-permute-start.10
  95.2 0.4 collective-permute-start.7
  95.6 3.1 %collective-permute-start.8 = (bf16[8,264,128]{2,1,0:T(8,128)(2,1)S(1)}, bf16[8,264,128]{2,1,0:T(8,128)(2,1)S(1)}, u32[]{:S(2)}, u32[]{:S(2)}) collective-permute-start(bf16[8,264,128]{2,1,0:T(8,128)(2,1)S(1)} %copy-done.10), channel_id=1, source_target_pairs={{0,16},{1,17},{2,18},{3,19},{4,20},{5,21},{6,22},{7,23},{8,24},{9,... | collective-permute-start | bytes 1622024 | tf_op jit(solution)/shard_map/ppermute | solution.py:401
  98.7 1.3 collective-permute-start.9
  100.1 0.2 slice_reduce_fusion
  100.2 0.2 convert_reduce_fusion
  100.4 0.7 select_reduce_fusion
  101.1 20.2 %collective-permute-done.7.refs_4_ = bf16[8,264,128]{2,1,0:T(8,128)(2,1)S(1)} collective-permute-done((bf16[8,264,128]{2,1,0:T(8,128)(2,1)}, bf16[8,264,128]{2,1,0:T(8,128)(2,1)S(1)}, u32[]{:S(2)}, u32[]{:S(2)}) %collective-permute-start.7) | collective-permute-done | bytes 540704 | tf_op jit(solution)/shard_map/ppermute | solution.py:401
  121.3 14.4 %collective-permute-done.9.refs_6_ = bf16[8,264,128]{2,1,0:T(8,128)(2,1)S(1)} collective-permute-done((bf16[8,264,128]{2,1,0:T(8,128)(2,1)S(1)}, bf16[8,264,128]{2,1,0:T(8,128)(2,1)S(1)}, u32[]{:S(2)}, u32[]{:S(2)}) %collective-permute-start.9) | collective-permute-done | bytes 540704 | tf_op jit(solution)/shard_map/ppermute | solution.py:401
  135.7 0.8 copy-done.6
  136.5 5.5 %place.1 = (bf16[2048,4096]{1,0:T(8,128)(2,1)}, bf16[2048,4096]{1,0:T(8,128)(2,1)}, f32[4,1,128]{2,1,0:T(1,128)}) custom-call(s32[32,128]{1,0:T(8,128)} %bitcast.41, s32[32]{0:T(128)} %get-tuple-element.58.refs_1_, s32[32]{0:T(128)} %get-tuple-element.57.refs_2_, bf16[8,264,128]{2,1,0:T(8,128)(2,1)} %copy-done.3, ...), custom_call_target="tpu_custom_call", output_to_operand_aliasing={{0}: (7, {}), {1}: (8, {})} | custom-call | tf_op jit(solution)/shard_map/place/pallas_call | solution.py:534
  142.1 1.5 add_convert_fusion.2
  143.6 0.6 collective-permute-start.18
  144.2 1.7 collective-permute-start.19
  145.9 1.3 collective-permute-start.20
  147.2 0.3 add_convert_fusion.5
  147.5 0.6 collective-permute-start.11
  148.0 1.7 collective-permute-start.12
  149.8 3.1 %collective-permute-done.18 = bf16[4,32,1024]{2,1,0:T(8,128)(2,1)S(1)} collective-permute-done((bf16[4,32,1024]{2,1,0:T(8,128)(2,1)S(1)}, bf16[4,32,1024]{2,1,0:T(8,128)(2,1)S(1)}, u32[]{:S(2)}, u32[]{:S(2)}) %collective-permute-start.18) | collective-permute-done | bytes 262176 | tf_op jit(solution)/shard_map/ppermute | solution.py:401
  152.9 1.7 collective-permute-start.13
  154.5 4.4 %collective-permute-done.19 = bf16[4,32,1024]{2,1,0:T(8,128)(2,1)S(1)} collective-permute-done((bf16[4,32,1024]{2,1,0:T(8,128)(2,1)S(1)}, bf16[4,32,1024]{2,1,0:T(8,128)(2,1)S(1)}, u32[]{:S(2)}, u32[]{:S(2)}) %collective-permute-start.19) | collective-permute-done | bytes 262176 | tf_op jit(solution)/shard_map/ppermute | solution.py:401
  159.0 1.2 fusion.8
  160.2 11.2 %collective-permute-start.21 = (bf16[32,1024]{1,0:T(8,128)(2,1)S(1)}, bf16[32,1024]{1,0:T(8,128)(2,1)S(1)}, u32[]{:S(2)}, u32[]{:S(2)}) collective-permute-start(bf16[32,1024]{1,0:T(8,128)(2,1)S(1)} %get-tuple-element.101), channel_id=1, source_target_pairs={{0,8},{1,9},{2,10},{3,11},{4,12},{5,13},{6,14},{7,15},{8,0},{9,1},... | collective-permute-start | bytes 196616 | tf_op jit(solution)/shard_map/ppermute | solution.py:401
  171.3 1.6 collective-permute-start.22
  173.0 1.4 collective-permute-start.23
  174.4 0.2 fusion.9
  174.6 5.0 %collective-permute-start.14 = (bf16[32,1024]{1,0:T(8,128)(2,1)S(1)}, bf16[32,1024]{1,0:T(8,128)(2,1)S(1)}, u32[]{:S(2)}, u32[]{:S(2)}) collective-permute-start(bf16[32,1024]{1,0:T(8,128)(2,1)S(1)} %get-tuple-element.104), channel_id=1, source_target_pairs={{0,8},{1,9},{2,10},{3,11},{4,12},{5,13},{6,14},{7,15},{8,0},{9,1},... | collective-permute-start | bytes 196616 | tf_op jit(solution)/shard_map/ppermute | solution.py:401
  179.6 1.7 collective-permute-start.15
  181.4 1.4 collective-permute-start.16
  182.7 0.7 fusion.2
  183.4 1.3 collective-permute-done.15
  184.8 2.7 %collective-permute-done.16 = bf16[32,1024]{1,0:T(8,128)(2,1)S(1)} collective-permute-done((bf16[32,1024]{1,0:T(8,128)(2,1)S(1)}, bf16[32,1024]{1,0:T(8,128)(2,1)S(1)}, u32[]{:S(2)}, u32[]{:S(2)}) %collective-permute-start.16) | collective-permute-done | bytes 65568 | tf_op jit(solution)/shard_map/ppermute | solution.py:401
  187.5 0.7 fusion.5
  (38 shorter events, 0.1 us)
Async XLA Ops:
  2.0 14.4 %all-to-all-start = ((s32[32,1,128]{2,1,0:T(1,128)}), s32[32,1,128]{2,1,0:T(1,128)S(1)}, u32[]{:S(2)}, u32[]{:S(2)}) async-start(s32[32,1,128]{2,1,0:T(1,128)} %bitcast.43), calls=%async_computation | async-start | bytes 32768 | tf_op jit(solution)/shard_map/all_to_all | solution.py:32
  16.4 0.6 copy-start.7
  19.8 55.0 %all-to-all-start.1 = ((bf16[32,2,128,128]{3,2,1,0:T(8,128)(2,1)}), bf16[32,2,128,128]{3,2,1,0:T(8,128)(2,1)S(1)}, u32[]{:S(2)}, u32[]{:S(2)}) async-start(bf16[32,2,128,128]{3,2,1,0:T(8,128)(2,1)} %pick_modes.1), calls=%async_computation.1 | async-start | bytes 4194304 | tf_op jit(solution)/shard_map/all_to_all | solution.py:32
  32.0 16.6 %collective-permute-start = (bf16[4,264,128]{2,1,0:T(8,128)(2,1)}, bf16[4,264,128]{2,1,0:T(8,128)(2,1)}, u32[]{:S(2)}, u32[]{:S(2)}) collective-permute-start(bf16[4,264,128]{2,1,0:T(8,128)(2,1)} %get-tuple-element.32), channel_id=1, source_target_pairs={{0,1},{1,0},{2,3},{3,2},{4,5},{5,4},{6,7},{7,6},{8,9},{9,8},{10,11... | collective-permute-start | bytes 811016 | tf_op jit(solution)/shard_map/ppermute | solution.py:401
  32.2 20.7 %collective-permute-start.1 = (bf16[4,264,128]{2,1,0:T(8,128)(2,1)}, bf16[4,264,128]{2,1,0:T(8,128)(2,1)}, u32[]{:S(2)}, u32[]{:S(2)}) collective-permute-start(bf16[4,264,128]{2,1,0:T(8,128)(2,1)} %get-tuple-element.33), channel_id=1, source_target_pairs={{0,2},{1,3},{2,0},{3,1},{4,6},{5,7},{6,4},{7,5},{8,10},{9,11},{10,... | collective-permute-start | bytes 811016 | tf_op jit(solution)/shard_map/ppermute | solution.py:401
  33.8 23.0 %collective-permute-start.2 = (bf16[4,264,128]{2,1,0:T(8,128)(2,1)}, bf16[4,264,128]{2,1,0:T(8,128)(2,1)S(1)}, u32[]{:S(2)}, u32[]{:S(2)}) collective-permute-start(bf16[4,264,128]{2,1,0:T(8,128)(2,1)} %get-tuple-element.34), channel_id=1, source_target_pairs={{0,3},{1,2},{2,1},{3,0},{4,7},{5,6},{6,5},{7,4},{8,11},{9,10},{10,... | collective-permute-start | bytes 811016 | tf_op jit(solution)/shard_map/ppermute | solution.py:401
  34.0 23.6 %collective-permute-start.3 = (bf16[4,264,128]{2,1,0:T(8,128)(2,1)}, bf16[4,264,128]{2,1,0:T(8,128)(2,1)S(1)}, u32[]{:S(2)}, u32[]{:S(2)}) collective-permute-start(bf16[4,264,128]{2,1,0:T(8,128)(2,1)} %get-tuple-element.35), channel_id=1, source_target_pairs={{0,4},{1,5},{2,6},{3,7},{4,0},{5,1},{6,2},{7,3},{8,12},{9,13},{10,... | collective-permute-start | bytes 811016 | tf_op jit(solution)/shard_map/ppermute | solution.py:401
  35.6 37.0 %collective-permute-start.4 = (bf16[4,264,128]{2,1,0:T(8,128)(2,1)}, bf16[4,264,128]{2,1,0:T(8,128)(2,1)S(1)}, u32[]{:S(2)}, u32[]{:S(2)}) collective-permute-start(bf16[4,264,128]{2,1,0:T(8,128)(2,1)} %get-tuple-element.36), channel_id=1, source_target_pairs={{0,5},{1,4},{2,7},{3,6},{4,1},{5,0},{6,3},{7,2},{8,13},{9,12},{10,... | collective-permute-start | bytes 811016 | tf_op jit(solution)/shard_map/ppermute | solution.py:401
  48.6 24.8 %collective-permute-start.5 = (bf16[4,264,128]{2,1,0:T(8,128)(2,1)}, bf16[4,264,128]{2,1,0:T(8,128)(2,1)S(1)}, u32[]{:S(2)}, u32[]{:S(2)}) collective-permute-start(bf16[4,264,128]{2,1,0:T(8,128)(2,1)} %get-tuple-element.37), channel_id=1, source_target_pairs={{0,6},{1,7},{2,4},{3,5},{4,2},{5,3},{6,0},{7,1},{8,14},{9,15},{10,... | collective-permute-start | bytes 811016 | tf_op jit(solution)/shard_map/ppermute | solution.py:401
  52.9 21.1 %collective-permute-start.6 = (bf16[4,264,128]{2,1,0:T(8,128)(2,1)}, bf16[4,264,128]{2,1,0:T(8,128)(2,1)S(1)}, u32[]{:S(2)}, u32[]{:S(2)}) collective-permute-start(bf16[4,264,128]{2,1,0:T(8,128)(2,1)} %get-tuple-element.38), channel_id=1, source_target_pairs={{0,7},{1,6},{2,5},{3,4},{4,3},{5,2},{6,1},{7,0},{8,15},{9,14},{10,... | collective-permute-start | bytes 811016 | tf_op jit(solution)/shard_map/ppermute | solution.py:401
  74.7 19.9 %copy-start.3 = (bf16[8,264,128]{2,1,0:T(8,128)(2,1)}, bf16[8,264,128]{2,1,0:T(8,128)(2,1)S(1)}, u32[]{:S(2)}) copy-start(bf16[8,264,128]{2,1,0:T(8,128)(2,1)S(1)} %get-tuple-element.72.refs_3_) | copy-start | bytes 1622020
  74.7 1.4 copy-start
  88.6 7.0 %copy-start.10 = (bf16[8,264,128]{2,1,0:T(8,128)(2,1)S(1)}, bf16[8,264,128]{2,1,0:T(8,128)(2,1)}, u32[]{:S(2)}) copy-start(bf16[8,264,128]{2,1,0:T(8,128)(2,1)} %get-tuple-element.41) | copy-start | bytes 1622020
  88.6 10.2 %copy-start.9 = (bf16[8,264,128]{2,1,0:T(8,128)(2,1)S(1)}, bf16[8,264,128]{2,1,0:T(8,128)(2,1)}, u32[]{:S(2)}) copy-start(bf16[8,264,128]{2,1,0:T(8,128)(2,1)} %get-tuple-element.42) | copy-start | bytes 1622020
  88.6 11.5 %copy-start.8 = (s32[32,1,128]{2,1,0:T(1,128)S(1)}, s32[32,1,128]{2,1,0:T(1,128)}, u32[]{:S(2)}) copy-start(s32[32,1,128]{2,1,0:T(1,128)} %copy-done.7) | copy-start | bytes 49156
  94.6 47.5 %collective-permute-start.17 = (bf16[16,32,1024]{2,1,0:T(8,128)(2,1)}, bf16[16,32,1024]{2,1,0:T(8,128)(2,1)}, u32[]{:S(2)}, u32[]{:S(2)}) collective-permute-start(bf16[16,32,1024]{2,1,0:T(8,128)(2,1)} %get-tuple-element.55), channel_id=1, source_target_pairs={{0,1},{1,0},{2,3},{3,2},{4,5},{5,4},{6,7},{7,6},{8,9},{9,8},{10,11... | collective-permute-start | bytes 3145736 | tf_op jit(solution)/shard_map/ppermute | solution.py:401
  94.8 52.4 %collective-permute-start.10 = (bf16[16,32,1024]{2,1,0:T(8,128)(2,1)}, bf16[16,32,1024]{2,1,0:T(8,128)(2,1)S(1)}, u32[]{:S(2)}, u32[]{:S(2)}) collective-permute-start(bf16[16,32,1024]{2,1,0:T(8,128)(2,1)} %get-tuple-element.50), channel_id=1, source_target_pairs={{0,1},{1,0},{2,3},{3,2},{4,5},{5,4},{6,7},{7,6},{8,9},{9,8},{10,11... | collective-permute-start | bytes 3145736 | tf_op jit(solution)/shard_map/ppermute | solution.py:401
  95.2 26.1 %collective-permute-start.7 = (bf16[8,264,128]{2,1,0:T(8,128)(2,1)}, bf16[8,264,128]{2,1,0:T(8,128)(2,1)S(1)}, u32[]{:S(2)}, u32[]{:S(2)}) collective-permute-start(bf16[8,264,128]{2,1,0:T(8,128)(2,1)} %get-tuple-element.71), channel_id=1, source_target_pairs={{0,8},{1,9},{2,10},{3,11},{4,12},{5,13},{6,14},{7,15},{8,0},{9,1},... | collective-permute-start | bytes 1622024 | tf_op jit(solution)/shard_map/ppermute | solution.py:401
  95.6 25.7 %collective-permute-start.8 = (bf16[8,264,128]{2,1,0:T(8,128)(2,1)S(1)}, bf16[8,264,128]{2,1,0:T(8,128)(2,1)S(1)}, u32[]{:S(2)}, u32[]{:S(2)}) collective-permute-start(bf16[8,264,128]{2,1,0:T(8,128)(2,1)S(1)} %copy-done.10), channel_id=1, source_target_pairs={{0,16},{1,17},{2,18},{3,19},{4,20},{5,21},{6,22},{7,23},{8,24},{9,... | collective-permute-start | bytes 1622024 | tf_op jit(solution)/shard_map/ppermute | solution.py:401
  98.7 37.0 %collective-permute-start.9 = (bf16[8,264,128]{2,1,0:T(8,128)(2,1)S(1)}, bf16[8,264,128]{2,1,0:T(8,128)(2,1)S(1)}, u32[]{:S(2)}, u32[]{:S(2)}) collective-permute-start(bf16[8,264,128]{2,1,0:T(8,128)(2,1)S(1)} %copy-done.9), channel_id=1, source_target_pairs={{0,24},{1,25},{2,26},{3,27},{4,28},{5,29},{6,30},{7,31},{8,16},{9,... | collective-permute-start | bytes 1622024 | tf_op jit(solution)/shard_map/ppermute | solution.py:401
  121.3 14.4 %copy-start.4 = (bf16[8,264,128]{2,1,0:T(8,128)(2,1)}, bf16[8,264,128]{2,1,0:T(8,128)(2,1)S(1)}, u32[]{:S(2)}) copy-start(bf16[8,264,128]{2,1,0:T(8,128)(2,1)S(1)} %collective-permute-done.7.refs_4_) | copy-start | bytes 1622020
  121.3 14.4 %copy-start.5 = (bf16[8,264,128]{2,1,0:T(8,128)(2,1)}, bf16[8,264,128]{2,1,0:T(8,128)(2,1)S(1)}, u32[]{:S(2)}) copy-start(bf16[8,264,128]{2,1,0:T(8,128)(2,1)S(1)} %collective-permute-done.8.refs_5_) | copy-start | bytes 1622020
  135.7 0.8 copy-start.6
  136.5 5.6 %copy-start.2 = (f32[16,32,1024]{2,1,0:T(8,128)S(1)}, f32[16,32,1024]{2,1,0:T(8,128)}, u32[]{:S(2)}) copy-start(f32[16,32,1024]{2,1,0:T(8,128)} %get-tuple-element.54) | copy-start | bytes 6291460
  142.1 5.1 %copy-start.1 = (f32[16,32,1024]{2,1,0:T(8,128)S(1)}, f32[16,32,1024]{2,1,0:T(8,128)}, u32[]{:S(2)}) copy-start(f32[16,32,1024]{2,1,0:T(8,128)} %get-tuple-element.49) | copy-start | bytes 6291460
  143.6 9.2 %collective-permute-start.18 = (bf16[4,32,1024]{2,1,0:T(8,128)(2,1)S(1)}, bf16[4,32,1024]{2,1,0:T(8,128)(2,1)S(1)}, u32[]{:S(2)}, u32[]{:S(2)}) collective-permute-start(bf16[4,32,1024]{2,1,0:T(8,128)(2,1)S(1)} %get-tuple-element.63), channel_id=1, source_target_pairs={{0,2},{1,3},{2,0},{3,1},{4,6},{5,7},{6,4},{7,5},{8,10},{9,11},{10,... | collective-permute-start | bytes 786440 | tf_op jit(solution)/shard_map/ppermute | solution.py:401
  144.2 14.8 %collective-permute-start.19 = (bf16[4,32,1024]{2,1,0:T(8,128)(2,1)S(1)}, bf16[4,32,1024]{2,1,0:T(8,128)(2,1)S(1)}, u32[]{:S(2)}, u32[]{:S(2)}) collective-permute-start(bf16[4,32,1024]{2,1,0:T(8,128)(2,1)S(1)} %get-tuple-element.65), channel_id=1, source_target_pairs={{0,4},{1,5},{2,6},{3,7},{4,0},{5,1},{6,2},{7,3},{8,12},{9,13},{10,... | collective-permute-start | bytes 786440 | tf_op jit(solution)/shard_map/ppermute | solution.py:401
  145.9 13.1 %collective-permute-start.20 = (bf16[4,32,1024]{2,1,0:T(8,128)(2,1)S(1)}, bf16[4,32,1024]{2,1,0:T(8,128)(2,1)S(1)}, u32[]{:S(2)}, u32[]{:S(2)}) collective-permute-start(bf16[4,32,1024]{2,1,0:T(8,128)(2,1)S(1)} %get-tuple-element.64), channel_id=1, source_target_pairs={{0,6},{1,7},{2,4},{3,5},{4,2},{5,3},{6,0},{7,1},{8,14},{9,15},{10,... | collective-permute-start | bytes 786440 | tf_op jit(solution)/shard_map/ppermute | solution.py:401
  147.5 25.5 %collective-permute-start.11 = (bf16[4,32,1024]{2,1,0:T(8,128)(2,1)S(1)}, bf16[4,32,1024]{2,1,0:T(8,128)(2,1)S(1)}, u32[]{:S(2)}, u32[]{:S(2)}) collective-permute-start(bf16[4,32,1024]{2,1,0:T(8,128)(2,1)S(1)} %get-tuple-element.66), channel_id=1, source_target_pairs={{0,2},{1,3},{2,0},{3,1},{4,6},{5,7},{6,4},{7,5},{8,10},{9,11},{10,... | collective-permute-start | bytes 786440 | tf_op jit(solution)/shard_map/ppermute | solution.py:401
  148.0 26.3 %collective-permute-start.12 = (bf16[4,32,1024]{2,1,0:T(8,128)(2,1)S(1)}, bf16[4,32,1024]{2,1,0:T(8,128)(2,1)S(1)}, u32[]{:S(2)}, u32[]{:S(2)}) collective-permute-start(bf16[4,32,1024]{2,1,0:T(8,128)(2,1)S(1)} %get-tuple-element.68), channel_id=1, source_target_pairs={{0,4},{1,5},{2,6},{3,7},{4,0},{5,1},{6,2},{7,3},{8,12},{9,13},{10,... | collective-permute-start | bytes 786440 | tf_op jit(solution)/shard_map/ppermute | solution.py:401
  152.9 21.5 %collective-permute-start.13 = (bf16[4,32,1024]{2,1,0:T(8,128)(2,1)S(1)}, bf16[4,32,1024]{2,1,0:T(8,128)(2,1)S(1)}, u32[]{:S(2)}, u32[]{:S(2)}) collective-permute-start(bf16[4,32,1024]{2,1,0:T(8,128)(2,1)S(1)} %get-tuple-element.67), channel_id=1, source_target_pairs={{0,6},{1,7},{2,4},{3,5},{4,2},{5,3},{6,0},{7,1},{8,14},{9,15},{10,... | collective-permute-start | bytes 786440 | tf_op jit(solution)/shard_map/ppermute | solution.py:401
  160.2 21.2 %collective-permute-start.21 = (bf16[32,1024]{1,0:T(8,128)(2,1)S(1)}, bf16[32,1024]{1,0:T(8,128)(2,1)S(1)}, u32[]{:S(2)}, u32[]{:S(2)}) collective-permute-start(bf16[32,1024]{1,0:T(8,128)(2,1)S(1)} %get-tuple-element.101), channel_id=1, source_target_pairs={{0,8},{1,9},{2,10},{3,11},{4,12},{5,13},{6,14},{7,15},{8,0},{9,1},... | collective-permute-start | bytes 196616 | tf_op jit(solution)/shard_map/ppermute | solution.py:401
  171.3 11.4 %collective-permute-start.22 = (bf16[32,1024]{1,0:T(8,128)(2,1)S(1)}, bf16[32,1024]{1,0:T(8,128)(2,1)S(1)}, u32[]{:S(2)}, u32[]{:S(2)}) collective-permute-start(bf16[32,1024]{1,0:T(8,128)(2,1)S(1)} %get-tuple-element.103), channel_id=1, source_target_pairs={{0,16},{1,17},{2,18},{3,19},{4,20},{5,21},{6,22},{7,23},{8,24},{9,... | collective-permute-start | bytes 196616 | tf_op jit(solution)/shard_map/ppermute | solution.py:401
  173.0 9.8 %collective-permute-start.23 = (bf16[32,1024]{1,0:T(8,128)(2,1)S(1)}, bf16[32,1024]{1,0:T(8,128)(2,1)S(1)}, u32[]{:S(2)}, u32[]{:S(2)}) collective-permute-start(bf16[32,1024]{1,0:T(8,128)(2,1)S(1)} %get-tuple-element.102), channel_id=1, source_target_pairs={{0,24},{1,25},{2,26},{3,27},{4,28},{5,29},{6,30},{7,31},{8,16},{9,... | collective-permute-start | bytes 196616 | tf_op jit(solution)/shard_map/ppermute | solution.py:401
  174.6 8.8 %collective-permute-start.14 = (bf16[32,1024]{1,0:T(8,128)(2,1)S(1)}, bf16[32,1024]{1,0:T(8,128)(2,1)S(1)}, u32[]{:S(2)}, u32[]{:S(2)}) collective-permute-start(bf16[32,1024]{1,0:T(8,128)(2,1)S(1)} %get-tuple-element.104), channel_id=1, source_target_pairs={{0,8},{1,9},{2,10},{3,11},{4,12},{5,13},{6,14},{7,15},{8,0},{9,1},... | collective-permute-start | bytes 196616 | tf_op jit(solution)/shard_map/ppermute | solution.py:401
  179.6 5.2 %collective-permute-start.15 = (bf16[32,1024]{1,0:T(8,128)(2,1)S(1)}, bf16[32,1024]{1,0:T(8,128)(2,1)S(1)}, u32[]{:S(2)}, u32[]{:S(2)}) collective-permute-start(bf16[32,1024]{1,0:T(8,128)(2,1)S(1)} %get-tuple-element.106), channel_id=1, source_target_pairs={{0,16},{1,17},{2,18},{3,19},{4,20},{5,21},{6,22},{7,23},{8,24},{9,... | collective-permute-start | bytes 196616 | tf_op jit(solution)/shard_map/ppermute | solution.py:401
  181.4 6.2 %collective-permute-start.16 = (bf16[32,1024]{1,0:T(8,128)(2,1)S(1)}, bf16[32,1024]{1,0:T(8,128)(2,1)S(1)}, u32[]{:S(2)}, u32[]{:S(2)}) collective-permute-start(bf16[32,1024]{1,0:T(8,128)(2,1)S(1)} %get-tuple-element.105), channel_id=1, source_target_pairs={{0,24},{1,25},{2,26},{3,27},{4,28},{5,29},{6,30},{7,31},{8,16},{9,... | collective-permute-start | bytes 196616 | tf_op jit(solution)/shard_map/ppermute | solution.py:401

commit v7 on v6

--- a/solution.py
+++ b/solution.py
@@ -10,6 +10,7 @@
 
 BLK = 128
 EXTRA = 8
+CHIP = 2
 AXES = ("row", "col")
 F32 = jnp.float32
 BF16 = jnp.bfloat16
@@ -90,19 +91,31 @@
     device_count = table.shape[0]
     width = modes.shape[1]
 
-    def kernel(table_ref, modes_ref, out_ref):
-        def one(device, carry):
+    def kernel(table_ref, modes_ref, out_ref, sem):
+        def copy(device, h):
+            return pltpu.make_async_copy(
+                modes_ref.at[table_ref[device, h]], out_ref.at[device, h], sem.at[device, h]
+            )
+
+        def start(device, carry):
             for h in range(ratio):
-                out_ref[device, h] = modes_ref[table_ref[device, h]]
+                copy(device, h).start()
             return carry
 
-        lax.fori_loop(0, device_count, one, 0, unroll=4)
+        def wait(device, carry):
+            for h in range(ratio):
+                copy(device, h).wait()
+            return carry
+
+        lax.fori_loop(0, device_count, start, 0, unroll=4)
+        lax.fori_loop(0, device_count, wait, 0, unroll=4)
 
     return pl.pallas_call(
         kernel,
         out_shape=jax.ShapeDtypeStruct((device_count, ratio, width, BLK), BF16),
-        in_specs=[SMEM, VMEM],
-        out_specs=VMEM,
+        in_specs=[SMEM, ANY],
+        out_specs=ANY,
+        scratch_shapes=[pltpu.SemaphoreType.DMA((device_count, ratio))],
         name="pick_modes",
     )(table, modes)
 
@@ -422,7 +435,11 @@
     near = [blocks[0]]
     for d in range(1, sizes.plane):
         near.append(swap(blocks[d], d, sizes.devices))
-    return [jnp.stack([part[z] for part in near]) for z in range(sizes.devices // sizes.plane)]
+    return near
+
+
+def regroup(near, z):
+    return jnp.stack([part[z] for part in near])
 
 
 def clear_tiles(table, sizes):
@@ -456,20 +473,19 @@
 def place(table, order, slots, arrived, stiff_tile, mass_tile, sizes):
     count = sizes.devices
     limit = sizes.row_blocks * sizes.col_blocks
-    depth = len(arrived)
+    parts = len(arrived)
     height = 2 * BLK + EXTRA
 
     def kernel(*refs):
         table_ref, order_ref, slot_ref = refs[:3]
-        in_refs = refs[3 : 3 + depth]
+        in_refs = refs[3 : 3 + parts]
         stiff_ref, mass_ref, share_ref, held_ref, sums_ref, in_sem, sem = refs[-7:]
         me = lax.axis_index("row") * sizes.cols + lax.axis_index("col")
-        loads = [
-            pltpu.make_async_copy(
-                ref, held_ref.at[pl.ds(z * sizes.plane, sizes.plane)], in_sem.at[z]
-            )
-            for z, ref in enumerate(in_refs)
-        ]
+        loads, first = [], 0
+        for i, ref in enumerate(in_refs):
+            span = pl.ds(first, ref.shape[0])
+            loads.append(pltpu.make_async_copy(ref, held_ref.at[span], in_sem.at[i]))
+            first += ref.shape[0]
         for load in loads:
             load.start()
         for load in loads:
@@ -533,18 +549,18 @@
 
     return pl.pallas_call(
         kernel,
-        in_specs=[SMEM, SMEM, SMEM] + [ANY] * (depth + 2),
+        in_specs=[SMEM, SMEM, SMEM] + [ANY] * (parts + 2),
         out_specs=[ANY, ANY, VMEM],
         out_shape=[
             jax.ShapeDtypeStruct(stiff_tile.shape, BF16),
             jax.ShapeDtypeStruct(mass_tile.shape, BF16),
             jax.ShapeDtypeStruct((sizes.share_blocks, 1, BLK), F32),
         ],
-        input_output_aliases={3 + depth: 0, 4 + depth: 1},
+        input_output_aliases={3 + parts: 0, 4 + parts: 1},
         scratch_shapes=[
             pltpu.VMEM((count, height, BLK), BF16),
             pltpu.VMEM((count, 2 * BLK, BLK), BF16),
-            pltpu.SemaphoreType.DMA((depth,)),
+            pltpu.SemaphoreType.DMA((parts,)),
             pltpu.SemaphoreType.DMA((count, 2)),
         ],
         name="place",
@@ -568,6 +584,7 @@
     x_size = col_count // 2
     y_size = x_size
     dims = (row_count // y_size, y_size, x_size)
+    depth = dims[0]
 
     table = exchange(describe(block_map, sizes))
     turned = jnp.swapaxes(modes.reshape(sizes.col_blocks, BLK, width), 1, 2)
@@ -576,14 +593,15 @@
     stiff, mass, diagonal, *blocks = condense(
         block_map, inv_interior, coupling, boundary_stiff, mass_interior, mass_boundary, sizes
     )
-    spread = spread_in_plane(blocks, sizes)
-    beside = swap(spread[1], sizes.plane, sizes.devices)
+    near = spread_in_plane(blocks, sizes)
+    depth = dims[0]
+    early = [swap(regroup(near[:CHIP], z), z * sizes.plane, sizes.devices) for z in range(2, depth)]
     stiff_tile, mass_tile = clear_tiles(table, sizes)
-    late, fetched, stiff_tile, mass_tile = lax.optimization_barrier(
-        (spread[2:], fetched, stiff_tile, mass_tile)
-    )
-    late = [swap(part, (2 + d) * sizes.plane, sizes.devices) for d, part in enumerate(late)]
-    arrived = [spread[0], beside, *late]
+    late = [swap(regroup(near[CHIP:], z), z * sizes.plane, sizes.devices) for z in range(2, depth)]
+    beside = swap(regroup(near, 1), sizes.plane, sizes.devices)
+    arrived = [regroup(near, 0), beside]
+    for pieces in zip(early, late):
+        arrived.extend(pieces)
 
     fetched = fetched.reshape(row_count, col_count, sizes.ratio, width, BLK)
     send, keep, qt = project_stiff(block_map, fetched, stiff, dims, sizes.row_blocks)

time: 189 us -> 247 us (1.31)
  Pallas kernels: 48.8 us -> 112 us
  starting transfers between devices: 51.7 us -> 37.2 us
  waiting for transfers between devices: 67.6 us -> 76.7 us
    pallas_call x1, Pallas kernels: 2.76 us -> 66.1 us  [pick_modes(): pl.pallas_call(kernel, out_shape=jax.ShapeDtypeStruct((device_count, rati...]
    all_to_all x2, waiting for transfers between devices: 4.84 us -> 20.6 us  [exchange(): return lax.all_to_all(value, AXES, split_axis=0, concat_axis=0, tiled=True)]
    ppermute x24 -> x26, starting transfers between devices: 41.7 us -> 27.1 us  [swap(): lax.ppermute(value, AXES, [(i, i ^ offset) for i in range(device_count)])]
    ppermute x24 -> x26, waiting for transfers between devices: 62.8 us -> 56.1 us  [swap(): lax.ppermute(value, AXES, [(i, i ^ offset) for i in range(device_count)])]
    unnamed x29 -> x25, local copies, waits for them, and re-layouts: 10.7 us -> 7.38 us
  transfers between devices with their start and end apart: 26 -> 28, of which waited for: 9 -> 15; matrix products, arithmetic and copies ran while one was open for 8% -> 7% of each run, Pallas kernels for 14% -> 18%
where the time goes in v7:
time: 247 us; the launch traced here: 246 us
  Pallas kernels  112 us (45%)
  waiting for transfers between devices  76.7 us (31%)
  starting transfers between devices  37.2 us (15%)
  local copies, waits for them, and re-layouts  12.8 us (5%)
  other arithmetic  6.78 us (3%)
    pallas_call x1, Pallas kernels, pick_modes(): pl.pallas_call(kernel, out_shape=jax.ShapeDtypeStruct((device_count, rati...  66.1 us
    ppermute x26, waiting for transfers between devices, swap(): lax.ppermute(value, AXES, [(i, i ^ offset) for i in range(device_count)])  56.1 us
    ppermute x26, starting transfers between devices, swap(): lax.ppermute(value, AXES, [(i, i ^ offset) for i in range(device_count)])  27.1 us
    all_to_all x2, waiting for transfers between devices, exchange(): return lax.all_to_all(value, AXES, split_axis=0, concat_axis=0, tiled=True)  20.6 us
    pallas_call x1, Pallas kernels, clear_tiles(): pl.pallas_call(kernel, in_specs=[ANY], out_specs=[ANY, ANY], out_shape=[j...  11.2 us
    all_to_all x2, starting transfers between devices, exchange(): return lax.all_to_all(value, AXES, split_axis=0, concat_axis=0, tiled=True)  10.1 us
    pallas_call x1, Pallas kernels, condense(): pl.pallas_call(kernel, grid=(local_subs,), in_specs=[SMEM, piece(interior...  9.53 us
    pallas_call x1, Pallas kernels, project_stiff(): pl.pallas_call(kernel, grid=(2,), in_specs=[SMEM, whole(*fetched.shape),...  7.46 us
  transfers between devices with their start and end apart: 28, of which 15 were waited for; matrix products, arithmetic and copies ran while one was open for 7% of the time, Pallas kernels for 18%

profile of v7, /device:TPU:0, one launch (start us, length us, event | category | flops | bytes accessed | tf_op | source)
XLA Modules:
  0.0 246.3 jit_solution(6917506874643722527)
XLA Ops:
  0.6 1.4 describe.1
  2.0 7.3 %all-to-all-start = ((s32[32,1,128]{2,1,0:T(1,128)}), s32[32,1,128]{2,1,0:T(1,128)S(1)}, u32[]{:S(2)}, u32[]{:S(2)}) async-start(s32[32,1,128]{2,1,0:T(1,128)} %bitcast.43), calls=%async_computation | async-start | bytes 32768 | tf_op jit(solution)/shard_map/all_to_all | solution.py:33
  9.3 2.3 copy.18
  11.6 4.8 %all-to-all-done = s32[32,1,128]{2,1,0:T(1,128)S(1)} async-done(((s32[32,1,128]{2,1,0:T(1,128)}), s32[32,1,128]{2,1,0:T(1,128)S(1)}, u32[]{:S(2)}, u32[]{:S(2)}) %all-to-all-start) | async-done | bytes 16416 | tf_op jit(solution)/shard_map/all_to_all | solution.py:33
  16.4 0.6 copy-done.5
  17.0 66.1 %pick_modes.1 = bf16[32,2,128,128]{3,2,1,0:T(8,128)(2,1)} custom-call(s32[32,128]{1,0:T(8,128)} %bitcast.39, bf16[32,128,128]{2,1,0:T(8,128)(2,1)} %bitcast.37), custom_call_target="tpu_custom_call" | custom-call | tf_op jit(solution)/shard_map/pick_modes/pallas_call | solution.py:113
  83.2 2.7 %all-to-all-start.1 = ((bf16[32,2,128,128]{3,2,1,0:T(8,128)(2,1)}), bf16[32,2,128,128]{3,2,1,0:T(8,128)(2,1)S(1)}, u32[]{:S(2)}, u32[]{:S(2)}) async-start(bf16[32,2,128,128]{3,2,1,0:T(8,128)(2,1)} %pick_modes.1), calls=%async_computation.1 | async-start | bytes 4194304 | tf_op jit(solution)/shard_map/all_to_all | solution.py:33
  85.9 9.5 %condense.1 = (bf16[2,512,512]{2,1,0:T(8,128)(2,1)}, bf16[2,512,512]{2,1,0:T(8,128)(2,1)}, f32[2,1,512]{2,1,0:T(1,128)}, bf16[4,264,128]{2,1,0:T(8,128)(2,1)}, b...) custom-call(s32[2,4]{1,0:T(2,128)} %map_ref.5, ...), custom_call_target="tpu_custom_call" | custom-call | tf_op jit(solution)/shard_map/condense/pallas_call | solution.py:219
  95.6 1.6 collective-permute-start.1
  97.4 1.7 collective-permute-start.3
  99.1 1.6 fusion.10
  100.7 2.6 %collective-permute-start.5 = (bf16[4,264,128]{2,1,0:T(8,128)(2,1)}, bf16[4,264,128]{2,1,0:T(8,128)(2,1)S(1)}, u32[]{:S(2)}, u32[]{:S(2)}) collective-permute-start(bf16[4,264,128]{2,1,0:T(8,128)(2,1)} %get-tuple-element.32), channel_id=1, source_target_pairs={{0,6},{1,7},{2,4},{3,5},{4,2},{5,3},{6,0},{7,1},{8,14},{9,15},{10,... | collective-permute-start | bytes 811016 | tf_op jit(solution)/shard_map/ppermute | solution.py:414
  103.3 0.6 fusion.11
  104.0 0.7 pad_maximum_fusion
  104.6 8.0 %collective-permute-done.1 = bf16[4,264,128]{2,1,0:T(8,128)(2,1)S(1)} collective-permute-done((bf16[4,264,128]{2,1,0:T(8,128)(2,1)}, bf16[4,264,128]{2,1,0:T(8,128)(2,1)S(1)}, u32[]{:S(2)}, u32[]{:S(2)}) %collective-permute-start.1) | collective-permute-done | bytes 270368 | tf_op jit(solution)/shard_map/ppermute | solution.py:414
  112.7 0.4 collective-permute-start.6
  113.1 0.7 slice_dynamic-update-slice_fusion.5
  113.7 6.5 %collective-permute-done.2 = bf16[4,264,128]{2,1,0:T(8,128)(2,1)S(1)} collective-permute-done((bf16[4,264,128]{2,1,0:T(8,128)(2,1)}, bf16[4,264,128]{2,1,0:T(8,128)(2,1)S(1)}, u32[]{:S(2)}, u32[]{:S(2)}) %collective-permute-start.2) | collective-permute-done | bytes 270368 | tf_op jit(solution)/shard_map/ppermute | solution.py:414
  120.3 2.0 collective-permute-start.8
  122.3 0.7 slice_dynamic-update-slice_fusion.4
  123.0 0.7 pad_maximum_fusion.1
  123.7 1.4 collective-permute-start.10
  125.1 0.7 slice_dynamic-update-slice_fusion.3
  125.8 15.8 %all-to-all-done.1 = bf16[32,2,128,128]{3,2,1,0:T(8,128)(2,1)S(1)} async-done(((bf16[32,2,128,128]{3,2,1,0:T(8,128)(2,1)}), bf16[32,2,128,128]{3,2,1,0:T(8,128)(2,1)S(1)}, u32[]{:S(2)}, u32[]{:S(2)}) %all-to-all-start.1) | async-done | bytes 2097184 | tf_op jit(solution)/shard_map/all_to_all | solution.py:33
  141.6 1.3 copy-done
  142.9 7.5 %project_stiff.1 = (bf16[16,32,1024]{2,1,0:T(8,128)(2,1)}, f32[16,32,1024]{2,1,0:T(8,128)}, bf16[1024,1024]{1,0:T(8,128)(2,1)}) custom-call(s32[2,4]{1,0:T(2,128)} %map_ref.5, bf16[8,4,2,128,128]{4,3,2,1,0:T(8,128)(2,1)} %bitcast.36, bf16[2,512,512]{2,1,0:T(8,128)(2,1)} %get-tuple-element.38.m_ref), custom_call_target="tpu_custom_call" | custom-call | tf_op jit(solution)/shard_map/project_stiff/pallas_call | solution.py:338
  150.4 5.0 %mix_mass.1.y_ref = bf16[1024,1024]{1,0:T(8,128)(2,1)} custom-call(bf16[1024,1024]{1,0:T(8,128)(2,1)} %get-tuple-element.41.t_ref, bf16[2,512,512]{2,1,0:T(8,128)(2,1)} %get-tuple-element.42.m_ref, f32[2,1,512]{2,1,0:T(1,128)} %get-tuple-element.43.d_ref), custom_call_target="tpu_custom_call" | custom-call | tf_op jit(solution)/shard_map/mix_mass/pallas_call | solution.py:373
  155.3 5.8 %project_mass.1 = (bf16[16,32,1024]{2,1,0:T(8,128)(2,1)}, f32[16,32,1024]{2,1,0:T(8,128)}) custom-call(bf16[1024,1024]{1,0:T(8,128)(2,1)} %mix_mass.1.y_ref, bf16[1024,1024]{1,0:T(8,128)(2,1)} %get-tuple-element.41.t_ref), custom_call_target="tpu_custom_call" | custom-call | tf_op jit(solution)/shard_map/project_mass/pallas_call | solution.py:395
  161.2 1.7 slice_dynamic-update-slice_fusion.2
  162.9 0.5 collective-permute-start.12
  163.4 0.7 slice_dynamic-update-slice_fusion.1
  164.1 0.7 slice_dynamic-update-slice_fusion
  164.9 1.1 collective-permute-start.11
  166.0 2.3 collective-permute-start.9
  168.3 11.2 %clear_tiles.1 = (bf16[2048,4096]{1,0:T(8,128)(2,1)}, bf16[2048,4096]{1,0:T(8,128)(2,1)}) custom-call(s32[32,128]{1,0:T(8,128)} %bitcast.40), custom_call_target="tpu_custom_call" | custom-call | tf_op jit(solution)/shard_map/clear_tiles/pallas_call | solution.py:460
  179.9 0.7 select_reduce_fusion
  180.7 7.5 %collective-permute-done.11.refs_8_ = bf16[6,264,128]{2,1,0:T(8,128)(2,1)S(1)} collective-permute-done((bf16[6,264,128]{2,1,0:T(8,128)(2,1)}, bf16[6,264,128]{2,1,0:T(8,128)(2,1)S(1)}, u32[]{:S(2)}, u32[]{:S(2)}) %collective-permute-start.11) | collective-permute-done | bytes 405536 | tf_op jit(solution)/shard_map/ppermute | solution.py:414
  188.1 15.5 %collective-permute-done.9.refs_6_ = bf16[6,264,128]{2,1,0:T(8,128)(2,1)S(1)} collective-permute-done((bf16[6,264,128]{2,1,0:T(8,128)(2,1)}, bf16[6,264,128]{2,1,0:T(8,128)(2,1)S(1)}, u32[]{:S(2)}, u32[]{:S(2)}) %collective-permute-start.9) | collective-permute-done | bytes 405536 | tf_op jit(solution)/shard_map/ppermute | solution.py:414
  203.6 0.7 copy-done.8
  204.6 5.6 %place.1 = (bf16[2048,4096]{1,0:T(8,128)(2,1)}, bf16[2048,4096]{1,0:T(8,128)(2,1)}, f32[4,1,128]{2,1,0:T(1,128)}) custom-call(s32[32,128]{1,0:T(8,128)} %bitcast.41, s32[32]{0:T(128)} %get-tuple-element.48.refs_1_, s32[32]{0:T(128)} %get-tuple-element.47.refs_2_, bf16[8,264,128]{2,1,0:T(8,128)(2,1)} %copy-done.3, ...), custom_call_target="tpu_custom_call", output_to_operand_aliasing={{0}: (9, {}), {1}: (10, {})} | custom-call | tf_op jit(solution)/shard_map/place/pallas_call | solution.py:550
  210.2 1.5 add_convert_fusion.2
  211.7 1.1 collective-permute-start.20
  212.8 1.4 collective-permute-start.22
  214.1 1.1 collective-permute-start.21
  215.3 0.3 add_convert_fusion.5
  215.5 1.1 collective-permute-start.13
  216.6 1.3 collective-permute-start.15
  218.0 2.9 %collective-permute-done.20 = bf16[4,32,1024]{2,1,0:T(8,128)(2,1)S(1)} collective-permute-done((bf16[4,32,1024]{2,1,0:T(8,128)(2,1)S(1)}, bf16[4,32,1024]{2,1,0:T(8,128)(2,1)S(1)}, u32[]{:S(2)}, u32[]{:S(2)}) %collective-permute-start.20) | collective-permute-done | bytes 262176 | tf_op jit(solution)/shard_map/ppermute | solution.py:414
  220.9 0.9 collective-permute-start.14
  221.9 5.1 %collective-permute-done.22 = bf16[4,32,1024]{2,1,0:T(8,128)(2,1)S(1)} collective-permute-done((bf16[4,32,1024]{2,1,0:T(8,128)(2,1)S(1)}, bf16[4,32,1024]{2,1,0:T(8,128)(2,1)S(1)}, u32[]{:S(2)}, u32[]{:S(2)}) %collective-permute-start.22) | collective-permute-done | bytes 262176 | tf_op jit(solution)/shard_map/ppermute | solution.py:414
  227.0 1.9 collective-permute-done.21
  228.9 1.2 fusion.8
  230.1 1.1 collective-permute-start.25
  231.2 1.0 collective-permute-done.13
  232.2 1.4 collective-permute-start.24
  233.6 2.6 %collective-permute-done.15 = bf16[4,32,1024]{2,1,0:T(8,128)(2,1)S(1)} collective-permute-done((bf16[4,32,1024]{2,1,0:T(8,128)(2,1)S(1)}, bf16[4,32,1024]{2,1,0:T(8,128)(2,1)S(1)}, u32[]{:S(2)}, u32[]{:S(2)}) %collective-permute-start.15) | collective-permute-done | bytes 262176 | tf_op jit(solution)/shard_map/ppermute | solution.py:414
  236.2 1.3 collective-permute-done.14
  237.5 0.2 fusion.9
  237.8 1.6 collective-permute-start.18
  239.4 1.9 collective-permute-start.17
  241.3 0.7 fusion.2
  242.1 2.0 collective-permute-done.18
  244.1 1.6 collective-permute-done.17
  245.7 0.7 fusion.5
  (42 shorter events, 1.3 us)
Async XLA Ops:
  2.0 14.4 %all-to-all-start = ((s32[32,1,128]{2,1,0:T(1,128)}), s32[32,1,128]{2,1,0:T(1,128)S(1)}, u32[]{:S(2)}, u32[]{:S(2)}) async-start(s32[32,1,128]{2,1,0:T(1,128)} %bitcast.43), calls=%async_computation | async-start | bytes 32768 | tf_op jit(solution)/shard_map/all_to_all | solution.py:33
  16.4 0.6 copy-start.5
  83.2 58.4 %all-to-all-start.1 = ((bf16[32,2,128,128]{3,2,1,0:T(8,128)(2,1)}), bf16[32,2,128,128]{3,2,1,0:T(8,128)(2,1)S(1)}, u32[]{:S(2)}, u32[]{:S(2)}) async-start(bf16[32,2,128,128]{3,2,1,0:T(8,128)(2,1)} %pick_modes.1), calls=%async_computation.1 | async-start | bytes 4194304 | tf_op jit(solution)/shard_map/all_to_all | solution.py:33
  95.4 5.3 %collective-permute-start = (bf16[4,264,128]{2,1,0:T(8,128)(2,1)}, bf16[4,264,128]{2,1,0:T(8,128)(2,1)S(1)}, u32[]{:S(2)}, u32[]{:S(2)}) collective-permute-start(bf16[4,264,128]{2,1,0:T(8,128)(2,1)} %get-tuple-element.27), channel_id=1, source_target_pairs={{0,1},{1,0},{2,3},{3,2},{4,5},{5,4},{6,7},{7,6},{8,9},{9,8},{10,11... | collective-permute-start | bytes 811016 | tf_op jit(solution)/shard_map/ppermute | solution.py:414
  95.6 17.0 %collective-permute-start.1 = (bf16[4,264,128]{2,1,0:T(8,128)(2,1)}, bf16[4,264,128]{2,1,0:T(8,128)(2,1)S(1)}, u32[]{:S(2)}, u32[]{:S(2)}) collective-permute-start(bf16[4,264,128]{2,1,0:T(8,128)(2,1)} %get-tuple-element.28), channel_id=1, source_target_pairs={{0,2},{1,3},{2,0},{3,1},{4,6},{5,7},{6,4},{7,5},{8,10},{9,11},{10,... | collective-permute-start | bytes 811016 | tf_op jit(solution)/shard_map/ppermute | solution.py:414
  97.3 23.0 %collective-permute-start.2 = (bf16[4,264,128]{2,1,0:T(8,128)(2,1)}, bf16[4,264,128]{2,1,0:T(8,128)(2,1)S(1)}, u32[]{:S(2)}, u32[]{:S(2)}) collective-permute-start(bf16[4,264,128]{2,1,0:T(8,128)(2,1)} %get-tuple-element.29), channel_id=1, source_target_pairs={{0,3},{1,2},{2,1},{3,0},{4,7},{5,6},{6,5},{7,4},{8,11},{9,10},{10,... | collective-permute-start | bytes 811016 | tf_op jit(solution)/shard_map/ppermute | solution.py:414
  97.4 26.3 %collective-permute-start.3 = (bf16[4,264,128]{2,1,0:T(8,128)(2,1)}, bf16[4,264,128]{2,1,0:T(8,128)(2,1)S(1)}, u32[]{:S(2)}, u32[]{:S(2)}) collective-permute-start(bf16[4,264,128]{2,1,0:T(8,128)(2,1)} %get-tuple-element.30), channel_id=1, source_target_pairs={{0,4},{1,5},{2,6},{3,7},{4,0},{5,1},{6,2},{7,3},{8,12},{9,13},{10,... | collective-permute-start | bytes 811016 | tf_op jit(solution)/shard_map/ppermute | solution.py:414
  99.0 62.1 %collective-permute-start.4 = (bf16[4,264,128]{2,1,0:T(8,128)(2,1)}, bf16[4,264,128]{2,1,0:T(8,128)(2,1)}, u32[]{:S(2)}, u32[]{:S(2)}) collective-permute-start(bf16[4,264,128]{2,1,0:T(8,128)(2,1)} %get-tuple-element.31), channel_id=1, source_target_pairs={{0,5},{1,4},{2,7},{3,6},{4,1},{5,0},{6,3},{7,2},{8,13},{9,12},{10,... | collective-permute-start | bytes 811016 | tf_op jit(solution)/shard_map/ppermute | solution.py:414
  100.7 62.2 %collective-permute-start.5 = (bf16[4,264,128]{2,1,0:T(8,128)(2,1)}, bf16[4,264,128]{2,1,0:T(8,128)(2,1)S(1)}, u32[]{:S(2)}, u32[]{:S(2)}) collective-permute-start(bf16[4,264,128]{2,1,0:T(8,128)(2,1)} %get-tuple-element.32), channel_id=1, source_target_pairs={{0,6},{1,7},{2,4},{3,5},{4,2},{5,3},{6,0},{7,1},{8,14},{9,15},{10,... | collective-permute-start | bytes 811016 | tf_op jit(solution)/shard_map/ppermute | solution.py:414
  112.7 51.5 %collective-permute-start.6 = (bf16[4,264,128]{2,1,0:T(8,128)(2,1)}, bf16[4,264,128]{2,1,0:T(8,128)(2,1)S(1)}, u32[]{:S(2)}, u32[]{:S(2)}) collective-permute-start(bf16[4,264,128]{2,1,0:T(8,128)(2,1)} %get-tuple-element.33), channel_id=1, source_target_pairs={{0,7},{1,6},{2,5},{3,4},{4,3},{5,2},{6,1},{7,0},{8,15},{9,14},{10,... | collective-permute-start | bytes 811016 | tf_op jit(solution)/shard_map/ppermute | solution.py:414
  120.3 44.6 %collective-permute-start.8 = (bf16[2,264,128]{2,1,0:T(8,128)(2,1)}, bf16[2,264,128]{2,1,0:T(8,128)(2,1)S(1)}, u32[]{:S(2)}, u32[]{:S(2)}) collective-permute-start(bf16[2,264,128]{2,1,0:T(8,128)(2,1)} %pad_maximum_fusion), channel_id=1, source_target_pairs={{0,16},{1,17},{2,18},{3,19},{4,20},{5,21},{6,22},{7,23},{8,24},{9,... | collective-permute-start | bytes 405512 | tf_op jit(solution)/shard_map/ppermute | solution.py:414
  123.7 42.3 %collective-permute-start.10 = (bf16[2,264,128]{2,1,0:T(8,128)(2,1)}, bf16[2,264,128]{2,1,0:T(8,128)(2,1)}, u32[]{:S(2)}, u32[]{:S(2)}) collective-permute-start(bf16[2,264,128]{2,1,0:T(8,128)(2,1)} %pad_maximum_fusion.1), channel_id=1, source_target_pairs={{0,24},{1,25},{2,26},{3,27},{4,28},{5,29},{6,30},{7,31},{8,16},{9,... | collective-permute-start | bytes 405512 | tf_op jit(solution)/shard_map/ppermute | solution.py:414
  141.6 1.3 copy-start
  155.3 24.3 %copy-start.6 = (s32[32,1,128]{2,1,0:T(1,128)S(1)}, s32[32,1,128]{2,1,0:T(1,128)}, u32[]{:S(2)}) copy-start(s32[32,1,128]{2,1,0:T(1,128)} %copy-done.5) | copy-start | bytes 49156
  161.2 49.0 %collective-permute-start.19 = (bf16[16,32,1024]{2,1,0:T(8,128)(2,1)}, bf16[16,32,1024]{2,1,0:T(8,128)(2,1)}, u32[]{:S(2)}, u32[]{:S(2)}) collective-permute-start(bf16[16,32,1024]{2,1,0:T(8,128)(2,1)} %get-tuple-element.45), channel_id=1, source_target_pairs={{0,1},{1,0},{2,3},{3,2},{4,5},{5,4},{6,7},{7,6},{8,9},{9,8},{10,11... | collective-permute-start | bytes 3145736 | tf_op jit(solution)/shard_map/ppermute | solution.py:414
  162.9 52.3 %collective-permute-start.12 = (bf16[16,32,1024]{2,1,0:T(8,128)(2,1)}, bf16[16,32,1024]{2,1,0:T(8,128)(2,1)S(1)}, u32[]{:S(2)}, u32[]{:S(2)}) collective-permute-start(bf16[16,32,1024]{2,1,0:T(8,128)(2,1)} %get-tuple-element.40), channel_id=1, source_target_pairs={{0,1},{1,0},{2,3},{3,2},{4,5},{5,4},{6,7},{7,6},{8,9},{9,8},{10,11... | collective-permute-start | bytes 3145736 | tf_op jit(solution)/shard_map/ppermute | solution.py:414
  164.8 38.8 %copy-start.3 = (bf16[8,264,128]{2,1,0:T(8,128)(2,1)}, bf16[8,264,128]{2,1,0:T(8,128)(2,1)S(1)}, u32[]{:S(2)}) copy-start(bf16[8,264,128]{2,1,0:T(8,128)(2,1)S(1)} %get-tuple-element.62.refs_3_) | copy-start | bytes 1622020
  164.8 38.8 %collective-permute-start.7 = (bf16[8,264,128]{2,1,0:T(8,128)(2,1)}, bf16[8,264,128]{2,1,0:T(8,128)(2,1)S(1)}, u32[]{:S(2)}, u32[]{:S(2)}) collective-permute-start(bf16[8,264,128]{2,1,0:T(8,128)(2,1)} %get-tuple-element.61), channel_id=1, source_target_pairs={{0,8},{1,9},{2,10},{3,11},{4,12},{5,13},{6,14},{7,15},{8,0},{9,1},... | collective-permute-start | bytes 1622024 | tf_op jit(solution)/shard_map/ppermute | solution.py:414
  164.9 1.2 copy-start.9
  164.9 23.3 %collective-permute-start.11 = (bf16[6,264,128]{2,1,0:T(8,128)(2,1)}, bf16[6,264,128]{2,1,0:T(8,128)(2,1)S(1)}, u32[]{:S(2)}, u32[]{:S(2)}) collective-permute-start(bf16[6,264,128]{2,1,0:T(8,128)(2,1)} %get-tuple-element.59), channel_id=1, source_target_pairs={{0,24},{1,25},{2,26},{3,27},{4,28},{5,29},{6,30},{7,31},{8,16},{9,... | collective-permute-start | bytes 1216520 | tf_op jit(solution)/shard_map/ppermute | solution.py:414
  166.0 37.6 %collective-permute-start.9 = (bf16[6,264,128]{2,1,0:T(8,128)(2,1)}, bf16[6,264,128]{2,1,0:T(8,128)(2,1)S(1)}, u32[]{:S(2)}, u32[]{:S(2)}) collective-permute-start(bf16[6,264,128]{2,1,0:T(8,128)(2,1)} %get-tuple-element.60), channel_id=1, source_target_pairs={{0,16},{1,17},{2,18},{3,19},{4,20},{5,21},{6,22},{7,23},{8,24},{9,... | collective-permute-start | bytes 1216520 | tf_op jit(solution)/shard_map/ppermute | solution.py:414
  188.1 15.5 %copy-start.7 = (bf16[6,264,128]{2,1,0:T(8,128)(2,1)}, bf16[6,264,128]{2,1,0:T(8,128)(2,1)S(1)}, u32[]{:S(2)}) copy-start(bf16[6,264,128]{2,1,0:T(8,128)(2,1)S(1)} %collective-permute-done.11.refs_8_) | copy-start | bytes 1216516
  203.6 0.8 copy-start.8
  203.6 1.0 copy-start.4
  204.6 5.6 %copy-start.2 = (f32[16,32,1024]{2,1,0:T(8,128)S(1)}, f32[16,32,1024]{2,1,0:T(8,128)}, u32[]{:S(2)}) copy-start(f32[16,32,1024]{2,1,0:T(8,128)} %get-tuple-element.44) | copy-start | bytes 6291460
  210.2 5.1 %copy-start.1 = (f32[16,32,1024]{2,1,0:T(8,128)S(1)}, f32[16,32,1024]{2,1,0:T(8,128)}, u32[]{:S(2)}) copy-start(f32[16,32,1024]{2,1,0:T(8,128)} %get-tuple-element.39) | copy-start | bytes 6291460
  211.7 9.2 %collective-permute-start.20 = (bf16[4,32,1024]{2,1,0:T(8,128)(2,1)S(1)}, bf16[4,32,1024]{2,1,0:T(8,128)(2,1)S(1)}, u32[]{:S(2)}, u32[]{:S(2)}) collective-permute-start(bf16[4,32,1024]{2,1,0:T(8,128)(2,1)S(1)} %get-tuple-element.53), channel_id=1, source_target_pairs={{0,2},{1,3},{2,0},{3,1},{4,6},{5,7},{6,4},{7,5},{8,10},{9,11},{10,... | collective-permute-start | bytes 786440 | tf_op jit(solution)/shard_map/ppermute | solution.py:414
  212.8 14.2 %collective-permute-start.22 = (bf16[4,32,1024]{2,1,0:T(8,128)(2,1)S(1)}, bf16[4,32,1024]{2,1,0:T(8,128)(2,1)S(1)}, u32[]{:S(2)}, u32[]{:S(2)}) collective-permute-start(bf16[4,32,1024]{2,1,0:T(8,128)(2,1)S(1)} %get-tuple-element.54), channel_id=1, source_target_pairs={{0,6},{1,7},{2,4},{3,5},{4,2},{5,3},{6,0},{7,1},{8,14},{9,15},{10,... | collective-permute-start | bytes 786440 | tf_op jit(solution)/shard_map/ppermute | solution.py:414
  214.1 14.7 %collective-permute-start.21 = (bf16[4,32,1024]{2,1,0:T(8,128)(2,1)S(1)}, bf16[4,32,1024]{2,1,0:T(8,128)(2,1)S(1)}, u32[]{:S(2)}, u32[]{:S(2)}) collective-permute-start(bf16[4,32,1024]{2,1,0:T(8,128)(2,1)S(1)} %get-tuple-element.55), channel_id=1, source_target_pairs={{0,4},{1,5},{2,6},{3,7},{4,0},{5,1},{6,2},{7,3},{8,12},{9,13},{10,... | collective-permute-start | bytes 786440 | tf_op jit(solution)/shard_map/ppermute | solution.py:414
  215.5 16.7 %collective-permute-start.13 = (bf16[4,32,1024]{2,1,0:T(8,128)(2,1)S(1)}, bf16[4,32,1024]{2,1,0:T(8,128)(2,1)S(1)}, u32[]{:S(2)}, u32[]{:S(2)}) collective-permute-start(bf16[4,32,1024]{2,1,0:T(8,128)(2,1)S(1)} %get-tuple-element.56), channel_id=1, source_target_pairs={{0,2},{1,3},{2,0},{3,1},{4,6},{5,7},{6,4},{7,5},{8,10},{9,11},{10,... | collective-permute-start | bytes 786440 | tf_op jit(solution)/shard_map/ppermute | solution.py:414
  216.6 19.6 %collective-permute-start.15 = (bf16[4,32,1024]{2,1,0:T(8,128)(2,1)S(1)}, bf16[4,32,1024]{2,1,0:T(8,128)(2,1)S(1)}, u32[]{:S(2)}, u32[]{:S(2)}) collective-permute-start(bf16[4,32,1024]{2,1,0:T(8,128)(2,1)S(1)} %get-tuple-element.57), channel_id=1, source_target_pairs={{0,6},{1,7},{2,4},{3,5},{4,2},{5,3},{6,0},{7,1},{8,14},{9,15},{10,... | collective-permute-start | bytes 786440 | tf_op jit(solution)/shard_map/ppermute | solution.py:414
  220.9 16.6 %collective-permute-start.14 = (bf16[4,32,1024]{2,1,0:T(8,128)(2,1)S(1)}, bf16[4,32,1024]{2,1,0:T(8,128)(2,1)S(1)}, u32[]{:S(2)}, u32[]{:S(2)}) collective-permute-start(bf16[4,32,1024]{2,1,0:T(8,128)(2,1)S(1)} %get-tuple-element.58), channel_id=1, source_target_pairs={{0,4},{1,5},{2,6},{3,7},{4,0},{5,1},{6,2},{7,3},{8,12},{9,13},{10,... | collective-permute-start | bytes 786440 | tf_op jit(solution)/shard_map/ppermute | solution.py:414
  230.1 9.3 %collective-permute-start.23 = (bf16[32,1024]{1,0:T(8,128)(2,1)S(1)}, bf16[32,1024]{1,0:T(8,128)(2,1)S(1)}, u32[]{:S(2)}, u32[]{:S(2)}) collective-permute-start(bf16[32,1024]{1,0:T(8,128)(2,1)S(1)} %get-tuple-element.91), channel_id=1, source_target_pairs={{0,8},{1,9},{2,10},{3,11},{4,12},{5,13},{6,14},{7,15},{8,0},{9,1},... | collective-permute-start | bytes 196616 | tf_op jit(solution)/shard_map/ppermute | solution.py:414
  230.1 11.2 %collective-permute-start.25 = (bf16[32,1024]{1,0:T(8,128)(2,1)S(1)}, bf16[32,1024]{1,0:T(8,128)(2,1)S(1)}, u32[]{:S(2)}, u32[]{:S(2)}) collective-permute-start(bf16[32,1024]{1,0:T(8,128)(2,1)S(1)} %get-tuple-element.92), channel_id=1, source_target_pairs={{0,24},{1,25},{2,26},{3,27},{4,28},{5,29},{6,30},{7,31},{8,16},{9,... | collective-permute-start | bytes 196616 | tf_op jit(solution)/shard_map/ppermute | solution.py:414
  232.2 9.1 %collective-permute-start.24 = (bf16[32,1024]{1,0:T(8,128)(2,1)S(1)}, bf16[32,1024]{1,0:T(8,128)(2,1)S(1)}, u32[]{:S(2)}, u32[]{:S(2)}) collective-permute-start(bf16[32,1024]{1,0:T(8,128)(2,1)S(1)} %get-tuple-element.93), channel_id=1, source_target_pairs={{0,16},{1,17},{2,18},{3,19},{4,20},{5,21},{6,22},{7,23},{8,24},{9,... | collective-permute-start | bytes 196616 | tf_op jit(solution)/shard_map/ppermute | solution.py:414
  237.8 4.3 %collective-permute-start.16 = (bf16[32,1024]{1,0:T(8,128)(2,1)S(1)}, bf16[32,1024]{1,0:T(8,128)(2,1)S(1)}, u32[]{:S(2)}, u32[]{:S(2)}) collective-permute-start(bf16[32,1024]{1,0:T(8,128)(2,1)S(1)} %get-tuple-element.94), channel_id=1, source_target_pairs={{0,8},{1,9},{2,10},{3,11},{4,12},{5,13},{6,14},{7,15},{8,0},{9,1},... | collective-permute-start | bytes 196616 | tf_op jit(solution)/shard_map/ppermute | solution.py:414
  237.8 6.2 %collective-permute-start.18 = (bf16[32,1024]{1,0:T(8,128)(2,1)S(1)}, bf16[32,1024]{1,0:T(8,128)(2,1)S(1)}, u32[]{:S(2)}, u32[]{:S(2)}) collective-permute-start(bf16[32,1024]{1,0:T(8,128)(2,1)S(1)} %get-tuple-element.95), channel_id=1, source_target_pairs={{0,24},{1,25},{2,26},{3,27},{4,28},{5,29},{6,30},{7,31},{8,16},{9,... | collective-permute-start | bytes 196616 | tf_op jit(solution)/shard_map/ppermute | solution.py:414
  239.4 6.3 %collective-permute-start.17 = (bf16[32,1024]{1,0:T(8,128)(2,1)S(1)}, bf16[32,1024]{1,0:T(8,128)(2,1)S(1)}, u32[]{:S(2)}, u32[]{:S(2)}) collective-permute-start(bf16[32,1024]{1,0:T(8,128)(2,1)S(1)} %get-tuple-element.96), channel_id=1, source_target_pairs={{0,16},{1,17},{2,18},{3,19},{4,20},{5,21},{6,22},{7,23},{8,24},{9,... | collective-permute-start | bytes 196616 | tf_op jit(solution)/shard_map/ppermute | solution.py:414

commit v8 on v6

--- a/solution.py
+++ b/solution.py
@@ -90,19 +90,31 @@
     device_count = table.shape[0]
     width = modes.shape[1]
 
-    def kernel(table_ref, modes_ref, out_ref):
-        def one(device, carry):
+    def kernel(table_ref, modes_ref, out_ref, sem):
+        def copy(device, h):
+            return pltpu.make_async_copy(
+                modes_ref.at[table_ref[device, h]], out_ref.at[device, h], sem.at[device, h]
+            )
+
+        def start(device, carry):
             for h in range(ratio):
-                out_ref[device, h] = modes_ref[table_ref[device, h]]
+                copy(device, h).start()
             return carry
 
-        lax.fori_loop(0, device_count, one, 0, unroll=4)
+        def wait(device, carry):
+            for h in range(ratio):
+                copy(device, h).wait()
+            return carry
+
+        lax.fori_loop(0, device_count, start, 0, unroll=4)
+        lax.fori_loop(0, device_count, wait, 0, unroll=4)
 
     return pl.pallas_call(
         kernel,
         out_shape=jax.ShapeDtypeStruct((device_count, ratio, width, BLK), BF16),
         in_specs=[SMEM, VMEM],
-        out_specs=VMEM,
+        out_specs=ANY,
+        scratch_shapes=[pltpu.SemaphoreType.DMA((device_count, ratio))],
         name="pick_modes",
     )(table, modes)
 
@@ -125,7 +137,8 @@
         d_ref,
         *refs,
     ):
-        near_refs, out_ref, sem = refs[: sizes.plane], refs[-2], refs[-1]
+        stiff_refs, mass_refs = refs[: sizes.plane], refs[sizes.plane : 2 * sizes.plane]
+        out_k_ref, out_m_ref, sem = refs[-3:]
         sub = pl.program_id(0)
         me = lax.axis_index("row") * sizes.cols + lax.axis_index("col")
         couple = cpl_ref[0]
@@ -176,22 +189,25 @@
                     low = diagonal - high - middle
                     parts = jnp.where(level == 0, high, jnp.where(level == 1, middle, low))
                     share = quotient(block_a, sizes.share_blocks) ^ me
-                    out_ref[
+                    out_m_ref[
                         remainder(share, sizes.plane),
                         quotient(share, sizes.plane),
-                        2 * BLK : 2 * BLK + EXTRA,
+                        BLK : BLK + EXTRA,
                     ] = parts.astype(BF16)
                     mass_block = jnp.where(eye, 0.0, mass_block)
                 mass_block = mass_block.astype(BF16)
-                out_ref[near, far, :BLK] = stiff_block
-                out_ref[near, far, BLK : 2 * BLK] = mass_block
+                out_k_ref[near, far] = stiff_block
+                out_m_ref[near, far, :BLK] = mass_block
                 k_ref[0, rows, cols] = stiff_block
                 m_ref[0, rows, cols] = mass_block
 
         @pl.when(sub == local_subs - 1)
         def _():
             copies = [
-                pltpu.make_async_copy(out_ref.at[d], ref, sem.at[d])
+                pltpu.make_async_copy(held.at[d], ref, sem.at[i, d])
+                for i, (held, near_refs) in enumerate(
+                    ((out_k_ref, stiff_refs), (out_m_ref, mass_refs))
+                )
                 for d, ref in enumerate(near_refs)
             ]
             for copy in copies:
@@ -202,7 +218,8 @@
     def piece(*shape):
         return pl.BlockSpec((1,) + shape, lambda s: (s, 0, 0))
 
-    out_blocks = (sizes.devices // sizes.plane, 2 * BLK + EXTRA, BLK)
+    out_k = (sizes.devices // sizes.plane, BLK, BLK)
+    out_m = (sizes.devices // sizes.plane, BLK + EXTRA, BLK)
     return pl.pallas_call(
         kernel,
         grid=(local_subs,),
@@ -219,16 +236,18 @@
             piece(boundary, boundary),
             piece(1, boundary),
         ]
-        + [ANY] * sizes.plane,
+        + [ANY] * (2 * sizes.plane),
         out_shape=[
             jax.ShapeDtypeStruct((local_subs, boundary, boundary), BF16),
             jax.ShapeDtypeStruct((local_subs, boundary, boundary), BF16),
             jax.ShapeDtypeStruct((local_subs, 1, boundary), F32),
         ]
-        + [jax.ShapeDtypeStruct(out_blocks, BF16)] * sizes.plane,
+        + [jax.ShapeDtypeStruct(out_k, BF16)] * sizes.plane
+        + [jax.ShapeDtypeStruct(out_m, BF16)] * sizes.plane,
         scratch_shapes=[
-            pltpu.VMEM((sizes.plane,) + out_blocks, BF16),
-            pltpu.SemaphoreType.DMA((sizes.plane,)),
+            pltpu.VMEM((sizes.plane,) + out_k, BF16),
+            pltpu.VMEM((sizes.plane,) + out_m, BF16),
+            pltpu.SemaphoreType.DMA((2, sizes.plane)),
         ],
         name="condense",
     )(
@@ -422,7 +441,32 @@
     near = [blocks[0]]
     for d in range(1, sizes.plane):
         near.append(swap(blocks[d], d, sizes.devices))
-    return [jnp.stack([part[z] for part in near]) for z in range(sizes.devices // sizes.plane)]
+    return near
+
+
+def regroup(near):
+    plane, (depth, height, _) = len(near), near[0].shape
+
+    def kernel(*refs):
+        in_refs, out_refs, sem = refs[:plane], refs[plane : plane + depth], refs[-1]
+        copies = [
+            pltpu.make_async_copy(in_ref.at[z], out_ref.at[d], sem.at[d, z])
+            for d, in_ref in enumerate(in_refs)
+            for z, out_ref in enumerate(out_refs)
+        ]
+        for copy in copies:
+            copy.start()
+        for copy in copies:
+            copy.wait()
+
+    return pl.pallas_call(
+        kernel,
+        in_specs=[VMEM] * plane,
+        out_specs=[ANY] * depth,
+        out_shape=[jax.ShapeDtypeStruct((plane, height, BLK), BF16)] * depth,
+        scratch_shapes=[pltpu.SemaphoreType.DMA((plane, depth))],
+        name="regroup",
+    )(*near)
 
 
 def clear_tiles(table, sizes):
@@ -453,16 +497,18 @@
     )(table)
 
 
-def place(table, order, slots, arrived, stiff_tile, mass_tile, sizes):
+def place(table, order, slots, arrived, tile, sizes):
     count = sizes.devices
     limit = sizes.row_blocks * sizes.col_blocks
     depth = len(arrived)
-    height = 2 * BLK + EXTRA
+    height = arrived[0].shape[1]
+    shared = height > BLK
 
     def kernel(*refs):
         table_ref, order_ref, slot_ref = refs[:3]
         in_refs = refs[3 : 3 + depth]
-        stiff_ref, mass_ref, share_ref, held_ref, sums_ref, in_sem, sem = refs[-7:]
+        tile_ref = refs[4 + depth]
+        held_ref, sums_ref, in_sem, sem = refs[-4:]
         me = lax.axis_index("row") * sizes.cols + lax.axis_index("col")
         loads = [
             pltpu.make_async_copy(
@@ -475,18 +521,13 @@
         for load in loads:
             load.wait()
 
-        def copies(j):
+        def copy(j):
             slot = slot_ref[j]
             row = pl.multiple_of(quotient(slot, sizes.col_blocks) * BLK, BLK)
             col = pl.multiple_of(remainder(slot, sizes.col_blocks) * BLK, BLK)
-            return [
-                pltpu.make_async_copy(
-                    sums_ref.at[j, pl.ds(i * BLK, BLK)],
-                    ref.at[pl.ds(row, BLK), pl.ds(col, BLK)],
-                    sem.at[j, i],
-                )
-                for i, ref in enumerate((stiff_ref, mass_ref))
-            ]
+            return pltpu.make_async_copy(
+                sums_ref.at[j], tile_ref.at[pl.ds(row, BLK), pl.ds(col, BLK)], sem.at[j]
+            )
 
         def last(j):
             ahead = slot_ref[jnp.minimum(j + 1, count - 1)]
@@ -494,61 +535,60 @@
             return jnp.logical_and(slot_ref[j] < limit, ends)
 
         def one(j, total):
-            block = held_ref[order_ref[j] ^ me, : 2 * BLK].astype(F32)
+            block = held_ref[order_ref[j] ^ me, :BLK].astype(F32)
             same = jnp.logical_and(j > 0, slot_ref[jnp.maximum(j - 1, 0)] == slot_ref[j])
             total = jnp.where(same, total + block, block)
             sums_ref[j] = total.astype(BF16)
 
             @pl.when(last(j))
             def _():
-                for copy in copies(j):
-                    copy.start()
+                copy(j).start()
 
             return total
 
-        lax.fori_loop(0, count, one, jnp.zeros((2 * BLK, BLK), F32))
-        share_ref[...] = jnp.zeros_like(share_ref)
-
-        def add(device, carry):
-            share = table_ref[device, sizes.ratio + 1]
-
-            @pl.when(share >= 0)
-            def _():
-                parts = held_ref[device ^ me, 2 * BLK : 2 * BLK + EXTRA].astype(F32)
-                share_ref[share] += parts[0:1] + parts[1:2] + parts[2:3]
-
-            return carry
-
-        lax.fori_loop(0, count, add, 0)
+        lax.fori_loop(0, count, one, jnp.zeros((BLK, BLK), F32))
+        if shared:
+            share_ref = refs[5 + depth]
+            share_ref[...] = jnp.zeros_like(share_ref)
+
+            def add(device, carry):
+                share = table_ref[device, sizes.ratio + 1]
+
+                @pl.when(share >= 0)
+                def _():
+                    parts = held_ref[device ^ me, BLK : BLK + EXTRA].astype(F32)
+                    share_ref[share] += parts[0:1] + parts[1:2] + parts[2:3]
+
+                return carry
+
+            lax.fori_loop(0, count, add, 0)
 
         def wait(j, carry):
             @pl.when(last(j))
             def _():
-                for copy in copies(j):
-                    copy.wait()
+                copy(j).wait()
 
             return carry
 
         lax.fori_loop(0, count, wait, 0)
 
-    return pl.pallas_call(
-        kernel,
-        in_specs=[SMEM, SMEM, SMEM] + [ANY] * (depth + 2),
-        out_specs=[ANY, ANY, VMEM],
-        out_shape=[
-            jax.ShapeDtypeStruct(stiff_tile.shape, BF16),
-            jax.ShapeDtypeStruct(mass_tile.shape, BF16),
-            jax.ShapeDtypeStruct((sizes.share_blocks, 1, BLK), F32),
-        ],
-        input_output_aliases={3 + depth: 0, 4 + depth: 1},
+    out_shape = [jax.ShapeDtypeStruct(tile.shape, BF16)]
+    if shared:
+        out_shape.append(jax.ShapeDtypeStruct((sizes.share_blocks, 1, BLK), F32))
+    return pl.pallas_call(
+        kernel,
+        in_specs=[SMEM, SMEM, SMEM] + [ANY] * (depth + 1),
+        out_specs=[ANY, VMEM][: len(out_shape)],
+        out_shape=out_shape,
+        input_output_aliases={3 + depth: 0},
         scratch_shapes=[
             pltpu.VMEM((count, height, BLK), BF16),
-            pltpu.VMEM((count, 2 * BLK, BLK), BF16),
+            pltpu.VMEM((count, BLK, BLK), BF16),
             pltpu.SemaphoreType.DMA((depth,)),
-            pltpu.SemaphoreType.DMA((count, 2)),
-        ],
-        name="place",
-    )(table, order, slots, *arrived, stiff_tile, mass_tile)
+            pltpu.SemaphoreType.DMA((count,)),
+        ],
+        name="place_mass" if shared else "place_stiff",
+    )(table, order, slots, *arrived, tile)
 
 
 def reduction(inv_interior, coupling, boundary_stiff, mass_interior, mass_boundary, block_map, modes):
@@ -576,14 +616,19 @@
     stiff, mass, diagonal, *blocks = condense(
         block_map, inv_interior, coupling, boundary_stiff, mass_interior, mass_boundary, sizes
     )
-    spread = spread_in_plane(blocks, sizes)
-    beside = swap(spread[1], sizes.plane, sizes.devices)
     stiff_tile, mass_tile = clear_tiles(table, sizes)
-    late, fetched, stiff_tile, mass_tile = lax.optimization_barrier(
-        (spread[2:], fetched, stiff_tile, mass_tile)
-    )
-    late = [swap(part, (2 + d) * sizes.plane, sizes.devices) for d, part in enumerate(late)]
-    arrived = [spread[0], beside, *late]
+    near_stiff = spread_in_plane(blocks[: sizes.plane], sizes)
+    near_mass = spread_in_plane(blocks[sizes.plane :], sizes)
+
+    def along_line(near):
+        parts = regroup(near)
+        arrived = [parts[0]]
+        for d in range(1, dims[0]):
+            arrived.append(swap(parts[d], d * sizes.plane, sizes.devices))
+        return arrived
+
+    stiff_arrived = along_line(near_stiff)
+    mass_arrived = along_line(near_mass)
 
     fetched = fetched.reshape(row_count, col_count, sizes.ratio, width, BLK)
     send, keep, qt = project_stiff(block_map, fetched, stiff, dims, sizes.row_blocks)
@@ -602,9 +647,8 @@
     chosen = rank[None, :] == ids[:, None]
     order = jnp.sum(jnp.where(chosen, ids[None, :], 0), axis=1)
     slots = jnp.sum(jnp.where(chosen, slot[None, :], 0), axis=1)
-    stiff_tile, mass_tile, mass_share = place(
-        table, order, slots, arrived, stiff_tile, mass_tile, sizes
-    )
+    (stiff_tile,) = place(table, order, slots, stiff_arrived, stiff_tile, sizes)
+    mass_tile, mass_share = place(table, order, slots, mass_arrived, mass_tile, sizes)
     return stiff_tile, mass_tile, reduced_stiff, reduced_mass, mass_share.reshape(-1)
 
 

time: 189 us -> 218 us (1.15)
  waiting for transfers between devices: 67.6 us -> 89.4 us
  local copies, waits for them, and re-layouts: 13.8 us -> 5.38 us
  Pallas kernels: 48.8 us -> 57 us
  starting transfers between devices: 51.7 us -> 59.3 us
    all_to_all x2, waiting for transfers between devices: 4.84 us -> 40.6 us  [exchange(): return lax.all_to_all(value, AXES, split_axis=0, concat_axis=0, tiled=True)]
    ppermute x24 -> x34, waiting for transfers between devices: 62.8 us -> 48.8 us  [swap(): lax.ppermute(value, AXES, [(i, i ^ offset) for i in range(device_count)])]
    pallas_call x1 -> x4, Pallas kernels: 5.55 us -> 13.6 us  [the longest x2 8.41 us: place(): pl.pallas_call(kernel, in_specs=[SMEM, SMEM, SMEM] + [ANY] * (depth + 1),...]
    unnamed x29 -> x66, local copies, waits for them, and re-layouts: 10.7 us -> 2.9 us
    ppermute x24 -> x34, starting transfers between devices: 41.7 us -> 49.2 us  [swap(): lax.ppermute(value, AXES, [(i, i ^ offset) for i in range(device_count)])]
  transfers between devices with their start and end apart: 26 -> 36, of which waited for: 9 -> 16; matrix products, arithmetic and copies ran while one was open for 8% -> 3% of each run, Pallas kernels for 14% -> 24%
where the time goes in v8:
time: 218 us; the launch traced here: 217 us
  waiting for transfers between devices  89.4 us (41%)
  starting transfers between devices  59.3 us (27%)
  Pallas kernels  57 us (26%)
  local copies, waits for them, and re-layouts  5.38 us (2%)
  other arithmetic  5.2 us (2%)
    ppermute x34, starting transfers between devices, swap(): lax.ppermute(value, AXES, [(i, i ^ offset) for i in range(device_count)])  49.2 us
    ppermute x34, waiting for transfers between devices, swap(): lax.ppermute(value, AXES, [(i, i ^ offset) for i in range(device_count)])  48.8 us
    all_to_all x2, waiting for transfers between devices, exchange(): return lax.all_to_all(value, AXES, split_axis=0, concat_axis=0, tiled=True)  40.6 us
    pallas_call x1, Pallas kernels, clear_tiles(): pl.pallas_call(kernel, in_specs=[ANY], out_specs=[ANY, ANY], out_shape=[j...  11.2 us
    all_to_all x2, starting transfers between devices, exchange(): return lax.all_to_all(value, AXES, split_axis=0, concat_axis=0, tiled=True)  10.1 us
    pallas_call x1, Pallas kernels, condense(): pl.pallas_call(kernel, grid=(local_subs,), in_specs=[SMEM, piece(interior...  9.45 us
    pallas_call x2, Pallas kernels, place(): pl.pallas_call(kernel, in_specs=[SMEM, SMEM, SMEM] + [ANY] * (depth + 1),...  8.41 us
    pallas_call x1, Pallas kernels, project_stiff(): pl.pallas_call(kernel, grid=(2,), in_specs=[SMEM, whole(*fetched.shape),...  7.44 us
  transfers between devices with their start and end apart: 36, of which 16 were waited for; matrix products, arithmetic and copies ran while one was open for 3% of the time, Pallas kernels for 24%

profile of v8, /device:TPU:0, one launch (start us, length us, event | category | flops | bytes accessed | tf_op | source)
XLA Modules:
  0.0 217.4 jit_solution(1939614032300167931)
XLA Ops:
  0.6 1.4 describe.1
  2.0 7.3 %all-to-all-start = ((s32[32,1,128]{2,1,0:T(1,128)}), s32[32,1,128]{2,1,0:T(1,128)S(1)}, u32[]{:S(2)}, u32[]{:S(2)}) async-start(s32[32,1,128]{2,1,0:T(1,128)} %bitcast.44), calls=%async_computation | async-start | bytes 32768 | tf_op jit(solution)/shard_map/all_to_all | solution.py:32
  9.3 2.3 %copy.18 = bf16[32,128,128]{1,2,0:T(8,128)(2,1)} copy(bf16[32,128,128]{2,1,0:T(8,128)(2,1)} %bitcast.38) | data formatting | bytes 2097152 | tf_op jit(solution)/shard_map/reshape | solution.py:613
  11.6 4.8 %all-to-all-done = s32[32,1,128]{2,1,0:T(1,128)S(1)} async-done(((s32[32,1,128]{2,1,0:T(1,128)}), s32[32,1,128]{2,1,0:T(1,128)S(1)}, u32[]{:S(2)}, u32[]{:S(2)}) %all-to-all-start) | async-done | bytes 16416 | tf_op jit(solution)/shard_map/all_to_all | solution.py:32
  16.4 0.6 copy-done.3
  17.0 3.1 %pick_modes.1 = bf16[32,2,128,128]{3,2,1,0:T(8,128)(2,1)} custom-call(s32[32,128]{1,0:T(8,128)} %bitcast.39, bf16[32,128,128]{2,1,0:T(8,128)(2,1)} %bitcast.37), custom_call_target="tpu_custom_call" | custom-call | tf_op jit(solution)/shard_map/pick_modes/pallas_call | solution.py:112
  20.1 2.7 %all-to-all-start.1 = ((bf16[32,2,128,128]{3,2,1,0:T(8,128)(2,1)}), bf16[32,2,128,128]{3,2,1,0:T(8,128)(2,1)S(1)}, u32[]{:S(2)}, u32[]{:S(2)}) async-start(bf16[32,2,128,128]{3,2,1,0:T(8,128)(2,1)} %pick_modes.1), calls=%async_computation.1 | async-start | bytes 4194304 | tf_op jit(solution)/shard_map/all_to_all | solution.py:32
  22.9 9.5 %condense.1 = (bf16[2,512,512]{2,1,0:T(8,128)(2,1)}, bf16[2,512,512]{2,1,0:T(8,128)(2,1)}, f32[2,1,512]{2,1,0:T(1,128)}, bf16[4,128,128]{2,1,0:T(8,128)(2,1)}, b...) custom-call(s32[2,4]{1,0:T(2,128)} %map_ref.5, ...), custom_call_target="tpu_custom_call" | custom-call | tf_op jit(solution)/shard_map/condense/pallas_call | solution.py:223
  32.5 1.6 collective-permute-start.1
  34.3 1.7 collective-permute-start.3
  35.9 35.8 %all-to-all-done.1 = bf16[32,2,128,128]{3,2,1,0:T(8,128)(2,1)S(1)} async-done(((bf16[32,2,128,128]{3,2,1,0:T(8,128)(2,1)}), bf16[32,2,128,128]{3,2,1,0:T(8,128)(2,1)S(1)}, u32[]{:S(2)}, u32[]{:S(2)}) %all-to-all-start.1) | async-done | bytes 2097184 | tf_op jit(solution)/shard_map/all_to_all | solution.py:32
  71.7 1.3 copy-done
  73.0 7.4 %project_stiff.1 = (bf16[16,32,1024]{2,1,0:T(8,128)(2,1)}, f32[16,32,1024]{2,1,0:T(8,128)}, bf16[1024,1024]{1,0:T(8,128)(2,1)}) custom-call(s32[2,4]{1,0:T(2,128)} %map_ref.5, bf16[8,4,2,128,128]{4,3,2,1,0:T(8,128)(2,1)} %bitcast.36, bf16[2,512,512]{2,1,0:T(8,128)(2,1)} %get-tuple-element.68.m_ref), custom_call_target="tpu_custom_call" | custom-call | tf_op jit(solution)/shard_map/project_stiff/pallas_call | solution.py:344
  80.5 5.0 %mix_mass.1.y_ref = bf16[1024,1024]{1,0:T(8,128)(2,1)} custom-call(bf16[1024,1024]{1,0:T(8,128)(2,1)} %get-tuple-element.71.t_ref, bf16[2,512,512]{2,1,0:T(8,128)(2,1)} %get-tuple-element.72.m_ref, f32[2,1,512]{2,1,0:T(1,128)} %get-tuple-element.73.d_ref), custom_call_target="tpu_custom_call" | custom-call | tf_op jit(solution)/shard_map/mix_mass/pallas_call | solution.py:379
  85.5 6.0 %project_mass.1 = (bf16[16,32,1024]{2,1,0:T(8,128)(2,1)}, f32[16,32,1024]{2,1,0:T(8,128)}) custom-call(bf16[1024,1024]{1,0:T(8,128)(2,1)} %mix_mass.1.y_ref, bf16[1024,1024]{1,0:T(8,128)(2,1)} %get-tuple-element.71.t_ref), custom_call_target="tpu_custom_call" | custom-call | tf_op jit(solution)/shard_map/project_mass/pallas_call | solution.py:401
  91.6 1.5 collective-permute-start.4
  93.1 1.6 collective-permute-start.5
  94.7 0.8 collective-permute-start.6
  95.5 0.7 collective-permute-start.10
  96.3 6.2 %collective-permute-done.4.refs_5_ = bf16[4,128,128]{2,1,0:T(8,128)(2,1)S(1)} collective-permute-done((bf16[4,128,128]{2,1,0:T(8,128)(2,1)S(1)}, bf16[4,128,128]{2,1,0:T(8,128)(2,1)S(1)}, u32[]{:S(2)}, u32[]{:S(2)}) %collective-permute-start.4) | collective-permute-done | bytes 131104 | tf_op jit(solution)/shard_map/ppermute | solution.py:420
  102.4 1.1 collective-permute-start.11
  103.6 0.8 collective-permute-start.12
  104.3 1.4 collective-permute-start.13
  105.8 3.2 %collective-permute-done.11.refs_2_ = bf16[4,136,128]{2,1,0:T(8,128)(2,1)S(1)} collective-permute-done((bf16[4,136,128]{2,1,0:T(8,128)(2,1)S(1)}, bf16[4,136,128]{2,1,0:T(8,128)(2,1)S(1)}, u32[]{:S(2)}, u32[]{:S(2)}) %collective-permute-start.11) | collective-permute-done | bytes 139296 | tf_op jit(solution)/shard_map/ppermute | solution.py:420
  109.1 1.9 collective-permute-done.12.refs_3_
  111.0 2.4 %collective-permute-start.15 = (bf16[4,136,128]{2,1,0:T(8,128)(2,1)S(1)}, bf16[4,136,128]{2,1,0:T(8,128)(2,1)S(1)}, u32[]{:S(2)}, u32[]{:S(2)}) collective-permute-start(bf16[4,136,128]{2,1,0:T(8,128)(2,1)S(1)} %copy-done.25), channel_id=1, source_target_pairs={{0,6},{1,7},{2,4},{3,5},{4,2},{5,3},{6,0},{7,1},{8,14},{9,15},{10,... | collective-permute-start | bytes 417800 | tf_op jit(solution)/shard_map/ppermute | solution.py:420
  113.7 2.5 %regroup.2 = (bf16[8,128,128]{2,1,0:T(8,128)(2,1)}, bf16[8,128,128]{2,1,0:T(8,128)(2,1)}, bf16[8,128,128]{2,1,0:T(8,128)(2,1)}, bf16[8,128,128]{2,1,0:T(8,128)(2,1)}) custom-call(bf16[4,128,128]{2,1,0:T(8,128)(2,1)} %get-tuple-element.41.refs_0_, bf16[4,128,128]{2,1,0:T(8,128)(2,1)} %copy-done.18, bf16[4,128,128]{2,1,0:T(8,128)(2,1)} %copy-done.19, ...), custom_call_target="tpu_custom_call" | custom-call | tf_op jit(solution)/shard_map/regroup/pallas_call | solution.py:462
  116.2 0.4 collective-permute-start.7
  116.6 1.8 collective-permute-done.15.refs_6_
  118.3 1.0 collective-permute-start.8
  119.3 1.1 collective-permute-done.16.refs_7_
  120.4 1.8 collective-permute-start.9
  122.2 2.7 %regroup.3 = (bf16[8,136,128]{2,1,0:T(8,128)(2,1)}, bf16[8,136,128]{2,1,0:T(8,128)(2,1)}, bf16[8,136,128]{2,1,0:T(8,128)(2,1)}, bf16[8,136,128]{2,1,0:T(8,128)(2,1)}) custom-call(bf16[4,136,128]{2,1,0:T(8,128)(2,1)} %get-tuple-element.54.refs_0_, bf16[4,136,128]{2,1,0:T(8,128)(2,1)} %copy-done.11, bf16[4,136,128]{2,1,0:T(8,128)(2,1)} %copy-done.12, ...), custom_call_target="tpu_custom_call" | custom-call | tf_op jit(solution)/shard_map/regroup/pallas_call | solution.py:462
  124.9 4.3 %collective-permute-done.7.refs_4_ = bf16[8,128,128]{2,1,0:T(8,128)(2,1)S(1)} collective-permute-done((bf16[8,128,128]{2,1,0:T(8,128)(2,1)}, bf16[8,128,128]{2,1,0:T(8,128)(2,1)S(1)}, u32[]{:S(2)}, u32[]{:S(2)}) %collective-permute-start.7) | collective-permute-done | bytes 262176 | tf_op jit(solution)/shard_map/ppermute | solution.py:420
  129.2 10.7 %collective-permute-done.8.refs_5_ = bf16[8,128,128]{2,1,0:T(8,128)(2,1)S(1)} collective-permute-done((bf16[8,128,128]{2,1,0:T(8,128)(2,1)}, bf16[8,128,128]{2,1,0:T(8,128)(2,1)S(1)}, u32[]{:S(2)}, u32[]{:S(2)}) %collective-permute-start.8) | collective-permute-done | bytes 262176 | tf_op jit(solution)/shard_map/ppermute | solution.py:420
  139.9 1.6 collective-permute-start.19
  141.7 11.2 %clear_tiles.1 = (bf16[2048,4096]{1,0:T(8,128)(2,1)}, bf16[2048,4096]{1,0:T(8,128)(2,1)}) custom-call(s32[32,128]{1,0:T(8,128)} %bitcast.40), custom_call_target="tpu_custom_call" | custom-call | tf_op jit(solution)/shard_map/clear_tiles/pallas_call | solution.py:487
  153.1 0.6 select_reduce_fusion
  153.7 3.7 %place_stiff.1 = bf16[2048,4096]{1,0:T(8,128)(2,1)} custom-call(s32[32,128]{1,0:T(8,128)} %bitcast.41, s32[32]{0:T(128)} %get-tuple-element.78.refs_1_, s32[32]{0:T(128)} %get-tuple-element.77.refs_2_, bf16[8,128,128]{2,1,0:T(8,128)(2,1)} %get-tuple-element.49.refs_3_, bf16[8,128,128]{2,1,0:T(8,128)(2,1)} %copy-done.8, ...), custom_call_target="tpu_custom_call", output_to_operand_aliasing={{}: (7, {})} | custom-call | tf_op jit(solution)/shard_map/place_stiff/pallas_call | solution.py:578
  157.5 6.0 %collective-permute-done.18.refs_5_ = bf16[8,136,128]{2,1,0:T(8,128)(2,1)S(1)} collective-permute-done((bf16[8,136,128]{2,1,0:T(8,128)(2,1)}, bf16[8,136,128]{2,1,0:T(8,128)(2,1)S(1)}, u32[]{:S(2)}, u32[]{:S(2)}) %collective-permute-start.18) | collective-permute-done | bytes 278560 | tf_op jit(solution)/shard_map/ppermute | solution.py:420
  163.4 0.7 copy-done.6
  164.3 4.7 %place_mass.1 = (bf16[2048,4096]{1,0:T(8,128)(2,1)}, f32[4,1,128]{2,1,0:T(1,128)}) custom-call(s32[32,128]{1,0:T(8,128)} %bitcast.42, s32[32]{0:T(128)} %get-tuple-element.78.refs_1_, s32[32]{0:T(128)} %get-tuple-element.77.refs_2_, bf16[8,136,128]{2,1,0:T(8,128)(2,1)} %get-tuple-element.62.refs_3_, ...), custom_call_target="tpu_custom_call", output_to_operand_aliasing={{0}: (7, {})} | custom-call | tf_op jit(solution)/shard_map/place_mass/pallas_call | solution.py:578
  169.0 0.3 add_convert_fusion.2
  169.3 2.0 collective-permute-start.28
  171.3 0.7 collective-permute-start.30
  171.9 0.9 collective-permute-start.29
  172.9 1.4 add_convert_fusion.5
  174.3 2.0 collective-permute-start.21
  176.2 0.7 collective-permute-start.23
  176.9 1.7 collective-permute-done.28
  178.6 1.0 collective-permute-start.22
  179.6 5.1 %collective-permute-done.30 = bf16[4,32,1024]{2,1,0:T(8,128)(2,1)S(1)} collective-permute-done((bf16[4,32,1024]{2,1,0:T(8,128)(2,1)S(1)}, bf16[4,32,1024]{2,1,0:T(8,128)(2,1)S(1)}, u32[]{:S(2)}, u32[]{:S(2)}) %collective-permute-start.30) | collective-permute-done | bytes 262176 | tf_op jit(solution)/shard_map/ppermute | solution.py:420
  184.7 2.1 collective-permute-done.29
  187.0 11.7 %collective-permute-start.31 = (bf16[32,1024]{1,0:T(8,128)(2,1)S(1)}, bf16[32,1024]{1,0:T(8,128)(2,1)S(1)}, u32[]{:S(2)}, u32[]{:S(2)}) collective-permute-start(bf16[32,1024]{1,0:T(8,128)(2,1)S(1)} %get-tuple-element.89), channel_id=1, source_target_pairs={{0,8},{1,9},{2,10},{3,11},{4,12},{5,13},{6,14},{7,15},{8,0},{9,1},... | collective-permute-start | bytes 196616 | tf_op jit(solution)/shard_map/ppermute | solution.py:420
  198.7 2.0 collective-permute-start.33
  200.6 0.8 collective-permute-start.32
  201.4 1.2 fusion.9
  202.6 6.6 %collective-permute-start.24 = (bf16[32,1024]{1,0:T(8,128)(2,1)S(1)}, bf16[32,1024]{1,0:T(8,128)(2,1)S(1)}, u32[]{:S(2)}, u32[]{:S(2)}) collective-permute-start(bf16[32,1024]{1,0:T(8,128)(2,1)S(1)} %get-tuple-element.92), channel_id=1, source_target_pairs={{0,8},{1,9},{2,10},{3,11},{4,12},{5,13},{6,14},{7,15},{8,0},{9,1},... | collective-permute-start | bytes 196616 | tf_op jit(solution)/shard_map/ppermute | solution.py:420
  209.2 1.9 collective-permute-start.26
  211.1 0.7 fusion.2
  211.8 0.4 collective-permute-done.24
  212.2 3.1 %collective-permute-done.26 = bf16[32,1024]{1,0:T(8,128)(2,1)S(1)} collective-permute-done((bf16[32,1024]{1,0:T(8,128)(2,1)S(1)}, bf16[32,1024]{1,0:T(8,128)(2,1)S(1)}, u32[]{:S(2)}, u32[]{:S(2)}) %collective-permute-start.26) | collective-permute-done | bytes 65568 | tf_op jit(solution)/shard_map/ppermute | solution.py:420
  215.3 1.4 collective-permute-done.25
  216.7 0.7 fusion.5
  (97 shorter events, 1.6 us)
Async XLA Ops:
  2.0 14.4 %all-to-all-start = ((s32[32,1,128]{2,1,0:T(1,128)}), s32[32,1,128]{2,1,0:T(1,128)S(1)}, u32[]{:S(2)}, u32[]{:S(2)}) async-start(s32[32,1,128]{2,1,0:T(1,128)} %bitcast.44), calls=%async_computation | async-start | bytes 32768 | tf_op jit(solution)/shard_map/all_to_all | solution.py:32
  20.1 51.6 %all-to-all-start.1 = ((bf16[32,2,128,128]{3,2,1,0:T(8,128)(2,1)}), bf16[32,2,128,128]{3,2,1,0:T(8,128)(2,1)S(1)}, u32[]{:S(2)}, u32[]{:S(2)}) async-start(bf16[32,2,128,128]{3,2,1,0:T(8,128)(2,1)} %pick_modes.1), calls=%async_computation.1 | async-start | bytes 4194304 | tf_op jit(solution)/shard_map/all_to_all | solution.py:32
  32.3 59.2 %collective-permute-start = (bf16[4,128,128]{2,1,0:T(8,128)(2,1)}, bf16[4,128,128]{2,1,0:T(8,128)(2,1)S(1)}, u32[]{:S(2)}, u32[]{:S(2)}) collective-permute-start(bf16[4,128,128]{2,1,0:T(8,128)(2,1)} %get-tuple-element.42), channel_id=1, source_target_pairs={{0,1},{1,0},{2,3},{3,2},{4,5},{5,4},{6,7},{7,6},{8,9},{9,8},{10,11... | collective-permute-start | bytes 393224 | tf_op jit(solution)/shard_map/ppermute | solution.py:420
  32.5 60.6 %collective-permute-start.1 = (bf16[4,128,128]{2,1,0:T(8,128)(2,1)}, bf16[4,128,128]{2,1,0:T(8,128)(2,1)S(1)}, u32[]{:S(2)}, u32[]{:S(2)}) collective-permute-start(bf16[4,128,128]{2,1,0:T(8,128)(2,1)} %get-tuple-element.43), channel_id=1, source_target_pairs={{0,2},{1,3},{2,0},{3,1},{4,6},{5,7},{6,4},{7,5},{8,10},{9,11},{10,... | collective-permute-start | bytes 393224 | tf_op jit(solution)/shard_map/ppermute | solution.py:420
  34.2 60.6 %collective-permute-start.2 = (bf16[4,128,128]{2,1,0:T(8,128)(2,1)}, bf16[4,128,128]{2,1,0:T(8,128)(2,1)S(1)}, u32[]{:S(2)}, u32[]{:S(2)}) collective-permute-start(bf16[4,128,128]{2,1,0:T(8,128)(2,1)} %get-tuple-element.44), channel_id=1, source_target_pairs={{0,3},{1,2},{2,1},{3,0},{4,7},{5,6},{6,5},{7,4},{8,11},{9,10},{10,... | collective-permute-start | bytes 393224 | tf_op jit(solution)/shard_map/ppermute | solution.py:420
  34.3 61.3 %collective-permute-start.3 = (bf16[4,128,128]{2,1,0:T(8,128)(2,1)}, bf16[4,128,128]{2,1,0:T(8,128)(2,1)}, u32[]{:S(2)}, u32[]{:S(2)}) collective-permute-start(bf16[4,128,128]{2,1,0:T(8,128)(2,1)} %get-tuple-element.45), channel_id=1, source_target_pairs={{0,4},{1,5},{2,6},{3,7},{4,0},{5,1},{6,2},{7,3},{8,12},{9,13},{10,... | collective-permute-start | bytes 393224 | tf_op jit(solution)/shard_map/ppermute | solution.py:420
  85.4 6.2 %copy-start.32 = (bf16[4,128,128]{2,1,0:T(8,128)(2,1)S(1)}, bf16[4,128,128]{2,1,0:T(8,128)(2,1)}, u32[]{:S(2)}) copy-start(bf16[4,128,128]{2,1,0:T(8,128)(2,1)} %get-tuple-element.46) | copy-start | bytes 393220
  85.4 7.7 %copy-start.31 = (bf16[4,128,128]{2,1,0:T(8,128)(2,1)S(1)}, bf16[4,128,128]{2,1,0:T(8,128)(2,1)}, u32[]{:S(2)}) copy-start(bf16[4,128,128]{2,1,0:T(8,128)(2,1)} %get-tuple-element.47) | copy-start | bytes 393220
  85.5 9.3 %copy-start.30 = (bf16[4,128,128]{2,1,0:T(8,128)(2,1)S(1)}, bf16[4,128,128]{2,1,0:T(8,128)(2,1)}, u32[]{:S(2)}) copy-start(bf16[4,128,128]{2,1,0:T(8,128)(2,1)} %get-tuple-element.48) | copy-start | bytes 393220
  85.5 17.0 %copy-start.29 = (bf16[4,136,128]{2,1,0:T(8,128)(2,1)S(1)}, bf16[4,136,128]{2,1,0:T(8,128)(2,1)}, u32[]{:S(2)}) copy-start(bf16[4,136,128]{2,1,0:T(8,128)(2,1)} %get-tuple-element.56) | copy-start | bytes 417796
  85.5 18.1 %copy-start.28 = (bf16[4,136,128]{2,1,0:T(8,128)(2,1)S(1)}, bf16[4,136,128]{2,1,0:T(8,128)(2,1)}, u32[]{:S(2)}) copy-start(bf16[4,136,128]{2,1,0:T(8,128)(2,1)} %get-tuple-element.57) | copy-start | bytes 417796
  85.5 18.9 %copy-start.27 = (bf16[4,136,128]{2,1,0:T(8,128)(2,1)S(1)}, bf16[4,136,128]{2,1,0:T(8,128)(2,1)}, u32[]{:S(2)}) copy-start(bf16[4,136,128]{2,1,0:T(8,128)(2,1)} %get-tuple-element.58) | copy-start | bytes 417796
  85.5 23.5 %copy-start.26 = (bf16[4,136,128]{2,1,0:T(8,128)(2,1)S(1)}, bf16[4,136,128]{2,1,0:T(8,128)(2,1)}, u32[]{:S(2)}) copy-start(bf16[4,136,128]{2,1,0:T(8,128)(2,1)} %get-tuple-element.59) | copy-start | bytes 417796
  85.5 25.5 %copy-start.25 = (bf16[4,136,128]{2,1,0:T(8,128)(2,1)S(1)}, bf16[4,136,128]{2,1,0:T(8,128)(2,1)}, u32[]{:S(2)}) copy-start(bf16[4,136,128]{2,1,0:T(8,128)(2,1)} %get-tuple-element.60) | copy-start | bytes 417796
  85.5 27.9 %copy-start.24 = (bf16[4,136,128]{2,1,0:T(8,128)(2,1)S(1)}, bf16[4,136,128]{2,1,0:T(8,128)(2,1)}, u32[]{:S(2)}) copy-start(bf16[4,136,128]{2,1,0:T(8,128)(2,1)} %get-tuple-element.61) | copy-start | bytes 417796
  91.5 50.0 %copy-start.4 = (s32[32,1,128]{2,1,0:T(1,128)S(1)}, s32[32,1,128]{2,1,0:T(1,128)}, u32[]{:S(2)}) copy-start(s32[32,1,128]{2,1,0:T(1,128)} %copy-done.3) | copy-start | bytes 49156
  91.5 77.5 %collective-permute-start.27 = (bf16[16,32,1024]{2,1,0:T(8,128)(2,1)}, bf16[16,32,1024]{2,1,0:T(8,128)(2,1)S(1)}, u32[]{:S(2)}, u32[]{:S(2)}) collective-permute-start(bf16[16,32,1024]{2,1,0:T(8,128)(2,1)} %get-tuple-element.75), channel_id=1, source_target_pairs={{0,1},{1,0},{2,3},{3,2},{4,5},{5,4},{6,7},{7,6},{8,9},{9,8},{10,11... | collective-permute-start | bytes 3145736 | tf_op jit(solution)/shard_map/ppermute | solution.py:420
  91.6 22.0 %copy-start.18 = (bf16[4,128,128]{2,1,0:T(8,128)(2,1)}, bf16[4,128,128]{2,1,0:T(8,128)(2,1)S(1)}, u32[]{:S(2)}) copy-start(bf16[4,128,128]{2,1,0:T(8,128)(2,1)S(1)} %collective-permute-done.refs_1_) | copy-start | bytes 393220
  91.6 10.8 %collective-permute-start.4 = (bf16[4,128,128]{2,1,0:T(8,128)(2,1)S(1)}, bf16[4,128,128]{2,1,0:T(8,128)(2,1)S(1)}, u32[]{:S(2)}, u32[]{:S(2)}) collective-permute-start(bf16[4,128,128]{2,1,0:T(8,128)(2,1)S(1)} %copy-done.32), channel_id=1, source_target_pairs={{0,5},{1,4},{2,7},{3,6},{4,1},{5,0},{6,3},{7,2},{8,13},{9,12},{10,... | collective-permute-start | bytes 393224 | tf_op jit(solution)/shard_map/ppermute | solution.py:420
  93.1 20.5 %copy-start.19 = (bf16[4,128,128]{2,1,0:T(8,128)(2,1)}, bf16[4,128,128]{2,1,0:T(8,128)(2,1)S(1)}, u32[]{:S(2)}) copy-start(bf16[4,128,128]{2,1,0:T(8,128)(2,1)S(1)} %collective-permute-done.1.refs_2_) | copy-start | bytes 393220
  93.1 10.4 %collective-permute-start.5 = (bf16[4,128,128]{2,1,0:T(8,128)(2,1)S(1)}, bf16[4,128,128]{2,1,0:T(8,128)(2,1)S(1)}, u32[]{:S(2)}, u32[]{:S(2)}) collective-permute-start(bf16[4,128,128]{2,1,0:T(8,128)(2,1)S(1)} %copy-done.31), channel_id=1, source_target_pairs={{0,6},{1,7},{2,4},{3,5},{4,2},{5,3},{6,0},{7,1},{8,14},{9,15},{10,... | collective-permute-start | bytes 393224 | tf_op jit(solution)/shard_map/ppermute | solution.py:420
  94.7 18.9 %copy-start.20 = (bf16[4,128,128]{2,1,0:T(8,128)(2,1)}, bf16[4,128,128]{2,1,0:T(8,128)(2,1)S(1)}, u32[]{:S(2)}) copy-start(bf16[4,128,128]{2,1,0:T(8,128)(2,1)S(1)} %collective-permute-done.2.refs_3_) | copy-start | bytes 393220
  94.7 9.6 %collective-permute-start.6 = (bf16[4,128,128]{2,1,0:T(8,128)(2,1)S(1)}, bf16[4,128,128]{2,1,0:T(8,128)(2,1)S(1)}, u32[]{:S(2)}, u32[]{:S(2)}) collective-permute-start(bf16[4,128,128]{2,1,0:T(8,128)(2,1)S(1)} %copy-done.30), channel_id=1, source_target_pairs={{0,7},{1,6},{2,5},{3,4},{4,3},{5,2},{6,1},{7,0},{8,15},{9,14},{10,... | collective-permute-start | bytes 393224 | tf_op jit(solution)/shard_map/ppermute | solution.py:420
  95.5 10.2 %collective-permute-start.10 = (bf16[4,136,128]{2,1,0:T(8,128)(2,1)}, bf16[4,136,128]{2,1,0:T(8,128)(2,1)S(1)}, u32[]{:S(2)}, u32[]{:S(2)}) collective-permute-start(bf16[4,136,128]{2,1,0:T(8,128)(2,1)} %get-tuple-element.55), channel_id=1, source_target_pairs={{0,1},{1,0},{2,3},{3,2},{4,5},{5,4},{6,7},{7,6},{8,9},{9,8},{10,11... | collective-permute-start | bytes 417800 | tf_op jit(solution)/shard_map/ppermute | solution.py:420
  102.4 11.2 %copy-start.21 = (bf16[4,128,128]{2,1,0:T(8,128)(2,1)}, bf16[4,128,128]{2,1,0:T(8,128)(2,1)S(1)}, u32[]{:S(2)}) copy-start(bf16[4,128,128]{2,1,0:T(8,128)(2,1)S(1)} %collective-permute-done.4.refs_5_) | copy-start | bytes 393220
  102.4 6.5 %collective-permute-start.11 = (bf16[4,136,128]{2,1,0:T(8,128)(2,1)S(1)}, bf16[4,136,128]{2,1,0:T(8,128)(2,1)S(1)}, u32[]{:S(2)}, u32[]{:S(2)}) collective-permute-start(bf16[4,136,128]{2,1,0:T(8,128)(2,1)S(1)} %copy-done.29), channel_id=1, source_target_pairs={{0,2},{1,3},{2,0},{3,1},{4,6},{5,7},{6,4},{7,5},{8,10},{9,11},{10,... | collective-permute-start | bytes 417800 | tf_op jit(solution)/shard_map/ppermute | solution.py:420
  103.6 10.1 %copy-start.22 = (bf16[4,128,128]{2,1,0:T(8,128)(2,1)}, bf16[4,128,128]{2,1,0:T(8,128)(2,1)S(1)}, u32[]{:S(2)}) copy-start(bf16[4,128,128]{2,1,0:T(8,128)(2,1)S(1)} %collective-permute-done.5.refs_6_) | copy-start | bytes 393220
  103.6 7.4 %collective-permute-start.12 = (bf16[4,136,128]{2,1,0:T(8,128)(2,1)S(1)}, bf16[4,136,128]{2,1,0:T(8,128)(2,1)S(1)}, u32[]{:S(2)}, u32[]{:S(2)}) collective-permute-start(bf16[4,136,128]{2,1,0:T(8,128)(2,1)S(1)} %copy-done.28), channel_id=1, source_target_pairs={{0,3},{1,2},{2,1},{3,0},{4,7},{5,6},{6,5},{7,4},{8,11},{9,10},{10,... | collective-permute-start | bytes 417800 | tf_op jit(solution)/shard_map/ppermute | solution.py:420
  104.3 9.3 %copy-start.23 = (bf16[4,128,128]{2,1,0:T(8,128)(2,1)}, bf16[4,128,128]{2,1,0:T(8,128)(2,1)S(1)}, u32[]{:S(2)}) copy-start(bf16[4,128,128]{2,1,0:T(8,128)(2,1)S(1)} %collective-permute-done.6.refs_7_) | copy-start | bytes 393220
  104.3 9.0 %collective-permute-start.13 = (bf16[4,136,128]{2,1,0:T(8,128)(2,1)S(1)}, bf16[4,136,128]{2,1,0:T(8,128)(2,1)S(1)}, u32[]{:S(2)}, u32[]{:S(2)}) collective-permute-start(bf16[4,136,128]{2,1,0:T(8,128)(2,1)S(1)} %copy-done.27), channel_id=1, source_target_pairs={{0,4},{1,5},{2,6},{3,7},{4,0},{5,1},{6,2},{7,3},{8,12},{9,13},{10,... | collective-permute-start | bytes 417800 | tf_op jit(solution)/shard_map/ppermute | solution.py:420
  105.8 16.4 %copy-start.11 = (bf16[4,136,128]{2,1,0:T(8,128)(2,1)}, bf16[4,136,128]{2,1,0:T(8,128)(2,1)S(1)}, u32[]{:S(2)}) copy-start(bf16[4,136,128]{2,1,0:T(8,128)(2,1)S(1)} %collective-permute-done.10.refs_1_) | copy-start | bytes 417796
  105.8 67.1 %collective-permute-start.20 = (bf16[16,32,1024]{2,1,0:T(8,128)(2,1)}, bf16[16,32,1024]{2,1,0:T(8,128)(2,1)}, u32[]{:S(2)}, u32[]{:S(2)}) collective-permute-start(bf16[16,32,1024]{2,1,0:T(8,128)(2,1)} %get-tuple-element.70), channel_id=1, source_target_pairs={{0,1},{1,0},{2,3},{3,2},{4,5},{5,4},{6,7},{7,6},{8,9},{9,8},{10,11... | collective-permute-start | bytes 3145736 | tf_op jit(solution)/shard_map/ppermute | solution.py:420
  109.0 13.2 %copy-start.12 = (bf16[4,136,128]{2,1,0:T(8,128)(2,1)}, bf16[4,136,128]{2,1,0:T(8,128)(2,1)S(1)}, u32[]{:S(2)}) copy-start(bf16[4,136,128]{2,1,0:T(8,128)(2,1)S(1)} %collective-permute-done.11.refs_2_) | copy-start | bytes 417796
  109.0 7.2 %collective-permute-start.14 = (bf16[4,136,128]{2,1,0:T(8,128)(2,1)S(1)}, bf16[4,136,128]{2,1,0:T(8,128)(2,1)S(1)}, u32[]{:S(2)}, u32[]{:S(2)}) collective-permute-start(bf16[4,136,128]{2,1,0:T(8,128)(2,1)S(1)} %copy-done.26), channel_id=1, source_target_pairs={{0,5},{1,4},{2,7},{3,6},{4,1},{5,0},{6,3},{7,2},{8,13},{9,12},{10,... | collective-permute-start | bytes 417800 | tf_op jit(solution)/shard_map/ppermute | solution.py:420
  111.0 11.2 %copy-start.13 = (bf16[4,136,128]{2,1,0:T(8,128)(2,1)}, bf16[4,136,128]{2,1,0:T(8,128)(2,1)S(1)}, u32[]{:S(2)}) copy-start(bf16[4,136,128]{2,1,0:T(8,128)(2,1)S(1)} %collective-permute-done.12.refs_3_) | copy-start | bytes 417796
  111.0 7.3 %collective-permute-start.15 = (bf16[4,136,128]{2,1,0:T(8,128)(2,1)S(1)}, bf16[4,136,128]{2,1,0:T(8,128)(2,1)S(1)}, u32[]{:S(2)}, u32[]{:S(2)}) collective-permute-start(bf16[4,136,128]{2,1,0:T(8,128)(2,1)S(1)} %copy-done.25), channel_id=1, source_target_pairs={{0,6},{1,7},{2,4},{3,5},{4,2},{5,3},{6,0},{7,1},{8,14},{9,15},{10,... | collective-permute-start | bytes 417800 | tf_op jit(solution)/shard_map/ppermute | solution.py:420
  113.4 8.8 %copy-start.14 = (bf16[4,136,128]{2,1,0:T(8,128)(2,1)}, bf16[4,136,128]{2,1,0:T(8,128)(2,1)S(1)}, u32[]{:S(2)}) copy-start(bf16[4,136,128]{2,1,0:T(8,128)(2,1)S(1)} %collective-permute-done.13.refs_4_) | copy-start | bytes 417796
  113.4 7.0 %collective-permute-start.16 = (bf16[4,136,128]{2,1,0:T(8,128)(2,1)S(1)}, bf16[4,136,128]{2,1,0:T(8,128)(2,1)S(1)}, u32[]{:S(2)}, u32[]{:S(2)}) collective-permute-start(bf16[4,136,128]{2,1,0:T(8,128)(2,1)S(1)} %copy-done.24), channel_id=1, source_target_pairs={{0,7},{1,6},{2,5},{3,4},{4,3},{5,2},{6,1},{7,0},{8,15},{9,14},{10,... | collective-permute-start | bytes 417800 | tf_op jit(solution)/shard_map/ppermute | solution.py:420
  116.2 6.0 %copy-start.15 = (bf16[4,136,128]{2,1,0:T(8,128)(2,1)}, bf16[4,136,128]{2,1,0:T(8,128)(2,1)S(1)}, u32[]{:S(2)}) copy-start(bf16[4,136,128]{2,1,0:T(8,128)(2,1)S(1)} %collective-permute-done.14.refs_5_) | copy-start | bytes 417796
  116.2 13.0 %collective-permute-start.7 = (bf16[8,128,128]{2,1,0:T(8,128)(2,1)}, bf16[8,128,128]{2,1,0:T(8,128)(2,1)S(1)}, u32[]{:S(2)}, u32[]{:S(2)}) collective-permute-start(bf16[8,128,128]{2,1,0:T(8,128)(2,1)} %get-tuple-element.50), channel_id=1, source_target_pairs={{0,8},{1,9},{2,10},{3,11},{4,12},{5,13},{6,14},{7,15},{8,0},{9,1},... | collective-permute-start | bytes 786440 | tf_op jit(solution)/shard_map/ppermute | solution.py:420
  118.3 3.9 %copy-start.16 = (bf16[4,136,128]{2,1,0:T(8,128)(2,1)}, bf16[4,136,128]{2,1,0:T(8,128)(2,1)S(1)}, u32[]{:S(2)}) copy-start(bf16[4,136,128]{2,1,0:T(8,128)(2,1)S(1)} %collective-permute-done.15.refs_6_) | copy-start | bytes 417796
  118.3 21.6 %collective-permute-start.8 = (bf16[8,128,128]{2,1,0:T(8,128)(2,1)}, bf16[8,128,128]{2,1,0:T(8,128)(2,1)S(1)}, u32[]{:S(2)}, u32[]{:S(2)}) collective-permute-start(bf16[8,128,128]{2,1,0:T(8,128)(2,1)} %get-tuple-element.51), channel_id=1, source_target_pairs={{0,16},{1,17},{2,18},{3,19},{4,20},{5,21},{6,22},{7,23},{8,24},{9,... | collective-permute-start | bytes 786440 | tf_op jit(solution)/shard_map/ppermute | solution.py:420
  120.4 19.5 %collective-permute-start.9 = (bf16[8,128,128]{2,1,0:T(8,128)(2,1)}, bf16[8,128,128]{2,1,0:T(8,128)(2,1)S(1)}, u32[]{:S(2)}, u32[]{:S(2)}) collective-permute-start(bf16[8,128,128]{2,1,0:T(8,128)(2,1)} %get-tuple-element.52), channel_id=1, source_target_pairs={{0,24},{1,25},{2,26},{3,27},{4,28},{5,29},{6,30},{7,31},{8,16},{9,... | collective-permute-start | bytes 786440 | tf_op jit(solution)/shard_map/ppermute | solution.py:420
  129.2 24.5 %copy-start.8 = (bf16[8,128,128]{2,1,0:T(8,128)(2,1)}, bf16[8,128,128]{2,1,0:T(8,128)(2,1)S(1)}, u32[]{:S(2)}) copy-start(bf16[8,128,128]{2,1,0:T(8,128)(2,1)S(1)} %collective-permute-done.7.refs_4_) | copy-start | bytes 786436
  129.2 28.2 %collective-permute-start.17 = (bf16[8,136,128]{2,1,0:T(8,128)(2,1)}, bf16[8,136,128]{2,1,0:T(8,128)(2,1)S(1)}, u32[]{:S(2)}, u32[]{:S(2)}) collective-permute-start(bf16[8,136,128]{2,1,0:T(8,128)(2,1)} %get-tuple-element.63), channel_id=1, source_target_pairs={{0,8},{1,9},{2,10},{3,11},{4,12},{5,13},{6,14},{7,15},{8,0},{9,1},... | collective-permute-start | bytes 835592 | tf_op jit(solution)/shard_map/ppermute | solution.py:420
  139.9 13.8 %copy-start.9 = (bf16[8,128,128]{2,1,0:T(8,128)(2,1)}, bf16[8,128,128]{2,1,0:T(8,128)(2,1)S(1)}, u32[]{:S(2)}) copy-start(bf16[8,128,128]{2,1,0:T(8,128)(2,1)S(1)} %collective-permute-done.8.refs_5_) | copy-start | bytes 786436
  139.9 23.5 %collective-permute-start.18 = (bf16[8,136,128]{2,1,0:T(8,128)(2,1)}, bf16[8,136,128]{2,1,0:T(8,128)(2,1)S(1)}, u32[]{:S(2)}, u32[]{:S(2)}) collective-permute-start(bf16[8,136,128]{2,1,0:T(8,128)(2,1)} %get-tuple-element.64), channel_id=1, source_target_pairs={{0,16},{1,17},{2,18},{3,19},{4,20},{5,21},{6,22},{7,23},{8,24},{9,... | collective-permute-start | bytes 835592 | tf_op jit(solution)/shard_map/ppermute | solution.py:420
  139.9 13.8 %copy-start.10 = (bf16[8,128,128]{2,1,0:T(8,128)(2,1)}, bf16[8,128,128]{2,1,0:T(8,128)(2,1)S(1)}, u32[]{:S(2)}) copy-start(bf16[8,128,128]{2,1,0:T(8,128)(2,1)S(1)} %collective-permute-done.9.refs_6_) | copy-start | bytes 786436
  139.9 23.5 %collective-permute-start.19 = (bf16[8,136,128]{2,1,0:T(8,128)(2,1)}, bf16[8,136,128]{2,1,0:T(8,128)(2,1)S(1)}, u32[]{:S(2)}, u32[]{:S(2)}) collective-permute-start(bf16[8,136,128]{2,1,0:T(8,128)(2,1)} %get-tuple-element.65), channel_id=1, source_target_pairs={{0,24},{1,25},{2,26},{3,27},{4,28},{5,29},{6,30},{7,31},{8,16},{9,... | collective-permute-start | bytes 835592 | tf_op jit(solution)/shard_map/ppermute | solution.py:420
  157.4 6.8 %copy-start.5 = (bf16[8,136,128]{2,1,0:T(8,128)(2,1)}, bf16[8,136,128]{2,1,0:T(8,128)(2,1)S(1)}, u32[]{:S(2)}) copy-start(bf16[8,136,128]{2,1,0:T(8,128)(2,1)S(1)} %collective-permute-done.17.refs_4_) | copy-start | bytes 835588
  164.3 4.7 %copy-start.2 = (f32[16,32,1024]{2,1,0:T(8,128)S(1)}, f32[16,32,1024]{2,1,0:T(8,128)}, u32[]{:S(2)}) copy-start(f32[16,32,1024]{2,1,0:T(8,128)} %get-tuple-element.74) | copy-start | bytes 6291460
  169.0 3.9 %copy-start.1 = (f32[16,32,1024]{2,1,0:T(8,128)S(1)}, f32[16,32,1024]{2,1,0:T(8,128)}, u32[]{:S(2)}) copy-start(f32[16,32,1024]{2,1,0:T(8,128)} %get-tuple-element.69) | copy-start | bytes 6291460
  169.3 9.2 %collective-permute-start.28 = (bf16[4,32,1024]{2,1,0:T(8,128)(2,1)S(1)}, bf16[4,32,1024]{2,1,0:T(8,128)(2,1)S(1)}, u32[]{:S(2)}, u32[]{:S(2)}) collective-permute-start(bf16[4,32,1024]{2,1,0:T(8,128)(2,1)S(1)} %get-tuple-element.83), channel_id=1, source_target_pairs={{0,2},{1,3},{2,0},{3,1},{4,6},{5,7},{6,4},{7,5},{8,10},{9,11},{10,... | collective-permute-start | bytes 786440 | tf_op jit(solution)/shard_map/ppermute | solution.py:420
  171.3 13.4 %collective-permute-start.30 = (bf16[4,32,1024]{2,1,0:T(8,128)(2,1)S(1)}, bf16[4,32,1024]{2,1,0:T(8,128)(2,1)S(1)}, u32[]{:S(2)}, u32[]{:S(2)}) collective-permute-start(bf16[4,32,1024]{2,1,0:T(8,128)(2,1)S(1)} %get-tuple-element.84), channel_id=1, source_target_pairs={{0,6},{1,7},{2,4},{3,5},{4,2},{5,3},{6,0},{7,1},{8,14},{9,15},{10,... | collective-permute-start | bytes 786440 | tf_op jit(solution)/shard_map/ppermute | solution.py:420
  171.9 14.8 %collective-permute-start.29 = (bf16[4,32,1024]{2,1,0:T(8,128)(2,1)S(1)}, bf16[4,32,1024]{2,1,0:T(8,128)(2,1)S(1)}, u32[]{:S(2)}, u32[]{:S(2)}) collective-permute-start(bf16[4,32,1024]{2,1,0:T(8,128)(2,1)S(1)} %get-tuple-element.85), channel_id=1, source_target_pairs={{0,4},{1,5},{2,6},{3,7},{4,0},{5,1},{6,2},{7,3},{8,12},{9,13},{10,... | collective-permute-start | bytes 786440 | tf_op jit(solution)/shard_map/ppermute | solution.py:420
  174.3 26.4 %collective-permute-start.21 = (bf16[4,32,1024]{2,1,0:T(8,128)(2,1)S(1)}, bf16[4,32,1024]{2,1,0:T(8,128)(2,1)S(1)}, u32[]{:S(2)}, u32[]{:S(2)}) collective-permute-start(bf16[4,32,1024]{2,1,0:T(8,128)(2,1)S(1)} %get-tuple-element.86), channel_id=1, source_target_pairs={{0,2},{1,3},{2,0},{3,1},{4,6},{5,7},{6,4},{7,5},{8,10},{9,11},{10,... | collective-permute-start | bytes 786440 | tf_op jit(solution)/shard_map/ppermute | solution.py:420
  176.2 25.2 %collective-permute-start.23 = (bf16[4,32,1024]{2,1,0:T(8,128)(2,1)S(1)}, bf16[4,32,1024]{2,1,0:T(8,128)(2,1)S(1)}, u32[]{:S(2)}, u32[]{:S(2)}) collective-permute-start(bf16[4,32,1024]{2,1,0:T(8,128)(2,1)S(1)} %get-tuple-element.87), channel_id=1, source_target_pairs={{0,6},{1,7},{2,4},{3,5},{4,2},{5,3},{6,0},{7,1},{8,14},{9,15},{10,... | collective-permute-start | bytes 786440 | tf_op jit(solution)/shard_map/ppermute | solution.py:420
  178.6 22.8 %collective-permute-start.22 = (bf16[4,32,1024]{2,1,0:T(8,128)(2,1)S(1)}, bf16[4,32,1024]{2,1,0:T(8,128)(2,1)S(1)}, u32[]{:S(2)}, u32[]{:S(2)}) collective-permute-start(bf16[4,32,1024]{2,1,0:T(8,128)(2,1)S(1)} %get-tuple-element.88), channel_id=1, source_target_pairs={{0,4},{1,5},{2,6},{3,7},{4,0},{5,1},{6,2},{7,3},{8,12},{9,13},{10,... | collective-permute-start | bytes 786440 | tf_op jit(solution)/shard_map/ppermute | solution.py:420
  187.0 24.1 %collective-permute-start.31 = (bf16[32,1024]{1,0:T(8,128)(2,1)S(1)}, bf16[32,1024]{1,0:T(8,128)(2,1)S(1)}, u32[]{:S(2)}, u32[]{:S(2)}) collective-permute-start(bf16[32,1024]{1,0:T(8,128)(2,1)S(1)} %get-tuple-element.89), channel_id=1, source_target_pairs={{0,8},{1,9},{2,10},{3,11},{4,12},{5,13},{6,14},{7,15},{8,0},{9,1},... | collective-permute-start | bytes 196616 | tf_op jit(solution)/shard_map/ppermute | solution.py:420
  198.7 12.4 %collective-permute-start.33 = (bf16[32,1024]{1,0:T(8,128)(2,1)S(1)}, bf16[32,1024]{1,0:T(8,128)(2,1)S(1)}, u32[]{:S(2)}, u32[]{:S(2)}) collective-permute-start(bf16[32,1024]{1,0:T(8,128)(2,1)S(1)} %get-tuple-element.90), channel_id=1, source_target_pairs={{0,24},{1,25},{2,26},{3,27},{4,28},{5,29},{6,30},{7,31},{8,16},{9,... | collective-permute-start | bytes 196616 | tf_op jit(solution)/shard_map/ppermute | solution.py:420
  200.6 10.5 %collective-permute-start.32 = (bf16[32,1024]{1,0:T(8,128)(2,1)S(1)}, bf16[32,1024]{1,0:T(8,128)(2,1)S(1)}, u32[]{:S(2)}, u32[]{:S(2)}) collective-permute-start(bf16[32,1024]{1,0:T(8,128)(2,1)S(1)} %get-tuple-element.91), channel_id=1, source_target_pairs={{0,16},{1,17},{2,18},{3,19},{4,20},{5,21},{6,22},{7,23},{8,24},{9,... | collective-permute-start | bytes 196616 | tf_op jit(solution)/shard_map/ppermute | solution.py:420
  202.6 9.6 %collective-permute-start.24 = (bf16[32,1024]{1,0:T(8,128)(2,1)S(1)}, bf16[32,1024]{1,0:T(8,128)(2,1)S(1)}, u32[]{:S(2)}, u32[]{:S(2)}) collective-permute-start(bf16[32,1024]{1,0:T(8,128)(2,1)S(1)} %get-tuple-element.92), channel_id=1, source_target_pairs={{0,8},{1,9},{2,10},{3,11},{4,12},{5,13},{6,14},{7,15},{8,0},{9,1},... | collective-permute-start | bytes 196616 | tf_op jit(solution)/shard_map/ppermute | solution.py:420
  209.2 6.1 %collective-permute-start.26 = (bf16[32,1024]{1,0:T(8,128)(2,1)S(1)}, bf16[32,1024]{1,0:T(8,128)(2,1)S(1)}, u32[]{:S(2)}, u32[]{:S(2)}) collective-permute-start(bf16[32,1024]{1,0:T(8,128)(2,1)S(1)} %get-tuple-element.93), channel_id=1, source_target_pairs={{0,24},{1,25},{2,26},{3,27},{4,28},{5,29},{6,30},{7,31},{8,16},{9,... | collective-permute-start | bytes 196616 | tf_op jit(solution)/shard_map/ppermute | solution.py:420
  211.1 5.6 %collective-permute-start.25 = (bf16[32,1024]{1,0:T(8,128)(2,1)S(1)}, bf16[32,1024]{1,0:T(8,128)(2,1)S(1)}, u32[]{:S(2)}, u32[]{:S(2)}) collective-permute-start(bf16[32,1024]{1,0:T(8,128)(2,1)S(1)} %get-tuple-element.94), channel_id=1, source_target_pairs={{0,16},{1,17},{2,18},{3,19},{4,20},{5,21},{6,22},{7,23},{8,24},{9,... | collective-permute-start | bytes 196616 | tf_op jit(solution)/shard_map/ppermute | solution.py:420
  (5 other events, 5.4 us)

commit v9 on v8

--- a/solution.py
+++ b/solution.py
@@ -90,31 +90,25 @@
     device_count = table.shape[0]
     width = modes.shape[1]
 
-    def kernel(table_ref, modes_ref, out_ref, sem):
-        def copy(device, h):
-            return pltpu.make_async_copy(
-                modes_ref.at[table_ref[device, h]], out_ref.at[device, h], sem.at[device, h]
-            )
-
-        def start(device, carry):
+    steps = 4
+    rows = device_count // steps
+
+    def kernel(table_ref, modes_ref, out_ref):
+        first = pl.program_id(0) * rows
+
+        def one(i, carry):
             for h in range(ratio):
-                copy(device, h).start()
+                out_ref[i, h] = modes_ref[table_ref[first + i, h]]
             return carry
 
-        def wait(device, carry):
-            for h in range(ratio):
-                copy(device, h).wait()
-            return carry
-
-        lax.fori_loop(0, device_count, start, 0, unroll=4)
-        lax.fori_loop(0, device_count, wait, 0, unroll=4)
-
-    return pl.pallas_call(
-        kernel,
+        lax.fori_loop(0, rows, one, 0, unroll=4)
+
+    return pl.pallas_call(
+        kernel,
+        grid=(steps,),
         out_shape=jax.ShapeDtypeStruct((device_count, ratio, width, BLK), BF16),
-        in_specs=[SMEM, VMEM],
-        out_specs=ANY,
-        scratch_shapes=[pltpu.SemaphoreType.DMA((device_count, ratio))],
+        in_specs=[SMEM, pl.BlockSpec(modes.shape, lambda i: (0, 0, 0))],
+        out_specs=pl.BlockSpec((rows, ratio, width, BLK), lambda i: (i, 0, 0, 0)),
         name="pick_modes",
     )(table, modes)
 
@@ -446,27 +440,13 @@
 
 def regroup(near):
     plane, (depth, height, _) = len(near), near[0].shape
-
-    def kernel(*refs):
-        in_refs, out_refs, sem = refs[:plane], refs[plane : plane + depth], refs[-1]
-        copies = [
-            pltpu.make_async_copy(in_ref.at[z], out_ref.at[d], sem.at[d, z])
-            for d, in_ref in enumerate(in_refs)
-            for z, out_ref in enumerate(out_refs)
+    parts = [jnp.zeros((plane, height, BLK), BF16)] * depth
+    for d, piece in enumerate(near):
+        parts = [
+            lax.dynamic_update_slice(part, piece[z : z + 1], (d, 0, 0))
+            for z, part in enumerate(parts)
         ]
-        for copy in copies:
-            copy.start()
-        for copy in copies:
-            copy.wait()
-
-    return pl.pallas_call(
-        kernel,
-        in_specs=[VMEM] * plane,
-        out_specs=[ANY] * depth,
-        out_shape=[jax.ShapeDtypeStruct((plane, height, BLK), BF16)] * depth,
-        scratch_shapes=[pltpu.SemaphoreType.DMA((plane, depth))],
-        name="regroup",
-    )(*near)
+    return parts
 
 
 def clear_tiles(table, sizes):

time: 218 us -> 182 us (0.83)
  waiting for transfers between devices: 89.4 us -> 52.9 us
  local copies, waits for them, and re-layouts: 5.38 us -> 20.8 us
  starting transfers between devices: 59.3 us -> 46.7 us
  Pallas kernels: 57 us -> 51.9 us
  other arithmetic: 5.2 us -> 7.73 us
    all_to_all x2, waiting for transfers between devices: 40.6 us -> 13.6 us  [exchange(): return lax.all_to_all(value, AXES, split_axis=0, concat_axis=0, tiled=True)]
    dynamic_update_slice x0 -> x22, local copies, waits for them, and re-layouts: none -> 13.8 us  [regroup(): lax.dynamic_update_slice(part, piece[z:z + 1], (d, 0, 0))]
    ppermute x34, starting transfers between devices: 49.2 us -> 36.7 us  [swap(): lax.ppermute(value, AXES, [(i, i ^ offset) for i in range(device_count)])]
    ppermute x34, waiting for transfers between devices: 48.8 us -> 39.3 us  [swap(): lax.ppermute(value, AXES, [(i, i ^ offset) for i in range(device_count)])]
    pallas_call x3 -> x1, Pallas kernels: 8.25 us -> 3.09 us  [pick_modes(): pl.pallas_call(kernel, grid=(steps,), out_shape=jax.ShapeDtypeStruct((dev...]
  transfers between devices with their start and end apart: 36 -> 36, of which waited for: 16 -> 15; matrix products, arithmetic and copies ran while one was open for 3% -> 14% of each run, Pallas kernels for 24% -> 26%
where the time goes in v9:
time: 182 us; the launch traced here: 181 us
  waiting for transfers between devices  52.9 us (29%)
  Pallas kernels  51.9 us (29%)
  starting transfers between devices  46.7 us (26%)
  local copies, waits for them, and re-layouts  20.8 us (11%)
  other arithmetic  7.73 us (4%)
    ppermute x34, waiting for transfers between devices, swap(): lax.ppermute(value, AXES, [(i, i ^ offset) for i in range(device_count)])  39.3 us
    ppermute x34, starting transfers between devices, swap(): lax.ppermute(value, AXES, [(i, i ^ offset) for i in range(device_count)])  36.7 us
    dynamic_update_slice x22, local copies, waits for them, and re-layouts, regroup(): lax.dynamic_update_slice(part, piece[z:z + 1], (d, 0, 0))  13.8 us
    all_to_all x2, waiting for transfers between devices, exchange(): return lax.all_to_all(value, AXES, split_axis=0, concat_axis=0, tiled=True)  13.6 us
    pallas_call x1, Pallas kernels, clear_tiles(): pl.pallas_call(kernel, in_specs=[ANY], out_specs=[ANY, ANY], out_shape=[j...  11.3 us
    all_to_all x2, starting transfers between devices, exchange(): return lax.all_to_all(value, AXES, split_axis=0, concat_axis=0, tiled=True)  10.1 us
    pallas_call x1, Pallas kernels, condense(): pl.pallas_call(kernel, grid=(local_subs,), in_specs=[SMEM, piece(interior...  9.45 us
    pallas_call x2, Pallas kernels, place(): pl.pallas_call(kernel, in_specs=[SMEM, SMEM, SMEM] + [ANY] * (depth + 1),...  8.28 us
  transfers between devices with their start and end apart: 36, of which 15 were waited for; matrix products, arithmetic and copies ran while one was open for 14% of the time, Pallas kernels for 26%

profile of v9, /device:TPU:0, one launch (start us, length us, event | category | flops | bytes accessed | tf_op | source)
XLA Modules:
  0.0 181.0 jit_solution(17333335491031320671)
XLA Ops:
  0.6 1.4 describe.1
  2.0 7.3 %all-to-all-start = ((s32[32,1,128]{2,1,0:T(1,128)}), s32[32,1,128]{2,1,0:T(1,128)S(1)}, u32[]{:S(2)}, u32[]{:S(2)}) async-start(s32[32,1,128]{2,1,0:T(1,128)} %bitcast.44), calls=%async_computation | async-start | bytes 32768 | tf_op jit(solution)/shard_map/all_to_all | solution.py:32
  9.3 2.3 %copy.18 = bf16[32,128,128]{1,2,0:T(8,128)(2,1)} copy(bf16[32,128,128]{2,1,0:T(8,128)(2,1)} %bitcast.38) | data formatting | bytes 2097152 | tf_op jit(solution)/shard_map/reshape | solution.py:593
  11.6 4.8 %all-to-all-done = s32[32,1,128]{2,1,0:T(1,128)S(1)} async-done(((s32[32,1,128]{2,1,0:T(1,128)}), s32[32,1,128]{2,1,0:T(1,128)S(1)}, u32[]{:S(2)}, u32[]{:S(2)}) %all-to-all-start) | async-done | bytes 16416 | tf_op jit(solution)/shard_map/all_to_all | solution.py:32
  17.0 3.1 %pick_modes.1 = bf16[32,2,128,128]{3,2,1,0:T(8,128)(2,1)} custom-call(s32[32,128]{1,0:T(8,128)} %bitcast.39, bf16[32,128,128]{2,1,0:T(8,128)(2,1)} %bitcast.37), custom_call_target="tpu_custom_call" | custom-call | tf_op jit(solution)/shard_map/pick_modes/pallas_call | solution.py:106
  20.1 2.7 %all-to-all-start.1 = ((bf16[32,2,128,128]{3,2,1,0:T(8,128)(2,1)}), bf16[32,2,128,128]{3,2,1,0:T(8,128)(2,1)S(1)}, u32[]{:S(2)}, u32[]{:S(2)}) async-start(bf16[32,2,128,128]{3,2,1,0:T(8,128)(2,1)} %pick_modes.1), calls=%async_computation.1 | async-start | bytes 4194304 | tf_op jit(solution)/shard_map/all_to_all | solution.py:32
  22.8 9.5 %condense.1 = (bf16[2,512,512]{2,1,0:T(8,128)(2,1)}, bf16[2,512,512]{2,1,0:T(8,128)(2,1)}, f32[2,1,512]{2,1,0:T(1,128)}, bf16[4,128,128]{2,1,0:T(8,128)(2,1)}, b...) custom-call(s32[2,4]{1,0:T(2,128)} %map_ref.5, ...), custom_call_target="tpu_custom_call" | custom-call | tf_op jit(solution)/shard_map/condense/pallas_call | solution.py:217
  32.5 1.6 collective-permute-start.1
  34.3 1.7 collective-permute-start.3
  36.0 0.8 fusion.11
  36.8 0.8 dynamic_update_slice.216
  37.6 0.8 fusion.10
  38.4 0.8 dynamic_update_slice.248
  39.3 0.8 dynamic_update_slice.240
  40.1 0.8 dynamic_update_slice.232
  40.9 2.6 %collective-permute-start.5 = (bf16[4,128,128]{2,1,0:T(8,128)(2,1)S(1)}, bf16[4,128,128]{2,1,0:T(8,128)(2,1)S(1)}, u32[]{:S(2)}, u32[]{:S(2)}) collective-permute-start(bf16[4,128,128]{2,1,0:T(8,128)(2,1)S(1)} %copy-done.19), channel_id=1, source_target_pairs={{0,6},{1,7},{2,4},{3,5},{4,2},{5,3},{6,0},{7,1},{8,14},{9,15},{10,... | collective-permute-start | bytes 393224 | tf_op jit(solution)/shard_map/ppermute | solution.py:414
  43.6 0.6 slice_dynamic-update-slice_fusion.34
  44.9 1.0 collective-permute-done.2
  47.0 3.0 %collective-permute-start.11 = (bf16[4,136,128]{2,1,0:T(8,128)(2,1)S(1)}, bf16[4,136,128]{2,1,0:T(8,128)(2,1)S(1)}, u32[]{:S(2)}, u32[]{:S(2)}) collective-permute-start(bf16[4,136,128]{2,1,0:T(8,128)(2,1)S(1)} %copy-done.16), channel_id=1, source_target_pairs={{0,2},{1,3},{2,0},{3,1},{4,6},{5,7},{6,4},{7,5},{8,10},{9,11},{10,... | collective-permute-start | bytes 417800 | tf_op jit(solution)/shard_map/ppermute | solution.py:414
  50.6 6.6 %collective-permute-done.4 = bf16[4,128,128]{2,1,0:T(8,128)(2,1)S(1)} collective-permute-done((bf16[4,128,128]{2,1,0:T(8,128)(2,1)}, bf16[4,128,128]{2,1,0:T(8,128)(2,1)S(1)}, u32[]{:S(2)}, u32[]{:S(2)}) %collective-permute-start.4) | collective-permute-done | bytes 131104 | tf_op jit(solution)/shard_map/ppermute | solution.py:414
  58.7 1.9 %collective-permute-start.14 = (bf16[4,136,128]{2,1,0:T(8,128)(2,1)}, bf16[4,136,128]{2,1,0:T(8,128)(2,1)S(1)}, u32[]{:S(2)}, u32[]{:S(2)}) collective-permute-start(bf16[4,136,128]{2,1,0:T(8,128)(2,1)} %get-tuple-element.47), channel_id=1, source_target_pairs={{0,5},{1,4},{2,7},{3,6},{4,1},{5,0},{6,3},{7,2},{8,13},{9,12},{10,... | collective-permute-start | bytes 417800 | tf_op jit(solution)/shard_map/ppermute | solution.py:414
  61.2 1.8 collective-permute-start.15
  63.0 0.6 slice_dynamic-update-slice_fusion.6
  64.3 0.7 slice_dynamic-update-slice_fusion.5
  64.9 3.8 %collective-permute-start.9 = (bf16[8,128,128]{2,1,0:T(8,128)(2,1)}, bf16[8,128,128]{2,1,0:T(8,128)(2,1)}, u32[]{:S(2)}, u32[]{:S(2)}) collective-permute-start(bf16[8,128,128]{2,1,0:T(8,128)(2,1)} %get-tuple-element.111), channel_id=1, source_target_pairs={{0,24},{1,25},{2,26},{3,27},{4,28},{5,29},{6,30},{7,31},{8,16},{9,... | collective-permute-start | bytes 786440 | tf_op jit(solution)/shard_map/ppermute | solution.py:414
  68.7 0.7 slice_dynamic-update-slice_fusion.4
  69.3 8.8 %all-to-all-done.1 = bf16[32,2,128,128]{3,2,1,0:T(8,128)(2,1)S(1)} async-done(((bf16[32,2,128,128]{3,2,1,0:T(8,128)(2,1)}), bf16[32,2,128,128]{3,2,1,0:T(8,128)(2,1)S(1)}, u32[]{:S(2)}, u32[]{:S(2)}) %all-to-all-start.1) | async-done | bytes 2097184 | tf_op jit(solution)/shard_map/all_to_all | solution.py:32
  78.1 1.3 copy-done
  79.5 7.5 %project_stiff.1 = (bf16[16,32,1024]{2,1,0:T(8,128)(2,1)}, f32[16,32,1024]{2,1,0:T(8,128)}, bf16[1024,1024]{1,0:T(8,128)(2,1)}) custom-call(s32[2,4]{1,0:T(2,128)} %map_ref.5, bf16[8,4,2,128,128]{4,3,2,1,0:T(8,128)(2,1)} %bitcast.36, bf16[2,512,512]{2,1,0:T(8,128)(2,1)} %get-tuple-element.52.m_ref), custom_call_target="tpu_custom_call" | custom-call | tf_op jit(solution)/shard_map/project_stiff/pallas_call | solution.py:338
  86.9 5.0 %mix_mass.1.y_ref = bf16[1024,1024]{1,0:T(8,128)(2,1)} custom-call(bf16[1024,1024]{1,0:T(8,128)(2,1)} %get-tuple-element.55.t_ref, bf16[2,512,512]{2,1,0:T(8,128)(2,1)} %get-tuple-element.56.m_ref, f32[2,1,512]{2,1,0:T(1,128)} %get-tuple-element.57.d_ref), custom_call_target="tpu_custom_call" | custom-call | tf_op jit(solution)/shard_map/mix_mass/pallas_call | solution.py:373
  91.9 5.9 %project_mass.1 = (bf16[16,32,1024]{2,1,0:T(8,128)(2,1)}, f32[16,32,1024]{2,1,0:T(8,128)}) custom-call(bf16[1024,1024]{1,0:T(8,128)(2,1)} %mix_mass.1.y_ref, bf16[1024,1024]{1,0:T(8,128)(2,1)} %get-tuple-element.55.t_ref), custom_call_target="tpu_custom_call" | custom-call | tf_op jit(solution)/shard_map/project_mass/pallas_call | solution.py:395
  97.9 0.7 slice_dynamic-update-slice_fusion.3
  98.6 0.7 slice_dynamic-update-slice_fusion.2
  99.8 1.5 slice_dynamic-update-slice_fusion.1
  101.3 1.5 slice_dynamic-update-slice_fusion
  102.8 3.9 %collective-permute-start.19 = (bf16[8,136,128]{2,1,0:T(8,128)(2,1)}, bf16[8,136,128]{2,1,0:T(8,128)(2,1)S(1)}, u32[]{:S(2)}, u32[]{:S(2)}) collective-permute-start(bf16[8,136,128]{2,1,0:T(8,128)(2,1)} %get-tuple-element.79), channel_id=1, source_target_pairs={{0,24},{1,25},{2,26},{3,27},{4,28},{5,29},{6,30},{7,31},{8,16},{9,... | collective-permute-start | bytes 835592 | tf_op jit(solution)/shard_map/ppermute | solution.py:414
  106.7 6.7 %collective-permute-done.8.refs_5_ = bf16[8,128,128]{2,1,0:T(8,128)(2,1)S(1)} collective-permute-done((bf16[8,128,128]{2,1,0:T(8,128)(2,1)S(1)}, bf16[8,128,128]{2,1,0:T(8,128)(2,1)S(1)}, u32[]{:S(2)}, u32[]{:S(2)}) %collective-permute-start.8) | collective-permute-done | bytes 262176 | tf_op jit(solution)/shard_map/ppermute | solution.py:414
  113.3 6.2 %collective-permute-done.7.refs_4_ = bf16[8,128,128]{2,1,0:T(8,128)(2,1)S(1)} collective-permute-done((bf16[8,128,128]{2,1,0:T(8,128)(2,1)S(1)}, bf16[8,128,128]{2,1,0:T(8,128)(2,1)S(1)}, u32[]{:S(2)}, u32[]{:S(2)}) %collective-permute-start.7) | collective-permute-done | bytes 262176 | tf_op jit(solution)/shard_map/ppermute | solution.py:414
  119.8 11.3 %clear_tiles.1 = (bf16[2048,4096]{1,0:T(8,128)(2,1)}, bf16[2048,4096]{1,0:T(8,128)(2,1)}) custom-call(s32[32,128]{1,0:T(8,128)} %bitcast.40), custom_call_target="tpu_custom_call" | custom-call | tf_op jit(solution)/shard_map/clear_tiles/pallas_call | solution.py:467
  131.3 0.6 select_reduce_fusion
  131.9 3.7 %place_stiff.1 = bf16[2048,4096]{1,0:T(8,128)(2,1)} custom-call(s32[32,128]{1,0:T(8,128)} %bitcast.41, s32[32]{0:T(128)} %get-tuple-element.62.refs_1_, s32[32]{0:T(128)} %get-tuple-element.61.refs_2_, bf16[8,128,128]{2,1,0:T(8,128)(2,1)} %copy-done.3, bf16[8,128,128]{2,1,0:T(8,128)(2,1)} %copy-done.10, ...), custom_call_target="tpu_custom_call", output_to_operand_aliasing={{}: (7, {})} | custom-call | tf_op jit(solution)/shard_map/place_stiff/pallas_call | solution.py:558
  137.1 4.6 %place_mass.1 = (bf16[2048,4096]{1,0:T(8,128)(2,1)}, f32[4,1,128]{2,1,0:T(1,128)}) custom-call(s32[32,128]{1,0:T(8,128)} %bitcast.42, s32[32]{0:T(128)} %get-tuple-element.62.refs_1_, s32[32]{0:T(128)} %get-tuple-element.61.refs_2_, bf16[8,136,128]{2,1,0:T(8,128)(2,1)} %copy-done.2, bf16[8,136,128]{2,1,0:T(8,128)(2,1)} %copy-done.8, ...), custom_call_target="tpu_custom_call", output_to_operand_aliasing={{0}: (7, {})} | custom-call | tf_op jit(solution)/shard_map/place_mass/pallas_call | solution.py:558
  141.7 1.7 add_convert_fusion.2
  143.5 1.7 collective-permute-start.28
  145.7 1.3 collective-permute-start.29
  147.0 1.4 add_convert_fusion.5
  148.4 1.7 collective-permute-start.21
  150.6 2.1 %collective-permute-done.28 = bf16[4,32,1024]{2,1,0:T(8,128)(2,1)S(1)} collective-permute-done((bf16[4,32,1024]{2,1,0:T(8,128)(2,1)S(1)}, bf16[4,32,1024]{2,1,0:T(8,128)(2,1)S(1)}, u32[]{:S(2)}, u32[]{:S(2)}) %collective-permute-start.28) | collective-permute-done | bytes 262176 | tf_op jit(solution)/shard_map/ppermute | solution.py:414
  152.7 0.7 collective-permute-start.22
  153.4 5.1 %collective-permute-done.30 = bf16[4,32,1024]{2,1,0:T(8,128)(2,1)S(1)} collective-permute-done((bf16[4,32,1024]{2,1,0:T(8,128)(2,1)S(1)}, bf16[4,32,1024]{2,1,0:T(8,128)(2,1)S(1)}, u32[]{:S(2)}, u32[]{:S(2)}) %collective-permute-start.30) | collective-permute-done | bytes 262176 | tf_op jit(solution)/shard_map/ppermute | solution.py:414
  158.5 1.7 collective-permute-done.29
  160.2 1.2 fusion.8
  161.5 2.2 %collective-permute-start.31 = (bf16[32,1024]{1,0:T(8,128)(2,1)S(1)}, bf16[32,1024]{1,0:T(8,128)(2,1)S(1)}, u32[]{:S(2)}, u32[]{:S(2)}) collective-permute-start(bf16[32,1024]{1,0:T(8,128)(2,1)S(1)} %get-tuple-element.73), channel_id=1, source_target_pairs={{0,8},{1,9},{2,10},{3,11},{4,12},{5,13},{6,14},{7,15},{8,0},{9,1},... | collective-permute-start | bytes 196616 | tf_op jit(solution)/shard_map/ppermute | solution.py:414
  163.7 1.9 %collective-permute-start.33 = (bf16[32,1024]{1,0:T(8,128)(2,1)S(1)}, bf16[32,1024]{1,0:T(8,128)(2,1)S(1)}, u32[]{:S(2)}, u32[]{:S(2)}) collective-permute-start(bf16[32,1024]{1,0:T(8,128)(2,1)S(1)} %get-tuple-element.74), channel_id=1, source_target_pairs={{0,24},{1,25},{2,26},{3,27},{4,28},{5,29},{6,30},{7,31},{8,16},{9,... | collective-permute-start | bytes 196616 | tf_op jit(solution)/shard_map/ppermute | solution.py:414
  165.6 3.0 %collective-permute-done.23 = bf16[4,32,1024]{2,1,0:T(8,128)(2,1)S(1)} collective-permute-done((bf16[4,32,1024]{2,1,0:T(8,128)(2,1)S(1)}, bf16[4,32,1024]{2,1,0:T(8,128)(2,1)S(1)}, u32[]{:S(2)}, u32[]{:S(2)}) %collective-permute-start.23) | collective-permute-done | bytes 262176 | tf_op jit(solution)/shard_map/ppermute | solution.py:414
  168.6 1.4 collective-permute-done.22
  170.0 1.2 fusion.9
  171.2 1.6 collective-permute-start.24
  172.8 1.1 collective-permute-start.26
  173.9 0.9 collective-permute-start.25
  174.8 0.7 fusion.2
  175.8 3.1 %collective-permute-done.26 = bf16[32,1024]{1,0:T(8,128)(2,1)S(1)} collective-permute-done((bf16[32,1024]{1,0:T(8,128)(2,1)S(1)}, bf16[32,1024]{1,0:T(8,128)(2,1)S(1)}, u32[]{:S(2)}, u32[]{:S(2)}) %collective-permute-start.26) | collective-permute-done | bytes 65568 | tf_op jit(solution)/shard_map/ppermute | solution.py:414
  179.0 1.3 collective-permute-done.25
  180.3 0.7 fusion.5
  (93 shorter events, 10.0 us)
Async XLA Ops:
  2.0 14.4 %all-to-all-start = ((s32[32,1,128]{2,1,0:T(1,128)}), s32[32,1,128]{2,1,0:T(1,128)S(1)}, u32[]{:S(2)}, u32[]{:S(2)}) async-start(s32[32,1,128]{2,1,0:T(1,128)} %bitcast.44), calls=%async_computation | async-start | bytes 32768 | tf_op jit(solution)/shard_map/all_to_all | solution.py:32
  16.4 0.6 copy-start.4
  20.1 58.0 %all-to-all-start.1 = ((bf16[32,2,128,128]{3,2,1,0:T(8,128)(2,1)}), bf16[32,2,128,128]{3,2,1,0:T(8,128)(2,1)S(1)}, u32[]{:S(2)}, u32[]{:S(2)}) async-start(bf16[32,2,128,128]{3,2,1,0:T(8,128)(2,1)} %pick_modes.1), calls=%async_computation.1 | async-start | bytes 4194304 | tf_op jit(solution)/shard_map/all_to_all | solution.py:32
  32.3 8.6 %copy-start.19 = (bf16[4,128,128]{2,1,0:T(8,128)(2,1)S(1)}, bf16[4,128,128]{2,1,0:T(8,128)(2,1)}, u32[]{:S(2)}) copy-start(bf16[4,128,128]{2,1,0:T(8,128)(2,1)} %get-tuple-element.39) | copy-start | bytes 393220
  32.3 11.9 %copy-start.18 = (bf16[4,128,128]{2,1,0:T(8,128)(2,1)S(1)}, bf16[4,128,128]{2,1,0:T(8,128)(2,1)}, u32[]{:S(2)}) copy-start(bf16[4,128,128]{2,1,0:T(8,128)(2,1)} %get-tuple-element.40) | copy-start | bytes 393220
  32.3 13.6 %copy-start.17 = (bf16[4,136,128]{2,1,0:T(8,128)(2,1)S(1)}, bf16[4,136,128]{2,1,0:T(8,128)(2,1)}, u32[]{:S(2)}) copy-start(bf16[4,136,128]{2,1,0:T(8,128)(2,1)} %get-tuple-element.43) | copy-start | bytes 417796
  32.3 14.6 %copy-start.16 = (bf16[4,136,128]{2,1,0:T(8,128)(2,1)S(1)}, bf16[4,136,128]{2,1,0:T(8,128)(2,1)}, u32[]{:S(2)}) copy-start(bf16[4,136,128]{2,1,0:T(8,128)(2,1)} %get-tuple-element.44) | copy-start | bytes 417796
  32.3 24.9 %copy-start.15 = (bf16[4,136,128]{2,1,0:T(8,128)(2,1)S(1)}, bf16[4,136,128]{2,1,0:T(8,128)(2,1)}, u32[]{:S(2)}) copy-start(bf16[4,136,128]{2,1,0:T(8,128)(2,1)} %get-tuple-element.45) | copy-start | bytes 417796
  32.4 8.6 %collective-permute-start = (bf16[4,128,128]{2,1,0:T(8,128)(2,1)}, bf16[4,128,128]{2,1,0:T(8,128)(2,1)S(1)}, u32[]{:S(2)}, u32[]{:S(2)}) collective-permute-start(bf16[4,128,128]{2,1,0:T(8,128)(2,1)} %get-tuple-element.34), channel_id=1, source_target_pairs={{0,1},{1,0},{2,3},{3,2},{4,5},{5,4},{6,7},{7,6},{8,9},{9,8},{10,11... | collective-permute-start | bytes 393224 | tf_op jit(solution)/shard_map/ppermute | solution.py:414
  32.5 11.7 %collective-permute-start.1 = (bf16[4,128,128]{2,1,0:T(8,128)(2,1)}, bf16[4,128,128]{2,1,0:T(8,128)(2,1)S(1)}, u32[]{:S(2)}, u32[]{:S(2)}) collective-permute-start(bf16[4,128,128]{2,1,0:T(8,128)(2,1)} %get-tuple-element.35), channel_id=1, source_target_pairs={{0,2},{1,3},{2,0},{3,1},{4,6},{5,7},{6,4},{7,5},{8,10},{9,11},{10,... | collective-permute-start | bytes 393224 | tf_op jit(solution)/shard_map/ppermute | solution.py:414
  34.2 11.7 %collective-permute-start.2 = (bf16[4,128,128]{2,1,0:T(8,128)(2,1)}, bf16[4,128,128]{2,1,0:T(8,128)(2,1)S(1)}, u32[]{:S(2)}, u32[]{:S(2)}) collective-permute-start(bf16[4,128,128]{2,1,0:T(8,128)(2,1)} %get-tuple-element.36), channel_id=1, source_target_pairs={{0,3},{1,2},{2,1},{3,0},{4,7},{5,6},{6,5},{7,4},{8,11},{9,10},{10,... | collective-permute-start | bytes 393224 | tf_op jit(solution)/shard_map/ppermute | solution.py:414
  34.3 12.7 %collective-permute-start.3 = (bf16[4,128,128]{2,1,0:T(8,128)(2,1)}, bf16[4,128,128]{2,1,0:T(8,128)(2,1)S(1)}, u32[]{:S(2)}, u32[]{:S(2)}) collective-permute-start(bf16[4,128,128]{2,1,0:T(8,128)(2,1)} %get-tuple-element.37), channel_id=1, source_target_pairs={{0,4},{1,5},{2,6},{3,7},{4,0},{5,1},{6,2},{7,3},{8,12},{9,13},{10,... | collective-permute-start | bytes 393224 | tf_op jit(solution)/shard_map/ppermute | solution.py:414
  35.9 21.3 %collective-permute-start.4 = (bf16[4,128,128]{2,1,0:T(8,128)(2,1)}, bf16[4,128,128]{2,1,0:T(8,128)(2,1)S(1)}, u32[]{:S(2)}, u32[]{:S(2)}) collective-permute-start(bf16[4,128,128]{2,1,0:T(8,128)(2,1)} %get-tuple-element.38), channel_id=1, source_target_pairs={{0,5},{1,4},{2,7},{3,6},{4,1},{5,0},{6,3},{7,2},{8,13},{9,12},{10,... | collective-permute-start | bytes 393224 | tf_op jit(solution)/shard_map/ppermute | solution.py:414
  40.9 17.0 %collective-permute-start.5 = (bf16[4,128,128]{2,1,0:T(8,128)(2,1)S(1)}, bf16[4,128,128]{2,1,0:T(8,128)(2,1)S(1)}, u32[]{:S(2)}, u32[]{:S(2)}) collective-permute-start(bf16[4,128,128]{2,1,0:T(8,128)(2,1)S(1)} %copy-done.19), channel_id=1, source_target_pairs={{0,6},{1,7},{2,4},{3,5},{4,2},{5,3},{6,0},{7,1},{8,14},{9,15},{10,... | collective-permute-start | bytes 393224 | tf_op jit(solution)/shard_map/ppermute | solution.py:414
  44.2 14.5 %collective-permute-start.6 = (bf16[4,128,128]{2,1,0:T(8,128)(2,1)S(1)}, bf16[4,128,128]{2,1,0:T(8,128)(2,1)S(1)}, u32[]{:S(2)}, u32[]{:S(2)}) collective-permute-start(bf16[4,128,128]{2,1,0:T(8,128)(2,1)S(1)} %copy-done.18), channel_id=1, source_target_pairs={{0,7},{1,6},{2,5},{3,4},{4,3},{5,2},{6,1},{7,0},{8,15},{9,14},{10,... | collective-permute-start | bytes 393224 | tf_op jit(solution)/shard_map/ppermute | solution.py:414
  45.9 15.3 %collective-permute-start.10 = (bf16[4,136,128]{2,1,0:T(8,128)(2,1)S(1)}, bf16[4,136,128]{2,1,0:T(8,128)(2,1)S(1)}, u32[]{:S(2)}, u32[]{:S(2)}) collective-permute-start(bf16[4,136,128]{2,1,0:T(8,128)(2,1)S(1)} %copy-done.17), channel_id=1, source_target_pairs={{0,1},{1,0},{2,3},{3,2},{4,5},{5,4},{6,7},{7,6},{8,9},{9,8},{10,11... | collective-permute-start | bytes 417800 | tf_op jit(solution)/shard_map/ppermute | solution.py:414
  47.0 16.7 %collective-permute-start.11 = (bf16[4,136,128]{2,1,0:T(8,128)(2,1)S(1)}, bf16[4,136,128]{2,1,0:T(8,128)(2,1)S(1)}, u32[]{:S(2)}, u32[]{:S(2)}) collective-permute-start(bf16[4,136,128]{2,1,0:T(8,128)(2,1)S(1)} %copy-done.16), channel_id=1, source_target_pairs={{0,2},{1,3},{2,0},{3,1},{4,6},{5,7},{6,4},{7,5},{8,10},{9,11},{10,... | collective-permute-start | bytes 417800 | tf_op jit(solution)/shard_map/ppermute | solution.py:414
  57.3 7.7 %collective-permute-start.12 = (bf16[4,136,128]{2,1,0:T(8,128)(2,1)S(1)}, bf16[4,136,128]{2,1,0:T(8,128)(2,1)S(1)}, u32[]{:S(2)}, u32[]{:S(2)}) collective-permute-start(bf16[4,136,128]{2,1,0:T(8,128)(2,1)S(1)} %copy-done.15), channel_id=1, source_target_pairs={{0,3},{1,2},{2,1},{3,0},{4,7},{5,6},{6,5},{7,4},{8,11},{9,10},{10,... | collective-permute-start | bytes 417800 | tf_op jit(solution)/shard_map/ppermute | solution.py:414
  57.9 39.9 %collective-permute-start.13 = (bf16[4,136,128]{2,1,0:T(8,128)(2,1)}, bf16[4,136,128]{2,1,0:T(8,128)(2,1)S(1)}, u32[]{:S(2)}, u32[]{:S(2)}) collective-permute-start(bf16[4,136,128]{2,1,0:T(8,128)(2,1)} %get-tuple-element.46), channel_id=1, source_target_pairs={{0,4},{1,5},{2,6},{3,7},{4,0},{5,1},{6,2},{7,3},{8,12},{9,13},{10,... | collective-permute-start | bytes 417800 | tf_op jit(solution)/shard_map/ppermute | solution.py:414
  58.7 39.9 %collective-permute-start.14 = (bf16[4,136,128]{2,1,0:T(8,128)(2,1)}, bf16[4,136,128]{2,1,0:T(8,128)(2,1)S(1)}, u32[]{:S(2)}, u32[]{:S(2)}) collective-permute-start(bf16[4,136,128]{2,1,0:T(8,128)(2,1)} %get-tuple-element.47), channel_id=1, source_target_pairs={{0,5},{1,4},{2,7},{3,6},{4,1},{5,0},{6,3},{7,2},{8,13},{9,12},{10,... | collective-permute-start | bytes 417800 | tf_op jit(solution)/shard_map/ppermute | solution.py:414
  61.2 7.5 %copy-start.11 = (bf16[8,128,128]{2,1,0:T(8,128)(2,1)}, bf16[8,128,128]{2,1,0:T(8,128)(2,1)S(1)}, u32[]{:S(2)}) copy-start(bf16[8,128,128]{2,1,0:T(8,128)(2,1)S(1)} %get-tuple-element.112) | copy-start | bytes 786436
  61.2 7.5 %copy-start.13 = (bf16[8,128,128]{2,1,0:T(8,128)(2,1)}, bf16[8,128,128]{2,1,0:T(8,128)(2,1)S(1)}, u32[]{:S(2)}) copy-start(bf16[8,128,128]{2,1,0:T(8,128)(2,1)S(1)} %get-tuple-element.113) | copy-start | bytes 786436
  61.2 30.7 %copy-start.3 = (bf16[8,128,128]{2,1,0:T(8,128)(2,1)}, bf16[8,128,128]{2,1,0:T(8,128)(2,1)S(1)}, u32[]{:S(2)}) copy-start(bf16[8,128,128]{2,1,0:T(8,128)(2,1)S(1)} %get-tuple-element.114.refs_3_) | copy-start | bytes 786436
  61.2 38.0 %collective-permute-start.15 = (bf16[4,136,128]{2,1,0:T(8,128)(2,1)}, bf16[4,136,128]{2,1,0:T(8,128)(2,1)}, u32[]{:S(2)}, u32[]{:S(2)}) collective-permute-start(bf16[4,136,128]{2,1,0:T(8,128)(2,1)} %get-tuple-element.48), channel_id=1, source_target_pairs={{0,6},{1,7},{2,4},{3,5},{4,2},{5,3},{6,0},{7,1},{8,14},{9,15},{10,... | collective-permute-start | bytes 417800 | tf_op jit(solution)/shard_map/ppermute | solution.py:414
  63.7 35.6 %collective-permute-start.16 = (bf16[4,136,128]{2,1,0:T(8,128)(2,1)}, bf16[4,136,128]{2,1,0:T(8,128)(2,1)}, u32[]{:S(2)}, u32[]{:S(2)}) collective-permute-start(bf16[4,136,128]{2,1,0:T(8,128)(2,1)} %get-tuple-element.49), channel_id=1, source_target_pairs={{0,7},{1,6},{2,5},{3,4},{4,3},{5,2},{6,1},{7,0},{8,15},{9,14},{10,... | collective-permute-start | bytes 417800 | tf_op jit(solution)/shard_map/ppermute | solution.py:414
  64.9 37.9 %collective-permute-start.9 = (bf16[8,128,128]{2,1,0:T(8,128)(2,1)}, bf16[8,128,128]{2,1,0:T(8,128)(2,1)}, u32[]{:S(2)}, u32[]{:S(2)}) collective-permute-start(bf16[8,128,128]{2,1,0:T(8,128)(2,1)} %get-tuple-element.111), channel_id=1, source_target_pairs={{0,24},{1,25},{2,26},{3,27},{4,28},{5,29},{6,30},{7,31},{8,16},{9,... | collective-permute-start | bytes 786440 | tf_op jit(solution)/shard_map/ppermute | solution.py:414
  78.1 1.3 copy-start
  91.9 6.7 %copy-start.12 = (bf16[8,128,128]{2,1,0:T(8,128)(2,1)S(1)}, bf16[8,128,128]{2,1,0:T(8,128)(2,1)}, u32[]{:S(2)}) copy-start(bf16[8,128,128]{2,1,0:T(8,128)(2,1)} %copy-done.11) | copy-start | bytes 786436
  91.9 7.4 %copy-start.14 = (bf16[8,128,128]{2,1,0:T(8,128)(2,1)S(1)}, bf16[8,128,128]{2,1,0:T(8,128)(2,1)}, u32[]{:S(2)}) copy-start(bf16[8,128,128]{2,1,0:T(8,128)(2,1)} %copy-done.13) | copy-start | bytes 786436
  91.9 27.7 %copy-start.5 = (s32[32,1,128]{2,1,0:T(1,128)S(1)}, s32[32,1,128]{2,1,0:T(1,128)}, u32[]{:S(2)}) copy-start(s32[32,1,128]{2,1,0:T(1,128)} %copy-done.4) | copy-start | bytes 49156
  97.9 43.8 %collective-permute-start.27 = (bf16[16,32,1024]{2,1,0:T(8,128)(2,1)}, bf16[16,32,1024]{2,1,0:T(8,128)(2,1)S(1)}, u32[]{:S(2)}, u32[]{:S(2)}) collective-permute-start(bf16[16,32,1024]{2,1,0:T(8,128)(2,1)} %get-tuple-element.59), channel_id=1, source_target_pairs={{0,1},{1,0},{2,3},{3,2},{4,5},{5,4},{6,7},{7,6},{8,9},{9,8},{10,11... | collective-permute-start | bytes 3145736 | tf_op jit(solution)/shard_map/ppermute | solution.py:414
  98.6 14.7 %collective-permute-start.8 = (bf16[8,128,128]{2,1,0:T(8,128)(2,1)S(1)}, bf16[8,128,128]{2,1,0:T(8,128)(2,1)S(1)}, u32[]{:S(2)}, u32[]{:S(2)}) collective-permute-start(bf16[8,128,128]{2,1,0:T(8,128)(2,1)S(1)} %copy-done.12), channel_id=1, source_target_pairs={{0,16},{1,17},{2,18},{3,19},{4,20},{5,21},{6,22},{7,23},{8,24},{9,... | collective-permute-start | bytes 786440 | tf_op jit(solution)/shard_map/ppermute | solution.py:414
  99.3 20.3 %collective-permute-start.7 = (bf16[8,128,128]{2,1,0:T(8,128)(2,1)S(1)}, bf16[8,128,128]{2,1,0:T(8,128)(2,1)S(1)}, u32[]{:S(2)}, u32[]{:S(2)}) collective-permute-start(bf16[8,128,128]{2,1,0:T(8,128)(2,1)S(1)} %copy-done.14), channel_id=1, source_target_pairs={{0,8},{1,9},{2,10},{3,11},{4,12},{5,13},{6,14},{7,15},{8,0},{9,1},... | collective-permute-start | bytes 786440 | tf_op jit(solution)/shard_map/ppermute | solution.py:414
  99.3 47.7 %collective-permute-start.20 = (bf16[16,32,1024]{2,1,0:T(8,128)(2,1)}, bf16[16,32,1024]{2,1,0:T(8,128)(2,1)}, u32[]{:S(2)}, u32[]{:S(2)}) collective-permute-start(bf16[16,32,1024]{2,1,0:T(8,128)(2,1)} %get-tuple-element.54), channel_id=1, source_target_pairs={{0,1},{1,0},{2,3},{3,2},{4,5},{5,4},{6,7},{7,6},{8,9},{9,8},{10,11... | collective-permute-start | bytes 3145736 | tf_op jit(solution)/shard_map/ppermute | solution.py:414
  102.8 32.8 %copy-start.2 = (bf16[8,136,128]{2,1,0:T(8,128)(2,1)}, bf16[8,136,128]{2,1,0:T(8,128)(2,1)S(1)}, u32[]{:S(2)}) copy-start(bf16[8,136,128]{2,1,0:T(8,128)(2,1)S(1)} %get-tuple-element.82.refs_3_) | copy-start | bytes 835588
  102.8 32.8 %collective-permute-start.19 = (bf16[8,136,128]{2,1,0:T(8,128)(2,1)}, bf16[8,136,128]{2,1,0:T(8,128)(2,1)S(1)}, u32[]{:S(2)}, u32[]{:S(2)}) collective-permute-start(bf16[8,136,128]{2,1,0:T(8,128)(2,1)} %get-tuple-element.79), channel_id=1, source_target_pairs={{0,24},{1,25},{2,26},{3,27},{4,28},{5,29},{6,30},{7,31},{8,16},{9,... | collective-permute-start | bytes 835592 | tf_op jit(solution)/shard_map/ppermute | solution.py:414
  113.3 18.6 %copy-start.9 = (bf16[8,128,128]{2,1,0:T(8,128)(2,1)}, bf16[8,128,128]{2,1,0:T(8,128)(2,1)S(1)}, u32[]{:S(2)}) copy-start(bf16[8,128,128]{2,1,0:T(8,128)(2,1)S(1)} %collective-permute-done.8.refs_5_) | copy-start | bytes 786436
  113.3 22.9 %collective-permute-start.18 = (bf16[8,136,128]{2,1,0:T(8,128)(2,1)}, bf16[8,136,128]{2,1,0:T(8,128)(2,1)S(1)}, u32[]{:S(2)}, u32[]{:S(2)}) collective-permute-start(bf16[8,136,128]{2,1,0:T(8,128)(2,1)} %get-tuple-element.80), channel_id=1, source_target_pairs={{0,16},{1,17},{2,18},{3,19},{4,20},{5,21},{6,22},{7,23},{8,24},{9,... | collective-permute-start | bytes 835592 | tf_op jit(solution)/shard_map/ppermute | solution.py:414
  119.6 12.4 %copy-start.10 = (bf16[8,128,128]{2,1,0:T(8,128)(2,1)}, bf16[8,128,128]{2,1,0:T(8,128)(2,1)S(1)}, u32[]{:S(2)}) copy-start(bf16[8,128,128]{2,1,0:T(8,128)(2,1)S(1)} %collective-permute-done.7.refs_4_) | copy-start | bytes 786436
  119.6 16.6 %collective-permute-start.17 = (bf16[8,136,128]{2,1,0:T(8,128)(2,1)}, bf16[8,136,128]{2,1,0:T(8,128)(2,1)S(1)}, u32[]{:S(2)}, u32[]{:S(2)}) collective-permute-start(bf16[8,136,128]{2,1,0:T(8,128)(2,1)} %get-tuple-element.81), channel_id=1, source_target_pairs={{0,8},{1,9},{2,10},{3,11},{4,12},{5,13},{6,14},{7,15},{8,0},{9,1},... | collective-permute-start | bytes 835592 | tf_op jit(solution)/shard_map/ppermute | solution.py:414
  135.6 0.8 copy-start.6
  136.2 0.7 copy-start.7
  136.2 0.9 copy-start.8
  141.7 5.3 %copy-start.1 = (f32[16,32,1024]{2,1,0:T(8,128)S(1)}, f32[16,32,1024]{2,1,0:T(8,128)}, u32[]{:S(2)}) copy-start(f32[16,32,1024]{2,1,0:T(8,128)} %get-tuple-element.53) | copy-start | bytes 6291460
  143.5 9.2 %collective-permute-start.28 = (bf16[4,32,1024]{2,1,0:T(8,128)(2,1)S(1)}, bf16[4,32,1024]{2,1,0:T(8,128)(2,1)S(1)}, u32[]{:S(2)}, u32[]{:S(2)}) collective-permute-start(bf16[4,32,1024]{2,1,0:T(8,128)(2,1)S(1)} %get-tuple-element.67), channel_id=1, source_target_pairs={{0,2},{1,3},{2,0},{3,1},{4,6},{5,7},{6,4},{7,5},{8,10},{9,11},{10,... | collective-permute-start | bytes 786440 | tf_op jit(solution)/shard_map/ppermute | solution.py:414
  145.2 13.3 %collective-permute-start.30 = (bf16[4,32,1024]{2,1,0:T(8,128)(2,1)S(1)}, bf16[4,32,1024]{2,1,0:T(8,128)(2,1)S(1)}, u32[]{:S(2)}, u32[]{:S(2)}) collective-permute-start(bf16[4,32,1024]{2,1,0:T(8,128)(2,1)S(1)} %get-tuple-element.68), channel_id=1, source_target_pairs={{0,6},{1,7},{2,4},{3,5},{4,2},{5,3},{6,0},{7,1},{8,14},{9,15},{10,... | collective-permute-start | bytes 786440 | tf_op jit(solution)/shard_map/ppermute | solution.py:414
  145.7 14.5 %collective-permute-start.29 = (bf16[4,32,1024]{2,1,0:T(8,128)(2,1)S(1)}, bf16[4,32,1024]{2,1,0:T(8,128)(2,1)S(1)}, u32[]{:S(2)}, u32[]{:S(2)}) collective-permute-start(bf16[4,32,1024]{2,1,0:T(8,128)(2,1)S(1)} %get-tuple-element.69), channel_id=1, source_target_pairs={{0,4},{1,5},{2,6},{3,7},{4,0},{5,1},{6,2},{7,3},{8,12},{9,13},{10,... | collective-permute-start | bytes 786440 | tf_op jit(solution)/shard_map/ppermute | solution.py:414
  148.4 17.2 %collective-permute-start.21 = (bf16[4,32,1024]{2,1,0:T(8,128)(2,1)S(1)}, bf16[4,32,1024]{2,1,0:T(8,128)(2,1)S(1)}, u32[]{:S(2)}, u32[]{:S(2)}) collective-permute-start(bf16[4,32,1024]{2,1,0:T(8,128)(2,1)S(1)} %get-tuple-element.70), channel_id=1, source_target_pairs={{0,2},{1,3},{2,0},{3,1},{4,6},{5,7},{6,4},{7,5},{8,10},{9,11},{10,... | collective-permute-start | bytes 786440 | tf_op jit(solution)/shard_map/ppermute | solution.py:414
  150.1 18.5 %collective-permute-start.23 = (bf16[4,32,1024]{2,1,0:T(8,128)(2,1)S(1)}, bf16[4,32,1024]{2,1,0:T(8,128)(2,1)S(1)}, u32[]{:S(2)}, u32[]{:S(2)}) collective-permute-start(bf16[4,32,1024]{2,1,0:T(8,128)(2,1)S(1)} %get-tuple-element.71), channel_id=1, source_target_pairs={{0,6},{1,7},{2,4},{3,5},{4,2},{5,3},{6,0},{7,1},{8,14},{9,15},{10,... | collective-permute-start | bytes 786440 | tf_op jit(solution)/shard_map/ppermute | solution.py:414
  152.7 17.3 %collective-permute-start.22 = (bf16[4,32,1024]{2,1,0:T(8,128)(2,1)S(1)}, bf16[4,32,1024]{2,1,0:T(8,128)(2,1)S(1)}, u32[]{:S(2)}, u32[]{:S(2)}) collective-permute-start(bf16[4,32,1024]{2,1,0:T(8,128)(2,1)S(1)} %get-tuple-element.72), channel_id=1, source_target_pairs={{0,4},{1,5},{2,6},{3,7},{4,0},{5,1},{6,2},{7,3},{8,12},{9,13},{10,... | collective-permute-start | bytes 786440 | tf_op jit(solution)/shard_map/ppermute | solution.py:414
  161.5 12.4 %collective-permute-start.31 = (bf16[32,1024]{1,0:T(8,128)(2,1)S(1)}, bf16[32,1024]{1,0:T(8,128)(2,1)S(1)}, u32[]{:S(2)}, u32[]{:S(2)}) collective-permute-start(bf16[32,1024]{1,0:T(8,128)(2,1)S(1)} %get-tuple-element.73), channel_id=1, source_target_pairs={{0,8},{1,9},{2,10},{3,11},{4,12},{5,13},{6,14},{7,15},{8,0},{9,1},... | collective-permute-start | bytes 196616 | tf_op jit(solution)/shard_map/ppermute | solution.py:414
  163.7 11.1 %collective-permute-start.33 = (bf16[32,1024]{1,0:T(8,128)(2,1)S(1)}, bf16[32,1024]{1,0:T(8,128)(2,1)S(1)}, u32[]{:S(2)}, u32[]{:S(2)}) collective-permute-start(bf16[32,1024]{1,0:T(8,128)(2,1)S(1)} %get-tuple-element.74), channel_id=1, source_target_pairs={{0,24},{1,25},{2,26},{3,27},{4,28},{5,29},{6,30},{7,31},{8,16},{9,... | collective-permute-start | bytes 196616 | tf_op jit(solution)/shard_map/ppermute | solution.py:414
  165.6 9.2 %collective-permute-start.32 = (bf16[32,1024]{1,0:T(8,128)(2,1)S(1)}, bf16[32,1024]{1,0:T(8,128)(2,1)S(1)}, u32[]{:S(2)}, u32[]{:S(2)}) collective-permute-start(bf16[32,1024]{1,0:T(8,128)(2,1)S(1)} %get-tuple-element.75), channel_id=1, source_target_pairs={{0,16},{1,17},{2,18},{3,19},{4,20},{5,21},{6,22},{7,23},{8,24},{9,... | collective-permute-start | bytes 196616 | tf_op jit(solution)/shard_map/ppermute | solution.py:414
  171.2 4.6 %collective-permute-start.24 = (bf16[32,1024]{1,0:T(8,128)(2,1)S(1)}, bf16[32,1024]{1,0:T(8,128)(2,1)S(1)}, u32[]{:S(2)}, u32[]{:S(2)}) collective-permute-start(bf16[32,1024]{1,0:T(8,128)(2,1)S(1)} %get-tuple-element.76), channel_id=1, source_target_pairs={{0,8},{1,9},{2,10},{3,11},{4,12},{5,13},{6,14},{7,15},{8,0},{9,1},... | collective-permute-start | bytes 196616 | tf_op jit(solution)/shard_map/ppermute | solution.py:414
  172.8 6.1 %collective-permute-start.26 = (bf16[32,1024]{1,0:T(8,128)(2,1)S(1)}, bf16[32,1024]{1,0:T(8,128)(2,1)S(1)}, u32[]{:S(2)}, u32[]{:S(2)}) collective-permute-start(bf16[32,1024]{1,0:T(8,128)(2,1)S(1)} %get-tuple-element.77), channel_id=1, source_target_pairs={{0,24},{1,25},{2,26},{3,27},{4,28},{5,29},{6,30},{7,31},{8,16},{9,... | collective-permute-start | bytes 196616 | tf_op jit(solution)/shard_map/ppermute | solution.py:414
  173.9 6.4 %collective-permute-start.25 = (bf16[32,1024]{1,0:T(8,128)(2,1)S(1)}, bf16[32,1024]{1,0:T(8,128)(2,1)S(1)}, u32[]{:S(2)}, u32[]{:S(2)}) collective-permute-start(bf16[32,1024]{1,0:T(8,128)(2,1)S(1)} %get-tuple-element.78), channel_id=1, source_target_pairs={{0,16},{1,17},{2,18},{3,19},{4,20},{5,21},{6,22},{7,23},{8,24},{9,... | collective-permute-start | bytes 196616 | tf_op jit(solution)/shard_map/ppermute | solution.py:414

commit v10 on v6

--- a/solution.py
+++ b/solution.py
@@ -128,30 +128,25 @@
         near_refs, out_ref, sem = refs[: sizes.plane], refs[-2], refs[-1]
         sub = pl.program_id(0)
         me = lax.axis_index("row") * sizes.cols + lax.axis_index("col")
-        couple = cpl_ref[0]
-        static_modes = (-jnp.dot(inv_ref[0], couple, preferred_element_type=F32)).astype(BF16)
-        contract = (((0,), (0,)), ((), ()))
+
+        def own_row(ref):
+            mine = lax.broadcasted_iota(jnp.int32, ref.shape, 0) == sub
+            return jnp.sum(jnp.where(mine, ref[...], 0.0), axis=0, keepdims=True)
+
+        masses, boundary_masses = own_row(mi_ref), own_row(mb_ref)
+        contract = (((1,), (1,)), ((), ()))
+        couple = cpl_ref[0].T
+        static_modes = (
+            -lax.dot_general(couple, inv_ref[0], contract, preferred_element_type=F32)
+        ).astype(BF16)
         stiff = stiff_ref[0].astype(F32) + lax.dot_general(
             couple, static_modes, contract, preferred_element_type=F32
         )
+        weighted = (static_modes.astype(F32) * masses).astype(BF16)
+        mass = lax.dot_general(static_modes, weighted, contract, preferred_element_type=F32)
         eye = lax.broadcasted_iota(jnp.int32, (BLK, BLK), 0) == lax.broadcasted_iota(
             jnp.int32, (BLK, BLK), 1
         )
-
-        def own_row(ref):
-            mine = lax.broadcasted_iota(jnp.int32, ref.shape, 0) == sub
-            return jnp.sum(jnp.where(mine, ref[...], 0.0), axis=0, keepdims=True)
-
-        masses, boundary_masses = own_row(mi_ref), own_row(mb_ref)
-        column = jnp.concatenate(
-            [
-                jnp.sum(jnp.where(eye, masses[:, i : i + BLK], 0.0), axis=1, keepdims=True)
-                for i in range(0, interior, BLK)
-            ],
-            axis=0,
-        )
-        weighted = (static_modes.astype(F32) * column).astype(BF16)
-        mass = lax.dot_general(static_modes, weighted, contract, preferred_element_type=F32)
         level = lax.broadcasted_iota(jnp.int32, (EXTRA, BLK), 0)
         for a in range(per_sub):
             block_a = map_ref[sub, a]
@@ -419,9 +414,9 @@
 
 
 def spread_in_plane(blocks, sizes):
-    near = [blocks[0]]
-    for d in range(1, sizes.plane):
-        near.append(swap(blocks[d], d, sizes.devices))
+    near = list(blocks)
+    for d in reversed(range(1, sizes.plane)):
+        near[d] = swap(blocks[d], d, sizes.devices)
     return [jnp.stack([part[z] for part in near]) for z in range(sizes.devices // sizes.plane)]
 
 

time: 189 us -> 189 us (level)
  no operation moved by 1% of the time
where the time goes in v10:
time: 189 us; the launch traced here: 188 us
  waiting for transfers between devices  67.7 us (36%)
  starting transfers between devices  51.7 us (27%)
  Pallas kernels  48.9 us (26%)
  local copies, waits for them, and re-layouts  13.8 us (7%)
  other arithmetic  5.37 us (3%)
    ppermute x24, waiting for transfers between devices, swap(): lax.ppermute(value, AXES, [(i, i ^ offset) for i in range(device_count)])  62.8 us
    ppermute x24, starting transfers between devices, swap(): lax.ppermute(value, AXES, [(i, i ^ offset) for i in range(device_count)])  41.6 us
    pallas_call x1, Pallas kernels, clear_tiles(): pl.pallas_call(kernel, in_specs=[ANY], out_specs=[ANY, ANY], out_shape=[j...  11.2 us
    unnamed x29, local copies, waits for them, and re-layouts  10.7 us
    all_to_all x2, starting transfers between devices, exchange(): return lax.all_to_all(value, AXES, split_axis=0, concat_axis=0, tiled=True)  10.1 us
    pallas_call x1, Pallas kernels, condense(): pl.pallas_call(kernel, grid=(local_subs,), in_specs=[SMEM, piece(interior...  9.54 us
    pallas_call x1, Pallas kernels, project_stiff(): pl.pallas_call(kernel, grid=(2,), in_specs=[SMEM, whole(*fetched.shape),...  7.44 us
    pallas_call x1, Pallas kernels, project_mass(): pl.pallas_call(kernel, grid=(2,), in_specs=[pl.BlockSpec((chunk, depth),...  6.01 us
  transfers between devices with their start and end apart: 26, of which 9 were waited for; matrix products, arithmetic and copies ran while one was open for 8% of the time, Pallas kernels for 14%

profile of v10, /device:TPU:0, one launch (start us, length us, event | category | flops | bytes accessed | tf_op | source)
XLA Modules:
  0.0 188.2 jit_solution(9095347523217785510)
XLA Ops:
  0.6 1.4 describe.1
  2.0 7.3 %all-to-all-start = ((s32[32,1,128]{2,1,0:T(1,128)}), s32[32,1,128]{2,1,0:T(1,128)S(1)}, u32[]{:S(2)}, u32[]{:S(2)}) async-start(s32[32,1,128]{2,1,0:T(1,128)} %bitcast.43), calls=%async_computation | async-start | bytes 32768 | tf_op jit(solution)/shard_map/all_to_all | solution.py:32
  9.3 2.3 %copy.18 = bf16[32,128,128]{1,2,0:T(8,128)(2,1)} copy(bf16[32,128,128]{2,1,0:T(8,128)(2,1)} %bitcast.38) | data formatting | bytes 2097152 | tf_op jit(solution)/shard_map/reshape | solution.py:568
  11.6 4.8 %all-to-all-done = s32[32,1,128]{2,1,0:T(1,128)S(1)} async-done(((s32[32,1,128]{2,1,0:T(1,128)}), s32[32,1,128]{2,1,0:T(1,128)S(1)}, u32[]{:S(2)}, u32[]{:S(2)}) %all-to-all-start) | async-done | bytes 16416 | tf_op jit(solution)/shard_map/all_to_all | solution.py:32
  16.4 0.6 copy-done.7
  17.0 2.8 %pick_modes.1 = bf16[32,2,128,128]{3,2,1,0:T(8,128)(2,1)} custom-call(s32[32,128]{1,0:T(8,128)} %bitcast.39, bf16[32,128,128]{2,1,0:T(8,128)(2,1)} %bitcast.37), custom_call_target="tpu_custom_call" | custom-call | tf_op jit(solution)/shard_map/pick_modes/pallas_call | solution.py:101
  19.8 2.7 %all-to-all-start.1 = ((bf16[32,2,128,128]{3,2,1,0:T(8,128)(2,1)}), bf16[32,2,128,128]{3,2,1,0:T(8,128)(2,1)S(1)}, u32[]{:S(2)}, u32[]{:S(2)}) async-start(bf16[32,2,128,128]{3,2,1,0:T(8,128)(2,1)} %pick_modes.1), calls=%async_computation.1 | async-start | bytes 4194304 | tf_op jit(solution)/shard_map/all_to_all | solution.py:32
  22.5 9.5 %condense.1 = (bf16[2,512,512]{2,1,0:T(8,128)(2,1)}, bf16[2,512,512]{2,1,0:T(8,128)(2,1)}, f32[2,1,512]{2,1,0:T(1,128)}, bf16[4,264,128]{2,1,0:T(8,128)(2,1)}, b...) custom-call(s32[2,4]{1,0:T(2,128)} %map_ref.5, ...), custom_call_target="tpu_custom_call" | custom-call | tf_op jit(solution)/shard_map/condense/pallas_call | solution.py:201
  32.1 0.2 collective-permute-start
  32.2 1.7 collective-permute-start.1
  33.9 0.1 collective-permute-start.2
  34.0 1.7 collective-permute-start.3
  35.6 0.1 collective-permute-start.4
  35.7 1.7 constant_dynamic-update-slice_fusion.3
  37.4 11.2 %clear_tiles.1 = (bf16[2048,4096]{1,0:T(8,128)(2,1)}, bf16[2048,4096]{1,0:T(8,128)(2,1)}) custom-call(s32[32,128]{1,0:T(8,128)} %bitcast.40), custom_call_target="tpu_custom_call" | custom-call | tf_op jit(solution)/shard_map/clear_tiles/pallas_call | solution.py:438
  48.6 2.6 %collective-permute-start.5 = (bf16[4,264,128]{2,1,0:T(8,128)(2,1)}, bf16[4,264,128]{2,1,0:T(8,128)(2,1)S(1)}, u32[]{:S(2)}, u32[]{:S(2)}) collective-permute-start(bf16[4,264,128]{2,1,0:T(8,128)(2,1)} %get-tuple-element.37), channel_id=1, source_target_pairs={{0,6},{1,7},{2,4},{3,5},{4,2},{5,3},{6,0},{7,1},{8,14},{9,15},{10,... | collective-permute-start | bytes 811016 | tf_op jit(solution)/shard_map/ppermute | solution.py:396
  51.3 1.7 slice_dynamic-update-slice_fusion.6
  53.0 0.1 collective-permute-start.6
  53.1 1.7 slice_dynamic-update-slice_fusion.5
  54.8 2.1 %collective-permute-done.2 = bf16[4,264,128]{2,1,0:T(8,128)(2,1)S(1)} collective-permute-done((bf16[4,264,128]{2,1,0:T(8,128)(2,1)}, bf16[4,264,128]{2,1,0:T(8,128)(2,1)S(1)}, u32[]{:S(2)}, u32[]{:S(2)}) %collective-permute-start.2) | collective-permute-done | bytes 270368 | tf_op jit(solution)/shard_map/ppermute | solution.py:396
  56.9 0.7 slice_dynamic-update-slice_fusion.4
  57.6 0.7 slice_dynamic-update-slice_fusion.3
  58.3 14.4 %collective-permute-done.4 = bf16[4,264,128]{2,1,0:T(8,128)(2,1)S(1)} collective-permute-done((bf16[4,264,128]{2,1,0:T(8,128)(2,1)}, bf16[4,264,128]{2,1,0:T(8,128)(2,1)S(1)}, u32[]{:S(2)}, u32[]{:S(2)}) %collective-permute-start.4) | collective-permute-done | bytes 270368 | tf_op jit(solution)/shard_map/ppermute | solution.py:396
  72.7 0.7 slice_dynamic-update-slice_fusion.2
  73.4 0.7 slice_dynamic-update-slice_fusion.1
  74.1 0.7 slice_dynamic-update-slice_fusion
  74.8 1.4 copy-done
  76.1 7.4 %project_stiff.1 = (bf16[16,32,1024]{2,1,0:T(8,128)(2,1)}, f32[16,32,1024]{2,1,0:T(8,128)}, bf16[1024,1024]{1,0:T(8,128)(2,1)}) custom-call(s32[2,4]{1,0:T(2,128)} %map_ref.5, bf16[8,4,2,128,128]{4,3,2,1,0:T(8,128)(2,1)} %bitcast.36, bf16[2,512,512]{2,1,0:T(8,128)(2,1)} %get-tuple-element.48.m_ref), custom_call_target="tpu_custom_call" | custom-call | tf_op jit(solution)/shard_map/project_stiff/pallas_call | solution.py:320
  83.6 5.0 %mix_mass.1.y_ref = bf16[1024,1024]{1,0:T(8,128)(2,1)} custom-call(bf16[1024,1024]{1,0:T(8,128)(2,1)} %get-tuple-element.51.t_ref, bf16[2,512,512]{2,1,0:T(8,128)(2,1)} %get-tuple-element.52.m_ref, f32[2,1,512]{2,1,0:T(1,128)} %get-tuple-element.53.d_ref), custom_call_target="tpu_custom_call" | custom-call | tf_op jit(solution)/shard_map/mix_mass/pallas_call | solution.py:355
  88.6 6.0 %project_mass.1 = (bf16[16,32,1024]{2,1,0:T(8,128)(2,1)}, f32[16,32,1024]{2,1,0:T(8,128)}) custom-call(bf16[1024,1024]{1,0:T(8,128)(2,1)} %mix_mass.1.y_ref, bf16[1024,1024]{1,0:T(8,128)(2,1)} %get-tuple-element.51.t_ref), custom_call_target="tpu_custom_call" | custom-call | tf_op jit(solution)/shard_map/project_mass/pallas_call | solution.py:377
  94.6 0.2 collective-permute-start.17
  94.8 0.4 collective-permute-start.10
  95.2 0.4 collective-permute-start.7
  95.6 3.1 %collective-permute-start.8 = (bf16[8,264,128]{2,1,0:T(8,128)(2,1)S(1)}, bf16[8,264,128]{2,1,0:T(8,128)(2,1)S(1)}, u32[]{:S(2)}, u32[]{:S(2)}) collective-permute-start(bf16[8,264,128]{2,1,0:T(8,128)(2,1)S(1)} %copy-done.10), channel_id=1, source_target_pairs={{0,16},{1,17},{2,18},{3,19},{4,20},{5,21},{6,22},{7,23},{8,24},{9,... | collective-permute-start | bytes 1622024 | tf_op jit(solution)/shard_map/ppermute | solution.py:396
  98.7 1.3 collective-permute-start.9
  100.1 0.2 slice_reduce_fusion
  100.3 0.2 convert_reduce_fusion
  100.5 0.7 select_reduce_fusion
  101.1 20.2 %collective-permute-done.7.refs_4_ = bf16[8,264,128]{2,1,0:T(8,128)(2,1)S(1)} collective-permute-done((bf16[8,264,128]{2,1,0:T(8,128)(2,1)}, bf16[8,264,128]{2,1,0:T(8,128)(2,1)S(1)}, u32[]{:S(2)}, u32[]{:S(2)}) %collective-permute-start.7) | collective-permute-done | bytes 540704 | tf_op jit(solution)/shard_map/ppermute | solution.py:396
  121.3 14.4 %collective-permute-done.9.refs_6_ = bf16[8,264,128]{2,1,0:T(8,128)(2,1)S(1)} collective-permute-done((bf16[8,264,128]{2,1,0:T(8,128)(2,1)S(1)}, bf16[8,264,128]{2,1,0:T(8,128)(2,1)S(1)}, u32[]{:S(2)}, u32[]{:S(2)}) %collective-permute-start.9) | collective-permute-done | bytes 540704 | tf_op jit(solution)/shard_map/ppermute | solution.py:396
  135.8 0.8 copy-done.6
  136.6 5.5 %place.1 = (bf16[2048,4096]{1,0:T(8,128)(2,1)}, bf16[2048,4096]{1,0:T(8,128)(2,1)}, f32[4,1,128]{2,1,0:T(1,128)}) custom-call(s32[32,128]{1,0:T(8,128)} %bitcast.41, s32[32]{0:T(128)} %get-tuple-element.58.refs_1_, s32[32]{0:T(128)} %get-tuple-element.57.refs_2_, bf16[8,264,128]{2,1,0:T(8,128)(2,1)} %copy-done.3, ...), custom_call_target="tpu_custom_call", output_to_operand_aliasing={{0}: (7, {}), {1}: (8, {})} | custom-call | tf_op jit(solution)/shard_map/place/pallas_call | solution.py:529
  142.2 1.5 add_convert_fusion.2
  143.7 0.6 collective-permute-start.18
  144.2 1.7 collective-permute-start.19
  145.9 1.3 collective-permute-start.20
  147.2 0.3 add_convert_fusion.5
  147.5 0.6 collective-permute-start.11
  148.1 1.7 collective-permute-start.12
  149.8 3.1 %collective-permute-done.18 = bf16[4,32,1024]{2,1,0:T(8,128)(2,1)S(1)} collective-permute-done((bf16[4,32,1024]{2,1,0:T(8,128)(2,1)S(1)}, bf16[4,32,1024]{2,1,0:T(8,128)(2,1)S(1)}, u32[]{:S(2)}, u32[]{:S(2)}) %collective-permute-start.18) | collective-permute-done | bytes 262176 | tf_op jit(solution)/shard_map/ppermute | solution.py:396
  152.9 1.6 collective-permute-start.13
  154.6 4.5 %collective-permute-done.19 = bf16[4,32,1024]{2,1,0:T(8,128)(2,1)S(1)} collective-permute-done((bf16[4,32,1024]{2,1,0:T(8,128)(2,1)S(1)}, bf16[4,32,1024]{2,1,0:T(8,128)(2,1)S(1)}, u32[]{:S(2)}, u32[]{:S(2)}) %collective-permute-start.19) | collective-permute-done | bytes 262176 | tf_op jit(solution)/shard_map/ppermute | solution.py:396
  159.0 1.2 fusion.8
  160.2 11.1 %collective-permute-start.21 = (bf16[32,1024]{1,0:T(8,128)(2,1)S(1)}, bf16[32,1024]{1,0:T(8,128)(2,1)S(1)}, u32[]{:S(2)}, u32[]{:S(2)}) collective-permute-start(bf16[32,1024]{1,0:T(8,128)(2,1)S(1)} %get-tuple-element.101), channel_id=1, source_target_pairs={{0,8},{1,9},{2,10},{3,11},{4,12},{5,13},{6,14},{7,15},{8,0},{9,1},... | collective-permute-start | bytes 196616 | tf_op jit(solution)/shard_map/ppermute | solution.py:396
  171.3 1.7 collective-permute-start.22
  173.0 1.4 collective-permute-start.23
  174.4 0.2 fusion.9
  174.6 5.0 %collective-permute-start.14 = (bf16[32,1024]{1,0:T(8,128)(2,1)S(1)}, bf16[32,1024]{1,0:T(8,128)(2,1)S(1)}, u32[]{:S(2)}, u32[]{:S(2)}) collective-permute-start(bf16[32,1024]{1,0:T(8,128)(2,1)S(1)} %get-tuple-element.104), channel_id=1, source_target_pairs={{0,8},{1,9},{2,10},{3,11},{4,12},{5,13},{6,14},{7,15},{8,0},{9,1},... | collective-permute-start | bytes 196616 | tf_op jit(solution)/shard_map/ppermute | solution.py:396
  179.6 1.7 collective-permute-start.15
  181.4 1.4 collective-permute-start.16
  182.8 0.7 fusion.2
  183.5 1.3 collective-permute-done.15
  184.8 2.8 %collective-permute-done.16 = bf16[32,1024]{1,0:T(8,128)(2,1)S(1)} collective-permute-done((bf16[32,1024]{1,0:T(8,128)(2,1)S(1)}, bf16[32,1024]{1,0:T(8,128)(2,1)S(1)}, u32[]{:S(2)}, u32[]{:S(2)}) %collective-permute-start.16) | collective-permute-done | bytes 65568 | tf_op jit(solution)/shard_map/ppermute | solution.py:396
  187.6 0.7 fusion.5
  (38 shorter events, 0.1 us)
Async XLA Ops:
  2.0 14.4 %all-to-all-start = ((s32[32,1,128]{2,1,0:T(1,128)}), s32[32,1,128]{2,1,0:T(1,128)S(1)}, u32[]{:S(2)}, u32[]{:S(2)}) async-start(s32[32,1,128]{2,1,0:T(1,128)} %bitcast.43), calls=%async_computation | async-start | bytes 32768 | tf_op jit(solution)/shard_map/all_to_all | solution.py:32
  16.4 0.6 copy-start.7
  19.8 55.0 %all-to-all-start.1 = ((bf16[32,2,128,128]{3,2,1,0:T(8,128)(2,1)}), bf16[32,2,128,128]{3,2,1,0:T(8,128)(2,1)S(1)}, u32[]{:S(2)}, u32[]{:S(2)}) async-start(bf16[32,2,128,128]{3,2,1,0:T(8,128)(2,1)} %pick_modes.1), calls=%async_computation.1 | async-start | bytes 4194304 | tf_op jit(solution)/shard_map/all_to_all | solution.py:32
  32.1 16.6 %collective-permute-start = (bf16[4,264,128]{2,1,0:T(8,128)(2,1)}, bf16[4,264,128]{2,1,0:T(8,128)(2,1)}, u32[]{:S(2)}, u32[]{:S(2)}) collective-permute-start(bf16[4,264,128]{2,1,0:T(8,128)(2,1)} %get-tuple-element.32), channel_id=1, source_target_pairs={{0,1},{1,0},{2,3},{3,2},{4,5},{5,4},{6,7},{7,6},{8,9},{9,8},{10,11... | collective-permute-start | bytes 811016 | tf_op jit(solution)/shard_map/ppermute | solution.py:396
  32.2 20.7 %collective-permute-start.1 = (bf16[4,264,128]{2,1,0:T(8,128)(2,1)}, bf16[4,264,128]{2,1,0:T(8,128)(2,1)}, u32[]{:S(2)}, u32[]{:S(2)}) collective-permute-start(bf16[4,264,128]{2,1,0:T(8,128)(2,1)} %get-tuple-element.33), channel_id=1, source_target_pairs={{0,2},{1,3},{2,0},{3,1},{4,6},{5,7},{6,4},{7,5},{8,10},{9,11},{10,... | collective-permute-start | bytes 811016 | tf_op jit(solution)/shard_map/ppermute | solution.py:396
  33.9 23.0 %collective-permute-start.2 = (bf16[4,264,128]{2,1,0:T(8,128)(2,1)}, bf16[4,264,128]{2,1,0:T(8,128)(2,1)S(1)}, u32[]{:S(2)}, u32[]{:S(2)}) collective-permute-start(bf16[4,264,128]{2,1,0:T(8,128)(2,1)} %get-tuple-element.34), channel_id=1, source_target_pairs={{0,3},{1,2},{2,1},{3,0},{4,7},{5,6},{6,5},{7,4},{8,11},{9,10},{10,... | collective-permute-start | bytes 811016 | tf_op jit(solution)/shard_map/ppermute | solution.py:396
  34.0 23.6 %collective-permute-start.3 = (bf16[4,264,128]{2,1,0:T(8,128)(2,1)}, bf16[4,264,128]{2,1,0:T(8,128)(2,1)S(1)}, u32[]{:S(2)}, u32[]{:S(2)}) collective-permute-start(bf16[4,264,128]{2,1,0:T(8,128)(2,1)} %get-tuple-element.35), channel_id=1, source_target_pairs={{0,4},{1,5},{2,6},{3,7},{4,0},{5,1},{6,2},{7,3},{8,12},{9,13},{10,... | collective-permute-start | bytes 811016 | tf_op jit(solution)/shard_map/ppermute | solution.py:396
  35.6 37.0 %collective-permute-start.4 = (bf16[4,264,128]{2,1,0:T(8,128)(2,1)}, bf16[4,264,128]{2,1,0:T(8,128)(2,1)S(1)}, u32[]{:S(2)}, u32[]{:S(2)}) collective-permute-start(bf16[4,264,128]{2,1,0:T(8,128)(2,1)} %get-tuple-element.36), channel_id=1, source_target_pairs={{0,5},{1,4},{2,7},{3,6},{4,1},{5,0},{6,3},{7,2},{8,13},{9,12},{10,... | collective-permute-start | bytes 811016 | tf_op jit(solution)/shard_map/ppermute | solution.py:396
  48.6 24.7 %collective-permute-start.5 = (bf16[4,264,128]{2,1,0:T(8,128)(2,1)}, bf16[4,264,128]{2,1,0:T(8,128)(2,1)S(1)}, u32[]{:S(2)}, u32[]{:S(2)}) collective-permute-start(bf16[4,264,128]{2,1,0:T(8,128)(2,1)} %get-tuple-element.37), channel_id=1, source_target_pairs={{0,6},{1,7},{2,4},{3,5},{4,2},{5,3},{6,0},{7,1},{8,14},{9,15},{10,... | collective-permute-start | bytes 811016 | tf_op jit(solution)/shard_map/ppermute | solution.py:396
  53.0 21.1 %collective-permute-start.6 = (bf16[4,264,128]{2,1,0:T(8,128)(2,1)}, bf16[4,264,128]{2,1,0:T(8,128)(2,1)S(1)}, u32[]{:S(2)}, u32[]{:S(2)}) collective-permute-start(bf16[4,264,128]{2,1,0:T(8,128)(2,1)} %get-tuple-element.38), channel_id=1, source_target_pairs={{0,7},{1,6},{2,5},{3,4},{4,3},{5,2},{6,1},{7,0},{8,15},{9,14},{10,... | collective-permute-start | bytes 811016 | tf_op jit(solution)/shard_map/ppermute | solution.py:396
  74.8 19.9 %copy-start.3 = (bf16[8,264,128]{2,1,0:T(8,128)(2,1)}, bf16[8,264,128]{2,1,0:T(8,128)(2,1)S(1)}, u32[]{:S(2)}) copy-start(bf16[8,264,128]{2,1,0:T(8,128)(2,1)S(1)} %get-tuple-element.72.refs_3_) | copy-start | bytes 1622020
  74.8 1.4 copy-start
  88.6 7.0 %copy-start.10 = (bf16[8,264,128]{2,1,0:T(8,128)(2,1)S(1)}, bf16[8,264,128]{2,1,0:T(8,128)(2,1)}, u32[]{:S(2)}) copy-start(bf16[8,264,128]{2,1,0:T(8,128)(2,1)} %get-tuple-element.41) | copy-start | bytes 1622020
  88.6 10.2 %copy-start.9 = (bf16[8,264,128]{2,1,0:T(8,128)(2,1)S(1)}, bf16[8,264,128]{2,1,0:T(8,128)(2,1)}, u32[]{:S(2)}) copy-start(bf16[8,264,128]{2,1,0:T(8,128)(2,1)} %get-tuple-element.42) | copy-start | bytes 1622020
  88.6 11.5 %copy-start.8 = (s32[32,1,128]{2,1,0:T(1,128)S(1)}, s32[32,1,128]{2,1,0:T(1,128)}, u32[]{:S(2)}) copy-start(s32[32,1,128]{2,1,0:T(1,128)} %copy-done.7) | copy-start | bytes 49156
  94.6 47.5 %collective-permute-start.17 = (bf16[16,32,1024]{2,1,0:T(8,128)(2,1)}, bf16[16,32,1024]{2,1,0:T(8,128)(2,1)}, u32[]{:S(2)}, u32[]{:S(2)}) collective-permute-start(bf16[16,32,1024]{2,1,0:T(8,128)(2,1)} %get-tuple-element.55), channel_id=1, source_target_pairs={{0,1},{1,0},{2,3},{3,2},{4,5},{5,4},{6,7},{7,6},{8,9},{9,8},{10,11... | collective-permute-start | bytes 3145736 | tf_op jit(solution)/shard_map/ppermute | solution.py:396
  94.8 52.4 %collective-permute-start.10 = (bf16[16,32,1024]{2,1,0:T(8,128)(2,1)}, bf16[16,32,1024]{2,1,0:T(8,128)(2,1)S(1)}, u32[]{:S(2)}, u32[]{:S(2)}) collective-permute-start(bf16[16,32,1024]{2,1,0:T(8,128)(2,1)} %get-tuple-element.50), channel_id=1, source_target_pairs={{0,1},{1,0},{2,3},{3,2},{4,5},{5,4},{6,7},{7,6},{8,9},{9,8},{10,11... | collective-permute-start | bytes 3145736 | tf_op jit(solution)/shard_map/ppermute | solution.py:396
  95.2 26.1 %collective-permute-start.7 = (bf16[8,264,128]{2,1,0:T(8,128)(2,1)}, bf16[8,264,128]{2,1,0:T(8,128)(2,1)S(1)}, u32[]{:S(2)}, u32[]{:S(2)}) collective-permute-start(bf16[8,264,128]{2,1,0:T(8,128)(2,1)} %get-tuple-element.71), channel_id=1, source_target_pairs={{0,8},{1,9},{2,10},{3,11},{4,12},{5,13},{6,14},{7,15},{8,0},{9,1},... | collective-permute-start | bytes 1622024 | tf_op jit(solution)/shard_map/ppermute | solution.py:396
  95.6 25.7 %collective-permute-start.8 = (bf16[8,264,128]{2,1,0:T(8,128)(2,1)S(1)}, bf16[8,264,128]{2,1,0:T(8,128)(2,1)S(1)}, u32[]{:S(2)}, u32[]{:S(2)}) collective-permute-start(bf16[8,264,128]{2,1,0:T(8,128)(2,1)S(1)} %copy-done.10), channel_id=1, source_target_pairs={{0,16},{1,17},{2,18},{3,19},{4,20},{5,21},{6,22},{7,23},{8,24},{9,... | collective-permute-start | bytes 1622024 | tf_op jit(solution)/shard_map/ppermute | solution.py:396
  98.7 37.0 %collective-permute-start.9 = (bf16[8,264,128]{2,1,0:T(8,128)(2,1)S(1)}, bf16[8,264,128]{2,1,0:T(8,128)(2,1)S(1)}, u32[]{:S(2)}, u32[]{:S(2)}) collective-permute-start(bf16[8,264,128]{2,1,0:T(8,128)(2,1)S(1)} %copy-done.9), channel_id=1, source_target_pairs={{0,24},{1,25},{2,26},{3,27},{4,28},{5,29},{6,30},{7,31},{8,16},{9,... | collective-permute-start | bytes 1622024 | tf_op jit(solution)/shard_map/ppermute | solution.py:396
  121.3 14.5 %copy-start.4 = (bf16[8,264,128]{2,1,0:T(8,128)(2,1)}, bf16[8,264,128]{2,1,0:T(8,128)(2,1)S(1)}, u32[]{:S(2)}) copy-start(bf16[8,264,128]{2,1,0:T(8,128)(2,1)S(1)} %collective-permute-done.7.refs_4_) | copy-start | bytes 1622020
  121.3 14.5 %copy-start.5 = (bf16[8,264,128]{2,1,0:T(8,128)(2,1)}, bf16[8,264,128]{2,1,0:T(8,128)(2,1)S(1)}, u32[]{:S(2)}) copy-start(bf16[8,264,128]{2,1,0:T(8,128)(2,1)S(1)} %collective-permute-done.8.refs_5_) | copy-start | bytes 1622020
  135.8 0.8 copy-start.6
  136.6 5.6 %copy-start.2 = (f32[16,32,1024]{2,1,0:T(8,128)S(1)}, f32[16,32,1024]{2,1,0:T(8,128)}, u32[]{:S(2)}) copy-start(f32[16,32,1024]{2,1,0:T(8,128)} %get-tuple-element.54) | copy-start | bytes 6291460
  142.1 5.1 %copy-start.1 = (f32[16,32,1024]{2,1,0:T(8,128)S(1)}, f32[16,32,1024]{2,1,0:T(8,128)}, u32[]{:S(2)}) copy-start(f32[16,32,1024]{2,1,0:T(8,128)} %get-tuple-element.49) | copy-start | bytes 6291460
  143.7 9.2 %collective-permute-start.18 = (bf16[4,32,1024]{2,1,0:T(8,128)(2,1)S(1)}, bf16[4,32,1024]{2,1,0:T(8,128)(2,1)S(1)}, u32[]{:S(2)}, u32[]{:S(2)}) collective-permute-start(bf16[4,32,1024]{2,1,0:T(8,128)(2,1)S(1)} %get-tuple-element.63), channel_id=1, source_target_pairs={{0,2},{1,3},{2,0},{3,1},{4,6},{5,7},{6,4},{7,5},{8,10},{9,11},{10,... | collective-permute-start | bytes 786440 | tf_op jit(solution)/shard_map/ppermute | solution.py:396
  144.2 14.8 %collective-permute-start.19 = (bf16[4,32,1024]{2,1,0:T(8,128)(2,1)S(1)}, bf16[4,32,1024]{2,1,0:T(8,128)(2,1)S(1)}, u32[]{:S(2)}, u32[]{:S(2)}) collective-permute-start(bf16[4,32,1024]{2,1,0:T(8,128)(2,1)S(1)} %get-tuple-element.65), channel_id=1, source_target_pairs={{0,4},{1,5},{2,6},{3,7},{4,0},{5,1},{6,2},{7,3},{8,12},{9,13},{10,... | collective-permute-start | bytes 786440 | tf_op jit(solution)/shard_map/ppermute | solution.py:396
  145.9 13.1 %collective-permute-start.20 = (bf16[4,32,1024]{2,1,0:T(8,128)(2,1)S(1)}, bf16[4,32,1024]{2,1,0:T(8,128)(2,1)S(1)}, u32[]{:S(2)}, u32[]{:S(2)}) collective-permute-start(bf16[4,32,1024]{2,1,0:T(8,128)(2,1)S(1)} %get-tuple-element.64), channel_id=1, source_target_pairs={{0,6},{1,7},{2,4},{3,5},{4,2},{5,3},{6,0},{7,1},{8,14},{9,15},{10,... | collective-permute-start | bytes 786440 | tf_op jit(solution)/shard_map/ppermute | solution.py:396
  147.5 25.5 %collective-permute-start.11 = (bf16[4,32,1024]{2,1,0:T(8,128)(2,1)S(1)}, bf16[4,32,1024]{2,1,0:T(8,128)(2,1)S(1)}, u32[]{:S(2)}, u32[]{:S(2)}) collective-permute-start(bf16[4,32,1024]{2,1,0:T(8,128)(2,1)S(1)} %get-tuple-element.66), channel_id=1, source_target_pairs={{0,2},{1,3},{2,0},{3,1},{4,6},{5,7},{6,4},{7,5},{8,10},{9,11},{10,... | collective-permute-start | bytes 786440 | tf_op jit(solution)/shard_map/ppermute | solution.py:396
  148.1 26.3 %collective-permute-start.12 = (bf16[4,32,1024]{2,1,0:T(8,128)(2,1)S(1)}, bf16[4,32,1024]{2,1,0:T(8,128)(2,1)S(1)}, u32[]{:S(2)}, u32[]{:S(2)}) collective-permute-start(bf16[4,32,1024]{2,1,0:T(8,128)(2,1)S(1)} %get-tuple-element.68), channel_id=1, source_target_pairs={{0,4},{1,5},{2,6},{3,7},{4,0},{5,1},{6,2},{7,3},{8,12},{9,13},{10,... | collective-permute-start | bytes 786440 | tf_op jit(solution)/shard_map/ppermute | solution.py:396
  152.9 21.5 %collective-permute-start.13 = (bf16[4,32,1024]{2,1,0:T(8,128)(2,1)S(1)}, bf16[4,32,1024]{2,1,0:T(8,128)(2,1)S(1)}, u32[]{:S(2)}, u32[]{:S(2)}) collective-permute-start(bf16[4,32,1024]{2,1,0:T(8,128)(2,1)S(1)} %get-tuple-element.67), channel_id=1, source_target_pairs={{0,6},{1,7},{2,4},{3,5},{4,2},{5,3},{6,0},{7,1},{8,14},{9,15},{10,... | collective-permute-start | bytes 786440 | tf_op jit(solution)/shard_map/ppermute | solution.py:396
  160.2 21.2 %collective-permute-start.21 = (bf16[32,1024]{1,0:T(8,128)(2,1)S(1)}, bf16[32,1024]{1,0:T(8,128)(2,1)S(1)}, u32[]{:S(2)}, u32[]{:S(2)}) collective-permute-start(bf16[32,1024]{1,0:T(8,128)(2,1)S(1)} %get-tuple-element.101), channel_id=1, source_target_pairs={{0,8},{1,9},{2,10},{3,11},{4,12},{5,13},{6,14},{7,15},{8,0},{9,1},... | collective-permute-start | bytes 196616 | tf_op jit(solution)/shard_map/ppermute | solution.py:396
  171.3 11.4 %collective-permute-start.22 = (bf16[32,1024]{1,0:T(8,128)(2,1)S(1)}, bf16[32,1024]{1,0:T(8,128)(2,1)S(1)}, u32[]{:S(2)}, u32[]{:S(2)}) collective-permute-start(bf16[32,1024]{1,0:T(8,128)(2,1)S(1)} %get-tuple-element.103), channel_id=1, source_target_pairs={{0,16},{1,17},{2,18},{3,19},{4,20},{5,21},{6,22},{7,23},{8,24},{9,... | collective-permute-start | bytes 196616 | tf_op jit(solution)/shard_map/ppermute | solution.py:396
  173.0 9.8 %collective-permute-start.23 = (bf16[32,1024]{1,0:T(8,128)(2,1)S(1)}, bf16[32,1024]{1,0:T(8,128)(2,1)S(1)}, u32[]{:S(2)}, u32[]{:S(2)}) collective-permute-start(bf16[32,1024]{1,0:T(8,128)(2,1)S(1)} %get-tuple-element.102), channel_id=1, source_target_pairs={{0,24},{1,25},{2,26},{3,27},{4,28},{5,29},{6,30},{7,31},{8,16},{9,... | collective-permute-start | bytes 196616 | tf_op jit(solution)/shard_map/ppermute | solution.py:396
  174.6 8.8 %collective-permute-start.14 = (bf16[32,1024]{1,0:T(8,128)(2,1)S(1)}, bf16[32,1024]{1,0:T(8,128)(2,1)S(1)}, u32[]{:S(2)}, u32[]{:S(2)}) collective-permute-start(bf16[32,1024]{1,0:T(8,128)(2,1)S(1)} %get-tuple-element.104), channel_id=1, source_target_pairs={{0,8},{1,9},{2,10},{3,11},{4,12},{5,13},{6,14},{7,15},{8,0},{9,1},... | collective-permute-start | bytes 196616 | tf_op jit(solution)/shard_map/ppermute | solution.py:396
  179.6 5.2 %collective-permute-start.15 = (bf16[32,1024]{1,0:T(8,128)(2,1)S(1)}, bf16[32,1024]{1,0:T(8,128)(2,1)S(1)}, u32[]{:S(2)}, u32[]{:S(2)}) collective-permute-start(bf16[32,1024]{1,0:T(8,128)(2,1)S(1)} %get-tuple-element.106), channel_id=1, source_target_pairs={{0,16},{1,17},{2,18},{3,19},{4,20},{5,21},{6,22},{7,23},{8,24},{9,... | collective-permute-start | bytes 196616 | tf_op jit(solution)/shard_map/ppermute | solution.py:396
  181.4 6.2 %collective-permute-start.16 = (bf16[32,1024]{1,0:T(8,128)(2,1)S(1)}, bf16[32,1024]{1,0:T(8,128)(2,1)S(1)}, u32[]{:S(2)}, u32[]{:S(2)}) collective-permute-start(bf16[32,1024]{1,0:T(8,128)(2,1)S(1)} %get-tuple-element.105), channel_id=1, source_target_pairs={{0,24},{1,25},{2,26},{3,27},{4,28},{5,29},{6,30},{7,31},{8,16},{9,... | collective-permute-start | bytes 196616 | tf_op jit(solution)/shard_map/ppermute | solution.py:396
